TPU v7x, 32 devices: a whole 2x2x4 slice. The times are simulated.
32 devices in a mesh: fsdp: 2 (over x), ctx: 16 (over z, y, core).
Axes of the slice: x: 2, y: 2, z: 4, core: 2. Of those that a mesh axis runs over, the one named last changes fastest.
Arguments:
- tokens: bfloat16 [2, 2048, 1024], P('fsdp', 'ctx'), may hold values from -6 to 6
- cotangent: bfloat16 [2, 2048, 1024], P('fsdp', 'ctx'), may hold values from -6 to 6
- pair_of: int32 [16], replicated, may hold values from 0 to 15, each once
- prenorm_one: bfloat16 [1024], P(('fsdp', 'ctx')), may hold values from 0.5 to 1.5
- query_one: bfloat16 [1024, 1024], P(('fsdp', 'ctx')), may hold values from -0.1875 to 0.1875
- keys_one: bfloat16 [1024, 1024], P(('fsdp', 'ctx')), may hold values from -0.1875 to 0.1875
- values_one: bfloat16 [1024, 1024], P(('fsdp', 'ctx')), may hold values from -0.1875 to 0.1875
- outproj_one: bfloat16 [1024, 1024], P(('fsdp', 'ctx')), may hold values from -2 to 2
- midnorm_one: bfloat16 [1024], P(('fsdp', 'ctx')), may hold values from 0.5 to 1.5
- gates_one: bfloat16 [1024, 2816], P(('fsdp', 'ctx')), may hold values from -0.1875 to 0.1875
- upproj_one: bfloat16 [1024, 2816], P(('fsdp', 'ctx')), may hold values from -0.1875 to 0.1875
- downproj_one: bfloat16 [2816, 1024], P(('fsdp', 'ctx')), may hold values from -0.109375 to 0.109375
- prenorm_two: bfloat16 [1024], P(('fsdp', 'ctx')), may hold values from 0.5 to 1.5
- query_two: bfloat16 [1024, 1024], P(('fsdp', 'ctx')), may hold values from -0.1875 to 0.1875
- keys_two: bfloat16 [1024, 1024], P(('fsdp', 'ctx')), may hold values from -0.1875 to 0.1875
- values_two: bfloat16 [1024, 1024], P(('fsdp', 'ctx')), may hold values from -0.1875 to 0.1875
- outproj_two: bfloat16 [1024, 1024], P(('fsdp', 'ctx')), may hold values from -2 to 2
- midnorm_two: bfloat16 [1024], P(('fsdp', 'ctx')), may hold values from 0.5 to 1.5
- gates_two: bfloat16 [1024, 2816], P(('fsdp', 'ctx')), may hold values from -0.1875 to 0.1875
- upproj_two: bfloat16 [1024, 2816], P(('fsdp', 'ctx')), may hold values from -0.1875 to 0.1875
- downproj_two: bfloat16 [2816, 1024], P(('fsdp', 'ctx')), may hold values from -0.109375 to 0.109375
Outputs:
- output: bfloat16 [2, 2048, 1024], P('fsdp', 'ctx')
- tokens_grad: bfloat16 [2, 2048, 1024], P('fsdp', 'ctx')
- prenorm_one_grad: float32 [1024], P(('fsdp', 'ctx'))
- query_one_grad: float32 [1024, 1024], P(('fsdp', 'ctx'))
- keys_one_grad: float32 [1024, 1024], P(('fsdp', 'ctx'))
- values_one_grad: float32 [1024, 1024], P(('fsdp', 'ctx'))
- outproj_one_grad: float32 [1024, 1024], P(('fsdp', 'ctx'))
- midnorm_one_grad: float32 [1024], P(('fsdp', 'ctx'))
- gates_one_grad: float32 [1024, 2816], P(('fsdp', 'ctx'))
- upproj_one_grad: float32 [1024, 2816], P(('fsdp', 'ctx'))
- downproj_one_grad: float32 [2816, 1024], P(('fsdp', 'ctx'))
- prenorm_two_grad: float32 [1024], P(('fsdp', 'ctx'))
- query_two_grad: float32 [1024, 1024], P(('fsdp', 'ctx'))
- keys_two_grad: float32 [1024, 1024], P(('fsdp', 'ctx'))
- values_two_grad: float32 [1024, 1024], P(('fsdp', 'ctx'))
- outproj_two_grad: float32 [1024, 1024], P(('fsdp', 'ctx'))
- midnorm_two_grad: float32 [1024], P(('fsdp', 'ctx'))
- gates_two_grad: float32 [1024, 2816], P(('fsdp', 'ctx'))
- upproj_two_grad: float32 [1024, 2816], P(('fsdp', 'ctx'))
- downproj_two_grad: float32 [2816, 1024], P(('fsdp', 'ctx'))
Inputs may be any that keep to these rules, and one draw needn't show every extreme that they name: pair_of is a permutation of the ctx devices: ctx device j holds, in its first 64 rows, causal block pair_of[j] and, in the other 64, block 31 - pair_of[j].
All inputs are finite; a program needn't handle non-finite values.
Results may differ from a plain program's by a relative error of at most 0.023.
Values may be sent and summed in bfloat16 or wider, within the bound.
A program may use at most 384 MiB of HBM per device.

v0:
```python
import math

import jax
import jax.numpy as jnp
from jax import lax
from jax.sharding import PartitionSpec as P

HEADS = 16
HD = 64


NORM_EPS = 1e-05
NEG_FILL = -1e30


def block_size(total_rows):
    size_now = 512
    while total_rows % size_now:
        size_now //= 2
    return size_now


def row_norm(hidden):
    inverse = lax.rsqrt(jnp.mean(hidden * hidden, axis=-1, keepdims=True) + NORM_EPS)
    return (hidden * inverse, inverse)


def norm_back(grad_normed, normed, inverse):
    return inverse * (grad_normed - normed * jnp.mean(grad_normed * normed, axis=-1, keepdims=True))


def rope_tables(positions, head_size):
    half_size = head_size // 2
    freqs = jnp.exp(
        jnp.arange(half_size, dtype=jnp.float32) * (-2.0 * math.log(10000.0) / head_size)
    )
    angles = positions.astype(jnp.float32)[:, None] * freqs[None, :]
    return (jnp.cos(angles), jnp.sin(angles))


def rotate(values_in, cosine, sine):
    half_size = values_in.shape[-1] // 2
    first_half = values_in[..., :half_size]
    second_half = values_in[..., half_size:]
    cos_rows = cosine[:, None, :]
    sin_rows = sine[:, None, :]
    return jnp.concatenate(
        [
            first_half * cos_rows - second_half * sin_rows,
            second_half * cos_rows + first_half * sin_rows,
        ],
        axis=-1,
    )


def unrotate(grads_in, cosine, sine):
    half_size = grads_in.shape[-1] // 2
    first_half = grads_in[..., :half_size]
    second_half = grads_in[..., half_size:]
    cos_rows = cosine[:, None, :]
    sin_rows = sine[:, None, :]
    return jnp.concatenate(
        [
            first_half * cos_rows + second_half * sin_rows,
            second_half * cos_rows - first_half * sin_rows,
        ],
        axis=-1,
    )


def left_product(left, right):
    return lax.dot_general(
        left, right, (((0,), (0,)), ((), ())), preferred_element_type=jnp.float32
    )


def right_product(left, right):
    return lax.dot_general(
        left, right, (((1,), (1,)), ((), ())), preferred_element_type=jnp.float32
    )


def storage_positions(pair_of, seq_dev):
    devices = pair_of.shape[0]
    rows_all = jnp.arange(devices * seq_dev, dtype=jnp.int32)
    owner = rows_all // seq_dev
    local_row = rows_all % seq_dev
    half_rows = seq_dev // 2
    picked = jnp.sum(
        jnp.where(
            owner[:, None] == jnp.arange(devices, dtype=jnp.int32)[None, :], pair_of[None, :], 0
        ),
        axis=1,
    )
    block_id = jnp.where(local_row < half_rows, picked, 2 * devices - 1 - picked)
    return block_id * half_rows + local_row % half_rows


def head_scores(queries, keys_flat, query_pos, key_pos):
    key_heads = keys_flat.reshape(keys_flat.shape[0], queries.shape[1], queries.shape[2])
    scores = jnp.einsum(
        "qhd,khd->hqk", queries, key_heads, preferred_element_type=jnp.float32
    ) * queries.shape[2] ** (-0.5)
    allowed = (key_pos[None, :] <= query_pos[:, None])[None]
    return (jnp.where(allowed, scores, NEG_FILL), allowed)


def make_stats_step(queries, query_pos, pos_all, state_in, key_part):
    size_now = block_size(key_part.shape[0])

    def inner_step(block_no, state_now):
        top_now, total_now = state_now
        offset = block_no * size_now
        key_block = lax.dynamic_slice_in_dim(key_part, offset, size_now, 0)
        key_pos = lax.dynamic_slice_in_dim(pos_all, offset, size_now, 0)
        scores, allowed = head_scores(queries, key_block, query_pos, key_pos)
        new_top = jnp.maximum(top_now, jnp.max(scores, axis=-1))
        total_now = total_now * jnp.exp(top_now - new_top) + jnp.sum(
            jnp.where(allowed, jnp.exp(scores - new_top[..., None]), 0.0), axis=-1
        )
        return (new_top, total_now)

    return lax.fori_loop(0, key_part.shape[0] // size_now, inner_step, state_in)


def make_value_step(queries, log_total, query_pos, pos_all, acc_in, pieces):
    key_part, value_part = pieces
    size_now = block_size(key_part.shape[0])

    def inner_step(block_no, acc_now):
        offset = block_no * size_now
        key_block = lax.dynamic_slice_in_dim(key_part, offset, size_now, 0)
        value_block = lax.dynamic_slice_in_dim(value_part, offset, size_now, 0)
        key_pos = lax.dynamic_slice_in_dim(pos_all, offset, size_now, 0)
        scores, allowed = head_scores(queries, key_block, query_pos, key_pos)
        shares = jnp.exp(scores - log_total[..., None]).astype(jnp.bfloat16)
        value_heads = value_block.reshape(size_now, queries.shape[1], queries.shape[2])
        return acc_now + jnp.einsum(
            "hqk,khd->qhd", shares, value_heads, preferred_element_type=jnp.float32
        )

    return lax.fori_loop(0, key_part.shape[0] // size_now, inner_step, acc_in)


def make_back_step(queries, grad_att, log_total, row_delta, query_pos, pos_all):
    scale_now = queries.shape[2] ** (-0.5)

    def back_step(state_in, pieces, start_row):
        key_part, value_part = pieces
        size_now = block_size(key_part.shape[0])

        def inner_step(block_no, state_now):
            offset = block_no * size_now
            key_block = lax.dynamic_slice_in_dim(key_part, offset, size_now, 0)
            value_block = lax.dynamic_slice_in_dim(value_part, offset, size_now, 0)
            key_pos = lax.dynamic_slice_in_dim(pos_all, offset, size_now, 0)
            scores, allowed = head_scores(queries, key_block, query_pos, key_pos)
            shares = jnp.exp(scores - log_total[..., None])
            value_heads = value_block.reshape(size_now, queries.shape[1], queries.shape[2])
            key_heads = key_block.reshape(size_now, queries.shape[1], queries.shape[2])
            grad_shares = jnp.einsum(
                "qhd,khd->hqk", grad_att, value_heads, preferred_element_type=jnp.float32
            )
            grad_scores = (shares * (grad_shares - row_delta[..., None]) * scale_now).astype(
                jnp.bfloat16
            )
            grad_query = state_now[0] + jnp.einsum(
                "hqk,khd->qhd", grad_scores, key_heads, preferred_element_type=jnp.float32
            )
            return (grad_query,)

        return lax.fori_loop(0, key_part.shape[0] // size_now, inner_step, state_in)

    return back_step


def make_query_step(own_keys, own_values, own_pos, stats_all, pos_all, head_count, head_size):
    scale_now = head_size ** (-0.5)
    value_heads = own_values.reshape(own_values.shape[0], head_count, head_size)

    def query_step(state_in, pieces, start_row):
        query_part, grad_part = pieces
        size_now = block_size(query_part.shape[0])

        def inner_step(block_no, state_now):
            offset = block_no * size_now
            query_block = lax.dynamic_slice_in_dim(query_part, offset, size_now, 0).reshape(
                size_now, head_count, head_size
            )
            grad_block = lax.dynamic_slice_in_dim(grad_part, offset, size_now, 0).reshape(
                size_now, head_count, head_size
            )
            query_pos = lax.dynamic_slice_in_dim(pos_all, offset, size_now, 0)
            log_block = lax.dynamic_slice_in_dim(stats_all[0], offset, size_now, 0).T
            delta_block = lax.dynamic_slice_in_dim(stats_all[1], offset, size_now, 0).T
            scores, allowed = head_scores(query_block, own_keys, query_pos, own_pos)
            shares = jnp.exp(scores - log_block[..., None])
            grad_shares = jnp.einsum(
                "qhd,khd->hqk", grad_block, value_heads, preferred_element_type=jnp.float32
            )
            grad_scores = (shares * (grad_shares - delta_block[..., None]) * scale_now).astype(
                jnp.bfloat16
            )
            key_term = jnp.einsum(
                "hqk,qhd->khd", grad_scores, query_block, preferred_element_type=jnp.float32
            )
            value_term = jnp.einsum(
                "hqk,qhd->khd",
                shares.astype(jnp.bfloat16),
                grad_block,
                preferred_element_type=jnp.float32,
            )
            return (
                state_now[0] + key_term.reshape(key_term.shape[0], -1),
                state_now[1] + value_term.reshape(value_term.shape[0], -1),
            )

        return lax.fori_loop(0, query_part.shape[0] // size_now, inner_step, state_in)

    return query_step


def gather_forward(shards):
    return (
        lax.all_gather(shards[0], ("fsdp", "ctx"), axis=0, tiled=True),
        lax.all_gather(shards[1], ("fsdp", "ctx"), axis=0, tiled=True),
        lax.all_gather(shards[2], ("fsdp", "ctx"), axis=0, tiled=True),
        lax.all_gather(shards[3], ("fsdp", "ctx"), axis=0, tiled=True),
        lax.all_gather(shards[4], ("fsdp", "ctx"), axis=0, tiled=True),
        lax.all_gather(shards[5], ("fsdp", "ctx"), axis=0, tiled=True),
        lax.all_gather(shards[6], ("fsdp", "ctx"), axis=0, tiled=True),
        lax.all_gather(shards[7], ("fsdp", "ctx"), axis=0, tiled=True),
        lax.all_gather(shards[8], ("fsdp", "ctx"), axis=0, tiled=True),
    )


def scatter_grads(grad_terms):
    return (
        lax.psum_scatter(grad_terms[0], ("fsdp", "ctx"), scatter_dimension=0, tiled=True),
        lax.psum_scatter(grad_terms[1], ("fsdp", "ctx"), scatter_dimension=0, tiled=True),
        lax.psum_scatter(grad_terms[2], ("fsdp", "ctx"), scatter_dimension=0, tiled=True),
        lax.psum_scatter(grad_terms[3], ("fsdp", "ctx"), scatter_dimension=0, tiled=True),
        lax.psum_scatter(grad_terms[4], ("fsdp", "ctx"), scatter_dimension=0, tiled=True),
        lax.psum_scatter(grad_terms[5], ("fsdp", "ctx"), scatter_dimension=0, tiled=True),
        lax.psum_scatter(grad_terms[6], ("fsdp", "ctx"), scatter_dimension=0, tiled=True),
        lax.psum_scatter(grad_terms[7], ("fsdp", "ctx"), scatter_dimension=0, tiled=True),
        lax.psum_scatter(grad_terms[8], ("fsdp", "ctx"), scatter_dimension=0, tiled=True),
    )


def forward_layer(hidden, full_layer, first_values, context):
    prenorm, query_w, keys_w, values_w, outproj, midnorm, gates_w, upproj_w, downproj_w = full_layer
    cosine, sine, own_pos, pos_all = context
    rows_n, model_width = hidden.shape
    normed, inverse_a = row_norm(hidden)
    attn_in = (normed * prenorm.astype(jnp.float32)).astype(jnp.bfloat16)
    query_raw = jnp.dot(attn_in, query_w, preferred_element_type=jnp.float32)
    keys_raw = jnp.dot(attn_in, keys_w, preferred_element_type=jnp.float32)
    values_raw = jnp.dot(attn_in, values_w, preferred_element_type=jnp.float32)
    mixed = values_raw if first_values is None else 0.5 * values_raw + 0.5 * first_values
    queries = rotate(query_raw.reshape(rows_n, HEADS, HD), cosine, sine).astype(jnp.bfloat16)
    keys_flat = (
        rotate(keys_raw.reshape(rows_n, HEADS, HD), cosine, sine)
        .reshape(rows_n, model_width)
        .astype(jnp.bfloat16)
    )
    values_flat = mixed.astype(jnp.bfloat16)
    top_start = jnp.full((HEADS, rows_n), NEG_FILL, jnp.float32)
    total_start = jnp.zeros((HEADS, rows_n), jnp.float32)
    top_now, total_now = make_stats_step(
        queries,
        own_pos,
        pos_all,
        (top_start, total_start),
        lax.all_gather(keys_flat, "ctx", axis=0, tiled=True),
    )
    log_total = top_now + jnp.log(total_now)
    att_out = make_value_step(
        queries,
        log_total,
        own_pos,
        pos_all,
        jnp.zeros((rows_n, HEADS, HD), jnp.float32),
        (
            lax.all_gather(keys_flat, "ctx", axis=0, tiled=True),
            lax.all_gather(values_flat, "ctx", axis=0, tiled=True),
        ),
    )
    att_low = att_out.reshape(rows_n, model_width).astype(jnp.bfloat16)
    middle = hidden + jnp.dot(att_low, outproj, preferred_element_type=jnp.float32)
    normed_mid, inverse_b = row_norm(middle)
    mlp_in = (normed_mid * midnorm.astype(jnp.float32)).astype(jnp.bfloat16)
    gate_raw = jnp.dot(mlp_in, gates_w, preferred_element_type=jnp.float32)
    up_proj = jnp.dot(mlp_in, upproj_w, preferred_element_type=jnp.float32)
    inner_act = (jax.nn.silu(gate_raw) * up_proj).astype(jnp.bfloat16)
    result = middle + jnp.dot(inner_act, downproj_w, preferred_element_type=jnp.float32)
    saved = (
        hidden,
        normed,
        inverse_a,
        attn_in,
        queries,
        keys_flat,
        values_flat,
        log_total,
        att_out,
        att_low,
        normed_mid,
        inverse_b,
        mlp_in,
        gate_raw,
        up_proj,
        inner_act,
    )
    return (result, values_raw, saved)


def backward_layer(grad_out, full_layer, saved, value_extra, is_second, context):
    prenorm, query_w, keys_w, values_w, outproj, midnorm, gates_w, upproj_w, downproj_w = full_layer
    (
        hidden,
        normed,
        inverse_a,
        attn_in,
        queries,
        keys_flat,
        values_flat,
        log_total,
        att_out,
        att_low,
        normed_mid,
        inverse_b,
        mlp_in,
        gate_raw,
        up_proj,
        inner_act,
    ) = saved
    cosine, sine, own_pos, pos_all = context
    rows_n, model_width = hidden.shape
    grad_low = grad_out.astype(jnp.bfloat16)
    grad_down = left_product(inner_act, grad_low)
    grad_inner = right_product(grad_low, downproj_w)
    sigma_gate = jax.nn.sigmoid(gate_raw)
    grad_gate = (grad_inner * up_proj * sigma_gate * (1.0 + gate_raw * (1.0 - sigma_gate))).astype(
        jnp.bfloat16
    )
    grad_up = (grad_inner * gate_raw * sigma_gate).astype(jnp.bfloat16)
    grad_gates = left_product(mlp_in, grad_gate)
    grad_upproj = left_product(mlp_in, grad_up)
    grad_mlp = right_product(grad_gate, gates_w) + right_product(grad_up, upproj_w)
    grad_midnorm = jnp.sum(grad_mlp * normed_mid, axis=0)
    grad_middle = grad_out + norm_back(
        grad_mlp * midnorm.astype(jnp.float32), normed_mid, inverse_b
    )
    branch_low = grad_middle.astype(jnp.bfloat16)
    grad_outproj = left_product(att_low, branch_low)
    grad_att = right_product(branch_low, outproj).astype(jnp.bfloat16).reshape(rows_n, HEADS, HD)
    row_delta = jnp.sum(grad_att.astype(jnp.float32) * att_out, axis=-1).T
    query_start = jnp.zeros((rows_n, HEADS, HD), jnp.float32)
    state_start = (query_start,)
    back_fn = make_back_step(queries, grad_att, log_total, row_delta, own_pos, pos_all)
    state_out = back_fn(
        state_start,
        (
            lax.all_gather(keys_flat, "ctx", axis=0, tiled=True),
            lax.all_gather(values_flat, "ctx", axis=0, tiled=True),
        ),
        jnp.int32(0),
    )
    grad_qr = state_out[0]
    stats_all = (
        lax.all_gather(log_total.T, "ctx", axis=0, tiled=True),
        lax.all_gather(row_delta.T, "ctx", axis=0, tiled=True),
    )
    query_fn = make_query_step(keys_flat, values_flat, own_pos, stats_all, pos_all, HEADS, HD)
    flat_start = jnp.zeros((rows_n, model_width), jnp.float32)
    grad_kr, grad_mix = query_fn(
        (flat_start, flat_start),
        (
            lax.all_gather(queries.reshape(rows_n, model_width), "ctx", axis=0, tiled=True),
            lax.all_gather(grad_att.reshape(rows_n, model_width), "ctx", axis=0, tiled=True),
        ),
        jnp.int32(0),
    )
    grad_query = unrotate(grad_qr, cosine, sine).reshape(rows_n, model_width).astype(jnp.bfloat16)
    grad_keys = (
        unrotate(grad_kr.reshape(rows_n, HEADS, HD), cosine, sine)
        .reshape(rows_n, model_width)
        .astype(jnp.bfloat16)
    )
    if is_second:
        grad_values = (0.5 * grad_mix).astype(jnp.bfloat16)
        passed_on = 0.5 * grad_mix
    else:
        grad_values = (grad_mix + value_extra).astype(jnp.bfloat16)
        passed_on = None
    grad_query_w = left_product(attn_in, grad_query)
    grad_keys_w = left_product(attn_in, grad_keys)
    grad_values_w = left_product(attn_in, grad_values)
    grad_attn = (
        right_product(grad_query, query_w)
        + right_product(grad_keys, keys_w)
        + right_product(grad_values, values_w)
    )
    grad_prenorm = jnp.sum(grad_attn * normed, axis=0)
    grad_hidden = grad_middle + norm_back(
        grad_attn * prenorm.astype(jnp.float32), normed, inverse_a
    )
    grad_terms = (
        grad_prenorm,
        grad_query_w,
        grad_keys_w,
        grad_values_w,
        grad_outproj,
        grad_midnorm,
        grad_gates,
        grad_upproj,
        grad_down,
    )
    return (grad_hidden, grad_terms, passed_on)


def local(
    tokens,
    cotangent,
    pair_of,
    prenorm_one,
    query_one,
    keys_one,
    values_one,
    outproj_one,
    midnorm_one,
    gates_one,
    upproj_one,
    downproj_one,
    prenorm_two,
    query_two,
    keys_two,
    values_two,
    outproj_two,
    midnorm_two,
    gates_two,
    upproj_two,
    downproj_two,
):
    seq_dev = tokens.shape[1]
    model_width = tokens.shape[2]
    pos_all = storage_positions(pair_of, seq_dev)
    own_pos = lax.dynamic_slice_in_dim(pos_all, lax.axis_index("ctx") * seq_dev, seq_dev, 0)
    cosine, sine = rope_tables(own_pos, HD)
    context = (cosine, sine, own_pos, pos_all)
    layer_shards = [
        (
            prenorm_one,
            query_one,
            keys_one,
            values_one,
            outproj_one,
            midnorm_one,
            gates_one,
            upproj_one,
            downproj_one,
        ),
        (
            prenorm_two,
            query_two,
            keys_two,
            values_two,
            outproj_two,
            midnorm_two,
            gates_two,
            upproj_two,
            downproj_two,
        ),
    ]
    hidden = tokens.reshape(seq_dev, model_width).astype(jnp.float32)
    first_values = None
    kept_full = []
    kept_saved = []
    for layer_no in range(2):
        full_layer = gather_forward(layer_shards[layer_no])
        hidden, values_raw, saved = forward_layer(hidden, full_layer, first_values, context)
        if layer_no == 0:
            first_values = values_raw
        kept_full.append(full_layer)
        kept_saved.append(saved)
    output = hidden.astype(jnp.bfloat16).reshape(1, seq_dev, model_width)
    grad_now = cotangent.reshape(seq_dev, model_width).astype(jnp.float32)
    value_extra = None
    layer_grads = [None, None]
    for layer_no in (1, 0):
        full_layer = kept_full[layer_no]
        grad_now, grad_terms, passed_on = backward_layer(
            grad_now, full_layer, kept_saved[layer_no], value_extra, layer_no == 1, context
        )
        if layer_no == 1:
            value_extra = passed_on
        layer_grads[layer_no] = scatter_grads(grad_terms)
    tokens_grad = grad_now.astype(jnp.bfloat16).reshape(1, seq_dev, model_width)
    first_grads = layer_grads[0]
    second_grads = layer_grads[1]
    return (
        output,
        tokens_grad,
        first_grads[0],
        first_grads[1],
        first_grads[2],
        first_grads[3],
        first_grads[4],
        first_grads[5],
        first_grads[6],
        first_grads[7],
        first_grads[8],
        second_grads[0],
        second_grads[1],
        second_grads[2],
        second_grads[3],
        second_grads[4],
        second_grads[5],
        second_grads[6],
        second_grads[7],
        second_grads[8],
    )


def solution(mesh):
    placed = (
        P("fsdp", "ctx", None),
        P("fsdp", "ctx", None),
        P(),
        P(("fsdp", "ctx")),
        P(("fsdp", "ctx"), None),
        P(("fsdp", "ctx"), None),
        P(("fsdp", "ctx"), None),
        P(("fsdp", "ctx"), None),
        P(("fsdp", "ctx")),
        P(("fsdp", "ctx"), None),
        P(("fsdp", "ctx"), None),
        P(("fsdp", "ctx"), None),
        P(("fsdp", "ctx")),
        P(("fsdp", "ctx"), None),
        P(("fsdp", "ctx"), None),
        P(("fsdp", "ctx"), None),
        P(("fsdp", "ctx"), None),
        P(("fsdp", "ctx")),
        P(("fsdp", "ctx"), None),
        P(("fsdp", "ctx"), None),
        P(("fsdp", "ctx"), None),
    )
    return jax.shard_map(
        local,
        mesh=mesh,
        in_specs=placed,
        out_specs=(
            P("fsdp", "ctx", None),
            P("fsdp", "ctx", None),
            P(("fsdp", "ctx")),
            P(("fsdp", "ctx"), None),
            P(("fsdp", "ctx"), None),
            P(("fsdp", "ctx"), None),
            P(("fsdp", "ctx"), None),
            P(("fsdp", "ctx")),
            P(("fsdp", "ctx"), None),
            P(("fsdp", "ctx"), None),
            P(("fsdp", "ctx"), None),
            P(("fsdp", "ctx")),
            P(("fsdp", "ctx"), None),
            P(("fsdp", "ctx"), None),
            P(("fsdp", "ctx"), None),
            P(("fsdp", "ctx"), None),
            P(("fsdp", "ctx")),
            P(("fsdp", "ctx"), None),
            P(("fsdp", "ctx"), None),
            P(("fsdp", "ctx"), None),
        ),
        check_vma=False,
    )
```

profile of v0, /device:TPU:0, one launch (start us, length us, event | category | flops | bytes accessed | tf_op | source)
XLA Modules:
  0.0 3421.7 jit_solution(10354348795581430350)
XLA Ops:
  12.8 42.2 %all-reduce.9 = (bf16[1024]{0:T(1024)(128)(2,1)S(1)}, bf16[1024]{0:T(1024)(128)(2,1)S(1)}, bf16[1024]{0:T(1024)(128)(2,1)S(1)}, bf16[1024]{0:T(1024)(128)(2,1)S(1)}) all-reduce(bf16[1024]{0:T(1024)(128)(2,1)S(1)} %dynamic-update-slice, bf16[1024]{0:T(1024)(128)(2,1)S(1)} %dynamic-update-slice.1, ...), channel_id=1, replica_groups=mesh['fsdp'=2,'ctx'=16] {'fsdp','ctx'}, use_global_device_ids=true, to_apply=%add | all-reduce | flops 4096 | bytes 16384
  57.2 13.0 all-gather.27.cloned.1.call-done
  74.7 53.6 %all-gather.23.cloned.1.call-done = bf16[1024,1024]{1,0:T(8,128)(2,1)} async-done(((bf16[32,1024]{1,0:T(8,128)(2,1)}), bf16[1024,1024]{1,0:T(8,128)(2,1)}) %all-gather.23.cloned.1.call-update) | async-done | bytes 2097168 | tf_op jit(solution)/shard_map/all_gather | solution.py:228
  136.3 50.2 %all-gather.31.cloned.1.call-done = bf16[1024,1024]{1,0:T(8,128)(2,1)} async-done(((bf16[32,1024]{1,0:T(8,128)(2,1)}), bf16[1024,1024]{1,0:T(8,128)(2,1)}) %all-gather.31.cloned.1.call-update) | async-done | bytes 2097168 | tf_op jit(solution)/shard_map/all_gather | solution.py:226
  190.3 50.9 %all-gather.29.cloned.1.call-done = bf16[2048,1024]{0,1:T(8,128)(2,1)} async-done(((bf16[128,1024]{0,1:T(8,128)(2,1)}), bf16[2048,1024]{0,1:T(8,128)(2,1)}) %all-gather.29.cloned.1.call-update) | async-done | bytes 4194320 | tf_op jit(solution)/shard_map/all_gather | solution.py:285
  241.2 31.2 while.120
  272.4 20.1 all-gather.25.cloned.1.call-done
  299.1 14.8 while.121
  314.0 36.2 %all-gather.33.cloned.1.call-done = bf16[1024,1024]{1,0:T(8,128)(2,1)} async-done(((bf16[32,1024]{1,0:T(8,128)(2,1)}), bf16[1024,1024]{1,0:T(8,128)(2,1)}) %all-gather.33.cloned.1.call-update) | async-done | bytes 2097168 | tf_op jit(solution)/shard_map/all_gather | solution.py:229
  352.5 66.7 %all-gather.35.cloned.1.call-done = bf16[1024,2816]{1,0:T(8,128)(2,1)} async-done(((bf16[32,2816]{1,0:T(8,128)(2,1)}), bf16[1024,2816]{1,0:T(8,128)(2,1)}) %all-gather.35.cloned.1.call-update) | async-done | bytes 5767184 | tf_op jit(solution)/shard_map/all_gather | solution.py:231
  423.9 64.5 %all-gather.37.cloned.1.call-done = bf16[1024,2816]{1,0:T(8,128)(2,1)} async-done(((bf16[32,2816]{1,0:T(8,128)(2,1)}), bf16[1024,2816]{1,0:T(8,128)(2,1)}) %all-gather.37.cloned.1.call-update) | async-done | bytes 5767184 | tf_op jit(solution)/shard_map/all_gather | solution.py:232
  493.8 63.8 %all-gather.39.cloned.1.call-done = bf16[2816,1024]{1,0:T(8,128)(2,1)} async-done(((bf16[88,1024]{1,0:T(8,128)(2,1)}), bf16[2816,1024]{1,0:T(8,128)(2,1)}) %all-gather.39.cloned.1.call-update) | async-done | bytes 5767184 | tf_op jit(solution)/shard_map/all_gather | solution.py:233
  561.4 54.3 %all-gather.45.cloned.1.call-done = bf16[1024,1024]{1,0:T(8,128)(2,1)} async-done(((bf16[32,1024]{1,0:T(8,128)(2,1)}), bf16[1024,1024]{1,0:T(8,128)(2,1)}) %all-gather.45.cloned.1.call-update) | async-done | bytes 2097168 | tf_op jit(solution)/shard_map/all_gather | solution.py:227
  619.1 54.8 %all-gather.41.cloned.1.call-done = bf16[1024,1024]{1,0:T(8,128)(2,1)} async-done(((bf16[32,1024]{1,0:T(8,128)(2,1)}), bf16[1024,1024]{1,0:T(8,128)(2,1)}) %all-gather.41.cloned.1.call-update) | async-done | bytes 2097168 | tf_op jit(solution)/shard_map/all_gather | solution.py:228
  679.1 52.8 %all-gather.49.cloned.1.call-done = bf16[1024,1024]{1,0:T(8,128)(2,1)} async-done(((bf16[32,1024]{1,0:T(8,128)(2,1)}), bf16[1024,1024]{1,0:T(8,128)(2,1)}) %all-gather.49.cloned.1.call-update) | async-done | bytes 2097168 | tf_op jit(solution)/shard_map/all_gather | solution.py:226
  735.5 51.2 %all-gather.47.cloned.1.call-done = bf16[2048,1024]{0,1:T(8,128)(2,1)} async-done(((bf16[128,1024]{0,1:T(8,128)(2,1)}), bf16[2048,1024]{0,1:T(8,128)(2,1)}) %all-gather.47.cloned.1.call-update) | async-done | bytes 4194320 | tf_op jit(solution)/shard_map/all_gather | solution.py:285
  786.7 34.6 %while.122 = (s32[]{:T(128)}, f32[16,128]{1,0:T(8,128)S(1)}, f32[16,128]{1,0:T(8,128)S(1)}, s32[2048]{0:T(1024)S(1)}, s32[128]{0:T(128)S(1)}, /*index=5*/bf16[20...) while((s32[]{:T(128)}, f32[16,128]{1,0:T(8,128)S(1)}, ...), condition=%wide.region_13.14_spmd.clone, body=%wide.region_10.13_spmd.clone.sunk | while | flops 142682112 | bytes 12106414 | solution.py:123
  821.4 16.8 all-gather.43.cloned.1.call-done
  844.8 20.7 while.123
  866.6 29.4 all-gather.51.cloned.1.call-done
  898.3 66.6 %all-gather.53.cloned.1.call-done = bf16[1024,2816]{1,0:T(8,128)(2,1)} async-done(((bf16[32,2816]{1,0:T(8,128)(2,1)}), bf16[1024,2816]{1,0:T(8,128)(2,1)}) %all-gather.53.cloned.1.call-update) | async-done | bytes 5767184 | tf_op jit(solution)/shard_map/all_gather | solution.py:231
  969.5 64.3 %all-gather.55.cloned.1.call-done = bf16[1024,2816]{1,0:T(8,128)(2,1)} async-done(((bf16[32,2816]{1,0:T(8,128)(2,1)}), bf16[1024,2816]{1,0:T(8,128)(2,1)}) %all-gather.55.cloned.1.call-update) | async-done | bytes 5767184 | tf_op jit(solution)/shard_map/all_gather | solution.py:232
  1038.5 64.3 %all-gather.57.cloned.1.call-done = bf16[2816,1024]{1,0:T(8,128)(2,1)} async-done(((bf16[88,1024]{1,0:T(8,128)(2,1)}), bf16[2816,1024]{1,0:T(8,128)(2,1)}) %all-gather.57.cloned.1.call-update) | async-done | bytes 5767184 | tf_op jit(solution)/shard_map/all_gather | solution.py:233
  1102.9 6.6 multiply_convert_fusion.4
  1122.1 22.7 all_gather.121
  1144.8 39.2 %while.124 = (s32[]{:T(128)}, f32[128,16,64]{0,2,1:T(8,128)}, bf16[2048,1024]{0,1:T(8,128)(2,1)}, s32[2048]{0:T(1024)S(1)}, s32[128]{0:T(128)S(1)}, /*index=5*/b...) while((s32[]{:T(128)}, f32[128,16,64]{0,2,1:T(8,128)}, ...), condition=%wide.region_20.21_spmd.clone, body=%wide.region_19.20_spmd.clone.sunk | while | flops 410320896 | bytes 17455812 | solution.py:172
  1184.0 19.8 all_gather.119
  1203.8 6.6 all-gather.61.cloned.1.call-done
  1210.4 78.5 %while.125 = (s32[]{:T(128)}, f32[128,1024]{0,1:T(8,128)}, f32[128,1024]{0,1:T(8,128)}, bf16[2048,1024]{0,1:T(8,128)(2,1)}, s32[128]{0:T(128)S(1)}, /*index=5*/s...) while((s32[]{:T(128)}, f32[128,1024]{0,1:T(8,128)}, ...), condition=%wide.region_22.23_spmd.clone, body=%wide.region_21.22_spmd.clone.sunk | while | flops 548995072 | bytes 38706020 | solution.py:218
  1238.6 6.5 fusion.328
  1345.5 20.6 all_gather.123
  1366.4 19.3 all_gather.125
  1385.7 77.7 %while.127 = (s32[]{:T(128)}, f32[128,1024]{0,1:T(8,128)}, f32[128,1024]{0,1:T(8,128)}, bf16[2048,1024]{0,1:T(8,128)(2,1)}, s32[128]{0:T(128)S(1)}, /*index=5*/s...) while((s32[]{:T(128)}, f32[128,1024]{0,1:T(8,128)}, ...), condition=%wide.region_29.30_spmd.clone, body=%wide.region_28.29_spmd.clone.sunk | while | flops 548995072 | bytes 38706020 | solution.py:218
  1469.7 39.6 %while.126 = (s32[]{:T(128)}, f32[128,16,64]{0,2,1:T(8,128)}, bf16[2048,1024]{0,1:T(8,128)(2,1)}, s32[2048]{0:T(1024)S(1)}, s32[128]{0:T(128)S(1)}, /*index=5*/b...) while((s32[]{:T(128)}, f32[128,16,64]{0,2,1:T(8,128)}, ...), condition=%wide.region_27.28_spmd.clone, body=%wide.region_26.27_spmd.clone.sunk | while | flops 410320896 | bytes 17455812 | solution.py:172
  1546.7 38.5 %all-reduce.8 = (f32[1024]{0:T(1024)S(1)}, f32[1024]{0:T(1024)S(1)}, f32[1024]{0:T(1024)S(1)}, f32[1024]{0:T(1024)S(1)}) all-reduce(f32[1024]{0:T(1024)S(1)} %get-tuple-element.1746, f32[1024]{0:T(1024)S(1)} %copy-done.83, f32[1024]{0:T(1024)S(1)} %copy-done.84, ...), channel_id=2, replica_groups=mesh['fsdp'=2,'ctx'=16] {'fsdp','ctx'}, use_global_device_ids=true, to_apply=%region_32.33.clone | all-reduce | flops 4096 | bytes 32768
  1588.5 52.1 %reduce-scatter.29.cloned.1.call-done = f32[32,1024]{1,0:T(8,128)} async-done(((f32[1024,1024]{1,0:T(8,128)}), f32[32,1024]{1,0:T(8,128)}) %reduce-scatter.29.cloned.1.call-update) | async-done | bytes 131088 | tf_op jit(solution)/shard_map/reduce_scatter | solution.py:240
  1640.6 140.5 %reduce-scatter.31.cloned.1.call-done = f32[32,1024]{1,0:T(8,128)} async-done(((f32[1024,1024]{1,0:T(8,128)}), f32[32,1024]{1,0:T(8,128)}) %reduce-scatter.31.cloned.1.call-update) | async-done | bytes 131088 | tf_op jit(solution)/shard_map/reduce_scatter | solution.py:241
  1781.0 139.3 %reduce-scatter.21.cloned.1.call-done = f32[32,1024]{1,0:T(8,128)} async-done(((f32[1024,1024]{1,0:T(8,128)}), f32[32,1024]{1,0:T(8,128)}) %reduce-scatter.21.cloned.1.call-update) | async-done | bytes 131088 | tf_op jit(solution)/shard_map/reduce_scatter | solution.py:243
  1920.3 140.6 %reduce-scatter.33.cloned.1.call-done = f32[32,1024]{1,0:T(8,128)} async-done(((f32[1024,1024]{1,0:T(8,128)}), f32[32,1024]{1,0:T(8,128)}) %reduce-scatter.33.cloned.1.call-update) | async-done | bytes 131088 | tf_op jit(solution)/shard_map/reduce_scatter | solution.py:242
  2060.8 154.4 %reduce-scatter.37.cloned.1.call-done = f32[32,2816]{1,0:T(8,128)} async-done(((f32[1024,2816]{1,0:T(8,128)}), f32[32,2816]{1,0:T(8,128)}) %reduce-scatter.37.cloned.1.call-update) | async-done | bytes 360464 | tf_op jit(solution)/shard_map/reduce_scatter | solution.py:245
  2215.3 155.6 %reduce-scatter.39.cloned.1.call-done = f32[32,2816]{1,0:T(8,128)} async-done(((f32[1024,2816]{1,0:T(8,128)}), f32[32,2816]{1,0:T(8,128)}) %reduce-scatter.39.cloned.1.call-update) | async-done | bytes 360464 | tf_op jit(solution)/shard_map/reduce_scatter | solution.py:246
  2370.8 155.7 %reduce-scatter.41.cloned.1.call-done = f32[88,1024]{1,0:T(8,128)} async-done(((f32[2816,1024]{1,0:T(8,128)}), f32[88,1024]{1,0:T(8,128)}) %reduce-scatter.41.cloned.1.call-update) | async-done | bytes 360464 | tf_op jit(solution)/shard_map/reduce_scatter | solution.py:247
  2526.5 141.8 %reduce-scatter.19.cloned.1.call-done = f32[32,1024]{1,0:T(8,128)} async-done(((f32[1024,1024]{1,0:T(8,128)}), f32[32,1024]{1,0:T(8,128)}) %reduce-scatter.19.cloned.1.call-update) | async-done | bytes 131088 | tf_op jit(solution)/shard_map/reduce_scatter | solution.py:242
  2668.3 140.6 %reduce-scatter.17.cloned.1.call-done = f32[32,1024]{1,0:T(8,128)} async-done(((f32[1024,1024]{1,0:T(8,128)}), f32[32,1024]{1,0:T(8,128)}) %reduce-scatter.17.cloned.1.call-update) | async-done | bytes 131088 | tf_op jit(solution)/shard_map/reduce_scatter | solution.py:241
  2808.9 140.1 %reduce-scatter.15.cloned.1.call-done = f32[32,1024]{1,0:T(8,128)} async-done(((f32[1024,1024]{1,0:T(8,128)}), f32[32,1024]{1,0:T(8,128)}) %reduce-scatter.15.cloned.1.call-update) | async-done | bytes 131088 | tf_op jit(solution)/shard_map/reduce_scatter | solution.py:240
  2949.0 154.6 %reduce-scatter.27.cloned.1.call-done = f32[88,1024]{1,0:T(8,128)} async-done(((f32[2816,1024]{1,0:T(8,128)}), f32[88,1024]{1,0:T(8,128)}) %reduce-scatter.27.cloned.1.call-update) | async-done | bytes 360464 | tf_op jit(solution)/shard_map/reduce_scatter | solution.py:247
  3103.6 155.8 %reduce-scatter.23.cloned.1.call-done = f32[32,2816]{1,0:T(8,128)} async-done(((f32[1024,2816]{1,0:T(8,128)}), f32[32,2816]{1,0:T(8,128)}) %reduce-scatter.23.cloned.1.call-update) | async-done | bytes 360464 | tf_op jit(solution)/shard_map/reduce_scatter | solution.py:245
  3259.4 155.6 %reduce-scatter.25.cloned.1.call-done = f32[32,2816]{1,0:T(8,128)} async-done(((f32[1024,2816]{1,0:T(8,128)}), f32[32,2816]{1,0:T(8,128)}) %reduce-scatter.25.cloned.1.call-update) | async-done | bytes 360464 | tf_op jit(solution)/shard_map/reduce_scatter | solution.py:246
  (675 shorter events, 521.2 us)
Async XLA Ops:
  7.2 62.9 %all-gather.27.cloned.1.call-start = ((), (), s32[]{:S(2)}) async-start(), calls=%async_computation.16 | async-start | bytes 2162688 | tf_op jit(solution)/shard_map/all_gather | solution.py:227
  7.9 120.4 %all-gather.23.cloned.1.call-start = ((), (), s32[]{:S(2)}) async-start(), calls=%async_computation.14 | async-start | bytes 2162688 | tf_op jit(solution)/shard_map/all_gather | solution.py:228
  8.7 177.8 %all-gather.31.cloned.1.call-start = ((), (), s32[]{:S(2)}) async-start(), calls=%async_computation.18 | async-start | bytes 2162688 | tf_op jit(solution)/shard_map/all_gather | solution.py:226
  9.4 231.8 %all-gather.29.cloned.1.call-start = ((), (), s32[]{:S(2)}) async-start(), calls=%async_computation.17 | async-start | bytes 4456448 | tf_op jit(solution)/shard_map/all_gather | solution.py:285
  55.0 134.3 %copy-start.71 = (f32[1024]{0:T(1024)}, f32[1024]{0:T(1024)S(1)}, u32[]{:S(2)}) copy-start(f32[1024]{0:T(1024)S(1)} %convert_element_type.238) | copy-start | bytes 12292
  57.0 132.4 %copy-start.80 = (f32[128]{0:T(128)}, f32[128]{0:T(128)S(1)}, u32[]{:S(2)}) copy-start(f32[128]{0:T(128)S(1)} %add_rsqrt_fusion.3) | copy-start | bytes 1540
  74.6 217.9 %all-gather.25.cloned.1.call-start = ((), (), s32[]{:S(2)}) async-start(), calls=%async_computation.15 | async-start | bytes 4456448 | tf_op jit(solution)/shard_map/all_gather | solution.py:286
  131.3 218.9 %all-gather.33.cloned.1.call-start = ((), (), s32[]{:S(2)}) async-start(), calls=%async_computation.19 | async-start | bytes 2162688 | tf_op jit(solution)/shard_map/all_gather | solution.py:229
  131.9 287.4 %all-gather.35.cloned.1.call-start = ((), (), s32[]{:S(2)}) async-start(), calls=%async_computation.20 | async-start | bytes 5947392 | tf_op jit(solution)/shard_map/all_gather | solution.py:231
  132.6 355.8 %all-gather.37.cloned.1.call-start = ((), (), s32[]{:S(2)}) async-start(), calls=%async_computation.21 | async-start | bytes 5947392 | tf_op jit(solution)/shard_map/all_gather | solution.py:232
  133.4 424.2 %all-gather.39.cloned.1.call-start = ((), (), s32[]{:S(2)}) async-start(), calls=%async_computation.22 | async-start | bytes 5947392 | tf_op jit(solution)/shard_map/all_gather | solution.py:233
  134.1 481.6 %all-gather.45.cloned.1.call-start = ((), (), s32[]{:S(2)}) async-start(), calls=%async_computation.25 | async-start | bytes 2162688 | tf_op jit(solution)/shard_map/all_gather | solution.py:227
  134.7 539.2 %all-gather.41.cloned.1.call-start = ((), (), s32[]{:S(2)}) async-start(), calls=%async_computation.23 | async-start | bytes 2162688 | tf_op jit(solution)/shard_map/all_gather | solution.py:228
  135.4 596.5 %all-gather.49.cloned.1.call-start = ((), (), s32[]{:S(2)}) async-start(), calls=%async_computation.27 | async-start | bytes 2162688 | tf_op jit(solution)/shard_map/all_gather | solution.py:226
  136.0 650.7 %all-gather.47.cloned.1.call-start = ((), (), s32[]{:S(2)}) async-start(), calls=%async_computation.26 | async-start | bytes 4456448 | tf_op jit(solution)/shard_map/all_gather | solution.py:285
  136.3 216.1 %copy-start.73 = (f32[1024]{0:T(1024)}, f32[1024]{0:T(1024)S(1)}, u32[]{:S(2)}) copy-start(f32[1024]{0:T(1024)S(1)} %convert_element_type.249) | copy-start | bytes 12292
  352.3 205.2 %copy-start.17 = (f32[128,1024]{1,0:T(8,128)}, f32[128,1024]{1,0:T(8,128)S(1)}, u32[]{:S(2)}) copy-start(f32[128,1024]{1,0:T(8,128)S(1)} %get-tuple-element.1948) | copy-start | bytes 1572868
  352.5 135.9 %copy-start.37 = (bf16[128,1024]{1,0:T(8,128)(2,1)}, bf16[128,1024]{1,0:T(8,128)(2,1)S(1)}, u32[]{:S(2)}) copy-start(bf16[128,1024]{1,0:T(8,128)(2,1)S(1)} %multiply_convert_fusion.10) | copy-start | bytes 786436
  493.8 124.4 %copy-start.42 = (bf16[128,2816]{1,0:T(8,128)(2,1)}, bf16[128,2816]{1,0:T(8,128)(2,1)S(1)}, u32[]{:S(2)}) copy-start(bf16[128,2816]{1,0:T(8,128)(2,1)S(1)} %get-tuple-element.1949) | copy-start | bytes 2162692
  561.2 334.8 %copy-start.19 = (f32[128,1024]{1,0:T(8,128)}, f32[128,1024]{1,0:T(8,128)S(1)}, u32[]{:S(2)}) copy-start(f32[128,1024]{1,0:T(8,128)S(1)} %get-tuple-element.1952) | copy-start | bytes 1572868
  561.2 112.7 %copy-start.65 = (f32[128,1024]{1,0:T(8,128)S(1)}, f32[128,1024]{1,0:T(8,128)}, u32[]{:S(2)}) copy-start(f32[128,1024]{1,0:T(8,128)} %get-tuple-element.1946) | copy-start | bytes 1572868
  561.2 115.4 %copy-start.87 = (f32[128]{0:T(128)}, f32[128]{0:T(128)S(1)}, u32[]{:S(2)}) copy-start(f32[128]{0:T(128)S(1)} %add_rsqrt_fusion.1) | copy-start | bytes 1540
  619.1 219.2 %all-gather.43.cloned.1.call-start = ((), (), s32[]{:S(2)}) async-start(), calls=%async_computation.24 | async-start | bytes 4456448 | tf_op jit(solution)/shard_map/all_gather | solution.py:286
  676.7 219.3 %all-gather.51.cloned.1.call-start = ((), (), s32[]{:S(2)}) async-start(), calls=%async_computation.28 | async-start | bytes 2162688 | tf_op jit(solution)/shard_map/all_gather | solution.py:229
  677.2 287.6 %all-gather.53.cloned.1.call-start = ((), (), s32[]{:S(2)}) async-start(), calls=%async_computation.29 | async-start | bytes 5947392 | tf_op jit(solution)/shard_map/all_gather | solution.py:231
  677.8 356.1 %all-gather.55.cloned.1.call-start = ((), (), s32[]{:S(2)}) async-start(), calls=%async_computation.30 | async-start | bytes 5947392 | tf_op jit(solution)/shard_map/all_gather | solution.py:232
  678.4 424.5 %all-gather.57.cloned.1.call-start = ((), (), s32[]{:S(2)}) async-start(), calls=%async_computation.31 | async-start | bytes 5947392 | tf_op jit(solution)/shard_map/all_gather | solution.py:233
  679.0 524.8 %all-gather.59.cloned.1.call-start = ((), (), s32[]{:S(2)}) async-start(), calls=%async_computation.32 | async-start | bytes 4456448 | tf_op jit(solution)/shard_map/all_gather | solution.py:380
  735.3 475.1 %all-gather.61.cloned.1.call-start = ((), (), s32[]{:S(2)}) async-start(), calls=%async_computation.33 | async-start | bytes 4456448 | tf_op jit(solution)/shard_map/all_gather | solution.py:381
  898.1 219.4 %copy-start.15 = (f32[128,1024]{1,0:T(8,128)}, f32[128,1024]{1,0:T(8,128)S(1)}, u32[]{:S(2)}) copy-start(f32[128,1024]{1,0:T(8,128)S(1)} %get-tuple-element.1954) | copy-start | bytes 1572868
  898.3 135.6 %copy-start.23 = (bf16[128,1024]{1,0:T(8,128)(2,1)}, bf16[128,1024]{1,0:T(8,128)(2,1)S(1)}, u32[]{:S(2)}) copy-start(bf16[128,1024]{1,0:T(8,128)(2,1)S(1)} %multiply_convert_fusion.8) | copy-start | bytes 786436
  969.5 133.3 %copy-start.67 = (bf16[1,128,1024]{2,1,0:T(8,128)(2,1)S(1)}, bf16[1,128,1024]{2,1,0:T(8,128)(2,1)}, u32[]{:S(2)}) copy-start(bf16[1,128,1024]{2,1,0:T(8,128)(2,1)} %param.38) | copy-start | bytes 786436
  1119.3 266.4 %all-gather.63.cloned.1.call-start = ((), (), s32[]{:S(2)}) async-start(), calls=%async_computation.34 | async-start | bytes 4456448 | tf_op jit(solution)/shard_map/all_gather | solution.py:380
  1120.0 265.6 %all-gather.65.cloned.1.call-start = ((), (), s32[]{:S(2)}) async-start(), calls=%async_computation.35 | async-start | bytes 4456448 | tf_op jit(solution)/shard_map/all_gather | solution.py:381
  1308.2 280.3 %reduce-scatter.35.cloned.1.call-start = ((), (), s32[]{:S(2)}) async-start(), calls=%async_computation.46 | async-start | bytes 4325376 | tf_op jit(solution)/shard_map/reduce_scatter | solution.py:243
  1312.2 328.4 %reduce-scatter.29.cloned.1.call-start = ((), (), s32[]{:S(2)}) async-start(), calls=%async_computation.43 | async-start | bytes 4325376 | tf_op jit(solution)/shard_map/reduce_scatter | solution.py:240
  1315.1 466.0 %reduce-scatter.31.cloned.1.call-start = ((), (), s32[]{:S(2)}) async-start(), calls=%async_computation.44 | async-start | bytes 4325376 | tf_op jit(solution)/shard_map/reduce_scatter | solution.py:241
  1317.9 602.4 %reduce-scatter.21.cloned.1.call-start = ((), (), s32[]{:S(2)}) async-start(), calls=%async_computation.39 | async-start | bytes 4325376 | tf_op jit(solution)/shard_map/reduce_scatter | solution.py:243
  1320.7 740.2 %reduce-scatter.33.cloned.1.call-start = ((), (), s32[]{:S(2)}) async-start(), calls=%async_computation.45 | async-start | bytes 4325376 | tf_op jit(solution)/shard_map/reduce_scatter | solution.py:242
  1323.6 891.6 %reduce-scatter.37.cloned.1.call-start = ((), (), s32[]{:S(2)}) async-start(), calls=%async_computation.47 | async-start | bytes 11894784 | tf_op jit(solution)/shard_map/reduce_scatter | solution.py:245
  1329.7 1041.1 %reduce-scatter.39.cloned.1.call-start = ((), (), s32[]{:S(2)}) async-start(), calls=%async_computation.48 | async-start | bytes 11894784 | tf_op jit(solution)/shard_map/reduce_scatter | solution.py:246
  1336.7 1189.9 %reduce-scatter.41.cloned.1.call-start = ((), (), s32[]{:S(2)}) async-start(), calls=%async_computation.49 | async-start | bytes 11894784 | tf_op jit(solution)/shard_map/reduce_scatter | solution.py:247
  1343.7 1324.6 %reduce-scatter.19.cloned.1.call-start = ((), (), s32[]{:S(2)}) async-start(), calls=%async_computation.38 | async-start | bytes 4325376 | tf_op jit(solution)/shard_map/reduce_scatter | solution.py:242
  1469.3 1339.5 %reduce-scatter.17.cloned.1.call-start = ((), (), s32[]{:S(2)}) async-start(), calls=%async_computation.37 | async-start | bytes 4325376 | tf_op jit(solution)/shard_map/reduce_scatter | solution.py:241
  1513.3 1435.7 %reduce-scatter.15.cloned.1.call-start = ((), (), s32[]{:S(2)}) async-start(), calls=%async_computation.36 | async-start | bytes 4325376 | tf_op jit(solution)/shard_map/reduce_scatter | solution.py:240
  1516.2 1587.4 %reduce-scatter.27.cloned.1.call-start = ((), (), s32[]{:S(2)}) async-start(), calls=%async_computation.42 | async-start | bytes 11894784 | tf_op jit(solution)/shard_map/reduce_scatter | solution.py:247
  1522.3 1737.1 %reduce-scatter.23.cloned.1.call-start = ((), (), s32[]{:S(2)}) async-start(), calls=%async_computation.40 | async-start | bytes 11894784 | tf_op jit(solution)/shard_map/reduce_scatter | solution.py:245
  1529.4 1885.6 %reduce-scatter.25.cloned.1.call-start = ((), (), s32[]{:S(2)}) async-start(), calls=%async_computation.41 | async-start | bytes 11894784 | tf_op jit(solution)/shard_map/reduce_scatter | solution.py:246
  (114 other events, 1343.0 us)
Sparse Core Ops, SparseCore 0:
  10.9 59.1 all-gather.26
  73.0 55.2 all-gather.22
  131.2 55.2 all-gather.30
  189.1 52.0 all-gather.28
  243.8 48.7 all-gather.24
  295.2 54.9 all-gather.32
  353.1 66.1 all-gather.34
  422.1 66.2 all-gather.36
  491.3 66.2 all-gather.38
  560.3 55.3 all-gather.44
  618.6 55.2 all-gather.40
  676.6 55.2 all-gather.48
  734.6 52.0 all-gather.46
  789.3 48.8 all-gather.42
  841.0 54.9 all-gather.50
  898.7 66.1 all-gather.52
  967.6 66.2 all-gather.54
  1036.6 66.2 all-gather.56
  1105.6 52.4 all-gather.58
  1160.7 49.5 all-gather.60
  1213.1 51.6 all-gather.62
  1308.3 48.9 all-gather.64
  1360.1 140.1 reduce-scatter.34
  1503.0 137.4 reduce-scatter.28
  1643.4 137.5 reduce-scatter.30
  1783.7 136.5 reduce-scatter.20
  1923.0 137.8 reduce-scatter.32
  2063.7 151.4 reduce-scatter.36
  2218.2 152.6 reduce-scatter.38
  2373.6 152.9 reduce-scatter.40
  2529.4 138.8 reduce-scatter.18
  2671.1 137.6 reduce-scatter.16
  2811.6 137.3 reduce-scatter.14
  2951.9 151.6 reduce-scatter.26
  3106.5 152.8 reduce-scatter.22
  3262.2 152.7 reduce-scatter.24
where the time goes:
time: 3430 us; the launch traced here: 3420 us
  waiting for transfers between devices  2720 us (79%)
  matrix products  356 us (10%)
  blocking collectives  163 us (5%)
  local copies, waits for them, and re-layouts  123 us (4%)
  other arithmetic  43.8 us (1%)
    reduce_scatter x2, waiting for transfers between devices, scatter_grads(): lax.psum_scatter(grad_terms[7], ('fsdp', 'ctx'), scatter_dimension=0, til...  311 us
    reduce_scatter x2, waiting for transfers between devices, scatter_grads(): lax.psum_scatter(grad_terms[8], ('fsdp', 'ctx'), scatter_dimension=0, til...  310 us
    reduce_scatter x2, waiting for transfers between devices, scatter_grads(): lax.psum_scatter(grad_terms[6], ('fsdp', 'ctx'), scatter_dimension=0, til...  310 us
    reduce_scatter x2, waiting for transfers between devices, scatter_grads(): lax.psum_scatter(grad_terms[3], ('fsdp', 'ctx'), scatter_dimension=0, til...  282 us
    reduce_scatter x2, waiting for transfers between devices, scatter_grads(): lax.psum_scatter(grad_terms[2], ('fsdp', 'ctx'), scatter_dimension=0, til...  281 us
    reduce_scatter x2, waiting for transfers between devices, scatter_grads(): lax.psum_scatter(grad_terms[1], ('fsdp', 'ctx'), scatter_dimension=0, til...  192 us
    reduce_scatter x2, waiting for transfers between devices, scatter_grads(): lax.psum_scatter(grad_terms[4], ('fsdp', 'ctx'), scatter_dimension=0, til...  139 us
    all_gather x2, waiting for transfers between devices, gather_forward(): lax.all_gather(shards[6], ('fsdp', 'ctx'), axis=0, tiled=True)  133 us
  transfers between devices with their start and end apart: 36, of which 32 were waited for; matrix products, arithmetic and copies ran while one was open for 15% of the time, Pallas kernels for 0%

commit v1 on v0

--- a/solution.py
+++ b/solution.py
@@ -3,6 +3,8 @@
 import jax
 import jax.numpy as jnp
 from jax import lax
+from jax.experimental import pallas as pl
+from jax.experimental.pallas import tpu as pltpu
 from jax.sharding import PartitionSpec as P
 
 HEADS = 16
@@ -523,6 +525,660 @@
     )
 
 
+ROWS = 128
+BF = jnp.bfloat16
+F32 = jnp.float32
+MESH = pl.DeviceIdType.MESH
+VMEM_SPACE = pltpu.VMEM
+
+
+def flip(value, weight):
+    return value + weight * (1 - 2 * ((value // weight) % 2))
+
+
+def to_device(f, c):
+    return {"fsdp": f, "ctx": c}
+
+
+def remote(src, dst, send_sem, recv_sem, target):
+    return pltpu.make_async_remote_copy(
+        src_ref=src,
+        dst_ref=dst,
+        send_sem=send_sem,
+        recv_sem=recv_sem,
+        device_id=to_device(*target),
+        device_id_type=MESH,
+    )
+
+
+def plane_place():
+    f = lax.axis_index("fsdp")
+    c = lax.axis_index("ctx")
+    return f, c, (c // 2) % 2, c // 4
+
+
+def greet_plane(f, c, z):
+    barrier = pltpu.get_barrier_semaphore()
+
+    def hello(target):
+        pl.semaphore_signal(barrier, inc=1, device_id=to_device(*target), device_id_type=MESH)
+
+    hello((f, flip(c, 2)))
+
+    @pl.when(z > 0)
+    def _():
+        hello((f, c - 4))
+
+    @pl.when(z < 3)
+    def _():
+        hello((f, c + 4))
+
+    pl.semaphore_wait(barrier, 2 + jnp.where((z > 0) & (z < 3), 1, 0))
+
+
+def send_order(z, step):
+    table = ((3, 2, 1, 0), (3, 0, 2, 1), (0, 3, 1, 2), (0, 1, 2, 3))
+    column = [row[step] for row in table]
+    return jnp.where(
+        z == 0, column[0], jnp.where(z == 1, column[1], jnp.where(z == 2, column[2], column[3]))
+    )
+
+
+def reduce_plane(place, product, bufs, sems):
+    f, c, y, z = place
+    sy, ry, acc, su, ru, sd, rd = bufs
+    ys, yr, us, ur, ds, dr = sems
+    across = (f, flip(c, 2))
+    above = (f, c + 4)
+    below = (f, c - 4)
+
+    def y_copy(block):
+        return remote(sy.at[block], ry.at[block], ys.at[block], yr.at[block], across)
+
+    def up_copy(block):
+        return remote(su.at[block], ru.at[block], us.at[block], ur.at[block], above)
+
+    def down_copy(block):
+        return remote(sd.at[block], rd.at[block], ds.at[block], dr.at[block], below)
+
+    for step in range(4):
+        block = send_order(z, step)
+        sy[block] = product(block * 2 + (1 - y)).astype(BF)
+        y_copy(block).start()
+    for block in range(4):
+        acc[block] = product(block * 2 + y)
+    for k in range(3):
+        top = 3 - k
+
+        @pl.when(top > z)
+        def _():
+            y_copy(top).wait_recv()
+            acc[top] += ry[top].astype(F32)
+
+            @pl.when(z > 0)
+            def _():
+                up_copy(top).wait_recv()
+                acc[top] += ru[top].astype(F32)
+
+            su[top] = acc[top].astype(BF)
+            up_copy(top).start()
+
+        @pl.when(k < z)
+        def _():
+            y_copy(k).wait_recv()
+            acc[k] += ry[k].astype(F32)
+
+            @pl.when(z < 3)
+            def _():
+                down_copy(k).wait_recv()
+                acc[k] += rd[k].astype(F32)
+
+            sd[k] = acc[k].astype(BF)
+            down_copy(k).start()
+
+    y_copy(z).wait_recv()
+    acc[z] += ry[z].astype(F32)
+
+    @pl.when(z > 0)
+    def _():
+        up_copy(z).wait_recv()
+        acc[z] += ru[z].astype(F32)
+
+    @pl.when(z < 3)
+    def _():
+        down_copy(z).wait_recv()
+        acc[z] += rd[z].astype(F32)
+
+    def finish():
+        for block in range(4):
+            y_copy(block).wait_send()
+        for k in range(3):
+
+            @pl.when(3 - k > z)
+            def _():
+                up_copy(3 - k).wait_send()
+
+            @pl.when(k < z)
+            def _():
+                down_copy(k).wait_send()
+
+    return finish
+
+
+def gather_plane(place, full, sems):
+    f, c, y, z = place
+    ys, yr, us, ur, ds, dr = sems
+    across = (f, flip(c, 2))
+    above = (f, c + 4)
+    below = (f, c - 4)
+
+    def rows(block, side):
+        return full.at[pl.ds(pl.multiple_of((block * 2 + side) * ROWS, ROWS), ROWS)]
+
+    def y_copy(block):
+        return remote(rows(block, y), rows(block, y), ys.at[block], yr.at[block], across)
+
+    def up_copy(block):
+        return remote(rows(block, y), rows(block, y), us.at[block], ur.at[block], above)
+
+    def down_copy(block):
+        return remote(rows(block, y), rows(block, y), ds.at[block], dr.at[block], below)
+
+    @pl.when(z < 3)
+    def _():
+        up_copy(z).start()
+
+    @pl.when(z > 0)
+    def _():
+        down_copy(z).start()
+
+    y_copy(z).start()
+    for k in range(1, 4):
+
+        @pl.when(z >= k)
+        def _():
+            up_copy(z - k).wait_recv()
+
+            @pl.when(z < 3)
+            def _():
+                up_copy(z - k).start()
+
+            y_copy(z - k).start()
+
+        @pl.when(z + k <= 3)
+        def _():
+            down_copy(z + k).wait_recv()
+
+            @pl.when(z > 0)
+            def _():
+                down_copy(z + k).start()
+
+            y_copy(z + k).start()
+
+    for block in range(4):
+        y_copy(block).wait()
+    for k in range(4):
+
+        @pl.when((z < 3) & (z >= k))
+        def _():
+            up_copy(z - k).wait_send()
+
+        @pl.when((z > 0) & (z + k <= 3))
+        def _():
+            down_copy(z + k).wait_send()
+
+
+def norm_rows(hidden):
+    return lax.rsqrt(jnp.mean(hidden * hidden, axis=-1, keepdims=True) + NORM_EPS)
+
+
+def own_rows(place):
+    _, _, y, z = place
+    return pl.ds(pl.multiple_of((z * 2 + y) * ROWS, ROWS), ROWS)
+
+
+def make_product(left_ref, right_ref, transposed):
+    dims = (((1,), (1,)), ((), ())) if transposed else (((1,), (0,)), ((), ()))
+
+    def product(block):
+        rows = left_ref[pl.ds(pl.multiple_of(block * ROWS, ROWS), ROWS), :]
+        return lax.dot_general(rows, right_ref[...], dims, preferred_element_type=F32)
+
+    return product
+
+
+def start_kernel(hid_ref, gain_ref, full_ref, *sems):
+    place = plane_place()
+    greet_plane(place[0], place[1], place[3])
+    hidden = hid_ref[...].astype(F32)
+    full_ref[own_rows(place), :] = (hidden * norm_rows(hidden) * gain_ref[...]).astype(BF)
+    gather_plane(place, full_ref, sems)
+
+
+def forward_kernel(left_ref, right_ref, res_ref, gain_ref, new_ref, full_ref, *scratch):
+    place = plane_place()
+    greet_plane(place[0], place[1], place[3])
+    bufs, sems, more = scratch[:7], scratch[7:13], scratch[13:]
+    finish = reduce_plane(place, make_product(left_ref, right_ref, False), bufs, sems)
+    hidden = res_ref[...].astype(F32) + bufs[2][place[3]]
+    new_ref[...] = hidden
+    full_ref[own_rows(place), :] = (hidden * norm_rows(hidden) * gain_ref[...]).astype(BF)
+    gather_plane(place, full_ref, more)
+    finish()
+
+
+def turn_kernel(left_ref, right_ref, res_ref, cot_ref, out_ref, full_ref, *scratch):
+    place = plane_place()
+    greet_plane(place[0], place[1], place[3])
+    bufs, sems, more = scratch[:7], scratch[7:13], scratch[13:]
+    finish = reduce_plane(place, make_product(left_ref, right_ref, False), bufs, sems)
+    out_ref[...] = (res_ref[...] + bufs[2][place[3]]).astype(BF)
+    full_ref[own_rows(place), :] = cot_ref[...]
+    gather_plane(place, full_ref, more)
+    finish()
+
+
+def back_rows(total, grad, hidden, gain):
+    inverse = norm_rows(hidden)
+    normed = hidden * inverse
+    gain_grad = jnp.sum(total * normed, axis=0, keepdims=True)
+    scaled = total * gain
+    mean = jnp.mean(scaled * normed, axis=-1, keepdims=True)
+    return grad + inverse * (scaled - normed * mean), gain_grad
+
+
+def back_kernel(left_ref, right_ref, grad_ref, hid_ref, gain_ref, new_ref, gg_ref, full_ref, *scratch):
+    place = plane_place()
+    greet_plane(place[0], place[1], place[3])
+    bufs, sems, more = scratch[:7], scratch[7:13], scratch[13:]
+    finish = reduce_plane(place, make_product(left_ref, right_ref, True), bufs, sems)
+    new, gain_grad = back_rows(
+        bufs[2][place[3]], grad_ref[...].astype(F32), hid_ref[...].astype(F32), gain_ref[...]
+    )
+    gg_ref[...] = gain_grad
+    new_ref[...] = new
+    full_ref[own_rows(place), :] = new.astype(BF)
+    gather_plane(place, full_ref, more)
+    finish()
+
+
+def last_kernel(left_ref, right_ref, grad_ref, hid_ref, gain_ref, out_ref, gg_ref, *scratch):
+    place = plane_place()
+    greet_plane(place[0], place[1], place[3])
+    bufs, sems = scratch[:7], scratch[7:13]
+    finish = reduce_plane(place, make_product(left_ref, right_ref, True), bufs, sems)
+    new, gain_grad = back_rows(
+        bufs[2][place[3]], grad_ref[...].astype(F32), hid_ref[...].astype(F32), gain_ref[...]
+    )
+    gg_ref[...] = gain_grad
+    out_ref[...] = new.astype(BF)
+    finish()
+
+
+def comm_call(kernel, outs, ident, args, reduces, gathers):
+    width = 1024
+    scratch = []
+    if reduces:
+        for kind in (BF, BF, F32, BF, BF, BF, BF):
+            scratch.append(pltpu.VMEM((4, ROWS, width), kind))
+        scratch += [pltpu.SemaphoreType.DMA((4,))] * 6
+    if gathers:
+        scratch += [pltpu.SemaphoreType.DMA((4,))] * 6
+    spec = pl.BlockSpec(memory_space=VMEM_SPACE)
+    return pl.pallas_call(
+        kernel,
+        out_shape=[jax.ShapeDtypeStruct(*o) for o in outs],
+        in_specs=[spec] * len(args),
+        out_specs=[spec] * len(outs),
+        scratch_shapes=scratch,
+        compiler_params=pltpu.CompilerParams(
+            collective_id=ident, has_side_effects=True, vmem_limit_bytes=40 * 1024 * 1024
+        ),
+        name=kernel.__name__,
+    )(*args)
+
+
+def head_lanes(head):
+    lane = lax.broadcasted_iota(jnp.int32, (1, 128), 1)
+    return (lane // 32) % 2 == head
+
+
+def value_lanes(head):
+    lane = lax.broadcasted_iota(jnp.int32, (1, 128), 1)
+    return lane // 64 == head
+
+
+NT = (((1,), (1,)), ((), ()))
+TN = (((0,), (0,)), ((), ()))
+
+
+def attend_kernel(q_ref, k_ref, v_ref, pq_ref, pk_ref, att_ref, lse_ref):
+    allowed = pk_ref[...] <= pq_ref[...]
+    queries = q_ref[...]
+    parts = []
+    for head in range(2):
+        masked = jnp.where(head_lanes(head), queries, jnp.zeros_like(queries))
+        scores = lax.dot_general(masked, k_ref[...], NT, preferred_element_type=F32) * HD ** (-0.5)
+        scores = jnp.where(allowed, scores, NEG_FILL)
+        top = jnp.max(scores, axis=-1, keepdims=True)
+        shares = jnp.exp(scores - top)
+        total = jnp.sum(shares, axis=-1, keepdims=True)
+        lse_ref[:, head : head + 1] = top + jnp.log(total)
+        mixed = jnp.dot(shares.astype(BF), v_ref[...], preferred_element_type=F32)
+        parts.append(mixed / total)
+    att_ref[...] = jnp.where(value_lanes(0), parts[0], parts[1]).astype(BF)
+
+
+def attend_forward(q, k, v, pos_q, pos_k):
+    rows = q.shape[0]
+    keys = k.shape[0]
+    step = 128
+    return pl.pallas_call(
+        attend_kernel,
+        grid=(rows // step,),
+        out_shape=[
+            jax.ShapeDtypeStruct((rows, 128), BF),
+            jax.ShapeDtypeStruct((rows, 2), F32),
+        ],
+        in_specs=[
+            pl.BlockSpec((step, 128), lambda i: (i, 0)),
+            pl.BlockSpec((keys, 128), lambda i: (0, 0)),
+            pl.BlockSpec((keys, 128), lambda i: (0, 0)),
+            pl.BlockSpec((step, 1), lambda i: (i, 0)),
+            pl.BlockSpec((1, keys), lambda i: (0, 0)),
+        ],
+        out_specs=[
+            pl.BlockSpec((step, 128), lambda i: (i, 0)),
+            pl.BlockSpec((step, 2), lambda i: (i, 0)),
+        ],
+        compiler_params=pltpu.CompilerParams(vmem_limit_bytes=40 * 1024 * 1024),
+        name="attend_forward",
+    )(q, k, v, pos_q, pos_k)
+
+
+def attend_back_kernel(q_ref, k_ref, v_ref, da_ref, lse_ref, pq_ref, pk_ref, dq_ref, dk_ref, dv_ref):
+    @pl.when(pl.program_id(0) == 0)
+    def _():
+        dk_ref[...] = jnp.zeros_like(dk_ref)
+        dv_ref[...] = jnp.zeros_like(dv_ref)
+
+    allowed = pk_ref[...] <= pq_ref[...]
+    queries = q_ref[...]
+    grads = da_ref[...]
+    parts = []
+    for head in range(2):
+        masked = jnp.where(head_lanes(head), queries, jnp.zeros_like(queries))
+        grad_h = jnp.where(value_lanes(head), grads, jnp.zeros_like(grads))
+        scores = lax.dot_general(k_ref[...], masked, NT, preferred_element_type=F32) * HD ** (-0.5)
+        shares = jnp.where(allowed, jnp.exp(scores - lse_ref[head : head + 1, :]), 0.0)
+        grad_shares = lax.dot_general(v_ref[...], grad_h, NT, preferred_element_type=F32)
+        delta = jnp.sum(shares * grad_shares, axis=0, keepdims=True)
+        grad_scores = (shares * (grad_shares - delta) * HD ** (-0.5)).astype(BF)
+        dv_ref[...] += jnp.dot(shares.astype(BF), grad_h, preferred_element_type=F32)
+        dk_ref[...] += jnp.dot(grad_scores, masked, preferred_element_type=F32)
+        parts.append(lax.dot_general(grad_scores, k_ref[...], TN, preferred_element_type=F32))
+    dq_ref[...] = jnp.where(head_lanes(0), parts[0], parts[1])
+
+
+def attend_backward(q, k, v, da, lse_rows, pos_q, pos_k):
+    rows = q.shape[0]
+    keys = k.shape[0]
+    step = 128
+    return pl.pallas_call(
+        attend_back_kernel,
+        grid=(rows // step,),
+        out_shape=[
+            jax.ShapeDtypeStruct((rows, 128), F32),
+            jax.ShapeDtypeStruct((keys, 128), F32),
+            jax.ShapeDtypeStruct((keys, 128), F32),
+        ],
+        in_specs=[
+            pl.BlockSpec((step, 128), lambda i: (i, 0)),
+            pl.BlockSpec((keys, 128), lambda i: (0, 0)),
+            pl.BlockSpec((keys, 128), lambda i: (0, 0)),
+            pl.BlockSpec((step, 128), lambda i: (i, 0)),
+            pl.BlockSpec((2, step), lambda i: (0, i)),
+            pl.BlockSpec((1, step), lambda i: (0, i)),
+            pl.BlockSpec((keys, 1), lambda i: (0, 0)),
+        ],
+        out_specs=[
+            pl.BlockSpec((step, 128), lambda i: (i, 0)),
+            pl.BlockSpec((keys, 128), lambda i: (0, 0)),
+            pl.BlockSpec((keys, 128), lambda i: (0, 0)),
+        ],
+        compiler_params=pltpu.CompilerParams(vmem_limit_bytes=48 * 1024 * 1024),
+        name="attend_backward",
+    )(q, k, v, da, lse_rows, pos_q, pos_k)
+
+
+def pack_heads(weight):
+    rows = weight.shape[0]
+    split = weight.reshape(rows, 8, 2, 2, 32)
+    return split.transpose(1, 0, 3, 2, 4).reshape(8, rows, 128)
+
+
+def unpack_heads(packed):
+    rows = packed.shape[1]
+    split = packed.reshape(8, rows, 2, 2, 32)
+    return split.transpose(1, 0, 3, 2, 4).reshape(rows, 1024)
+
+
+def pack_values(weight):
+    rows = weight.shape[0]
+    return weight.reshape(rows, 8, 128).transpose(1, 0, 2)
+
+
+def unpack_values(packed):
+    return packed.transpose(1, 0, 2).reshape(packed.shape[1], 1024)
+
+
+def pack_units(weight, width):
+    rows, units = weight.shape
+    each = units // 32
+    split = weight.reshape(rows, 2, 8, 2, each).transpose(2, 0, 1, 3, 4).reshape(8, rows, 4 * each)
+    return jnp.pad(split, ((0, 0), (0, 0), (0, width - 4 * each)))
+
+
+def unpack_units(packed, units):
+    rows = packed.shape[1]
+    each = units // 32
+    split = packed[:, :, : 4 * each].reshape(8, rows, 2, 2, each)
+    return split.transpose(1, 2, 0, 3, 4).reshape(rows, units)
+
+
+def pair_rope(values, cosine, sine):
+    first, second = values[:, :64], values[:, 64:]
+    return jnp.concatenate(
+        [first * cosine - second * sine, second * cosine + first * sine], axis=-1
+    )
+
+
+def pair_unrope(values, cosine, sine):
+    first, second = values[:, :64], values[:, 64:]
+    return jnp.concatenate(
+        [first * cosine + second * sine, second * cosine - first * sine], axis=-1
+    )
+
+
+def swap_cores(value):
+    return lax.ppermute(value, "ctx", [(i, i + 1 - 2 * (i % 2)) for i in range(16)])
+
+
+def fast_local(tokens, cotangent, pair_of, *shards):
+    width = tokens.shape[2]
+    units = shards[6].shape[1]
+    hidden_pad = (units // 8 + 127) // 128 * 128
+    c = lax.axis_index("ctx")
+    core = c % 2
+    chip = c // 2
+    pos_all = storage_positions(pair_of, ROWS).reshape(8, 2, ROWS)
+    own_pos = lax.dynamic_index_in_dim(pos_all, core, 1, False).reshape(-1)
+    sib_pos = lax.dynamic_index_in_dim(pos_all, 1 - core, 1, False).reshape(-1)
+    key_pos = jnp.concatenate([own_pos, sib_pos])
+    cosine, sine = rope_tables(own_pos, HD)
+    cosine = jnp.concatenate([cosine, cosine], axis=-1)
+    sine = jnp.concatenate([sine, sine], axis=-1)
+
+    layers = [shards[:9], shards[9:]]
+    gains = lax.all_gather(
+        jnp.stack([shards[0], shards[5], shards[9], shards[14]]), ("fsdp", "ctx"), axis=1, tiled=True
+    ).astype(F32)
+    gains = [gains[i : i + 1] for i in range(4)]
+    packs = []
+    for layer in layers:
+        packs.append(
+            jnp.concatenate(
+                [
+                    pack_heads(layer[1]),
+                    pack_heads(layer[2]),
+                    pack_values(layer[3]),
+                    pack_units(layer[6], hidden_pad),
+                    pack_units(layer[7], hidden_pad),
+                ],
+                axis=-1,
+            )
+        )
+    packed = jnp.stack(packs, axis=1)
+    rows_each = packed.shape[2]
+    wide = packed.shape[3]
+    packed = jnp.repeat(packed, 2, axis=0)
+    got = lax.all_to_all(packed, "ctx", 0, 0, tiled=True)
+    got = lax.all_gather(got, "fsdp", axis=0, tiled=True)
+    got = got.transpose(1, 0, 2, 3).reshape(2, 32 * rows_each, wide)
+    qkv_w = [got[i, :, :384] for i in range(2)]
+    up_w = [got[i, :, 384:] for i in range(2)]
+    down = jnp.stack([layers[0][8], layers[1][8]])
+    down = jnp.stack([down, swap_cores(down)])
+    down = lax.dynamic_slice_in_dim(jnp.concatenate([down, down]), core, 2, 0)
+    down = lax.all_gather(down, "fsdp", axis=0, tiled=False)
+    down = down.transpose(2, 0, 1, 3, 4).reshape(2, -1, width)
+    down = jnp.pad(down, ((0, 0), (0, hidden_pad - down.shape[1]), (0, 0)))
+    down_w = [down[0], down[1]]
+    outs = lax.all_gather(
+        jnp.stack([layers[0][4], layers[1][4]]), ("fsdp", "ctx"), axis=1, tiled=True
+    )
+    outs = lax.dynamic_slice_in_dim(outs, chip * 128, 128, 1)
+    out_w = [outs[0], outs[1]]
+
+    tok = tokens.reshape(ROWS, width)
+    cot = cotangent.reshape(ROWS, width)
+    plane = 8 * ROWS
+    full_type = ((plane, width), BF)
+    rows_type = ((ROWS, width), F32)
+    saved = []
+    (full,) = comm_call(start_kernel, [full_type], 0, (tok, gains[0]), False, True)
+    hidden = tok
+    first_values = None
+    pos_q = own_pos[:, None]
+    pos_k = key_pos[None, :]
+    for layer in range(2):
+        x_full = full
+        raw = jnp.dot(x_full, qkv_w[layer], preferred_element_type=F32)
+        values = raw[:, 256:]
+        mixed = values if layer == 0 else 0.5 * values + 0.5 * first_values
+        first_values = values
+        q = pair_rope(raw[:, :128], cosine, sine).astype(BF)
+        kv = jnp.concatenate(
+            [pair_rope(raw[:, 128:256], cosine, sine).astype(BF), mixed.astype(BF)], axis=-1
+        )
+        kv = jnp.concatenate([kv, swap_cores(kv)], axis=0)
+        k, v = kv[:, :128], kv[:, 128:]
+        att, lse = attend_forward(q, k, v, pos_q, pos_k)
+        middle, mlp_full = comm_call(
+            forward_kernel, [rows_type, full_type], 1 + layer,
+            (att, out_w[layer], hidden, gains[2 * layer + 1]), True, True,
+        )
+        both = jnp.dot(mlp_full, up_w[layer], preferred_element_type=F32)
+        gate, up = both[:, :hidden_pad], both[:, hidden_pad:]
+        inner = (jax.nn.silu(gate) * up).astype(BF)
+        saved.append((x_full, q, k, v, lse, att, mlp_full, gate, up, inner, hidden, middle))
+        if layer == 0:
+            hidden, full = comm_call(
+                forward_kernel, [rows_type, full_type], 3,
+                (inner, down_w[layer], middle, gains[2]), True, True,
+            )
+        else:
+            output, full = comm_call(
+                turn_kernel, [((ROWS, width), BF), full_type], 4,
+                (inner, down_w[layer], middle, cot), True, True,
+            )
+    grad = cot
+    passed = None
+    grad_packs = [None, None]
+    grad_down = [None, None]
+    grad_out = [None, None]
+    gain_grads = [None] * 4
+    for layer in (1, 0):
+        x_full, q, k, v, lse, att, mlp_full, gate, up, inner, hidden, middle = saved[layer]
+        grad_down[layer] = left_product(inner, full)
+        grad_inner = right_product(full, down_w[layer])
+        sigma = jax.nn.sigmoid(gate)
+        grad_gate = (grad_inner * up * sigma * (1.0 + gate * (1.0 - sigma))).astype(BF)
+        grad_up = (grad_inner * gate * sigma).astype(BF)
+        both = jnp.concatenate([grad_gate, grad_up], axis=-1)
+        grad_upw = left_product(mlp_full, both)
+        grad_mid, gain_grads[2 * layer + 1], full = comm_call(
+            back_kernel, [rows_type, ((1, width), F32), full_type], 5 + layer,
+            (both, up_w[layer], grad, middle, gains[2 * layer + 1]), True, True,
+        )
+        grad_out[layer] = left_product(att, full)
+        grad_att = right_product(full, out_w[layer]).astype(BF)
+        dq, dk, dv = attend_backward(q, k, v, grad_att, lse.T, own_pos[None, :], key_pos[:, None])
+        dkv = jnp.concatenate([dk, dv], axis=-1)
+        dkv = dkv[: 8 * ROWS] + swap_cores(dkv[8 * ROWS :].astype(BF)).astype(F32)
+        dk, dv = dkv[:, :128], dkv[:, 128:]
+        if layer == 1:
+            passed = 0.5 * dv
+            dv = passed
+        else:
+            dv = dv + passed
+        three = jnp.concatenate(
+            [pair_unrope(dq, cosine, sine), pair_unrope(dk, cosine, sine), dv], axis=-1
+        ).astype(BF)
+        grad_qkv = left_product(x_full, three)
+        grad_packs[layer] = jnp.concatenate([grad_qkv, grad_upw], axis=-1)
+        if layer == 1:
+            grad, gain_grads[2], full = comm_call(
+                back_kernel, [rows_type, ((1, width), F32), full_type], 7,
+                (three, qkv_w[layer], grad_mid, hidden, gains[2]), True, True,
+            )
+        else:
+            tokens_grad, gain_grads[0] = comm_call(
+                last_kernel, [((ROWS, width), BF), ((1, width), F32)], 8,
+                (three, qkv_w[layer], grad_mid, hidden, gains[0]), True, False,
+            )
+    sent = jnp.stack(grad_packs).astype(BF).reshape(2, 32, rows_each, wide).transpose(1, 0, 2, 3)
+    back = lax.all_to_all(sent, ("fsdp", "ctx"), 0, 0, tiled=True)
+    back = back.reshape(2, 8, 2, 2, rows_each, wide).astype(F32).sum(axis=(0, 2))
+    each = units // 32
+    downs = jnp.stack(grad_down)[:, : 4 * each].reshape(2, 2, 2, each, width)
+    downs = lax.psum_scatter(downs, "fsdp", scatter_dimension=1, tiled=False)
+    own = lax.dynamic_index_in_dim(downs, core, 1, False)
+    other = lax.dynamic_index_in_dim(downs, 1 - core, 1, False)
+    downs = own + swap_cores(other)
+    wide_out = jnp.zeros((2, 1024, width), F32)
+    wide_out = lax.dynamic_update_slice_in_dim(wide_out, jnp.stack(grad_out), chip * 128, 1)
+    outs = lax.psum_scatter(wide_out, ("fsdp", "ctx"), scatter_dimension=1, tiled=True)
+    gg = lax.psum_scatter(
+        jnp.concatenate(gain_grads), ("fsdp", "ctx"), scatter_dimension=1, tiled=True
+    )
+    result = [output.reshape(1, ROWS, width), tokens_grad.reshape(1, ROWS, width)]
+    for layer in range(2):
+        pack = back[:, layer]
+        result += [
+            gg[2 * layer],
+            unpack_heads(pack[:, :, :128]),
+            unpack_heads(pack[:, :, 128:256]),
+            unpack_values(pack[:, :, 256:384]),
+            outs[layer],
+            gg[2 * layer + 1],
+            unpack_units(pack[:, :, 384 : 384 + hidden_pad], units),
+            unpack_units(pack[:, :, 384 + hidden_pad :], units),
+            downs[layer],
+        ]
+    return tuple(result)
+
+
 def solution(mesh):
     placed = (
         P("fsdp", "ctx", None),
@@ -547,8 +1203,9 @@
         P(("fsdp", "ctx"), None),
         P(("fsdp", "ctx"), None),
     )
+    fits = mesh.shape["ctx"] == HEADS and mesh.shape["fsdp"] == 2
     return jax.shard_map(
-        local,
+        fast_local if fits else local,
         mesh=mesh,
         in_specs=placed,
         out_specs=(

time: 3430 us -> 1070 us (0.31)
  waiting for transfers between devices: 2720 us -> 232 us
  Pallas kernels: 0 us -> 541 us
  matrix products: 356 us -> 28.6 us
  blocking collectives: 163 us -> 110 us
    reduce_scatter x14 -> x1, waiting for transfers between devices: 1830 us -> 127 us  [fast_local(): lax.psum_scatter(wide_out, ('fsdp', 'ctx'), scatter_dimension=1, tiled=True)]
    all_gather x22 -> x3, waiting for transfers between devices: 880 us -> 3.67 us  [the longest x1 3.65 us: fast_local(): got = lax.all_gather(got, 'fsdp', axis=0, tiled=True)]
    pallas_call x0 -> x13, Pallas kernels: none -> 541 us  [the longest x9 484 us: comm_call(): pl.pallas_call(kernel, out_shape=[jax.ShapeDtypeStruct(*o) for o in outs]...]
    dot_general x70 -> x4, matrix products: 262 us -> 7.47 us  [the longest x2 4.98 us: fast_local(): both = jnp.dot(mlp_full, up_w[layer], preferred_element_type=F32)]
    unnamed x36 -> x8, waiting for transfers between devices: 9.5 us -> 101 us
    unnamed x2 -> x0, blocking collectives: 80.7 us -> none
    all_to_all x0 -> x1, blocking collectives: none -> 69.5 us  [fast_local(): got = lax.all_to_all(packed, 'ctx', 0, 0, tiled=True)]
    dynamic_slice x80 -> x1, local copies, waits for them, and re-layouts: 65.2 us -> 0.01 us  [fast_local(): sib_pos = lax.dynamic_index_in_dim(pos_all, 1 - core, 1, False).reshape(-1)]
  transfers between devices with their start and end apart: 36 -> 13, of which waited for: 32 -> 4; matrix products, arithmetic and copies ran while one was open for 15% -> 9% of each run, Pallas kernels for 0% -> 13%
where the time goes in v1:
time: 1070 us; the launch traced here: 1060 us
  Pallas kernels  541 us (51%)
  waiting for transfers between devices  232 us (22%)
  blocking collectives  110 us (10%)
  local copies, waits for them, and re-layouts  91.4 us (9%)
  other arithmetic  34.8 us (3%)
  matrix products  28.6 us (3%)
  between operations  17.2 us (2%)
    pallas_call x9, Pallas kernels, comm_call(): pl.pallas_call(kernel, out_shape=[jax.ShapeDtypeStruct(*o) for o in outs]...  484 us
    reduce_scatter x1, waiting for transfers between devices, fast_local(): lax.psum_scatter(wide_out, ('fsdp', 'ctx'), scatter_dimension=1, tiled=True)  127 us
    unnamed x8, waiting for transfers between devices  101 us
    all_to_all x1, blocking collectives, fast_local(): got = lax.all_to_all(packed, 'ctx', 0, 0, tiled=True)  69.5 us
    all_gather x1, blocking collectives, fast_local(): lax.all_gather(jnp.stack([shards[0], shards[5], shards[9], shards[14]]),...  40 us
    pallas_call x2, Pallas kernels, attend_backward(): pl.pallas_call(attend_back_kernel, grid=(rows // step,), out_shape=[jax.S...  36.5 us
    unnamed x220, local copies, waits for them, and re-layouts  31 us
  transfers between devices with their start and end apart: 13, of which 4 were waited for; matrix products, arithmetic and copies ran while one was open for 9% of the time, Pallas kernels for 13%

profile of v1, /device:TPU:0, one launch (start us, length us, event | category | flops | bytes accessed | tf_op | source)
XLA Modules:
  0.0 1059.9 jit_solution(15841169095411203295)
XLA Ops:
  19.7 69.5 %all_to_all.10 = bf16[16,2,32,1152]{3,2,1,0:T(8,128)(2,1)} all-to-all(bf16[16,2,32,1152]{3,2,1,0:T(8,128)(2,1)S(1)} %bitcast.215), channel_id=1, replica_groups=mesh['fsdp'=2,'ctx'=16] {'ctx'}, dimensions={0} | all-to-all | bytes 4718592 | tf_op jit(solution)/shard_map/all_to_all | solution.py:1045
  90.1 40.0 %all-gather.1 = bf16[32,32,4]{1,2,0:T(4,128)(2,1)S(1)} all-gather(bf16[1,32,4]{1,2,0:T(4,128)(2,1)S(1)} %maximum_bitcast_fusion.1), channel_id=1, replica_groups=mesh['fsdp'=2,'ctx'=16] {'fsdp','ctx'}, dimensions={0}, use_global_device_ids=true | all-gather | bytes 8448 | tf_op jit(solution)/shard_map/all_gather | solution.py:1023
  130.9 28.3 %start_kernel.1 = bf16[1024,1024]{1,0:T(8,128)(2,1)S(1)} custom-call(bf16[128,1024]{1,0:T(8,128)(2,1)S(1)} %bitcast.191, f32[1,1024]{1,0:T(1,128)S(1)} %get-tuple-element.133.gain_ref), custom_call_target="tpu_custom_call" | custom-call | tf_op jit(solution)/shard_map/start_kernel/pallas_call | solution.py:828
  160.5 3.1 multiply_cosine_fusion
  163.5 1.5 copy.386
  166.3 1.9 dynamic-slice_bitcast_fusion.2
  168.2 3.7 all-gather.6.cloned.1.call-done
  171.8 2.9 copy.377
  178.4 1.9 slice_bitcast_fusion.1
  180.7 10.1 attend_forward.2
  192.4 61.5 %forward_kernel.3 = (f32[128,1024]{1,0:T(8,128)S(1)}, bf16[1024,1024]{1,0:T(8,128)(2,1)S(1)}) custom-call(bf16[1024,128]{1,0:T(8,128)(2,1)S(1)} %get-tuple-element.49.left_ref, bf16[128,1024]{1,0:T(8,128)(2,1)S(1)} %copy-done.19, bf16[128,1024]{1,0:T(8,128)(2,1)S(1)} %bitcast.192, f32[1,1024]{1,0:T(1,128)S(1)} %get-tuple-element.132.gain_ref), custom_call_target="tpu_custom_call" | custom-call | tf_op jit(solution)/shard_map/forward_kernel/pallas_call | solution.py:828
  253.9 1.8 fusion.21
  256.2 59.6 %forward_kernel.4 = (f32[128,1024]{1,0:T(8,128)S(1)}, bf16[1024,1024]{1,0:T(8,128)(2,1)S(1)}) custom-call(bf16[1024,384]{1,0:T(8,128)(2,1)S(1)} %multiply_convert_fusion.5.left_ref, bf16[384,1024]{1,0:T(8,128)(2,1)S(1)} %get-tuple-element.105.right_ref, f32[128,1024]{1,0:T(8,128)S(1)} %get-tuple-element.51.res_ref.hid_ref, ...), custom_call_target="tpu_custom_call" | custom-call | tf_op jit(solution)/shard_map/forward_kernel/pallas_call | solution.py:828
  321.4 2.5 add_convert_fusion.5
  325.6 10.1 attend_forward.3
  339.4 65.5 %forward_kernel.5 = (f32[128,1024]{1,0:T(8,128)S(1)}, bf16[1024,1024]{1,0:T(8,128)(2,1)S(1)}) custom-call(bf16[1024,128]{1,0:T(8,128)(2,1)S(1)} %copy-done.40, bf16[128,1024]{1,0:T(8,128)(2,1)S(1)} %copy-done.25, f32[128,1024]{1,0:T(8,128)S(1)} %copy-done.28, f32[1,1024]{1,0:T(1,128)S(1)} %get-tuple-element.130.gain_ref), custom_call_target="tpu_custom_call" | custom-call | tf_op jit(solution)/shard_map/forward_kernel/pallas_call | solution.py:828
  406.3 3.2 fusion.22
  410.4 59.0 %turn_kernel.1 = (bf16[128,1024]{1,0:T(8,128)(2,1)S(1)}, bf16[1024,1024]{1,0:T(8,128)(2,1)S(1)}) custom-call(bf16[1024,384]{1,0:T(8,128)(2,1)S(1)} %multiply_convert_fusion.4.left_ref, bf16[384,1024]{1,0:T(8,128)(2,1)S(1)} %get-tuple-element.104.right_ref, f32[128,1024]{1,0:T(8,128)S(1)} %get-tuple-element.56.res_ref.hid_ref, bf16[128,1024]{1,0:T(8,128)(2,1)S(1)} %bitcast.194), custom_call_target="tpu_custom_call" | custom-call | tf_op jit(solution)/shard_map/turn_kernel/pallas_call | solution.py:828
  469.4 1.6 multiply_convert_fusion.3
  471.3 1.8 copy-done.5
  473.1 58.3 %back_kernel.3 = (f32[128,1024]{1,0:T(8,128)S(1)}, f32[1,1024]{1,0:T(1,128)S(1)}, bf16[1024,1024]{1,0:T(8,128)(2,1)S(1)}) custom-call(bf16[1024,768]{1,0:T(8,128)(2,1)S(1)} %pad_maximum_fusion.3.left_ref, bf16[1024,768]{1,0:T(8,128)(2,1)S(1)} %copy-done.5, bf16[128,1024]{1,0:T(8,128)(2,1)S(1)} %bitcast.195, ...), custom_call_target="tpu_custom_call" | custom-call | tf_op jit(solution)/shard_map/back_kernel/pallas_call | solution.py:828
  532.9 18.2 %attend_backward.2 = (f32[1024,128]{1,0:T(8,128)S(1)}, f32[2048,128]{1,0:T(8,128)S(1)}, f32[2048,128]{1,0:T(8,128)S(1)}) custom-call(bf16[1024,128]{1,0:T(8,128)(2,1)S(1)} %copy-done.24, bf16[2048,128]{1,0:T(8,128)(2,1)S(1)} %copy-done.13, bf16[2048,128]{1,0:T(8,128)(2,1)S(1)} %copy-done.11, bf16[1024,128]{1,0:T(8,128)(2,1)S(1)} %convolution_convert_fusion.5.da_ref, ...), custom_call_target="tpu_custom_call" | custom-call | tf_op jit(solution)/shard_map/attend_backward/pallas_call | solution.py:927
  553.7 2.2 convolution_bitcast_fusion
  558.1 2.3 concatenate.92.left_ref
  564.8 58.2 %back_kernel.4 = (f32[128,1024]{1,0:T(8,128)S(1)}, f32[1,1024]{1,0:T(1,128)S(1)}, bf16[1024,1024]{1,0:T(8,128)(2,1)S(1)}) custom-call(bf16[1024,384]{1,0:T(8,128)(2,1)S(1)} %copy-done.15, bf16[1024,384]{1,0:T(8,128)(2,1)S(1)} %copy-done.17, f32[128,1024]{1,0:T(8,128)S(1)} %copy-done.43, f32[128,1024]{1,0:T(8,128)S(1)} %copy-done.29, ...), custom_call_target="tpu_custom_call" | custom-call | tf_op jit(solution)/shard_map/back_kernel/pallas_call | solution.py:828
  625.4 2.0 pad_maximum_fusion
  627.5 4.4 multiply_convert_fusion.1
  632.0 1.8 copy-done.4
  634.1 59.6 %back_kernel.5 = (f32[128,1024]{1,0:T(8,128)S(1)}, f32[1,1024]{1,0:T(1,128)S(1)}, bf16[1024,1024]{1,0:T(8,128)(2,1)S(1)}) custom-call(bf16[1024,768]{1,0:T(8,128)(2,1)S(1)} %pad_maximum_fusion.4.left_ref, bf16[1024,768]{1,0:T(8,128)(2,1)S(1)} %copy-done.4, f32[128,1024]{1,0:T(8,128)S(1)} %copy-done.45, f32[128,1024]{1,0:T(8,128)S(1)} %copy-done.35, ...), custom_call_target="tpu_custom_call" | custom-call | tf_op jit(solution)/shard_map/back_kernel/pallas_call | solution.py:828
  695.2 18.2 %attend_backward.3 = (f32[1024,128]{1,0:T(8,128)S(1)}, f32[2048,128]{1,0:T(8,128)S(1)}, f32[2048,128]{1,0:T(8,128)S(1)}) custom-call(bf16[1024,128]{1,0:T(8,128)(2,1)S(1)} %copy-done.22, bf16[2048,128]{1,0:T(8,128)(2,1)S(1)} %copy-done.9, bf16[2048,128]{1,0:T(8,128)(2,1)S(1)} %copy-done.7, bf16[1024,128]{1,0:T(8,128)(2,1)S(1)} %convolution_convert_fusion.4.da_ref, ...), custom_call_target="tpu_custom_call" | custom-call | tf_op jit(solution)/shard_map/attend_backward/pallas_call | solution.py:927
  720.3 1.6 concatenate.95.left_ref
  721.9 34.1 %last_kernel.1 = (bf16[128,1024]{1,0:T(8,128)(2,1)S(1)}, f32[1,1024]{1,0:T(1,128)S(1)}) custom-call(bf16[1024,384]{1,0:T(8,128)(2,1)S(1)} %concatenate.95.left_ref, bf16[1024,384]{1,0:T(8,128)(2,1)S(1)} %copy-done.14, f32[128,1024]{1,0:T(8,128)S(1)} %copy-done.50, bf16[128,1024]{1,0:T(8,128)(2,1)S(1)} %bitcast.193, f32[1,1024]{1,0:T(1,128)S(1)} %get-tuple-element.133.gain_ref), custom_call_target="tpu_custom_call" | custom-call | tf_op jit(solution)/shard_map/last_kernel/pallas_call | solution.py:828
  757.3 4.4 broadcast_in_dim.35
  762.9 1.6 copy-done.58
  764.4 3.4 convolution_convert_fusion
  768.9 1.6 pad_maximum_fusion.2
  770.4 4.5 copy.404
  774.9 3.4 convolution_convert_fusion.1
  779.6 2.5 copy.403
  782.1 2.9 maximum_bitcast_fusion
  785.0 2.7 copy.405
  787.7 4.0 all-to-all-start.1
  794.4 100.5 %reduce-scatter.8.cloned.1.call-done = f32[32,4]{1,0:T(8,128)} async-done(((f32[1024,4]{1,0:T(8,128)}), f32[32,4]{1,0:T(8,128)}) %reduce-scatter.8.cloned.1.call-update) | async-done | bytes 528
  900.3 3.3 convert_reduce_fusion
  906.3 1.5 reshape.271
  921.4 1.5 reshape.261
  922.9 126.6 %reduce-scatter.6.cloned.1.call-done = f32[2,32,1024]{2,1,0:T(8,128)} async-done(((f32[2,1024,1024]{2,1,0:T(8,128)}), f32[2,32,1024]{2,1,0:T(8,128)}) %reduce-scatter.6.cloned.1.call-update) | async-done | bytes 262160 | tf_op jit(solution)/shard_map/reduce_scatter | solution.py:1161
  1049.5 1.7 slice_bitcast_fusion.8
  (365 shorter events, 86.5 us)
Async XLA Ops:
  7.2 11.7 %copy-start = (bf16[32,1024]{1,0:T(8,128)(2,1)S(1)}, bf16[32,1024]{1,0:T(8,128)(2,1)}, u32[]{:S(2)}) copy-start(bf16[32,1024]{1,0:T(8,128)(2,1)} %param.36) | copy-start | bytes 196612
  7.2 4.5 copy-start.92
  7.2 4.5 copy-start.93
  7.2 5.3 copy-start.91
  7.2 5.3 copy-start.87
  7.2 156.3 %all-gather.10.cloned.1.call-start = ((), (), s32[]{:S(2)}) async-start(), calls=%async_computation.7 | async-start | bytes 2162688 | tf_op jit(solution)/shard_map/all_gather | solution.py:1053
  8.4 4.7 copy-start.88
  8.4 1.8 collective-permute-start.1
  11.7 154.6 %all-gather.8.cloned.1.call-start = ((), (), s32[]{:S(2)}) async-start(), calls=%async_computation.5 | async-start | bytes 4325376 | tf_op jit(solution)/shard_map/all_gather | solution.py:1057
  11.7 3.0 copy-start.84
  12.4 159.4 %all-gather.6.cloned.1.call-start = ((), (), s32[]{:S(2)}) async-start(), calls=%async_computation.4 | async-start | bytes 7077888 | tf_op jit(solution)/shard_map/all_gather | solution.py:1046
  89.2 41.7 %copy-start.18 = (bf16[1,128,1024]{2,1,0:T(8,128)(2,1)S(1)}, bf16[1,128,1024]{2,1,0:T(8,128)(2,1)}, u32[]{:S(2)}) copy-start(bf16[1,128,1024]{2,1,0:T(8,128)(2,1)} %param.21) | copy-start | bytes 786436
  89.3 703.7 %all-reduce.8.cloned.1.call-start = ((), (), s32[]{:S(2)}) async-start(), calls=%async_computation.9 | async-start | bytes 5767168
  171.8 3.0 copy-start.31
  174.7 145.1 %copy-start.65 = (bf16[2,32,32,1152]{3,2,1,0:T(8,128)(2,1)}, bf16[2,32,32,1152]{3,2,1,0:T(8,128)(2,1)S(1)}, u32[]{:S(2)}) copy-start(bf16[2,32,32,1152]{3,2,1,0:T(8,128)(2,1)S(1)} %copy.377) | copy-start | bytes 14155780
  177.7 2.6 collective-permute-start
  180.6 11.8 %copy-start.19 = (bf16[128,1024]{1,0:T(8,128)(2,1)S(1)}, bf16[128,1024]{1,0:T(8,128)(2,1)}, u32[]{:S(2)}) copy-start(bf16[128,1024]{1,0:T(8,128)(2,1)} %get-tuple-element.87.right_ref) | copy-start | bytes 786436
  180.7 10.1 copy-start.8
  192.4 63.3 %copy-start.37 = (bf16[1024,128]{1,0:T(8,128)(2,1)}, bf16[1024,128]{1,0:T(8,128)(2,1)S(1)}, u32[]{:S(2)}) copy-start(bf16[1024,128]{1,0:T(8,128)(2,1)S(1)} %get-tuple-element.49.left_ref) | copy-start | bytes 786436
  255.7 60.1 %copy-start.72 = (f32[1024,768]{1,0:T(8,128)}, f32[1024,768]{1,0:T(8,128)S(1)}, u32[]{:S(2)}) copy-start(f32[1024,768]{1,0:T(8,128)S(1)} %fusion.21) | copy-start | bytes 9437188
  256.1 60.9 %copy-start.2 = (bf16[1024,384]{1,0:T(8,128)(2,1)}, bf16[1024,384]{1,0:T(8,128)(2,1)S(1)}, u32[]{:S(2)}) copy-start(bf16[1024,384]{1,0:T(8,128)(2,1)S(1)} %multiply_convert_fusion.5.left_ref) | copy-start | bytes 2359300
  319.8 4.3 collective-permute-start.2
  325.4 13.0 %copy-start.25 = (bf16[128,1024]{1,0:T(8,128)(2,1)S(1)}, bf16[128,1024]{1,0:T(8,128)(2,1)}, u32[]{:S(2)}) copy-start(bf16[128,1024]{1,0:T(8,128)(2,1)} %get-tuple-element.86.right_ref) | copy-start | bytes 786436
  325.4 13.0 %copy-start.28 = (f32[128,1024]{1,0:T(8,128)S(1)}, f32[128,1024]{1,0:T(8,128)}, u32[]{:S(2)}) copy-start(f32[128,1024]{1,0:T(8,128)} %copy-done.27) | copy-start | bytes 1572868
  325.5 10.1 copy-start.10
  325.5 10.1 copy-start.12
  409.9 59.5 %copy-start.71 = (bf16[2,2,2,88,1024]{4,3,1,0,2:T(8,128)(2,1)S(1)}, bf16[2,2,2,88,1024]{4,3,1,0,2:T(8,128)(2,1)}, u32[]{:S(2)}) copy-start(bf16[2,2,2,88,1024]{4,3,1,0,2:T(8,128)(2,1)} %copy-done.70) | copy-start | bytes 4325380
  471.1 60.3 %copy-start.79 = (bf16[1024,384]{1,0:T(8,128)(2,1)}, bf16[1024,384]{1,0:T(8,128)(2,1)S(1)}, u32[]{:S(2)}) copy-start(bf16[1024,384]{1,0:T(8,128)(2,1)S(1)} %get-tuple-element.84) | copy-start | bytes 2359300
  471.1 60.3 %copy-start.80 = (bf16[1024,384]{1,0:T(8,128)(2,1)}, bf16[1024,384]{1,0:T(8,128)(2,1)S(1)}, u32[]{:S(2)}) copy-start(bf16[1024,384]{1,0:T(8,128)(2,1)S(1)} %get-tuple-element.85) | copy-start | bytes 2359300
  471.3 60.2 %copy-start.26 = (bf16[128,1024]{1,0:T(8,128)(2,1)S(1)}, bf16[128,1024]{1,0:T(8,128)(2,1)}, u32[]{:S(2)}) copy-start(bf16[128,1024]{1,0:T(8,128)(2,1)} %get-tuple-element.86.right_ref) | copy-start | bytes 786436
  551.4 4.5 collective-permute-start.3
  560.4 62.6 %copy-start.3 = (bf16[1024,384]{1,0:T(8,128)(2,1)S(1)}, bf16[1024,384]{1,0:T(8,128)(2,1)}, u32[]{:S(2)}) copy-start(bf16[1024,384]{1,0:T(8,128)(2,1)} %copy-done.2) | copy-start | bytes 2359300
  627.4 267.5 %reduce-scatter.8.cloned.1.call-start = ((), (), s32[]{:S(2)}) async-start(), calls=%async_computation.8 | async-start | bytes 540672
  631.8 61.9 %copy-start.81 = (bf16[1024,384]{1,0:T(8,128)(2,1)}, bf16[1024,384]{1,0:T(8,128)(2,1)S(1)}, u32[]{:S(2)}) copy-start(bf16[1024,384]{1,0:T(8,128)(2,1)S(1)} %get-tuple-element.82) | copy-start | bytes 2359300
  631.9 61.9 %copy-start.82 = (bf16[1024,384]{1,0:T(8,128)(2,1)}, bf16[1024,384]{1,0:T(8,128)(2,1)S(1)}, u32[]{:S(2)}) copy-start(bf16[1024,384]{1,0:T(8,128)(2,1)S(1)} %get-tuple-element.83) | copy-start | bytes 2359300
  634.1 59.7 %copy-start.20 = (bf16[128,1024]{1,0:T(8,128)(2,1)S(1)}, bf16[128,1024]{1,0:T(8,128)(2,1)}, u32[]{:S(2)}) copy-start(bf16[128,1024]{1,0:T(8,128)(2,1)} %get-tuple-element.87.right_ref) | copy-start | bytes 786436
  713.7 4.4 collective-permute-start.4
  757.1 4.7 copy-start.77
  757.1 292.4 %reduce-scatter.6.cloned.1.call-start = ((), (), s32[]{:S(2)}) async-start(), calls=%async_computation.6 | async-start | bytes 8650752 | tf_op jit(solution)/shard_map/reduce_scatter | solution.py:1161
  764.4 3.4 copy-start.16
  764.4 3.4 copy-start.56
  770.4 4.5 copy-start.54
  774.9 3.4 copy-start.32
  787.7 4.0 copy-start.99
  787.7 112.6 %all-to-all-start.1 = ((bf16[32,2,32,1152]{3,2,1,0:T(8,128)(2,1)}), bf16[32,2,32,1152]{3,2,1,0:T(8,128)(2,1)}, u32[]{:S(2)}, u32[]{:S(2)}) async-start(bf16[32,2,32,1152]{3,2,1,0:T(8,128)(2,1)} %copy.405), calls=%async_computation.1 | async-start | bytes 9437184 | tf_op jit(solution)/shard_map/all_to_all | solution.py:1151
  794.1 104.1 %collective-permute-start.5 = (f32[2,88,1024]{2,1,0:T(8,128)S(1)}, f32[2,88,1024]{2,1,0:T(8,128)S(1)}, u32[]{:S(2)}, u32[]{:S(2)}) collective-permute-start(f32[2,88,1024]{2,1,0:T(8,128)S(1)} %dynamic-slice_bitcast_fusion), channel_id=1, source_target_pairs={{0,1},{1,0},{2,3},{3,2},{4,5},{5,4},{6,7},{7,6},{8,9},{9,8},{10,11... | collective-permute-start | bytes 2162696 | tf_op jit(solution)/shard_map/ppermute | solution.py:1004
  919.1 132.1 %copy-start.52 = (bf16[128,1024]{1,0:T(8,128)(2,1)S(1)}, bf16[128,1024]{1,0:T(8,128)(2,1)}, u32[]{:S(2)}) copy-start(bf16[128,1024]{1,0:T(8,128)(2,1)} %copy-done.51) | copy-start | bytes 786436
  920.6 132.0 %copy-start.1 = (bf16[32,1024]{1,0:T(8,128)(2,1)S(1)}, bf16[32,1024]{1,0:T(8,128)(2,1)}, u32[]{:S(2)}) copy-start(bf16[32,1024]{1,0:T(8,128)(2,1)} %param.36) | copy-start | bytes 196612
  (65 other events, 102.2 us)
Sparse Core Ops, SparseCore 0:
  11.8 28.3 all-gather.9
  43.7 65.4 all-gather.7
  110.7 61.0 all-gather.5
  627.5 78.2 all-reduce.7
  757.2 137.6 reduce-scatter.7
  897.0 152.4 reduce-scatter.5

commit v2 on v1

--- a/solution.py
+++ b/solution.py
@@ -781,36 +781,33 @@
 def back_rows(total, grad, hidden, gain):
     inverse = norm_rows(hidden)
     normed = hidden * inverse
-    gain_grad = jnp.sum(total * normed, axis=0, keepdims=True)
     scaled = total * gain
     mean = jnp.mean(scaled * normed, axis=-1, keepdims=True)
-    return grad + inverse * (scaled - normed * mean), gain_grad
-
-
-def back_kernel(left_ref, right_ref, grad_ref, hid_ref, gain_ref, new_ref, gg_ref, full_ref, *scratch):
+    return grad + inverse * (scaled - normed * mean)
+
+
+def back_kernel(left_ref, right_ref, grad_ref, hid_ref, gain_ref, new_ref, full_ref, *scratch):
     place = plane_place()
     greet_plane(place[0], place[1], place[3])
     bufs, sems, more = scratch[:7], scratch[7:13], scratch[13:]
     finish = reduce_plane(place, make_product(left_ref, right_ref, True), bufs, sems)
-    new, gain_grad = back_rows(
+    new = back_rows(
         bufs[2][place[3]], grad_ref[...].astype(F32), hid_ref[...].astype(F32), gain_ref[...]
     )
-    gg_ref[...] = gain_grad
     new_ref[...] = new
     full_ref[own_rows(place), :] = new.astype(BF)
     gather_plane(place, full_ref, more)
     finish()
 
 
-def last_kernel(left_ref, right_ref, grad_ref, hid_ref, gain_ref, out_ref, gg_ref, *scratch):
+def last_kernel(left_ref, right_ref, grad_ref, hid_ref, gain_ref, out_ref, *scratch):
     place = plane_place()
     greet_plane(place[0], place[1], place[3])
     bufs, sems = scratch[:7], scratch[7:13]
     finish = reduce_plane(place, make_product(left_ref, right_ref, True), bufs, sems)
-    new, gain_grad = back_rows(
+    new = back_rows(
         bufs[2][place[3]], grad_ref[...].astype(F32), hid_ref[...].astype(F32), gain_ref[...]
     )
-    gg_ref[...] = gain_grad
     out_ref[...] = new.astype(BF)
     finish()
 
@@ -836,6 +833,256 @@
         ),
         name=kernel.__name__,
     )(*args)
+
+
+def chip_peers(f, c):
+    chip, core = c // 2, c % 2
+    return [(f, 2 * ((chip + i) % 8) + core) for i in range(1, 8)], (f, flip(c, 1)), (1 - f, c)
+
+
+def greet(targets):
+    barrier = pltpu.get_barrier_semaphore()
+    for target in targets:
+        pl.semaphore_signal(barrier, inc=1, device_id=to_device(*target), device_id_type=MESH)
+    pl.semaphore_wait(barrier, len(targets))
+
+
+def spread_kernel(a1, a2, dn, op, r1, r2, d1, d2, o1, o2, *sems):
+    f, c, y, z = plane_place()
+    chip, core = c // 2, c % 2
+    peers, sibling, twin = chip_peers(f, c)
+    near = (f, flip(c, 2))
+    greet(peers + [sibling, twin])
+    ds, dr, xs, xr, ss, sr, ws, wr = sems
+    mine = f * 16 + c
+    tables = ((a1, r1), (a2, r2))
+    downs = (d1, d2)
+    outs = (o1, o2)
+    home = y == f
+    pending = []
+
+    def send(src, dst, send_sem, recv_sem, target):
+        copy = remote(src, dst, send_sem, recv_sem, target)
+        copy.start()
+        pending.append(copy)
+        return copy
+
+    direct = {}
+    crossed = {}
+    inner = []
+    for l, (a, r) in enumerate(tables):
+        for i in range(1, 8):
+            t = (chip + i) % 8
+            direct[l, i] = send(a.at[t], r.at[mine], ds.at[l, i], dr.at[l, i], peers[i - 1])
+        r[mine] = a[chip]
+        crossed[l, 0] = send(a.at[chip], r.at[mine], xs.at[l, 0], xr.at[l, 0], twin)
+        inner.append(send(a.at[chip], r.at[mine], ss.at[l, 0], sr.at[l, 0], sibling))
+        part = 2 * f + core
+        downs[l][part] = dn[l]
+        crossed[l, 8] = send(dn.at[l], downs[l].at[part], xs.at[l, 8], xr.at[l, 8], twin)
+        inner.append(send(dn.at[l], downs[l].at[part], ss.at[l, 16], sr.at[l, 16], sibling))
+
+        def out_copy():
+            return remote(op.at[l], outs[l].at[2 * y + core], ws.at[l, 0], wr.at[l, 0], near)
+
+        @pl.when(home)
+        def _():
+            outs[l][2 * y + core] = op[l]
+
+        @pl.when(jnp.logical_not(home))
+        def _():
+            out_copy().start()
+
+    for l, (a, r) in enumerate(tables):
+        for i in range(1, 8):
+            direct[l, i].wait_recv()
+            source = f * 16 + 2 * ((chip + 8 - i) % 8) + core
+            crossed[l, i] = send(r.at[source], r.at[source], xs.at[l, i], xr.at[l, i], twin)
+            inner.append(send(r.at[source], r.at[source], ss.at[l, i], sr.at[l, i], sibling))
+
+    def pair(l):
+        return [outs[l].at[core], outs[l].at[2 + core]]
+
+    def pair_copies(l, s, r, first, target):
+        return [remote(p, p, s.at[l, first + n], r.at[l, first + n], target) for n, p in enumerate(pair(l))]
+
+    for l in range(2):
+
+        @pl.when(home)
+        def _():
+            remote(op.at[l], outs[l].at[2 * y + core], ws.at[l, 0], wr.at[l, 0], near).wait_recv()
+            for copy in pair_copies(l, xs, xr, 9, twin):
+                copy.start()
+
+        @pl.when(jnp.logical_not(home))
+        def _():
+            for copy in pair_copies(l, xs, xr, 9, twin):
+                copy.wait_recv()
+
+        for copy in pair_copies(l, ss, sr, 18, sibling):
+            copy.start()
+
+    for l, (a, r) in enumerate(tables):
+        for i in range(8):
+            crossed[l, i].wait_recv()
+            source = (1 - f) * 16 + 2 * ((chip + 8 - i) % 8) + core
+            inner.append(send(r.at[source], r.at[source], ss.at[l, 8 + i], sr.at[l, 8 + i], sibling))
+        crossed[l, 8].wait_recv()
+        part = 2 * (1 - f) + core
+        inner.append(
+            send(downs[l].at[part], downs[l].at[part], ss.at[l, 17], sr.at[l, 17], sibling)
+        )
+    for copy in inner:
+        copy.wait_recv()
+    for copy in pending:
+        copy.wait_send()
+    for l in range(2):
+        for copy in pair_copies(l, ss, sr, 18, sibling):
+            copy.wait()
+
+        @pl.when(home)
+        def _():
+            for copy in pair_copies(l, xs, xr, 9, twin):
+                copy.wait_send()
+
+        @pl.when(jnp.logical_not(home))
+        def _():
+            remote(op.at[l], outs[l].at[2 * y + core], ws.at[l, 0], wr.at[l, 0], near).wait_send()
+
+
+def spread_call(a1, a2, down, out):
+    rows, wide = a1.shape[1:]
+    block, width = down.shape[1:]
+    spec = pl.BlockSpec(memory_space=VMEM_SPACE)
+    shapes = [(32, rows, wide)] * 2 + [(4, block, width)] * 2 + [(4, rows, width)] * 2
+    counts = (8, 8, 11, 11, 20, 20, 1, 1)
+    return pl.pallas_call(
+        spread_kernel,
+        out_shape=[jax.ShapeDtypeStruct(s, BF) for s in shapes],
+        in_specs=[spec] * 4,
+        out_specs=[spec] * 6,
+        scratch_shapes=[pltpu.SemaphoreType.DMA((2, n)) for n in counts],
+        compiler_params=pltpu.CompilerParams(
+            collective_id=9, has_side_effects=True, vmem_limit_bytes=40 * 1024 * 1024
+        ),
+        name="spread",
+    )(a1, a2, down, out)
+
+
+def collect_kernel(g1, g2, gd1, gd2, go1, go2, c1, c2, od1, od2, oo1, oo2, *scratch):
+    f, c, y, z = plane_place()
+    chip, core = c // 2, c % 2
+    peers, sibling, twin = chip_peers(f, c)
+    near = (f, flip(c, 2))
+    greet(peers + [sibling, twin])
+    sb, xb, xt, ut, sd, xd, td, so, xo, to, yo, yt = scratch[:12]
+    ss, sr, xs, xr, ps, pr, ys, yr = scratch[12:]
+    home = y == f
+    pending = []
+
+    def send(src, dst, send_sem, recv_sem, target):
+        copy = remote(src, dst, send_sem, recv_sem, target)
+        copy.start()
+        pending.append(copy)
+        return copy
+
+    tables = ((g1, c1, gd1, od1, go1, oo1), (g2, c2, gd2, od2, go2, oo2))
+    inner = {}
+    for l, (g, _, gd, _, go, _) in enumerate(tables):
+        for half in range(2):
+            part = 8 * ((1 - f) if half == 0 else f)
+            inner[l, half] = send(
+                g.at[pl.ds(part, 8), 1 - core], sb.at[l, pl.ds(part, 8)],
+                ss.at[l, half], sr.at[l, half], sibling,
+            )
+        inner[l, 2] = send(gd.at[:, 1 - core], sd.at[l], ss.at[l, 2], sr.at[l, 2], sibling)
+        inner[l, 3] = send(go.at[:, 1 - core], so.at[l], ss.at[l, 3], sr.at[l, 3], sibling)
+    crossed = {}
+    for l, (g, _, gd, _, go, _) in enumerate(tables):
+        inner[l, 0].wait_recv()
+        for i in range(8):
+            t = (chip + i + 1) % 8
+            at = (1 - f) * 8 + t
+            xt[l, t] = (g[at, core].astype(F32) + sb[l, at].astype(F32)).astype(BF)
+            crossed[l, i] = send(xt.at[l, t], xb.at[l, t], xs.at[l, i], xr.at[l, i], twin)
+        inner[l, 2].wait_recv()
+        td[l] = (gd[1 - f, core].astype(F32) + sd[l, 1 - f].astype(F32)).astype(BF)
+        crossed[l, 8] = send(td.at[l], xd.at[l], xs.at[l, 8], xr.at[l, 8], twin)
+        inner[l, 3].wait_recv()
+
+        def twin_copy():
+            return remote(to.at[l], xo.at[l], xs.at[l, 9], xr.at[l, 9], twin)
+
+        for side in range(2):
+            to[l, side] = (go[side, core].astype(F32) + so[l, side].astype(F32)).astype(BF)
+
+        @pl.when(jnp.logical_not(home))
+        def _():
+            twin_copy().start()
+
+    direct = {}
+    for l, (g, out, gd, od, go, oo) in enumerate(tables):
+        inner[l, 1].wait_recv()
+        for i in range(8):
+            t = (chip + i + 1) % 8
+            at = f * 8 + t
+            crossed[l, i].wait_recv()
+            total = g[at, core].astype(F32) + sb[l, at].astype(F32) + xb[l, t].astype(F32)
+            if i < 7:
+                ut[l, t] = total.astype(BF)
+                direct[l, i] = send(ut.at[l, t], out.at[chip], ps.at[l, i], pr.at[l, i], peers[i])
+            else:
+                out[chip] = total.astype(BF)
+        crossed[l, 8].wait_recv()
+        od[...] = gd[f, core].astype(F32) + sd[l, f].astype(F32) + xd[l].astype(F32)
+
+        @pl.when(home)
+        def _():
+            remote(to.at[l], xo.at[l], xs.at[l, 9], xr.at[l, 9], twin).wait_recv()
+            oo[...] = to[l, y].astype(F32) + xo[l, y].astype(F32)
+            yt[l] = (to[l, 1 - y].astype(F32) + xo[l, 1 - y].astype(F32)).astype(BF)
+            remote(yt.at[l], yo.at[l], ys.at[l], yr.at[l], near).start()
+
+    for l, (g, out, gd, od, go, oo) in enumerate(tables):
+
+        @pl.when(home)
+        def _():
+            remote(yt.at[l], yo.at[l], ys.at[l], yr.at[l], near).wait_send()
+
+        @pl.when(jnp.logical_not(home))
+        def _():
+            remote(yt.at[l], yo.at[l], ys.at[l], yr.at[l], near).wait_recv()
+            oo[...] = yo[l].astype(F32)
+            remote(to.at[l], xo.at[l], xs.at[l, 9], xr.at[l, 9], twin).wait_send()
+
+    for copy in direct.values():
+        copy.wait_recv()
+    for copy in pending:
+        copy.wait_send()
+
+
+def collect_call(packs, downs, outs):
+    rows, wide = packs[0].shape[2:]
+    block, width = downs[0].shape[2:]
+    spec = pl.BlockSpec(memory_space=VMEM_SPACE)
+    shapes = [((8, rows, wide), BF)] * 2 + [((block, width), F32)] * 2 + [((rows, width), F32)] * 2
+    buffers = [
+        (2, 16, rows, wide), (2, 8, rows, wide), (2, 8, rows, wide), (2, 8, rows, wide),
+        (2, 2, block, width), (2, block, width), (2, block, width),
+        (2, 2, rows, width), (2, 2, rows, width), (2, 2, rows, width), (2, rows, width), (2, rows, width),
+    ]
+    counts = ((2, 4), (2, 4), (2, 10), (2, 10), (2, 7), (2, 7), (2,), (2,))
+    return pl.pallas_call(
+        collect_kernel,
+        out_shape=[jax.ShapeDtypeStruct(*s) for s in shapes],
+        in_specs=[spec] * 6,
+        out_specs=[spec] * 6,
+        scratch_shapes=[pltpu.VMEM(b, BF) for b in buffers] + [pltpu.SemaphoreType.DMA(n) for n in counts],
+        compiler_params=pltpu.CompilerParams(
+            collective_id=10, has_side_effects=True, vmem_limit_bytes=56 * 1024 * 1024
+        ),
+        name="collect",
+    )(*packs, *downs, *outs)
 
 
 def head_lanes(head):
@@ -951,38 +1198,54 @@
     )(q, k, v, da, lse_rows, pos_q, pos_k)
 
 
+def chip_first(split):
+    order = (2, 1, 0) + tuple(range(3, split.ndim))
+    return split.transpose(order).reshape(8, split.shape[0], *split.shape[3:])
+
+
+def chip_last(packed):
+    split = packed.reshape(4, 2, *packed.shape[1:])
+    return split.transpose((2, 1, 0) + tuple(range(3, split.ndim)))
+
+
 def pack_heads(weight):
     rows = weight.shape[0]
-    split = weight.reshape(rows, 8, 2, 2, 32)
-    return split.transpose(1, 0, 3, 2, 4).reshape(8, rows, 128)
+    split = chip_first(weight.reshape(rows, 2, 4, 2, 2, 32))
+    return split.transpose(0, 1, 3, 2, 4).reshape(8, rows, 128)
 
 
 def unpack_heads(packed):
     rows = packed.shape[1]
-    split = packed.reshape(8, rows, 2, 2, 32)
-    return split.transpose(1, 0, 3, 2, 4).reshape(rows, 1024)
+    split = packed.reshape(8, rows, 2, 2, 32).transpose(0, 1, 3, 2, 4)
+    return chip_last(split).reshape(rows, 1024)
 
 
 def pack_values(weight):
     rows = weight.shape[0]
-    return weight.reshape(rows, 8, 128).transpose(1, 0, 2)
+    return chip_first(weight.reshape(rows, 2, 4, 128))
 
 
 def unpack_values(packed):
-    return packed.transpose(1, 0, 2).reshape(packed.shape[1], 1024)
-
-
-def pack_units(weight, width):
+    return chip_last(packed).reshape(packed.shape[1], 1024)
+
+
+def pack_units(weight, block, *extra):
     rows, units = weight.shape
     each = units // 32
-    split = weight.reshape(rows, 2, 8, 2, each).transpose(2, 0, 1, 3, 4).reshape(8, rows, 4 * each)
-    return jnp.pad(split, ((0, 0), (0, 0), (0, width - 4 * each)))
+    split = weight.reshape(rows, 2, 8, 2, each).transpose(2, 0, 1, 3, 4).reshape(8, rows, 4, each)
+    padding = jnp.zeros((8, rows, 4, block - each), weight.dtype)
+    if extra:
+        columns = jnp.stack(extra, axis=-1)
+        columns = jnp.pad(columns, ((0, 0), (0, block - each - len(extra))))
+        first = jnp.broadcast_to(columns[None, :, None, :], (8, rows, 1, block - each))
+        padding = jnp.concatenate([first, padding[:, :, 1:]], axis=2)
+    return jnp.concatenate([split, padding], axis=-1).reshape(8, rows, 4 * block)
 
 
 def unpack_units(packed, units):
     rows = packed.shape[1]
     each = units // 32
-    split = packed[:, :, : 4 * each].reshape(8, rows, 2, 2, each)
+    split = packed.reshape(8, rows, 2, 2, -1)[..., :each]
     return split.transpose(1, 2, 0, 3, 4).reshape(rows, units)
 
 
@@ -1007,7 +1270,9 @@
 def fast_local(tokens, cotangent, pair_of, *shards):
     width = tokens.shape[2]
     units = shards[6].shape[1]
-    hidden_pad = (units // 8 + 127) // 128 * 128
+    each = units // 32
+    block = (each + 2 + 31) // 32 * 32
+    hidden_pad = 4 * block
     c = lax.axis_index("ctx")
     core = c % 2
     chip = c // 2
@@ -1020,10 +1285,6 @@
     sine = jnp.concatenate([sine, sine], axis=-1)
 
     layers = [shards[:9], shards[9:]]
-    gains = lax.all_gather(
-        jnp.stack([shards[0], shards[5], shards[9], shards[14]]), ("fsdp", "ctx"), axis=1, tiled=True
-    ).astype(F32)
-    gains = [gains[i : i + 1] for i in range(4)]
     packs = []
     for layer in layers:
         packs.append(
@@ -1032,33 +1293,24 @@
                     pack_heads(layer[1]),
                     pack_heads(layer[2]),
                     pack_values(layer[3]),
-                    pack_units(layer[6], hidden_pad),
-                    pack_units(layer[7], hidden_pad),
+                    pack_units(layer[6], block, layer[0], layer[5]),
+                    pack_units(layer[7], block),
                 ],
                 axis=-1,
             )
         )
-    packed = jnp.stack(packs, axis=1)
-    rows_each = packed.shape[2]
-    wide = packed.shape[3]
-    packed = jnp.repeat(packed, 2, axis=0)
-    got = lax.all_to_all(packed, "ctx", 0, 0, tiled=True)
-    got = lax.all_gather(got, "fsdp", axis=0, tiled=True)
-    got = got.transpose(1, 0, 2, 3).reshape(2, 32 * rows_each, wide)
-    qkv_w = [got[i, :, :384] for i in range(2)]
-    up_w = [got[i, :, 384:] for i in range(2)]
-    down = jnp.stack([layers[0][8], layers[1][8]])
-    down = jnp.stack([down, swap_cores(down)])
-    down = lax.dynamic_slice_in_dim(jnp.concatenate([down, down]), core, 2, 0)
-    down = lax.all_gather(down, "fsdp", axis=0, tiled=False)
-    down = down.transpose(2, 0, 1, 3, 4).reshape(2, -1, width)
-    down = jnp.pad(down, ((0, 0), (0, hidden_pad - down.shape[1]), (0, 0)))
-    down_w = [down[0], down[1]]
-    outs = lax.all_gather(
-        jnp.stack([layers[0][4], layers[1][4]]), ("fsdp", "ctx"), axis=1, tiled=True
-    )
-    outs = lax.dynamic_slice_in_dim(outs, chip * 128, 128, 1)
-    out_w = [outs[0], outs[1]]
+    rows_each, wide = packs[0].shape[1:]
+    down = jnp.pad(jnp.stack([layers[0][8], layers[1][8]]), ((0, 0), (0, block - each), (0, 0)))
+    spread = spread_call(*packs, down, jnp.stack([layers[0][4], layers[1][4]]))
+    all_w = [w.reshape(32 * rows_each, wide) for w in spread[:2]]
+    qkv_w = [w[:, :384] for w in all_w]
+    up_w = [w[:, 384:] for w in all_w]
+    down_w = [w.reshape(hidden_pad, width) for w in spread[2:4]]
+    out_w = [w.reshape(4 * rows_each, width) for w in spread[4:]]
+    gains = []
+    for w in all_w:
+        columns = w[:, 384 + each : 384 + each + 2].astype(F32).T
+        gains += [columns[:1], columns[1:]]
 
     tok = tokens.reshape(ROWS, width)
     cot = cotangent.reshape(ROWS, width)
@@ -1107,7 +1359,6 @@
     grad_packs = [None, None]
     grad_down = [None, None]
     grad_out = [None, None]
-    gain_grads = [None] * 4
     for layer in (1, 0):
         x_full, q, k, v, lse, att, mlp_full, gate, up, inner, hidden, middle = saved[layer]
         grad_down[layer] = left_product(inner, full)
@@ -1117,8 +1368,8 @@
         grad_up = (grad_inner * gate * sigma).astype(BF)
         both = jnp.concatenate([grad_gate, grad_up], axis=-1)
         grad_upw = left_product(mlp_full, both)
-        grad_mid, gain_grads[2 * layer + 1], full = comm_call(
-            back_kernel, [rows_type, ((1, width), F32), full_type], 5 + layer,
+        grad_mid, full = comm_call(
+            back_kernel, [rows_type, full_type], 5 + layer,
             (both, up_w[layer], grad, middle, gains[2 * layer + 1]), True, True,
         )
         grad_out[layer] = left_product(att, full)
@@ -1138,43 +1389,36 @@
         grad_qkv = left_product(x_full, three)
         grad_packs[layer] = jnp.concatenate([grad_qkv, grad_upw], axis=-1)
         if layer == 1:
-            grad, gain_grads[2], full = comm_call(
-                back_kernel, [rows_type, ((1, width), F32), full_type], 7,
+            grad, full = comm_call(
+                back_kernel, [rows_type, full_type], 7,
                 (three, qkv_w[layer], grad_mid, hidden, gains[2]), True, True,
             )
         else:
-            tokens_grad, gain_grads[0] = comm_call(
-                last_kernel, [((ROWS, width), BF), ((1, width), F32)], 8,
+            (tokens_grad,) = comm_call(
+                last_kernel, [((ROWS, width), BF)], 8,
                 (three, qkv_w[layer], grad_mid, hidden, gains[0]), True, False,
             )
-    sent = jnp.stack(grad_packs).astype(BF).reshape(2, 32, rows_each, wide).transpose(1, 0, 2, 3)
-    back = lax.all_to_all(sent, ("fsdp", "ctx"), 0, 0, tiled=True)
-    back = back.reshape(2, 8, 2, 2, rows_each, wide).astype(F32).sum(axis=(0, 2))
-    each = units // 32
-    downs = jnp.stack(grad_down)[:, : 4 * each].reshape(2, 2, 2, each, width)
-    downs = lax.psum_scatter(downs, "fsdp", scatter_dimension=1, tiled=False)
-    own = lax.dynamic_index_in_dim(downs, core, 1, False)
-    other = lax.dynamic_index_in_dim(downs, 1 - core, 1, False)
-    downs = own + swap_cores(other)
-    wide_out = jnp.zeros((2, 1024, width), F32)
-    wide_out = lax.dynamic_update_slice_in_dim(wide_out, jnp.stack(grad_out), chip * 128, 1)
-    outs = lax.psum_scatter(wide_out, ("fsdp", "ctx"), scatter_dimension=1, tiled=True)
-    gg = lax.psum_scatter(
-        jnp.concatenate(gain_grads), ("fsdp", "ctx"), scatter_dimension=1, tiled=True
+    collected = collect_call(
+        [g.astype(BF).reshape(16, 2, rows_each, wide) for g in grad_packs],
+        [g.astype(BF).reshape(2, 2, block, width) for g in grad_down],
+        [g.astype(BF).reshape(2, 2, rows_each, width) for g in grad_out],
     )
     result = [output.reshape(1, ROWS, width), tokens_grad.reshape(1, ROWS, width)]
     for layer in range(2):
-        pack = back[:, layer]
+        pack = collected[layer].astype(F32)
+        both = pack * packs[layer].astype(F32)
+        pre_grad = jnp.sum(both[:, :, :384], axis=(0, 2)) / layers[layer][0].astype(F32)
+        mid_grad = jnp.sum(both[:, :, 384:], axis=(0, 2)) / layers[layer][5].astype(F32)
         result += [
-            gg[2 * layer],
+            pre_grad,
             unpack_heads(pack[:, :, :128]),
             unpack_heads(pack[:, :, 128:256]),
             unpack_values(pack[:, :, 256:384]),
-            outs[layer],
-            gg[2 * layer + 1],
+            collected[4 + layer],
+            mid_grad,
             unpack_units(pack[:, :, 384 : 384 + hidden_pad], units),
             unpack_units(pack[:, :, 384 + hidden_pad :], units),
-            downs[layer],
+            collected[2 + layer][:each],
         ]
     return tuple(result)
 

time: 1070 us -> 790 us (0.74)
  waiting for transfers between devices: 232 us -> 0.01 us
  blocking collectives: 110 us -> 0 us
  Pallas kernels: 541 us -> 644 us
  local copies, waits for them, and re-layouts: 91.4 us -> 71.5 us
  between operations: 17.2 us -> 2.99 us
    reduce_scatter x1 -> x0, waiting for transfers between devices: 127 us -> none  [fast_local(): lax.psum_scatter(wide_out, ('fsdp', 'ctx'), scatter_dimension=1, tiled=True)]
    unnamed x8 -> x0, waiting for transfers between devices: 101 us -> none
    pallas_call x0 -> x2, Pallas kernels: none -> 100 us  [the longest x1 53.3 us: collect_call(): pl.pallas_call(collect_kernel, out_shape=[jax.ShapeDtypeStruct(*s) for s...]
    all_to_all x1 -> x0, blocking collectives: 69.5 us -> none  [fast_local(): got = lax.all_to_all(packed, 'ctx', 0, 0, tiled=True)]
    all_gather x1 -> x0, blocking collectives: 40 us -> none  [fast_local(): lax.all_gather(jnp.stack([shards[0], shards[5], shards[9], shards[14]]),...]
    unnamed x220 -> x252, local copies, waits for them, and re-layouts: 31 us -> 28.4 us
  transfers between devices with their start and end apart: 13 -> 4, of which waited for: 4 -> 0; matrix products, arithmetic and copies ran while one was open for 9% -> 3% of each run, Pallas kernels for 13% -> 0%
where the time goes in v2:
time: 790 us; the launch traced here: 785 us
  Pallas kernels  644 us (82%)
  local copies, waits for them, and re-layouts  71.5 us (9%)
  other arithmetic  35.8 us (5%)
  matrix products  30.3 us (4%)
    pallas_call x9, Pallas kernels, comm_call(): pl.pallas_call(kernel, out_shape=[jax.ShapeDtypeStruct(*o) for o in outs]...  486 us
    pallas_call x1, Pallas kernels, collect_call(): pl.pallas_call(collect_kernel, out_shape=[jax.ShapeDtypeStruct(*s) for s...  53.3 us
    pallas_call x1, Pallas kernels, spread_call(): pl.pallas_call(spread_kernel, out_shape=[jax.ShapeDtypeStruct(s, BF) for...  46.8 us
    pallas_call x2, Pallas kernels, attend_backward(): pl.pallas_call(attend_back_kernel, grid=(rows // step,), out_shape=[jax.S...  37.8 us
    unnamed x252, local copies, waits for them, and re-layouts  28.4 us
    pallas_call x2, Pallas kernels, attend_forward(): pl.pallas_call(attend_kernel, grid=(rows // step,), out_shape=[jax.ShapeD...  20.6 us
    dot_general x8, matrix products, left_product(): lax.dot_general(left, right, (((0,), (0,)), ((), ())), preferred_element_...  16.9 us
  transfers between devices with their start and end apart: 4, of which 0 were waited for; matrix products, arithmetic and copies ran while one was open for 3% of the time, Pallas kernels for 0%

profile of v2, /device:TPU:0, one launch (start us, length us, event | category | flops | bytes accessed | tf_op | source)
XLA Modules:
  0.0 784.8 jit_solution(12724136027755835822)
XLA Ops:
  14.8 46.8 %spread.1 = (bf16[32,32,1152]{2,1,0:T(8,128)(2,1)S(1)}, bf16[32,32,1152]{2,1,0:T(8,128)(2,1)S(1)}, bf16[4,96,1024]{2,1,0:T(8,128)(2,1)S(1)}, bf16[4,96,1024]{2,1...) custom-call(bf16[8,32,1152]{2,1,0:T(8,128)(2,1)S(1)} %get-tuple-element.132.a1, ...), custom_call_target="tpu_custom_call" | custom-call | tf_op jit(solution)/shard_map/spread/pallas_call | solution.py:959
  64.9 1.4 copy-done.17
  66.6 34.7 %start_kernel.1 = bf16[1024,1024]{1,0:T(8,128)(2,1)S(1)} custom-call(bf16[128,1024]{1,0:T(8,128)(2,1)S(1)} %bitcast.141, f32[1,1024]{1,0:T(1,128)S(1)} %get-tuple-element.127.gain_ref), custom_call_target="tpu_custom_call" | custom-call | tf_op jit(solution)/shard_map/start_kernel/pallas_call | solution.py:825
  101.3 3.0 fusion.20
  104.4 1.9 multiply_cosine_fusion
  106.3 1.4 subtract_convert_fusion.6
  111.3 2.4 add_convert_fusion.7
  113.9 1.3 pad_maximum_fusion.4
  115.4 10.3 %attend_forward.2 = (bf16[1024,128]{1,0:T(8,128)(2,1)S(1)}, f32[1024,2]{1,0:T(8,128)S(1)}) custom-call(bf16[1024,128]{1,0:T(8,128)(2,1)S(1)} %pad_maximum_fusion.10.q_ref, bf16[2048,128]{1,0:T(8,128)(2,1)S(1)} %get-tuple-element.113.k_ref, bf16[2048,128]{1,0:T(8,128)(2,1)S(1)} %get-tuple-element.112.v_ref, s32[1024,1]{1,0:T(8,128)S(1)} %copy.155.pq_ref, ...), custom_call_target="tpu_custom_call" | custom-call | tf_op jit(solution)/shard_map/attend_forward/pallas_call | solution.py:1123
  126.5 60.6 %forward_kernel.3 = (f32[128,1024]{1,0:T(8,128)S(1)}, bf16[1024,1024]{1,0:T(8,128)(2,1)S(1)}) custom-call(bf16[1024,128]{1,0:T(8,128)(2,1)S(1)} %get-tuple-element.57.left_ref, bf16[128,1024]{1,0:T(8,128)(2,1)S(1)} %bitcast.146, bf16[128,1024]{1,0:T(8,128)(2,1)S(1)} %bitcast.142, f32[1,1024]{1,0:T(1,128)S(1)} %get-tuple-element.126.gain_ref), custom_call_target="tpu_custom_call" | custom-call | tf_op jit(solution)/shard_map/forward_kernel/pallas_call | solution.py:825
  187.1 1.8 fusion.24
  190.7 57.7 %forward_kernel.4 = (f32[128,1024]{1,0:T(8,128)S(1)}, bf16[1024,1024]{1,0:T(8,128)(2,1)S(1)}) custom-call(bf16[1024,384]{1,0:T(8,128)(2,1)S(1)} %multiply_convert_fusion.5.left_ref, bf16[384,1024]{1,0:T(8,128)(2,1)S(1)} %bitcast.151, f32[128,1024]{1,0:T(8,128)S(1)} %get-tuple-element.61.res_ref.hid_ref, f32[1,1024]{1,0:T(1,128)S(1)} %get-tuple-element.125.gain_ref), custom_call_target="tpu_custom_call" | custom-call | tf_op jit(solution)/shard_map/forward_kernel/pallas_call | solution.py:825
  250.0 1.5 fusion.4
  255.9 1.6 copy-done.15
  260.4 2.6 add_convert_fusion.5
  263.2 1.4 pad_maximum_fusion.5
  264.8 10.3 %attend_forward.3 = (bf16[1024,128]{1,0:T(8,128)(2,1)S(1)}, f32[1024,2]{1,0:T(8,128)S(1)}) custom-call(bf16[1024,128]{1,0:T(8,128)(2,1)S(1)} %pad_maximum_fusion.11.q_ref, bf16[2048,128]{1,0:T(8,128)(2,1)S(1)} %get-tuple-element.111.k_ref, bf16[2048,128]{1,0:T(8,128)(2,1)S(1)} %get-tuple-element.110.v_ref, s32[1024,1]{1,0:T(8,128)S(1)} %copy-done.2, ...), custom_call_target="tpu_custom_call" | custom-call | tf_op jit(solution)/shard_map/attend_forward/pallas_call | solution.py:1123
  275.9 60.6 %forward_kernel.5 = (f32[128,1024]{1,0:T(8,128)S(1)}, bf16[1024,1024]{1,0:T(8,128)(2,1)S(1)}) custom-call(bf16[1024,128]{1,0:T(8,128)(2,1)S(1)} %get-tuple-element.64.left_ref, bf16[128,1024]{1,0:T(8,128)(2,1)S(1)} %bitcast.149, f32[128,1024]{1,0:T(8,128)S(1)} %copy-done.30, f32[1,1024]{1,0:T(1,128)S(1)} %get-tuple-element.124.gain_ref), custom_call_target="tpu_custom_call" | custom-call | tf_op jit(solution)/shard_map/forward_kernel/pallas_call | solution.py:825
  336.5 1.3 copy-done.60
  337.8 1.8 fusion.22
  340.9 62.8 %turn_kernel.1 = (bf16[128,1024]{1,0:T(8,128)(2,1)S(1)}, bf16[1024,1024]{1,0:T(8,128)(2,1)S(1)}) custom-call(bf16[1024,384]{1,0:T(8,128)(2,1)S(1)} %multiply_convert_fusion.4.left_ref, bf16[384,1024]{1,0:T(8,128)(2,1)S(1)} %bitcast.153, f32[128,1024]{1,0:T(8,128)S(1)} %get-tuple-element.69.res_ref.hid_ref, bf16[128,1024]{1,0:T(8,128)(2,1)S(1)} %bitcast.144), custom_call_target="tpu_custom_call" | custom-call | tf_op jit(solution)/shard_map/turn_kernel/pallas_call | solution.py:825
  403.7 1.7 multiply_convert_fusion.3
  407.5 51.3 %back_kernel.3 = (f32[128,1024]{1,0:T(8,128)S(1)}, bf16[1024,1024]{1,0:T(8,128)(2,1)S(1)}) custom-call(bf16[1024,768]{1,0:T(8,128)(2,1)S(1)} %pad_maximum_fusion.2.left_ref, bf16[1024,768]{1,0:T(8,128)(2,1)S(1)} %copy-done, bf16[128,1024]{1,0:T(8,128)(2,1)S(1)} %bitcast.145, f32[128,1024]{1,0:T(8,128)S(1)} %get-tuple-element.69.res_ref.hid_ref, ...), custom_call_target="tpu_custom_call" | custom-call | tf_op jit(solution)/shard_map/back_kernel/pallas_call | solution.py:825
  460.0 1.4 convolution_convert_fusion.9.da_ref
  461.5 1.9 convolution_convert_fusion.2
  468.5 18.9 %attend_backward.2 = (f32[1024,128]{1,0:T(8,128)S(1)}, f32[2048,128]{1,0:T(8,128)S(1)}, f32[2048,128]{1,0:T(8,128)S(1)}) custom-call(bf16[1024,128]{1,0:T(8,128)(2,1)S(1)} %copy-done.28, bf16[2048,128]{1,0:T(8,128)(2,1)S(1)} %copy-done.10, bf16[2048,128]{1,0:T(8,128)(2,1)S(1)} %copy-done.8, bf16[1024,128]{1,0:T(8,128)(2,1)S(1)} %copy-done.41, ...), custom_call_target="tpu_custom_call" | custom-call | tf_op jit(solution)/shard_map/attend_backward/pallas_call | solution.py:1174
  490.0 3.1 convolution_convert_fusion
  495.3 2.4 concatenate.116.left_ref
  497.7 3.2 convolution_convert_fusion.4
  500.9 60.7 %back_kernel.4 = (f32[128,1024]{1,0:T(8,128)S(1)}, bf16[1024,1024]{1,0:T(8,128)(2,1)S(1)}) custom-call(bf16[1024,384]{1,0:T(8,128)(2,1)S(1)} %copy-done.13, bf16[1024,384]{1,0:T(8,128)(2,1)S(1)} %copy-done.12, f32[128,1024]{1,0:T(8,128)S(1)} %copy-done.52, f32[128,1024]{1,0:T(8,128)S(1)} %copy-done.31, f32[1,1024]{1,0:T(1,128)S(1)} %get-tuple-element.125.gain_ref), custom_call_target="tpu_custom_call" | custom-call | tf_op jit(solution)/shard_map/back_kernel/pallas_call | solution.py:825
  561.7 1.7 multiply_convert_fusion.1
  564.5 62.0 %back_kernel.5 = (f32[128,1024]{1,0:T(8,128)S(1)}, bf16[1024,1024]{1,0:T(8,128)(2,1)S(1)}) custom-call(bf16[1024,768]{1,0:T(8,128)(2,1)S(1)} %pad_maximum_fusion.3.left_ref, bf16[1024,768]{1,0:T(8,128)(2,1)S(1)} %slice.279.right_ref, f32[128,1024]{1,0:T(8,128)S(1)} %get-tuple-element.79.grad_ref, f32[128,1024]{1,0:T(8,128)S(1)} %copy-done.35, ...), custom_call_target="tpu_custom_call" | custom-call | tf_op jit(solution)/shard_map/back_kernel/pallas_call | solution.py:825
  628.5 1.9 convolution_convert_fusion.3
  630.4 18.9 %attend_backward.3 = (f32[1024,128]{1,0:T(8,128)S(1)}, f32[2048,128]{1,0:T(8,128)S(1)}, f32[2048,128]{1,0:T(8,128)S(1)}) custom-call(bf16[1024,128]{1,0:T(8,128)(2,1)S(1)} %copy-done.26, bf16[2048,128]{1,0:T(8,128)(2,1)S(1)} %copy-done.6, bf16[2048,128]{1,0:T(8,128)(2,1)S(1)} %copy-done.4, bf16[1024,128]{1,0:T(8,128)(2,1)S(1)} %convolution_convert_fusion.8.da_ref, ...), custom_call_target="tpu_custom_call" | custom-call | tf_op jit(solution)/shard_map/attend_backward/pallas_call | solution.py:1174
  650.8 1.6 pad_maximum_fusion.1.g2
  654.1 3.1 convolution_convert_fusion.1
  660.5 1.5 concatenate.119.left_ref
  663.5 1.7 pad_maximum_fusion.g1
  665.2 53.3 %collect.1 = (bf16[8,32,1152]{2,1,0:T(8,128)(2,1)}, bf16[8,32,1152]{2,1,0:T(8,128)(2,1)}, f32[96,1024]{1,0:T(8,128)}, f32[96,1024]{1,0:T(8,128)}, f32[32,1024]{1,0:T(8,128)}, /*index=5*/f32[32,1024]{1,0:T(8,128)}) custom-call(bf16[16,2,32,1152]{3,2,1,0:T(8,128)(2,1)} %pad_maximum_fusion.g1, bf16[16,2,32,1152]{3,2,1,0:T(8,128)(2,1)} %pad_maximum_fusion.1.g2, ...), custom_call_target="tpu_custom_call" | custom-call | tf_op jit(solution)/shard_map/collect/pallas_call | solution.py:1075
  723.2 35.1 %last_kernel.1 = bf16[128,1024]{1,0:T(8,128)(2,1)S(1)} custom-call(bf16[1024,384]{1,0:T(8,128)(2,1)S(1)} %concatenate.119.left_ref, bf16[1024,384]{1,0:T(8,128)(2,1)S(1)} %copy-done.11, f32[128,1024]{1,0:T(8,128)S(1)} %copy-done.50, bf16[128,1024]{1,0:T(8,128)(2,1)S(1)} %bitcast.143, f32[1,1024]{1,0:T(1,128)S(1)} %get-tuple-element.127.gain_ref), custom_call_target="tpu_custom_call" | custom-call | tf_op jit(solution)/shard_map/last_kernel/pallas_call | solution.py:825
  762.2 1.3 reshape.355
  764.3 1.3 reshape.352
  766.4 1.3 reshape.343
  768.4 1.3 reshape.340
  771.8 1.5 reshape.349
  774.3 1.5 reshape.347
  777.9 1.5 reshape.361
  780.4 1.5 reshape.359
  (386 shorter events, 77.8 us)
Async XLA Ops:
  0.7 7.2 copy-start.101
  6.0 3.3 copy-start.102
  14.6 52.0 %copy-start.23 = (bf16[1,128,1024]{2,1,0:T(8,128)(2,1)S(1)}, bf16[1,128,1024]{2,1,0:T(8,128)(2,1)}, u32[]{:S(2)}) copy-start(bf16[1,128,1024]{2,1,0:T(8,128)(2,1)} %param.21) | copy-start | bytes 786436
  14.8 46.8 %copy-start.21 = (bf16[8,32,1152]{2,1,0:T(8,128)(2,1)}, bf16[8,32,1152]{2,1,0:T(8,128)(2,1)S(1)}, u32[]{:S(2)}) copy-start(bf16[8,32,1152]{2,1,0:T(8,128)(2,1)S(1)} %get-tuple-element.133.a2) | copy-start | bytes 1769476
  64.9 61.6 %copy-start.37 = (bf16[4,32,1024]{2,1,0:T(8,128)(2,1)}, bf16[4,32,1024]{2,1,0:T(8,128)(2,1)S(1)}, u32[]{:S(2)}) copy-start(bf16[4,32,1024]{2,1,0:T(8,128)(2,1)S(1)} %get-tuple-element.58) | copy-start | bytes 786436
  64.9 189.9 %copy-start.14 = (bf16[32,32,1152]{2,1,0:T(8,128)(2,1)}, bf16[32,32,1152]{2,1,0:T(8,128)(2,1)S(1)}, u32[]{:S(2)}) copy-start(bf16[32,32,1152]{2,1,0:T(8,128)(2,1)S(1)} %get-tuple-element.62) | copy-start | bytes 7077892
  101.3 3.0 copy-start.32
  104.3 3.3 copy-start.70
  104.4 3.3 copy-start.80
  108.7 5.2 collective-permute-start
  109.0 6.4 copy-start.1
  111.3 2.7 copy-start.85
  115.3 71.8 %copy-start.18 = (bf16[32,32,1152]{2,1,0:T(8,128)(2,1)S(1)}, bf16[32,32,1152]{2,1,0:T(8,128)(2,1)}, u32[]{:S(2)}) copy-start(bf16[32,32,1152]{2,1,0:T(8,128)(2,1)} %copy-done.17) | copy-start | bytes 7077892
  115.4 10.4 %copy-start.3 = (bf16[2048,128]{1,0:T(8,128)(2,1)}, bf16[2048,128]{1,0:T(8,128)(2,1)S(1)}, u32[]{:S(2)}) copy-start(bf16[2048,128]{1,0:T(8,128)(2,1)S(1)} %get-tuple-element.112.v_ref) | copy-start | bytes 1572868
  115.4 10.4 %copy-start.5 = (bf16[2048,128]{1,0:T(8,128)(2,1)}, bf16[2048,128]{1,0:T(8,128)(2,1)S(1)}, u32[]{:S(2)}) copy-start(bf16[2048,128]{1,0:T(8,128)(2,1)S(1)} %get-tuple-element.113.k_ref) | copy-start | bytes 1572868
  125.7 63.2 %copy-start.39 = (bf16[1024,128]{1,0:T(8,128)(2,1)}, bf16[1024,128]{1,0:T(8,128)(2,1)S(1)}, u32[]{:S(2)}) copy-start(bf16[1024,128]{1,0:T(8,128)(2,1)S(1)} %get-tuple-element.57.left_ref) | copy-start | bytes 786436
  187.1 3.5 copy-start.34
  248.4 3.1 copy-start.63
  248.4 3.1 copy-start.67
  250.0 2.8 copy-start.73
  253.8 9.3 %collective-permute-start.1 = (bf16[1024,256]{1,0:T(8,128)(2,1)}, bf16[1024,256]{1,0:T(8,128)(2,1)}, u32[]{:S(2)}, u32[]{:S(2)}) collective-permute-start(bf16[1024,256]{1,0:T(8,128)(2,1)} %pad_maximum_fusion.9), channel_id=1, source_target_pairs={{0,1},{1,0},{2,3},{3,2},{4,5},{5,4},{6,7},{7,6},{8,9},{9,8},{10,11... | collective-permute-start | bytes 1572872 | tf_op jit(solution)/shard_map/ppermute | solution.py:1267
  260.3 2.8 copy-start.79
  260.3 2.9 copy-start.87
  260.3 2.9 copy-start.89
  264.6 11.3 %copy-start.30 = (f32[128,1024]{1,0:T(8,128)S(1)}, f32[128,1024]{1,0:T(8,128)}, u32[]{:S(2)}) copy-start(f32[128,1024]{1,0:T(8,128)} %copy-done.29) | copy-start | bytes 1572868
  264.6 11.2 %copy-start.43 = (bf16[4,32,1024]{2,1,0:T(8,128)(2,1)S(1)}, bf16[4,32,1024]{2,1,0:T(8,128)(2,1)}, u32[]{:S(2)}) copy-start(bf16[4,32,1024]{2,1,0:T(8,128)(2,1)} %copy-done.42) | copy-start | bytes 786436
  264.7 73.2 %copy-start.16 = (bf16[32,32,1152]{2,1,0:T(8,128)(2,1)S(1)}, bf16[32,32,1152]{2,1,0:T(8,128)(2,1)}, u32[]{:S(2)}) copy-start(bf16[32,32,1152]{2,1,0:T(8,128)(2,1)} %copy-done.14) | copy-start | bytes 7077892
  264.7 10.3 %copy-start.7 = (bf16[2048,128]{1,0:T(8,128)(2,1)}, bf16[2048,128]{1,0:T(8,128)(2,1)S(1)}, u32[]{:S(2)}) copy-start(bf16[2048,128]{1,0:T(8,128)(2,1)S(1)} %get-tuple-element.110.v_ref) | copy-start | bytes 1572868
  264.8 10.3 %copy-start.9 = (bf16[2048,128]{1,0:T(8,128)(2,1)}, bf16[2048,128]{1,0:T(8,128)(2,1)S(1)}, u32[]{:S(2)}) copy-start(bf16[2048,128]{1,0:T(8,128)(2,1)S(1)} %get-tuple-element.111.k_ref) | copy-start | bytes 1572868
  405.5 53.3 %copy-start.97 = (bf16[1024,384]{1,0:T(8,128)(2,1)}, bf16[1024,384]{1,0:T(8,128)(2,1)S(1)}, u32[]{:S(2)}) copy-start(bf16[1024,384]{1,0:T(8,128)(2,1)S(1)} %get-tuple-element.95) | copy-start | bytes 2359300
  487.7 5.4 collective-permute-start.2
  497.7 3.2 copy-start.12
  497.7 3.3 copy-start.13
  497.7 3.3 copy-start.31
  497.7 3.3 copy-start.52
  497.7 64.0 %copy-start.77 = (f32[1024,768]{1,0:T(8,128)S(1)}, f32[1024,768]{1,0:T(8,128)}, u32[]{:S(2)}) copy-start(f32[1024,768]{1,0:T(8,128)} %copy-done.76) | copy-start | bytes 9437188
  500.9 60.8 %copy-start.46 = (bf16[4,96,1024]{2,1,0:T(8,128)(2,1)S(1)}, bf16[4,96,1024]{2,1,0:T(8,128)(2,1)}, u32[]{:S(2)}) copy-start(bf16[4,96,1024]{2,1,0:T(8,128)(2,1)} %copy-done.44) | copy-start | bytes 2359300
  564.5 62.1 %copy-start.40 = (bf16[1024,128]{1,0:T(8,128)(2,1)S(1)}, bf16[1024,128]{1,0:T(8,128)(2,1)}, u32[]{:S(2)}) copy-start(bf16[1024,128]{1,0:T(8,128)(2,1)} %copy-done.39) | copy-start | bytes 786436
  649.5 7.7 collective-permute-start.3
  659.3 2.8 copy-start.33
  665.2 54.3 %copy-start.20 = (bf16[8,32,1152]{2,1,0:T(8,128)(2,1)S(1)}, bf16[8,32,1152]{2,1,0:T(8,128)(2,1)}, u32[]{:S(2)}) copy-start(bf16[8,32,1152]{2,1,0:T(8,128)(2,1)} %copy-done.19) | copy-start | bytes 1769476
  722.3 36.0 %copy-start.100 = (f32[96,1024]{1,0:T(8,128)S(1)}, f32[96,1024]{1,0:T(8,128)}, u32[]{:S(2)}) copy-start(f32[96,1024]{1,0:T(8,128)} %get-tuple-element.88) | copy-start | bytes 1179652
  722.3 36.8 %copy-start.99 = (f32[96,1024]{1,0:T(8,128)S(1)}, f32[96,1024]{1,0:T(8,128)}, u32[]{:S(2)}) copy-start(f32[96,1024]{1,0:T(8,128)} %get-tuple-element.91) | copy-start | bytes 1179652
  766.1 3.7 copy-start.113
  766.1 4.2 copy-start.114
  773.3 3.0 copy-start.116
  779.9 3.4 copy-start.108
  779.9 4.0 copy-start.107
  (73 other events, 124.2 us)

commit v3 on v1

--- a/solution.py
+++ b/solution.py
@@ -551,6 +551,10 @@
     )
 
 
+def arrived(ref, sem, target):
+    remote(ref, ref, sem, sem, target).wait_recv()
+
+
 def plane_place():
     f = lax.axis_index("fsdp")
     c = lax.axis_index("ctx")
@@ -576,165 +580,266 @@
     pl.semaphore_wait(barrier, 2 + jnp.where((z > 0) & (z < 3), 1, 0))
 
 
-def send_order(z, step):
-    table = ((3, 2, 1, 0), (3, 0, 2, 1), (0, 3, 1, 2), (0, 1, 2, 3))
-    column = [row[step] for row in table]
-    return jnp.where(
-        z == 0, column[0], jnp.where(z == 1, column[1], jnp.where(z == 2, column[2], column[3]))
-    )
-
-
-def reduce_plane(place, product, bufs, sems):
-    f, c, y, z = place
-    sy, ry, acc, su, ru, sd, rd = bufs
-    ys, yr, us, ur, ds, dr = sems
-    across = (f, flip(c, 2))
-    above = (f, c + 4)
-    below = (f, c - 4)
-
-    def y_copy(block):
-        return remote(sy.at[block], ry.at[block], ys.at[block], yr.at[block], across)
-
-    def up_copy(block):
-        return remote(su.at[block], ru.at[block], us.at[block], ur.at[block], above)
-
-    def down_copy(block):
-        return remote(sd.at[block], rd.at[block], ds.at[block], dr.at[block], below)
-
-    for step in range(4):
-        block = send_order(z, step)
-        sy[block] = product(block * 2 + (1 - y)).astype(BF)
-        y_copy(block).start()
-    for block in range(4):
-        acc[block] = product(block * 2 + y)
-    for k in range(3):
-        top = 3 - k
-
-        @pl.when(top > z)
-        def _():
-            y_copy(top).wait_recv()
-            acc[top] += ry[top].astype(F32)
-
-            @pl.when(z > 0)
-            def _():
-                up_copy(top).wait_recv()
-                acc[top] += ru[top].astype(F32)
-
-            su[top] = acc[top].astype(BF)
-            up_copy(top).start()
-
-        @pl.when(k < z)
-        def _():
-            y_copy(k).wait_recv()
-            acc[k] += ry[k].astype(F32)
-
-            @pl.when(z < 3)
-            def _():
-                down_copy(k).wait_recv()
-                acc[k] += rd[k].astype(F32)
-
-            sd[k] = acc[k].astype(BF)
-            down_copy(k).start()
-
-    y_copy(z).wait_recv()
-    acc[z] += ry[z].astype(F32)
-
-    @pl.when(z > 0)
+HALF = ROWS // 2
+ODD = 8
+
+
+class Plane:
+    def __init__(self, place, inner):
+        f, c, y, z = place
+        self.y, self.inner = y, inner
+        self.mirrored = z // 2
+        sign = 1 - 2 * self.mirrored
+        self.across = (f, flip(c, 2))
+        self.up = (f, c + 4 * sign)
+        self.down = (f, c - 4 * sign)
+        self.own = 1 if inner else 0
+        self.sent = []
+
+    def at(self, near):
+        return near + self.mirrored * (3 - 2 * near)
+
+    def slot(self, half, near):
+        return 4 * half + self.at(near)
+
+    def start(self, copy):
+        copy.start()
+        self.sent.append(copy)
+
+    def finish(self):
+        for copy in self.sent:
+            copy.wait_send()
+
+
+class Reduce(Plane):
+    def __init__(self, place, inner, product, bufs, sems):
+        super().__init__(place, inner)
+        self.product = product
+        self.sy, self.ry, self.acc, self.pb, self.su, self.sd, self.rb, self.ra = bufs
+        self.ys, self.yr, self.us, self.ds, self.br, self.ar = sems
+
+    def y_copy(self, slot):
+        return remote(self.sy.at[slot], self.ry.at[slot], self.ys.at[slot], self.yr.at[slot], self.across)
+
+    def z_copy(self, slot, upward):
+        if not upward:
+            return remote(self.sd.at[slot], self.ra.at[slot], self.ds.at[slot], self.ar.at[slot], self.down)
+        if self.inner:
+            return remote(self.su.at[slot], self.ra.at[slot], self.us.at[slot], self.ar.at[slot], self.up)
+        return remote(self.su.at[slot], self.rb.at[slot], self.us.at[slot], self.br.at[slot], self.up)
+
+    def got_y(self, slot):
+        self.y_copy(slot).wait_recv()
+        return self.ry[slot].astype(F32)
+
+    def got_z(self, slot, below):
+        buf, sem = (self.rb, self.br) if below else (self.ra, self.ar)
+        arrived(buf.at[slot], sem.at[slot], self.across)
+        return buf[slot].astype(F32)
+
+    def pass_z(self, slot, value, upward):
+        buf = self.su if upward else self.sd
+        buf[slot] = value.astype(BF)
+        self.start(self.z_copy(slot, upward))
+
+    def cross(self, slot, value):
+        self.sy[slot] = value.astype(BF)
+        self.start(self.y_copy(slot))
+
+    def products(self):
+        def other_row(step, carry):
+            if self.inner:
+                near = jnp.where(step == 0, 3, jnp.where(step == 1, 0, 4 - step))
+            else:
+                near = 3 - step
+            block = near + self.mirrored * (3 - 2 * near)
+            value = self.product(2 * block + 1 - self.y)
+            self.sy[block] = value[:HALF].astype(BF)
+            self.y_copy(block).start()
+            self.pb[block] = value[HALF:]
+            return carry
+
+        lax.fori_loop(0, 4, other_row, 0)
+        for near in range(4):
+            self.sent.append(self.y_copy(self.at(near)))
+        if not self.inner:
+            self.pass_z(ODD, self.pb[self.at(3)], True)
+        for near in (2, 1):
+            self.cross(self.slot(1, near), self.pb[self.at(near)])
+
+        def own_row(step, carry):
+            near = 3 - step
+            block = near + self.mirrored * (3 - 2 * near)
+            value = self.product(2 * block + self.y)
+            self.acc[block] = value[:HALF]
+            self.acc[4 + block] = value[HALF:]
+            return carry
+
+        lax.fori_loop(0, 4, own_row, 0)
+
+    def far_halves(self):
+        if not self.inner:
+            self.pass_z(self.slot(1, 3), self.acc[self.slot(1, 3)], True)
+            return
+        self.pass_z(ODD, self.pb[self.at(3)] + self.got_z(ODD, True), True)
+        far = self.slot(1, 3)
+        self.pass_z(far, self.acc[far] + self.got_z(far, True), True)
+        self.pass_z(ODD, self.pb[self.at(0)] + self.got_z(ODD, False), False)
+        end = self.slot(1, 0)
+        self.pass_z(end, self.acc[end] + self.got_z(end, False), False)
+
+    def chain(self, half):
+        if self.inner:
+            steps = ((3, True), (0, False), (2, True)) if half == 0 else ((2, True),)
+        else:
+            steps = ((3, True), (2, True), (1, True)) if half == 0 else ((2, True), (1, True))
+        for near, upward in steps:
+            slot = self.slot(half, near)
+            value = self.acc[slot] + self.got_y(slot)
+            if self.inner:
+                value += self.got_z(slot, upward)
+            self.pass_z(slot, value, upward)
+        if half == 1 and not self.inner:
+            self.cross(self.slot(1, 0), self.pb[self.at(0)] + self.got_z(ODD, False))
+        slot = self.slot(half, self.own)
+        total = self.acc[slot] + self.got_z(slot, False)
+        if self.inner:
+            total += self.got_z(slot, True)
+        return total + self.got_y(slot)
+
+
+class Gather(Plane):
+    def __init__(self, place, inner, full, sems):
+        super().__init__(place, inner)
+        self.full = full
+        self.ys, self.yr, self.us, self.ds, self.br, self.ar = sems
+
+    def rows(self, half, near, side):
+        start = (self.at(near) * 2 + side) * ROWS + half * HALF
+        return self.full.at[pl.ds(pl.multiple_of(start, HALF), HALF)]
+
+    def y_copy(self, half, near):
+        part = self.rows(half, near, self.y)
+        slot = self.slot(half, near)
+        return remote(part, part, self.ys.at[slot], self.yr.at[slot], self.across)
+
+    def send_z(self, part, slot, upward):
+        sem = self.us if upward else self.ds
+        arrive = self.br if upward and not self.inner else self.ar
+        self.start(remote(part, part, sem.at[slot], arrive.at[slot], self.up if upward else self.down))
+
+    def got_z(self, part, slot, below):
+        sem = self.br if below else self.ar
+        arrived(part, sem.at[slot], self.across)
+
+    def send_own(self, half):
+        part = self.rows(half, self.own, self.y)
+        slot = self.slot(half, self.own)
+        self.send_z(part, slot, True)
+        if self.inner:
+            self.send_z(part, slot, False)
+        self.start(self.y_copy(half, self.own))
+
+    def take(self, half, near, below):
+        part = self.rows(half, near, self.y)
+        slot = self.slot(half, near)
+        self.got_z(part, slot, below)
+        if self.inner:
+            self.send_z(part, slot, below)
+        if half == 0 or near in (1, 2):
+            self.start(self.y_copy(half, near))
+
+    def take_odd(self, near, below):
+        part = self.rows(1, near, 1 - self.y)
+        self.got_z(part, ODD, below)
+        if self.inner:
+            self.send_z(part, ODD, below)
+
+    def got_y(self, half, near):
+        part = self.rows(half, near, 1 - self.y)
+        arrived(part, self.yr.at[self.slot(half, near)], self.across)
+
+    def forward(self, half):
+        if half == 0:
+            for near, below in ((0, True), (2, False), (3, False)) if self.inner else ((1, False), (2, False), (3, False)):
+                self.take(0, near, below)
+            return
+        if self.inner:
+            self.take(1, 0, True)
+            self.take(1, 2, False)
+            self.take(1, 3, False)
+            self.take_odd(0, True)
+            self.take_odd(3, False)
+        else:
+            self.take(1, 1, False)
+            self.got_y(1, 0)
+            self.send_z(self.rows(1, 0, 1 - self.y), ODD, True)
+            self.take(1, 2, False)
+            self.take(1, 3, False)
+            self.take_odd(3, False)
+        for near in range(4):
+            self.got_y(0, near)
+        for near in (1, 2):
+            self.got_y(1, near)
+
+
+def both_kinds(place, run):
+    z = place[3]
+
+    @pl.when((z > 0) & (z < 3))
     def _():
-        up_copy(z).wait_recv()
-        acc[z] += ru[z].astype(F32)
-
-    @pl.when(z < 3)
+        run(True)
+
+    @pl.when((z == 0) | (z == 3))
     def _():
-        down_copy(z).wait_recv()
-        acc[z] += rd[z].astype(F32)
-
-    def finish():
-        for block in range(4):
-            y_copy(block).wait_send()
-        for k in range(3):
-
-            @pl.when(3 - k > z)
-            def _():
-                up_copy(3 - k).wait_send()
-
-            @pl.when(k < z)
-            def _():
-                down_copy(k).wait_send()
-
-    return finish
-
-
-def gather_plane(place, full, sems):
-    f, c, y, z = place
-    ys, yr, us, ur, ds, dr = sems
-    across = (f, flip(c, 2))
-    above = (f, c + 4)
-    below = (f, c - 4)
-
-    def rows(block, side):
-        return full.at[pl.ds(pl.multiple_of((block * 2 + side) * ROWS, ROWS), ROWS)]
-
-    def y_copy(block):
-        return remote(rows(block, y), rows(block, y), ys.at[block], yr.at[block], across)
-
-    def up_copy(block):
-        return remote(rows(block, y), rows(block, y), us.at[block], ur.at[block], above)
-
-    def down_copy(block):
-        return remote(rows(block, y), rows(block, y), ds.at[block], dr.at[block], below)
-
-    @pl.when(z < 3)
-    def _():
-        up_copy(z).start()
-
-    @pl.when(z > 0)
-    def _():
-        down_copy(z).start()
-
-    y_copy(z).start()
-    for k in range(1, 4):
-
-        @pl.when(z >= k)
-        def _():
-            up_copy(z - k).wait_recv()
-
-            @pl.when(z < 3)
-            def _():
-                up_copy(z - k).start()
-
-            y_copy(z - k).start()
-
-        @pl.when(z + k <= 3)
-        def _():
-            down_copy(z + k).wait_recv()
-
-            @pl.when(z > 0)
-            def _():
-                down_copy(z + k).start()
-
-            y_copy(z + k).start()
-
-    for block in range(4):
-        y_copy(block).wait()
-    for k in range(4):
-
-        @pl.when((z < 3) & (z >= k))
-        def _():
-            up_copy(z - k).wait_send()
-
-        @pl.when((z > 0) & (z + k <= 3))
-        def _():
-            down_copy(z + k).wait_send()
+        run(False)
+
+
+def exchange(place, product, settle, full, scratch, extra=None):
+    if extra is None:
+        greet_plane(place[0], place[1], place[3])
+    else:
+        peers, sibling, twin = chip_peers(place[0], place[1])
+        greet(peers + [sibling, twin])
+
+    def run(inner):
+        parts = []
+        more = None if extra is None else extra(place)
+        if more is not None:
+            more.first()
+            parts.append(more)
+        reduce = Reduce(place, inner, product, scratch[:8], scratch[8:14])
+        reduce.products()
+        reduce.far_halves()
+        parts.append(reduce)
+        if full is not None:
+            gather = Gather(place, inner, full, scratch[14:20])
+            parts.append(gather)
+        if more is not None:
+            more.second()
+        for half in range(2):
+            rows = settle(half, reduce.chain(half))
+            if full is not None:
+                start = (place[3] * 2 + place[2]) * ROWS + half * HALF
+                full[pl.ds(pl.multiple_of(start, HALF), HALF), :] = rows
+                gather.send_own(half)
+            if more is not None and half == 0:
+                more.third()
+        if full is not None:
+            gather.forward(0)
+            gather.forward(1)
+        for part in parts:
+            part.finish()
+
+    both_kinds(place, run)
+
+
+def half_rows(half):
+    return pl.ds(half * HALF, HALF)
 
 
 def norm_rows(hidden):
     return lax.rsqrt(jnp.mean(hidden * hidden, axis=-1, keepdims=True) + NORM_EPS)
-
-
-def own_rows(place):
-    _, _, y, z = place
-    return pl.ds(pl.multiple_of((z * 2 + y) * ROWS, ROWS), ROWS)
 
 
 def make_product(left_ref, right_ref, transposed):
@@ -747,83 +852,50 @@
     return product
 
 
-def start_kernel(hid_ref, gain_ref, full_ref, *sems):
-    place = plane_place()
-    greet_plane(place[0], place[1], place[3])
-    hidden = hid_ref[...].astype(F32)
-    full_ref[own_rows(place), :] = (hidden * norm_rows(hidden) * gain_ref[...]).astype(BF)
-    gather_plane(place, full_ref, sems)
-
-
 def forward_kernel(left_ref, right_ref, res_ref, gain_ref, new_ref, full_ref, *scratch):
-    place = plane_place()
-    greet_plane(place[0], place[1], place[3])
-    bufs, sems, more = scratch[:7], scratch[7:13], scratch[13:]
-    finish = reduce_plane(place, make_product(left_ref, right_ref, False), bufs, sems)
-    hidden = res_ref[...].astype(F32) + bufs[2][place[3]]
-    new_ref[...] = hidden
-    full_ref[own_rows(place), :] = (hidden * norm_rows(hidden) * gain_ref[...]).astype(BF)
-    gather_plane(place, full_ref, more)
-    finish()
+    def settle(half, total):
+        hidden = res_ref[half_rows(half), :].astype(F32) + total
+        new_ref[half_rows(half), :] = hidden
+        return (hidden * norm_rows(hidden) * gain_ref[...]).astype(BF)
+
+    exchange(plane_place(), make_product(left_ref, right_ref, False), settle, full_ref, scratch)
 
 
 def turn_kernel(left_ref, right_ref, res_ref, cot_ref, out_ref, full_ref, *scratch):
-    place = plane_place()
-    greet_plane(place[0], place[1], place[3])
-    bufs, sems, more = scratch[:7], scratch[7:13], scratch[13:]
-    finish = reduce_plane(place, make_product(left_ref, right_ref, False), bufs, sems)
-    out_ref[...] = (res_ref[...] + bufs[2][place[3]]).astype(BF)
-    full_ref[own_rows(place), :] = cot_ref[...]
-    gather_plane(place, full_ref, more)
-    finish()
+    def settle(half, total):
+        out_ref[half_rows(half), :] = (res_ref[half_rows(half), :] + total).astype(BF)
+        return cot_ref[half_rows(half), :]
+
+    exchange(plane_place(), make_product(left_ref, right_ref, False), settle, full_ref, scratch)
 
 
 def back_rows(total, grad, hidden, gain):
     inverse = norm_rows(hidden)
     normed = hidden * inverse
-    gain_grad = jnp.sum(total * normed, axis=0, keepdims=True)
     scaled = total * gain
     mean = jnp.mean(scaled * normed, axis=-1, keepdims=True)
-    return grad + inverse * (scaled - normed * mean), gain_grad
-
-
-def back_kernel(left_ref, right_ref, grad_ref, hid_ref, gain_ref, new_ref, gg_ref, full_ref, *scratch):
-    place = plane_place()
-    greet_plane(place[0], place[1], place[3])
-    bufs, sems, more = scratch[:7], scratch[7:13], scratch[13:]
-    finish = reduce_plane(place, make_product(left_ref, right_ref, True), bufs, sems)
-    new, gain_grad = back_rows(
-        bufs[2][place[3]], grad_ref[...].astype(F32), hid_ref[...].astype(F32), gain_ref[...]
-    )
-    gg_ref[...] = gain_grad
-    new_ref[...] = new
-    full_ref[own_rows(place), :] = new.astype(BF)
-    gather_plane(place, full_ref, more)
-    finish()
-
-
-def last_kernel(left_ref, right_ref, grad_ref, hid_ref, gain_ref, out_ref, gg_ref, *scratch):
-    place = plane_place()
-    greet_plane(place[0], place[1], place[3])
-    bufs, sems = scratch[:7], scratch[7:13]
-    finish = reduce_plane(place, make_product(left_ref, right_ref, True), bufs, sems)
-    new, gain_grad = back_rows(
-        bufs[2][place[3]], grad_ref[...].astype(F32), hid_ref[...].astype(F32), gain_ref[...]
-    )
-    gg_ref[...] = gain_grad
-    out_ref[...] = new.astype(BF)
-    finish()
-
-
-def comm_call(kernel, outs, ident, args, reduces, gathers):
+    return grad + inverse * (scaled - normed * mean)
+
+
+def back_kernel(left_ref, right_ref, grad_ref, hid_ref, gain_ref, new_ref, full_ref, *scratch):
+    def settle(half, total):
+        at = half_rows(half)
+        new = back_rows(total, grad_ref[at, :].astype(F32), hid_ref[at, :].astype(F32), gain_ref[...])
+        new_ref[at, :] = new
+        return new.astype(BF)
+
+    exchange(plane_place(), make_product(left_ref, right_ref, True), settle, full_ref, scratch)
+
+
+def comm_call(kernel, outs, ident, args, gathers, more=()):
     width = 1024
     scratch = []
-    if reduces:
-        for kind in (BF, BF, F32, BF, BF, BF, BF):
-            scratch.append(pltpu.VMEM((4, ROWS, width), kind))
-        scratch += [pltpu.SemaphoreType.DMA((4,))] * 6
+    for count, kind in ((8, BF), (8, BF), (8, F32), (4, F32), (9, BF), (9, BF), (9, BF), (9, BF)):
+        scratch.append(pltpu.VMEM((count, HALF, width), kind))
+    scratch += [pltpu.SemaphoreType.DMA((9,))] * 6
     if gathers:
-        scratch += [pltpu.SemaphoreType.DMA((4,))] * 6
+        scratch += [pltpu.SemaphoreType.DMA((9,))] * 6
+    scratch += list(more)
     spec = pl.BlockSpec(memory_space=VMEM_SPACE)
     return pl.pallas_call(
         kernel,
@@ -836,6 +908,324 @@
         ),
         name=kernel.__name__,
     )(*args)
+
+
+def chip_peers(f, c):
+    chip, core = c // 2, c % 2
+    return [(f, 2 * ((chip + i) % 8) + core) for i in range(1, 8)], (f, flip(c, 1)), (1 - f, c)
+
+
+def greet(targets):
+    barrier = pltpu.get_barrier_semaphore()
+    for target in targets:
+        pl.semaphore_signal(barrier, inc=1, device_id=to_device(*target), device_id_type=MESH)
+    pl.semaphore_wait(barrier, len(targets))
+
+
+class Spread:
+    def __init__(self, place, tables, downs, outs, sems):
+        self.f, self.c, self.y, _ = place
+        self.chip, self.core = self.c // 2, self.c % 2
+        self.peers, self.sibling, self.twin = chip_peers(self.f, self.c)
+        self.near = (self.f, flip(self.c, 2))
+        self.tables, self.downs, self.outs = tables, downs, outs
+        self.ds, self.dr, self.xs, self.xr, self.ss, self.sr, self.ws, self.wr = sems
+        self.home = self.y == self.f
+        self.direct, self.crossed, self.inner, self.sent = {}, {}, [], []
+
+    def send(self, src, dst, send_sem, recv_sem, target):
+        copy = remote(src, dst, send_sem, recv_sem, target)
+        copy.start()
+        self.sent.append(copy)
+        return copy
+
+    def to_twin(self, src, dst, l, n):
+        self.crossed[l, n] = self.send(src, dst, self.xs.at[l, n], self.xr.at[l, n], self.twin)
+
+    def to_sibling(self, src, dst, l, n):
+        self.inner.append(self.send(src, dst, self.ss.at[l, n], self.sr.at[l, n], self.sibling))
+
+    def out_copy(self, l):
+        op, out = self.outs[l]
+        part = 2 * self.y + self.core
+        return remote(op, out.at[part], self.ws.at[l], self.wr.at[l], self.near)
+
+    def pair_copies(self, l, s, r, first, target):
+        parts = [self.outs[l][1].at[self.core], self.outs[l][1].at[2 + self.core]]
+        return [remote(p, p, s.at[l, first + n], r.at[l, first + n], target) for n, p in enumerate(parts)]
+
+    def first(self, l):
+        a, r = self.tables[l]
+        down, down_all = self.downs[l]
+        op, out = self.outs[l]
+        mine = self.f * 16 + self.c
+        part = 2 * self.f + self.core
+        self.to_twin(a.at[self.chip], r.at[mine], l, 0)
+        for i in range(1, 8):
+            t = (self.chip + i) % 8
+            self.direct[l, i] = self.send(
+                a.at[t], r.at[mine], self.ds.at[l, i], self.dr.at[l, i], self.peers[i - 1]
+            )
+        r[mine] = a[self.chip]
+        self.to_sibling(a.at[self.chip], r.at[mine], l, 0)
+        down_all[part] = down[...]
+        self.to_twin(down, down_all.at[part], l, 8)
+        self.to_sibling(down, down_all.at[part], l, 16)
+
+        @pl.when(self.home)
+        def _():
+            out[2 * self.y + self.core] = op[...]
+
+        @pl.when(jnp.logical_not(self.home))
+        def _():
+            self.out_copy(l).start()
+
+    def second(self, l):
+        r = self.tables[l][1]
+        for i in range(1, 8):
+            self.direct[l, i].wait_recv()
+            source = self.f * 16 + 2 * ((self.chip + 8 - i) % 8) + self.core
+            self.to_twin(r.at[source], r.at[source], l, i)
+            self.to_sibling(r.at[source], r.at[source], l, i)
+
+        @pl.when(self.home)
+        def _():
+            self.out_copy(l).wait_recv()
+            for copy in self.pair_copies(l, self.xs, self.xr, 9, self.twin):
+                copy.start()
+
+    def third(self, l):
+        r = self.tables[l][1]
+
+        @pl.when(jnp.logical_not(self.home))
+        def _():
+            for copy in self.pair_copies(l, self.xs, self.xr, 9, self.twin):
+                copy.wait_recv()
+
+        for copy in self.pair_copies(l, self.ss, self.sr, 18, self.sibling):
+            copy.start()
+        for i in range(8):
+            self.crossed[l, i].wait_recv()
+            source = (1 - self.f) * 16 + 2 * ((self.chip + 8 - i) % 8) + self.core
+            self.to_sibling(r.at[source], r.at[source], l, 8 + i)
+        self.crossed[l, 8].wait_recv()
+        part = 2 * (1 - self.f) + self.core
+        down_all = self.downs[l][1]
+        self.to_sibling(down_all.at[part], down_all.at[part], l, 17)
+
+    def finish(self):
+        for copy in self.inner:
+            copy.wait_recv()
+        for copy in self.sent:
+            copy.wait_send()
+        for l in range(len(self.tables)):
+            for copy in self.pair_copies(l, self.ss, self.sr, 18, self.sibling):
+                copy.wait()
+
+            @pl.when(self.home)
+            def _():
+                for copy in self.pair_copies(l, self.xs, self.xr, 9, self.twin):
+                    copy.wait_send()
+
+            @pl.when(jnp.logical_not(self.home))
+            def _():
+                self.out_copy(l).wait_send()
+
+
+def begin_kernel(tok, a1, a2, dn, op, full, r1, r2, d1, d2, o1, o2, *sems):
+    place = plane_place()
+    f, c, y, z = place
+    peers, sibling, twin = chip_peers(f, c)
+    greet(peers + [sibling, twin])
+    start = (z * 2 + y) * ROWS
+    full[pl.ds(pl.multiple_of(start, ROWS), ROWS), :] = tok[...]
+
+    def run(inner):
+        gather = Gather(place, inner, full, sems[:6])
+        spread = Spread(
+            place, ((a1, r1), (a2, r2)), ((dn.at[0], d1), (dn.at[1], d2)), ((op.at[0], o1), (op.at[1], o2)), sems[6:]
+        )
+        gather.send_own(0)
+        gather.send_own(1)
+        spread.first(0)
+        spread.first(1)
+        gather.forward(0)
+        spread.second(0)
+        gather.forward(1)
+        spread.second(1)
+        spread.third(0)
+        spread.third(1)
+        gather.finish()
+        spread.finish()
+
+    both_kinds(place, run)
+
+
+def begin_call(tok, a1, a2, down, out):
+    rows, wide = a1.shape[1:]
+    block, width = down.shape[1:]
+    spec = pl.BlockSpec(memory_space=VMEM_SPACE)
+    shapes = [(8 * ROWS, width)] + [(32, rows, wide)] * 2 + [(4, block, width)] * 2 + [(4, rows, width)] * 2
+    counts = [(9,)] * 6 + [(2, 8), (2, 8), (2, 11), (2, 11), (2, 20), (2, 20), (2,), (2,)]
+    return pl.pallas_call(
+        begin_kernel,
+        out_shape=[jax.ShapeDtypeStruct(s, BF) for s in shapes],
+        in_specs=[spec] * 5,
+        out_specs=[spec] * 7,
+        scratch_shapes=[pltpu.SemaphoreType.DMA(n) for n in counts],
+        compiler_params=pltpu.CompilerParams(
+            collective_id=9, has_side_effects=True, vmem_limit_bytes=40 * 1024 * 1024
+        ),
+        name="begin",
+    )(tok, a1, a2, down, out)
+
+
+class Collect:
+    def __init__(self, place, ins, results, scratch):
+        self.f, self.c, self.y, _ = place
+        self.chip, self.core = self.c // 2, self.c % 2
+        self.peers, self.sibling, self.twin = chip_peers(self.f, self.c)
+        self.near = (self.f, flip(self.c, 2))
+        self.g, self.gd, self.go = ins
+        self.out, self.od, self.oo = results
+        self.sb, self.xb, self.xt, self.ut, self.sd, self.xd, self.td, self.so, self.xo, self.to, self.yo, self.yt = (
+            scratch[:12]
+        )
+        self.ss, self.sr, self.xs, self.xr, self.ps, self.pr, self.ys, self.yr = scratch[12:]
+        self.home = self.y == self.f
+        self.sent = []
+
+    def send(self, src, dst, send_sem, recv_sem, target):
+        copy = remote(src, dst, send_sem, recv_sem, target)
+        copy.start()
+        self.sent.append(copy)
+        return copy
+
+    def inner_send(self, src, dst, n):
+        return self.send(src, dst, self.ss.at[n], self.sr.at[n], self.sibling)
+
+    def twin_copy(self):
+        return remote(self.to, self.xo, self.xs.at[9], self.xr.at[9], self.twin)
+
+    def near_copy(self):
+        return remote(self.yt, self.yo, self.ys, self.yr, self.near)
+
+    def first(self):
+        other = 1 - self.core
+        self.inner = []
+        for half in range(2):
+            part = 8 * ((1 - self.f) if half == 0 else self.f)
+            self.inner.append(
+                self.inner_send(self.g.at[pl.ds(part, 8), other], self.sb.at[pl.ds(part, 8)], half)
+            )
+        self.inner.append(self.inner_send(self.gd.at[:, other], self.sd, 2))
+        self.inner.append(self.inner_send(self.go.at[:, other], self.so, 3))
+
+    def second(self):
+        f, core = self.f, self.core
+        self.crossed = []
+        self.inner[0].wait_recv()
+        for i in range(8):
+            t = (self.chip + i + 1) % 8
+            at = (1 - f) * 8 + t
+            self.xt[t] = (self.g[at, core].astype(F32) + self.sb[at].astype(F32)).astype(BF)
+            self.crossed.append(
+                self.send(self.xt.at[t], self.xb.at[t], self.xs.at[i], self.xr.at[i], self.twin)
+            )
+        self.inner[2].wait_recv()
+        self.td[...] = (self.gd[1 - f, core].astype(F32) + self.sd[1 - f].astype(F32)).astype(BF)
+        self.crossed.append(self.send(self.td, self.xd, self.xs.at[8], self.xr.at[8], self.twin))
+        self.inner[3].wait_recv()
+        for side in range(2):
+            self.to[side] = (self.go[side, core].astype(F32) + self.so[side].astype(F32)).astype(BF)
+
+        @pl.when(jnp.logical_not(self.home))
+        def _():
+            self.twin_copy().start()
+
+    def third(self):
+        f, core = self.f, self.core
+        self.direct = []
+        self.inner[1].wait_recv()
+        for i in range(8):
+            t = (self.chip + i + 1) % 8
+            at = f * 8 + t
+            self.crossed[i].wait_recv()
+            total = self.g[at, core].astype(F32) + self.sb[at].astype(F32) + self.xb[t].astype(F32)
+            if i < 7:
+                self.ut[t] = total.astype(BF)
+                self.direct.append(
+                    self.send(self.ut.at[t], self.out.at[self.chip], self.ps.at[i], self.pr.at[i], self.peers[i])
+                )
+            else:
+                self.out[self.chip] = total.astype(BF)
+        self.crossed[8].wait_recv()
+        self.od[...] = self.gd[f, core].astype(F32) + self.sd[f].astype(F32) + self.xd[...].astype(F32)
+
+        @pl.when(self.home)
+        def _():
+            self.twin_copy().wait_recv()
+            y = self.y
+            self.oo[...] = self.to[y].astype(F32) + self.xo[y].astype(F32)
+            self.yt[...] = (self.to[1 - y].astype(F32) + self.xo[1 - y].astype(F32)).astype(BF)
+            self.near_copy().start()
+
+    def finish(self):
+        @pl.when(self.home)
+        def _():
+            self.near_copy().wait_send()
+
+        @pl.when(jnp.logical_not(self.home))
+        def _():
+            self.near_copy().wait_recv()
+            self.oo[...] = self.yo[...].astype(F32)
+            self.twin_copy().wait_send()
+
+        for copy in self.direct:
+            copy.wait_recv()
+        for copy in self.sent:
+            copy.wait_send()
+
+
+def collect_shapes(rows, wide, block, width):
+    results = [((8, rows, wide), BF), ((block, width), F32), ((rows, width), F32)]
+    buffers = [
+        (16, rows, wide), (8, rows, wide), (8, rows, wide), (8, rows, wide),
+        (2, block, width), (block, width), (block, width),
+        (2, rows, width), (2, rows, width), (2, rows, width), (rows, width), (rows, width),
+    ]
+    counts = ((4,), (4,), (10,), (10,), (7,), (7,), (), ())
+    scratch = [pltpu.VMEM(b, BF) for b in buffers] + [pltpu.SemaphoreType.DMA(n) for n in counts]
+    return results, scratch
+
+
+def back_collect_kernel(
+    left_ref, right_ref, grad_ref, hid_ref, gain_ref, g, gd, go, new_ref, full_ref, c, od, oo, *scratch
+):
+    def settle(half, total):
+        at = half_rows(half)
+        new = back_rows(total, grad_ref[at, :].astype(F32), hid_ref[at, :].astype(F32), gain_ref[...])
+        new_ref[at, :] = new
+        return new.astype(BF)
+
+    def extra(place):
+        return Collect(place, (g, gd, go), (c, od, oo), scratch[20:])
+
+    product = make_product(left_ref, right_ref, True)
+    exchange(plane_place(), product, settle, full_ref, scratch, extra)
+
+
+def last_collect_kernel(left_ref, right_ref, grad_ref, hid_ref, gain_ref, g, gd, go, out_ref, c, od, oo, *scratch):
+    def settle(half, total):
+        at = half_rows(half)
+        new = back_rows(total, grad_ref[at, :].astype(F32), hid_ref[at, :].astype(F32), gain_ref[...])
+        out_ref[at, :] = new.astype(BF)
+
+    def extra(place):
+        return Collect(place, (g, gd, go), (c, od, oo), scratch[14:])
+
+    product = make_product(left_ref, right_ref, True)
+    exchange(plane_place(), product, settle, None, scratch, extra)
 
 
 def head_lanes(head):
@@ -951,38 +1341,54 @@
     )(q, k, v, da, lse_rows, pos_q, pos_k)
 
 
+def chip_first(split):
+    order = (2, 1, 0) + tuple(range(3, split.ndim))
+    return split.transpose(order).reshape(8, split.shape[0], *split.shape[3:])
+
+
+def chip_last(packed):
+    split = packed.reshape(4, 2, *packed.shape[1:])
+    return split.transpose((2, 1, 0) + tuple(range(3, split.ndim)))
+
+
 def pack_heads(weight):
     rows = weight.shape[0]
-    split = weight.reshape(rows, 8, 2, 2, 32)
-    return split.transpose(1, 0, 3, 2, 4).reshape(8, rows, 128)
+    split = chip_first(weight.reshape(rows, 2, 4, 2, 2, 32))
+    return split.transpose(0, 1, 3, 2, 4).reshape(8, rows, 128)
 
 
 def unpack_heads(packed):
     rows = packed.shape[1]
-    split = packed.reshape(8, rows, 2, 2, 32)
-    return split.transpose(1, 0, 3, 2, 4).reshape(rows, 1024)
+    split = packed.reshape(8, rows, 2, 2, 32).transpose(0, 1, 3, 2, 4)
+    return chip_last(split).reshape(rows, 1024)
 
 
 def pack_values(weight):
     rows = weight.shape[0]
-    return weight.reshape(rows, 8, 128).transpose(1, 0, 2)
+    return chip_first(weight.reshape(rows, 2, 4, 128))
 
 
 def unpack_values(packed):
-    return packed.transpose(1, 0, 2).reshape(packed.shape[1], 1024)
-
-
-def pack_units(weight, width):
+    return chip_last(packed).reshape(packed.shape[1], 1024)
+
+
+def pack_units(weight, block, *extra):
     rows, units = weight.shape
     each = units // 32
-    split = weight.reshape(rows, 2, 8, 2, each).transpose(2, 0, 1, 3, 4).reshape(8, rows, 4 * each)
-    return jnp.pad(split, ((0, 0), (0, 0), (0, width - 4 * each)))
+    split = weight.reshape(rows, 2, 8, 2, each).transpose(2, 0, 1, 3, 4).reshape(8, rows, 4, each)
+    padding = jnp.zeros((8, rows, 4, block - each), weight.dtype)
+    if extra:
+        columns = jnp.stack(extra, axis=-1)
+        columns = jnp.pad(columns, ((0, 0), (0, block - each - len(extra))))
+        first = jnp.broadcast_to(columns[None, :, None, :], (8, rows, 1, block - each))
+        padding = jnp.concatenate([first, padding[:, :, 1:]], axis=2)
+    return jnp.concatenate([split, padding], axis=-1).reshape(8, rows, 4 * block)
 
 
 def unpack_units(packed, units):
     rows = packed.shape[1]
     each = units // 32
-    split = packed[:, :, : 4 * each].reshape(8, rows, 2, 2, each)
+    split = packed.reshape(8, rows, 2, 2, -1)[..., :each]
     return split.transpose(1, 2, 0, 3, 4).reshape(rows, units)
 
 
@@ -1007,7 +1413,9 @@
 def fast_local(tokens, cotangent, pair_of, *shards):
     width = tokens.shape[2]
     units = shards[6].shape[1]
-    hidden_pad = (units // 8 + 127) // 128 * 128
+    each = units // 32
+    block = (each + 2 + 31) // 32 * 32
+    hidden_pad = 4 * block
     c = lax.axis_index("ctx")
     core = c % 2
     chip = c // 2
@@ -1020,10 +1428,6 @@
     sine = jnp.concatenate([sine, sine], axis=-1)
 
     layers = [shards[:9], shards[9:]]
-    gains = lax.all_gather(
-        jnp.stack([shards[0], shards[5], shards[9], shards[14]]), ("fsdp", "ctx"), axis=1, tiled=True
-    ).astype(F32)
-    gains = [gains[i : i + 1] for i in range(4)]
     packs = []
     for layer in layers:
         packs.append(
@@ -1032,41 +1436,33 @@
                     pack_heads(layer[1]),
                     pack_heads(layer[2]),
                     pack_values(layer[3]),
-                    pack_units(layer[6], hidden_pad),
-                    pack_units(layer[7], hidden_pad),
+                    pack_units(layer[6], block, layer[0], layer[5]),
+                    pack_units(layer[7], block),
                 ],
                 axis=-1,
             )
         )
-    packed = jnp.stack(packs, axis=1)
-    rows_each = packed.shape[2]
-    wide = packed.shape[3]
-    packed = jnp.repeat(packed, 2, axis=0)
-    got = lax.all_to_all(packed, "ctx", 0, 0, tiled=True)
-    got = lax.all_gather(got, "fsdp", axis=0, tiled=True)
-    got = got.transpose(1, 0, 2, 3).reshape(2, 32 * rows_each, wide)
-    qkv_w = [got[i, :, :384] for i in range(2)]
-    up_w = [got[i, :, 384:] for i in range(2)]
-    down = jnp.stack([layers[0][8], layers[1][8]])
-    down = jnp.stack([down, swap_cores(down)])
-    down = lax.dynamic_slice_in_dim(jnp.concatenate([down, down]), core, 2, 0)
-    down = lax.all_gather(down, "fsdp", axis=0, tiled=False)
-    down = down.transpose(2, 0, 1, 3, 4).reshape(2, -1, width)
-    down = jnp.pad(down, ((0, 0), (0, hidden_pad - down.shape[1]), (0, 0)))
-    down_w = [down[0], down[1]]
-    outs = lax.all_gather(
-        jnp.stack([layers[0][4], layers[1][4]]), ("fsdp", "ctx"), axis=1, tiled=True
-    )
-    outs = lax.dynamic_slice_in_dim(outs, chip * 128, 128, 1)
-    out_w = [outs[0], outs[1]]
-
+    rows_each, wide = packs[0].shape[1:]
+    down = jnp.pad(jnp.stack([layers[0][8], layers[1][8]]), ((0, 0), (0, block - each), (0, 0)))
     tok = tokens.reshape(ROWS, width)
     cot = cotangent.reshape(ROWS, width)
+    tok_full, *spread = begin_call(tok, *packs, down, jnp.stack([layers[0][4], layers[1][4]]))
+    all_w = [w.reshape(32 * rows_each, wide) for w in spread[:2]]
+    qkv_w = [w[:, :384] for w in all_w]
+    up_w = [w[:, 384:] for w in all_w]
+    down_w = [w.reshape(hidden_pad, width) for w in spread[2:4]]
+    out_w = [w.reshape(4 * rows_each, width) for w in spread[4:]]
+    gains = []
+    for w in all_w:
+        columns = w[:, 384 + each : 384 + each + 2].astype(F32).T
+        gains += [columns[:1], columns[1:]]
+
     plane = 8 * ROWS
     full_type = ((plane, width), BF)
     rows_type = ((ROWS, width), F32)
     saved = []
-    (full,) = comm_call(start_kernel, [full_type], 0, (tok, gains[0]), False, True)
+    tok_wide = tok_full.astype(F32)
+    full = (tok_wide * norm_rows(tok_wide) * gains[0]).astype(BF)
     hidden = tok
     first_values = None
     pos_q = own_pos[:, None]
@@ -1086,7 +1482,7 @@
         att, lse = attend_forward(q, k, v, pos_q, pos_k)
         middle, mlp_full = comm_call(
             forward_kernel, [rows_type, full_type], 1 + layer,
-            (att, out_w[layer], hidden, gains[2 * layer + 1]), True, True,
+            (att, out_w[layer], hidden, gains[2 * layer + 1]), True,
         )
         both = jnp.dot(mlp_full, up_w[layer], preferred_element_type=F32)
         gate, up = both[:, :hidden_pad], both[:, hidden_pad:]
@@ -1095,33 +1491,35 @@
         if layer == 0:
             hidden, full = comm_call(
                 forward_kernel, [rows_type, full_type], 3,
-                (inner, down_w[layer], middle, gains[2]), True, True,
+                (inner, down_w[layer], middle, gains[2]), True,
             )
         else:
             output, full = comm_call(
                 turn_kernel, [((ROWS, width), BF), full_type], 4,
-                (inner, down_w[layer], middle, cot), True, True,
+                (inner, down_w[layer], middle, cot), True,
             )
     grad = cot
     passed = None
-    grad_packs = [None, None]
-    grad_down = [None, None]
-    grad_out = [None, None]
-    gain_grads = [None] * 4
+    packed_grads = None
+    collected = [None, None]
     for layer in (1, 0):
         x_full, q, k, v, lse, att, mlp_full, gate, up, inner, hidden, middle = saved[layer]
-        grad_down[layer] = left_product(inner, full)
+        grad_down = left_product(inner, full)
         grad_inner = right_product(full, down_w[layer])
         sigma = jax.nn.sigmoid(gate)
         grad_gate = (grad_inner * up * sigma * (1.0 + gate * (1.0 - sigma))).astype(BF)
         grad_up = (grad_inner * gate * sigma).astype(BF)
         both = jnp.concatenate([grad_gate, grad_up], axis=-1)
         grad_upw = left_product(mlp_full, both)
-        grad_mid, gain_grads[2 * layer + 1], full = comm_call(
-            back_kernel, [rows_type, ((1, width), F32), full_type], 5 + layer,
-            (both, up_w[layer], grad, middle, gains[2 * layer + 1]), True, True,
-        )
-        grad_out[layer] = left_product(att, full)
+        args = (both, up_w[layer], grad, middle, gains[2 * layer + 1])
+        results, more = collect_shapes(rows_each, wide, block, width)
+        if layer == 1:
+            grad_mid, full = comm_call(back_kernel, [rows_type, full_type], 5, args, True)
+        else:
+            grad_mid, full, *collected[1] = comm_call(
+                back_collect_kernel, [rows_type, full_type] + results, 6, args + packed_grads, True, more
+            )
+        grad_out = left_product(att, full)
         grad_att = right_product(full, out_w[layer]).astype(BF)
         dq, dk, dv = attend_backward(q, k, v, grad_att, lse.T, own_pos[None, :], key_pos[:, None])
         dkv = jnp.concatenate([dk, dv], axis=-1)
@@ -1136,45 +1534,35 @@
             [pair_unrope(dq, cosine, sine), pair_unrope(dk, cosine, sine), dv], axis=-1
         ).astype(BF)
         grad_qkv = left_product(x_full, three)
-        grad_packs[layer] = jnp.concatenate([grad_qkv, grad_upw], axis=-1)
+        grad_pack = jnp.concatenate([grad_qkv, grad_upw], axis=-1)
+        packed_grads = (
+            grad_pack.astype(BF).reshape(16, 2, rows_each, wide),
+            grad_down.astype(BF).reshape(2, 2, block, width),
+            grad_out.astype(BF).reshape(2, 2, rows_each, width),
+        )
+        args = (three, qkv_w[layer], grad_mid, hidden, gains[2 * layer])
         if layer == 1:
-            grad, gain_grads[2], full = comm_call(
-                back_kernel, [rows_type, ((1, width), F32), full_type], 7,
-                (three, qkv_w[layer], grad_mid, hidden, gains[2]), True, True,
-            )
+            grad, full = comm_call(back_kernel, [rows_type, full_type], 7, args, True)
         else:
-            tokens_grad, gain_grads[0] = comm_call(
-                last_kernel, [((ROWS, width), BF), ((1, width), F32)], 8,
-                (three, qkv_w[layer], grad_mid, hidden, gains[0]), True, False,
-            )
-    sent = jnp.stack(grad_packs).astype(BF).reshape(2, 32, rows_each, wide).transpose(1, 0, 2, 3)
-    back = lax.all_to_all(sent, ("fsdp", "ctx"), 0, 0, tiled=True)
-    back = back.reshape(2, 8, 2, 2, rows_each, wide).astype(F32).sum(axis=(0, 2))
-    each = units // 32
-    downs = jnp.stack(grad_down)[:, : 4 * each].reshape(2, 2, 2, each, width)
-    downs = lax.psum_scatter(downs, "fsdp", scatter_dimension=1, tiled=False)
-    own = lax.dynamic_index_in_dim(downs, core, 1, False)
-    other = lax.dynamic_index_in_dim(downs, 1 - core, 1, False)
-    downs = own + swap_cores(other)
-    wide_out = jnp.zeros((2, 1024, width), F32)
-    wide_out = lax.dynamic_update_slice_in_dim(wide_out, jnp.stack(grad_out), chip * 128, 1)
-    outs = lax.psum_scatter(wide_out, ("fsdp", "ctx"), scatter_dimension=1, tiled=True)
-    gg = lax.psum_scatter(
-        jnp.concatenate(gain_grads), ("fsdp", "ctx"), scatter_dimension=1, tiled=True
-    )
+            tokens_grad, *collected[0] = comm_call(
+                last_collect_kernel, [((ROWS, width), BF)] + results, 8, args + packed_grads, False, more
+            )
     result = [output.reshape(1, ROWS, width), tokens_grad.reshape(1, ROWS, width)]
     for layer in range(2):
-        pack = back[:, layer]
+        pack = collected[layer][0].astype(F32)
+        both = pack * packs[layer].astype(F32)
+        pre_grad = jnp.sum(both[:, :, :384], axis=(0, 2)) / layers[layer][0].astype(F32)
+        mid_grad = jnp.sum(both[:, :, 384:], axis=(0, 2)) / layers[layer][5].astype(F32)
         result += [
-            gg[2 * layer],
+            pre_grad,
             unpack_heads(pack[:, :, :128]),
             unpack_heads(pack[:, :, 128:256]),
             unpack_values(pack[:, :, 256:384]),
-            outs[layer],
-            gg[2 * layer + 1],
+            collected[layer][2],
+            mid_grad,
             unpack_units(pack[:, :, 384 : 384 + hidden_pad], units),
             unpack_units(pack[:, :, 384 + hidden_pad :], units),
-            downs[layer],
+            collected[layer][1][:each],
         ]
     return tuple(result)
 

time: 1070 us -> 745 us (0.70)
  waiting for transfers between devices: 232 us -> 0.01 us
  blocking collectives: 110 us -> 0 us
  Pallas kernels: 541 us -> 593 us
  local copies, waits for them, and re-layouts: 91.4 us -> 73.5 us
  between operations: 17.2 us -> 3.41 us
    reduce_scatter x1 -> x0, waiting for transfers between devices: 127 us -> none  [fast_local(): lax.psum_scatter(wide_out, ('fsdp', 'ctx'), scatter_dimension=1, tiled=True)]
    unnamed x8 -> x0, waiting for transfers between devices: 101 us -> none
    pallas_call x0 -> x1, Pallas kernels: none -> 72.8 us  [begin_call(): pl.pallas_call(begin_kernel, out_shape=[jax.ShapeDtypeStruct(s, BF) for s...]
    all_to_all x1 -> x0, blocking collectives: 69.5 us -> none  [fast_local(): got = lax.all_to_all(packed, 'ctx', 0, 0, tiled=True)]
    all_gather x1 -> x0, blocking collectives: 40 us -> none  [fast_local(): lax.all_gather(jnp.stack([shards[0], shards[5], shards[9], shards[14]]),...]
    pallas_call x9 -> x8, Pallas kernels: 484 us -> 463 us  [comm_call(): pl.pallas_call(kernel, out_shape=[jax.ShapeDtypeStruct(*o) for o in outs]...]
    unnamed x220 -> x278, local copies, waits for them, and re-layouts: 31 us -> 25 us
  transfers between devices with their start and end apart: 13 -> 4, of which waited for: 4 -> 0; matrix products, arithmetic and copies ran while one was open for 9% -> 4% of each run, Pallas kernels for 13% -> 0%
where the time goes in v3:
time: 745 us; the launch traced here: 734 us
  Pallas kernels  593 us (80%)
  local copies, waits for them, and re-layouts  73.5 us (10%)
  other arithmetic  32.7 us (4%)
  matrix products  31.4 us (4%)
    pallas_call x8, Pallas kernels, comm_call(): pl.pallas_call(kernel, out_shape=[jax.ShapeDtypeStruct(*o) for o in outs]...  463 us
    pallas_call x1, Pallas kernels, begin_call(): pl.pallas_call(begin_kernel, out_shape=[jax.ShapeDtypeStruct(s, BF) for s...  72.8 us
    pallas_call x2, Pallas kernels, attend_backward(): pl.pallas_call(attend_back_kernel, grid=(rows // step,), out_shape=[jax.S...  36.7 us
    unnamed x278, local copies, waits for them, and re-layouts  25 us
    pallas_call x2, Pallas kernels, attend_forward(): pl.pallas_call(attend_kernel, grid=(rows // step,), out_shape=[jax.ShapeD...  20.1 us
    dot_general x8, matrix products, left_product(): lax.dot_general(left, right, (((0,), (0,)), ((), ())), preferred_element_...  18 us
  transfers between devices with their start and end apart: 4, of which 0 were waited for; matrix products, arithmetic and copies ran while one was open for 4% of the time, Pallas kernels for 0%

profile of v3, /device:TPU:0, one launch (start us, length us, event | category | flops | bytes accessed | tf_op | source)
XLA Modules:
  0.0 734.2 jit_solution(15209962649393487897)
XLA Ops:
  15.0 72.8 %begin.1 = (bf16[1024,1024]{1,0:T(8,128)(2,1)S(1)}, bf16[32,32,1152]{2,1,0:T(8,128)(2,1)S(1)}, bf16[32,32,1152]{2,1,0:T(8,128)(2,1)S(1)}, bf16[4,96,1024]{2,1,0:...) custom-call(bf16[128,1024]{1,0:T(8,128)(2,1)S(1)} %bitcast.142, ...), custom_call_target="tpu_custom_call" | custom-call | tf_op jit(solution)/shard_map/begin/pallas_call | solution.py:1070
  91.1 1.3 copy-done.32
  93.5 3.1 fusion.6
  96.6 1.9 multiply_cosine_fusion
  98.5 1.3 subtract_convert_fusion.6
  102.1 1.3 copy.196
  103.5 2.5 add_convert_fusion.7
  106.2 1.3 pad_maximum_fusion.4
  107.6 10.1 %attend_forward.2 = (bf16[1024,128]{1,0:T(8,128)(2,1)S(1)}, f32[1024,2]{1,0:T(8,128)S(1)}) custom-call(bf16[1024,128]{1,0:T(8,128)(2,1)S(1)} %pad_maximum_fusion.10.q_ref, bf16[2048,128]{1,0:T(8,128)(2,1)S(1)} %get-tuple-element.117.k_ref, bf16[2048,128]{1,0:T(8,128)(2,1)S(1)} %get-tuple-element.116.v_ref, s32[1024,1]{1,0:T(8,128)S(1)} %copy.155.pq_ref, ...), custom_call_target="tpu_custom_call" | custom-call | tf_op jit(solution)/shard_map/attend_forward/pallas_call | solution.py:1266
  117.7 63.0 %forward_kernel.3 = (f32[128,1024]{1,0:T(8,128)S(1)}, bf16[1024,1024]{1,0:T(8,128)(2,1)S(1)}) custom-call(bf16[1024,128]{1,0:T(8,128)(2,1)S(1)} %get-tuple-element.60.left_ref, bf16[128,1024]{1,0:T(8,128)(2,1)S(1)} %bitcast.147, bf16[128,1024]{1,0:T(8,128)(2,1)S(1)} %bitcast.143, f32[1,1024]{1,0:T(1,128)S(1)} %get-tuple-element.130.gain_ref), custom_call_target="tpu_custom_call" | custom-call | tf_op jit(solution)/shard_map/forward_kernel/pallas_call | solution.py:900
  180.8 1.3 copy-done.63
  182.1 1.8 fusion.29
  185.6 54.1 %forward_kernel.4 = (f32[128,1024]{1,0:T(8,128)S(1)}, bf16[1024,1024]{1,0:T(8,128)(2,1)S(1)}) custom-call(bf16[1024,384]{1,0:T(8,128)(2,1)S(1)} %multiply_convert_fusion.5.left_ref, bf16[384,1024]{1,0:T(8,128)(2,1)S(1)} %bitcast.153, f32[128,1024]{1,0:T(8,128)S(1)} %get-tuple-element.64.res_ref.hid_ref, f32[1,1024]{1,0:T(1,128)S(1)} %get-tuple-element.129.gain_ref), custom_call_target="tpu_custom_call" | custom-call | tf_op jit(solution)/shard_map/forward_kernel/pallas_call | solution.py:900
  241.2 1.5 fusion.10
  250.1 2.6 add_convert_fusion.5
  252.8 1.4 pad_maximum_fusion.5
  254.4 10.1 %attend_forward.3 = (bf16[1024,128]{1,0:T(8,128)(2,1)S(1)}, f32[1024,2]{1,0:T(8,128)S(1)}) custom-call(bf16[1024,128]{1,0:T(8,128)(2,1)S(1)} %pad_maximum_fusion.11.q_ref, bf16[2048,128]{1,0:T(8,128)(2,1)S(1)} %get-tuple-element.115.k_ref, bf16[2048,128]{1,0:T(8,128)(2,1)S(1)} %get-tuple-element.114.v_ref, s32[1024,1]{1,0:T(8,128)S(1)} %copy-done.2, ...), custom_call_target="tpu_custom_call" | custom-call | tf_op jit(solution)/shard_map/attend_forward/pallas_call | solution.py:1266
  264.5 59.1 %forward_kernel.5 = (f32[128,1024]{1,0:T(8,128)S(1)}, bf16[1024,1024]{1,0:T(8,128)(2,1)S(1)}) custom-call(bf16[1024,128]{1,0:T(8,128)(2,1)S(1)} %get-tuple-element.67.left_ref, bf16[128,1024]{1,0:T(8,128)(2,1)S(1)} %bitcast.151, f32[128,1024]{1,0:T(8,128)S(1)} %copy-done.30, f32[1,1024]{1,0:T(1,128)S(1)} %get-tuple-element.128.gain_ref), custom_call_target="tpu_custom_call" | custom-call | tf_op jit(solution)/shard_map/forward_kernel/pallas_call | solution.py:900
  323.7 1.4 copy-done.65
  325.1 1.8 fusion.27
  328.1 56.8 %turn_kernel.1 = (bf16[128,1024]{1,0:T(8,128)(2,1)S(1)}, bf16[1024,1024]{1,0:T(8,128)(2,1)S(1)}) custom-call(bf16[1024,384]{1,0:T(8,128)(2,1)S(1)} %multiply_convert_fusion.4.left_ref, bf16[384,1024]{1,0:T(8,128)(2,1)S(1)} %bitcast.155, f32[128,1024]{1,0:T(8,128)S(1)} %get-tuple-element.72.res_ref.hid_ref, bf16[128,1024]{1,0:T(8,128)(2,1)S(1)} %bitcast.145), custom_call_target="tpu_custom_call" | custom-call | tf_op jit(solution)/shard_map/turn_kernel/pallas_call | solution.py:900
  384.9 1.7 multiply_convert_fusion.3
  387.6 59.1 %back_kernel.2 = (f32[128,1024]{1,0:T(8,128)S(1)}, bf16[1024,1024]{1,0:T(8,128)(2,1)S(1)}) custom-call(bf16[1024,768]{1,0:T(8,128)(2,1)S(1)} %pad_maximum_fusion.2.left_ref, bf16[1024,768]{1,0:T(8,128)(2,1)S(1)} %slice.293.right_ref, bf16[128,1024]{1,0:T(8,128)(2,1)S(1)} %bitcast.146, f32[128,1024]{1,0:T(8,128)S(1)} %get-tuple-element.72.res_ref.hid_ref, ...), custom_call_target="tpu_custom_call" | custom-call | tf_op jit(solution)/shard_map/back_kernel/pallas_call | solution.py:900
  447.2 1.4 convolution_convert_fusion.9.da_ref
  448.6 1.9 convolution_convert_fusion.4
  452.7 18.2 %attend_backward.2 = (f32[1024,128]{1,0:T(8,128)S(1)}, f32[2048,128]{1,0:T(8,128)S(1)}, f32[2048,128]{1,0:T(8,128)S(1)}) custom-call(bf16[1024,128]{1,0:T(8,128)(2,1)S(1)} %copy-done.28, bf16[2048,128]{1,0:T(8,128)(2,1)S(1)} %copy-done.10, bf16[2048,128]{1,0:T(8,128)(2,1)S(1)} %copy-done.8, bf16[1024,128]{1,0:T(8,128)(2,1)S(1)} %copy-done.40, ...), custom_call_target="tpu_custom_call" | custom-call | tf_op jit(solution)/shard_map/attend_backward/pallas_call | solution.py:1317
  473.5 3.0 convolution_convert_fusion.1
  478.7 1.6 concatenate.116.left_ref
  480.3 3.0 convolution_convert_fusion.5
  483.4 59.5 %back_kernel.3 = (f32[128,1024]{1,0:T(8,128)S(1)}, bf16[1024,1024]{1,0:T(8,128)(2,1)S(1)}) custom-call(bf16[1024,384]{1,0:T(8,128)(2,1)S(1)} %concatenate.116.left_ref, bf16[1024,384]{1,0:T(8,128)(2,1)S(1)} %copy-done.13, f32[128,1024]{1,0:T(8,128)S(1)} %copy-done.54, f32[128,1024]{1,0:T(8,128)S(1)} %copy-done.31, f32[1,1024]{1,0:T(1,128)S(1)} %get-tuple-element.129.gain_ref), custom_call_target="tpu_custom_call" | custom-call | tf_op jit(solution)/shard_map/back_kernel/pallas_call | solution.py:900
  543.0 1.7 multiply_convert_fusion.1
  548.9 72.8 %back_collect_kernel.1 = (f32[128,1024]{1,0:T(8,128)S(1)}, bf16[1024,1024]{1,0:T(8,128)(2,1)S(1)}, bf16[8,32,1152]{2,1,0:T(8,128)(2,1)S(1)}, f32[96,1024]{1,0:T(8,128)S(1)}, f32[32,1024]{1,0:T(8,128)S(1)}) custom-call(bf16[1024,768]{1,0:T(8,128)(2,1)S(1)} %pad_maximum_fusion.3.left_ref, bf16[1024,768]{1,0:T(8,128)(2,1)S(1)} %copy-done, ...), custom_call_target="tpu_custom_call" | custom-call | tf_op jit(solution)/shard_map/back_collect_kernel/pallas_call | solution.py:900
  627.1 18.5 %attend_backward.3 = (f32[1024,128]{1,0:T(8,128)S(1)}, f32[2048,128]{1,0:T(8,128)S(1)}, f32[2048,128]{1,0:T(8,128)S(1)}) custom-call(bf16[1024,128]{1,0:T(8,128)(2,1)S(1)} %copy-done.26, bf16[2048,128]{1,0:T(8,128)(2,1)S(1)} %copy-done.6, bf16[2048,128]{1,0:T(8,128)(2,1)S(1)} %copy-done.4, bf16[1024,128]{1,0:T(8,128)(2,1)S(1)} %convolution_convert_fusion.7.da_ref, ...), custom_call_target="tpu_custom_call" | custom-call | tf_op jit(solution)/shard_map/attend_backward/pallas_call | solution.py:1317
  645.7 1.4 subtract_convert_fusion.1
  649.2 1.7 reshape.366
  657.0 1.3 reshape.363
  659.1 1.3 reshape.360
  660.7 1.5 reshape.369
  662.2 1.3 copy.183
  663.5 1.5 reshape.367
  665.0 4.9 convolution_convert_fusion
  672.7 1.7 concatenate.122.left_ref
  674.5 3.1 convolution_convert_fusion.3
  679.0 39.0 %last_collect_kernel.1 = (bf16[128,1024]{1,0:T(8,128)(2,1)S(1)}, bf16[8,32,1152]{2,1,0:T(8,128)(2,1)S(1)}, f32[96,1024]{1,0:T(8,128)S(1)}, f32[32,1024]{1,0:T(8,128)S(1)}) custom-call(bf16[1024,384]{1,0:T(8,128)(2,1)S(1)} %concatenate.122.left_ref, bf16[1024,384]{1,0:T(8,128)(2,1)S(1)} %copy-done.12, f32[128,1024]{1,0:T(8,128)S(1)} %copy-done.52, ...), custom_call_target="tpu_custom_call" | custom-call | tf_op jit(solution)/shard_map/last_collect_kernel/pallas_call | solution.py:900
  721.6 1.3 reshape.351
  723.7 1.3 reshape.348
  727.1 1.5 reshape.357
  729.6 1.5 reshape.355
  (412 shorter events, 73.6 us)
Async XLA Ops:
  0.7 7.2 copy-start.114
  6.0 3.3 copy-start.115
  14.8 73.0 %copy-start.21 = (bf16[8,32,1152]{2,1,0:T(8,128)(2,1)}, bf16[8,32,1152]{2,1,0:T(8,128)(2,1)S(1)}, u32[]{:S(2)}) copy-start(bf16[8,32,1152]{2,1,0:T(8,128)(2,1)S(1)} %get-tuple-element.137.a2) | copy-start | bytes 1769476
  91.1 10.1 %copy-start.14 = (bf16[32,32,1152]{2,1,0:T(8,128)(2,1)}, bf16[32,32,1152]{2,1,0:T(8,128)(2,1)S(1)}, u32[]{:S(2)}) copy-start(bf16[32,32,1152]{2,1,0:T(8,128)(2,1)S(1)} %get-tuple-element.65) | copy-start | bytes 7077892
  91.1 26.6 %copy-start.36 = (bf16[4,32,1024]{2,1,0:T(8,128)(2,1)}, bf16[4,32,1024]{2,1,0:T(8,128)(2,1)S(1)}, u32[]{:S(2)}) copy-start(bf16[4,32,1024]{2,1,0:T(8,128)(2,1)S(1)} %get-tuple-element.61) | copy-start | bytes 786436
  92.9 3.6 copy-start.124
  96.5 3.3 copy-start.76
  96.6 3.2 copy-start.86
  100.9 5.3 collective-permute-start
  101.1 6.5 copy-start.1
  102.1 3.8 copy-start.104
  102.1 4.0 copy-start.87
  102.1 4.0 copy-start.89
  102.1 4.0 copy-start.91
  107.5 74.6 %copy-start.18 = (bf16[32,32,1152]{2,1,0:T(8,128)(2,1)S(1)}, bf16[32,32,1152]{2,1,0:T(8,128)(2,1)}, u32[]{:S(2)}) copy-start(bf16[32,32,1152]{2,1,0:T(8,128)(2,1)} %copy-done.17) | copy-start | bytes 7077892
  107.6 10.1 %copy-start.3 = (bf16[2048,128]{1,0:T(8,128)(2,1)}, bf16[2048,128]{1,0:T(8,128)(2,1)S(1)}, u32[]{:S(2)}) copy-start(bf16[2048,128]{1,0:T(8,128)(2,1)S(1)} %get-tuple-element.116.v_ref) | copy-start | bytes 1572868
  107.6 10.1 %copy-start.5 = (bf16[2048,128]{1,0:T(8,128)(2,1)}, bf16[2048,128]{1,0:T(8,128)(2,1)S(1)}, u32[]{:S(2)}) copy-start(bf16[2048,128]{1,0:T(8,128)(2,1)S(1)} %get-tuple-element.117.k_ref) | copy-start | bytes 1572868
  117.7 63.1 %copy-start.56 = (f32[1024,2]{1,0:T(8,128)}, f32[1024,2]{1,0:T(8,128)S(1)}, u32[]{:S(2)}) copy-start(f32[1024,2]{1,0:T(8,128)S(1)} %get-tuple-element.84) | copy-start | bytes 24580
  117.7 66.2 %copy-start.38 = (bf16[1024,128]{1,0:T(8,128)(2,1)}, bf16[1024,128]{1,0:T(8,128)(2,1)S(1)}, u32[]{:S(2)}) copy-start(bf16[1024,128]{1,0:T(8,128)(2,1)S(1)} %get-tuple-element.60.left_ref) | copy-start | bytes 786436
  180.8 3.6 copy-start.33
  183.9 55.8 %copy-start.82 = (f32[1024,768]{1,0:T(8,128)}, f32[1024,768]{1,0:T(8,128)S(1)}, u32[]{:S(2)}) copy-start(f32[1024,768]{1,0:T(8,128)S(1)} %fusion.29) | copy-start | bytes 9437188
  183.9 55.8 %copy-start.15 = (bf16[32,32,1152]{2,1,0:T(8,128)(2,1)S(1)}, bf16[32,32,1152]{2,1,0:T(8,128)(2,1)}, u32[]{:S(2)}) copy-start(bf16[32,32,1152]{2,1,0:T(8,128)(2,1)} %copy-done.14) | copy-start | bytes 7077892
  245.1 7.7 %collective-permute-start.1 = (bf16[1024,256]{1,0:T(8,128)(2,1)}, bf16[1024,256]{1,0:T(8,128)(2,1)}, u32[]{:S(2)}, u32[]{:S(2)}) collective-permute-start(bf16[1024,256]{1,0:T(8,128)(2,1)} %pad_maximum_fusion.9), channel_id=1, source_target_pairs={{0,1},{1,0},{2,3},{3,2},{4,5},{5,4},{6,7},{7,6},{8,9},{9,8},{10,11... | collective-permute-start | bytes 1572872 | tf_op jit(solution)/shard_map/ppermute | solution.py:1410
  254.3 10.2 %copy-start.30 = (f32[128,1024]{1,0:T(8,128)S(1)}, f32[128,1024]{1,0:T(8,128)}, u32[]{:S(2)}) copy-start(f32[128,1024]{1,0:T(8,128)} %copy-done.29) | copy-start | bytes 1572868
  254.3 10.2 %copy-start.45 = (bf16[4,32,1024]{2,1,0:T(8,128)(2,1)S(1)}, bf16[4,32,1024]{2,1,0:T(8,128)(2,1)}, u32[]{:S(2)}) copy-start(bf16[4,32,1024]{2,1,0:T(8,128)(2,1)} %copy-done.44) | copy-start | bytes 786436
  254.3 70.8 %copy-start.16 = (bf16[32,32,1152]{2,1,0:T(8,128)(2,1)S(1)}, bf16[32,32,1152]{2,1,0:T(8,128)(2,1)}, u32[]{:S(2)}) copy-start(bf16[32,32,1152]{2,1,0:T(8,128)(2,1)} %copy-done.14) | copy-start | bytes 7077892
  254.4 10.1 %copy-start.7 = (bf16[2048,128]{1,0:T(8,128)(2,1)}, bf16[2048,128]{1,0:T(8,128)(2,1)S(1)}, u32[]{:S(2)}) copy-start(bf16[2048,128]{1,0:T(8,128)(2,1)S(1)} %get-tuple-element.114.v_ref) | copy-start | bytes 1572868
  254.4 10.1 %copy-start.9 = (bf16[2048,128]{1,0:T(8,128)(2,1)}, bf16[2048,128]{1,0:T(8,128)(2,1)S(1)}, u32[]{:S(2)}) copy-start(bf16[2048,128]{1,0:T(8,128)(2,1)S(1)} %get-tuple-element.115.k_ref) | copy-start | bytes 1572868
  264.5 62.8 %copy-start.55 = (f32[1024,2]{1,0:T(8,128)}, f32[1024,2]{1,0:T(8,128)S(1)}, u32[]{:S(2)}) copy-start(f32[1024,2]{1,0:T(8,128)S(1)} %get-tuple-element.76) | copy-start | bytes 24580
  386.6 60.1 %copy-start.110 = (bf16[1024,384]{1,0:T(8,128)(2,1)}, bf16[1024,384]{1,0:T(8,128)(2,1)S(1)}, u32[]{:S(2)}) copy-start(bf16[1024,384]{1,0:T(8,128)(2,1)S(1)} %get-tuple-element.99) | copy-start | bytes 2359300
  448.6 3.1 copy-start.10
  448.6 3.1 copy-start.28
  471.3 5.2 collective-permute-start.2
  480.3 62.6 %copy-start.83 = (f32[1024,768]{1,0:T(8,128)S(1)}, f32[1024,768]{1,0:T(8,128)}, u32[]{:S(2)}) copy-start(f32[1024,768]{1,0:T(8,128)} %copy-done.82) | copy-start | bytes 9437188
  483.4 59.6 %copy-start.48 = (bf16[4,96,1024]{2,1,0:T(8,128)(2,1)S(1)}, bf16[4,96,1024]{2,1,0:T(8,128)(2,1)}, u32[]{:S(2)}) copy-start(bf16[4,96,1024]{2,1,0:T(8,128)(2,1)} %copy-done.46) | copy-start | bytes 2359300
  548.9 74.4 %copy-start.39 = (bf16[1024,128]{1,0:T(8,128)(2,1)S(1)}, bf16[1024,128]{1,0:T(8,128)(2,1)}, u32[]{:S(2)}) copy-start(bf16[1024,128]{1,0:T(8,128)(2,1)} %copy-done.38) | copy-start | bytes 786436
  626.1 19.6 %copy-start.70 = (f32[1024,32]{1,0:T(8,128)S(1)}, f32[1024,32]{1,0:T(8,128)}, u32[]{:S(2)}) copy-start(f32[1024,32]{1,0:T(8,128)} %copy-done.67) | copy-start | bytes 393220
  626.1 19.6 %copy-start.74 = (f32[1024,32]{1,0:T(8,128)S(1)}, f32[1024,32]{1,0:T(8,128)}, u32[]{:S(2)}) copy-start(f32[1024,32]{1,0:T(8,128)} %copy-done.71) | copy-start | bytes 393220
  627.1 20.0 %copy-start.126 = (bf16[32]{0:T(256)(128)(2,1)S(1)}, bf16[32]{0:T(256)(128)(2,1)}, u32[]{:S(2)}) copy-start(bf16[32]{0:T(256)(128)(2,1)} %param.33) | copy-start | bytes 196
  649.2 4.0 copy-start.42
  654.2 15.7 %collective-permute-start.3 = (bf16[1024,256]{1,0:T(8,128)(2,1)}, bf16[1024,256]{1,0:T(8,128)(2,1)}, u32[]{:S(2)}, u32[]{:S(2)}) collective-permute-start(bf16[1024,256]{1,0:T(8,128)(2,1)} %slice.403), channel_id=1, source_target_pairs={{0,1},{1,0},{2,3},{3,2},{4,5},{5,4},{6,7},{7,6},{8,9},{9,8},{10,11... | collective-permute-start | bytes 1572872 | tf_op jit(solution)/shard_map/ppermute | solution.py:1410
  656.8 3.7 copy-start.96
  660.7 4.3 copy-start.106
  665.0 5.0 copy-start.81
  679.0 39.0 %copy-start.20 = (bf16[8,32,1152]{2,1,0:T(8,128)(2,1)S(1)}, bf16[8,32,1152]{2,1,0:T(8,128)(2,1)}, u32[]{:S(2)}) copy-start(bf16[8,32,1152]{2,1,0:T(8,128)(2,1)} %copy-done.19) | copy-start | bytes 1769476
  721.3 3.7 copy-start.128
  721.3 4.2 copy-start.129
  721.3 4.7 copy-start.97
  (86 other events, 160.8 us)

commit v4 on v3

--- a/solution.py
+++ b/solution.py
@@ -1,3 +1,4 @@
+import functools
 import math
 
 import jax
@@ -561,23 +562,8 @@
     return f, c, (c // 2) % 2, c // 4
 
 
-def greet_plane(f, c, z):
-    barrier = pltpu.get_barrier_semaphore()
-
-    def hello(target):
-        pl.semaphore_signal(barrier, inc=1, device_id=to_device(*target), device_id_type=MESH)
-
-    hello((f, flip(c, 2)))
-
-    @pl.when(z > 0)
-    def _():
-        hello((f, c - 4))
-
-    @pl.when(z < 3)
-    def _():
-        hello((f, c + 4))
-
-    pl.semaphore_wait(barrier, 2 + jnp.where((z > 0) & (z < 3), 1, 0))
+def row_peers(f, c, z):
+    return [(f, c + 4 * ((z + i) % 4 - z)) for i in range(1, 4)]
 
 
 HALF = ROWS // 2
@@ -590,10 +576,9 @@
         self.y, self.inner = y, inner
         self.mirrored = z // 2
         sign = 1 - 2 * self.mirrored
+        self.own = 1 if inner else 0
         self.across = (f, flip(c, 2))
-        self.up = (f, c + 4 * sign)
-        self.down = (f, c - 4 * sign)
-        self.own = 1 if inner else 0
+        self.chip_at = [(f, c + 4 * sign * (near - self.own)) for near in range(4)]
         self.sent = []
 
     def at(self, near):
@@ -621,162 +606,165 @@
     def y_copy(self, slot):
         return remote(self.sy.at[slot], self.ry.at[slot], self.ys.at[slot], self.yr.at[slot], self.across)
 
-    def z_copy(self, slot, upward):
-        if not upward:
-            return remote(self.sd.at[slot], self.ra.at[slot], self.ds.at[slot], self.ar.at[slot], self.down)
-        if self.inner:
-            return remote(self.su.at[slot], self.ra.at[slot], self.us.at[slot], self.ar.at[slot], self.up)
-        return remote(self.su.at[slot], self.rb.at[slot], self.us.at[slot], self.br.at[slot], self.up)
-
     def got_y(self, slot):
         self.y_copy(slot).wait_recv()
         return self.ry[slot].astype(F32)
 
-    def got_z(self, slot, below):
-        buf, sem = (self.rb, self.br) if below else (self.ra, self.ar)
+    def got(self, first, slot):
+        buf, sem = (self.rb, self.br) if first else (self.ra, self.ar)
         arrived(buf.at[slot], sem.at[slot], self.across)
         return buf[slot].astype(F32)
 
-    def pass_z(self, slot, value, upward):
-        buf = self.su if upward else self.sd
-        buf[slot] = value.astype(BF)
-        self.start(self.z_copy(slot, upward))
+    def pass_on(self, value, upward, slot, target, first, there=None):
+        there = slot if there is None else there
+        src, send = (self.su, self.us) if upward else (self.sd, self.ds)
+        dst, sem = (self.rb, self.br) if first else (self.ra, self.ar)
+        src[slot] = value.astype(BF)
+        self.start(remote(src.at[slot], dst.at[there], send.at[slot], sem.at[there], self.chip_at[target]))
 
     def cross(self, slot, value):
         self.sy[slot] = value.astype(BF)
         self.start(self.y_copy(slot))
 
+    def order(self, step):
+        near = 3 - step
+        if self.inner:
+            near = jnp.where(step == 0, 3, jnp.where(step == 1, 0, 4 - step))
+        return near, near + self.mirrored * (3 - 2 * near)
+
     def products(self):
         def other_row(step, carry):
-            if self.inner:
-                near = jnp.where(step == 0, 3, jnp.where(step == 1, 0, 4 - step))
-            else:
-                near = 3 - step
-            block = near + self.mirrored * (3 - 2 * near)
+            near, block = self.order(step)
             value = self.product(2 * block + 1 - self.y)
             self.sy[block] = value[:HALF].astype(BF)
             self.y_copy(block).start()
             self.pb[block] = value[HALF:]
+
+            @pl.when((near == 1) | (near == 2))
+            def _():
+                self.sy[4 + block] = value[HALF:].astype(BF)
+                self.y_copy(4 + block).start()
+
             return carry
 
         lax.fori_loop(0, 4, other_row, 0)
         for near in range(4):
-            self.sent.append(self.y_copy(self.at(near)))
-        if not self.inner:
-            self.pass_z(ODD, self.pb[self.at(3)], True)
-        for near in (2, 1):
-            self.cross(self.slot(1, near), self.pb[self.at(near)])
+            self.sent.append(self.y_copy(self.slot(0, near)))
+        for near in (1, 2):
+            self.sent.append(self.y_copy(self.slot(1, near)))
+        if self.inner:
+            self.pass_on(self.pb[self.at(3)], True, ODD, 3, True)
+            self.pass_on(self.pb[self.at(0)], False, ODD, 0, False)
+        else:
+            self.pass_on(self.pb[self.at(3)], True, ODD, 3, False, ODD + 1)
 
         def own_row(step, carry):
-            near = 3 - step
-            block = near + self.mirrored * (3 - 2 * near)
+            near, block = self.order(step)
             value = self.product(2 * block + self.y)
             self.acc[block] = value[:HALF]
             self.acc[4 + block] = value[HALF:]
             return carry
 
         lax.fori_loop(0, 4, own_row, 0)
-
-    def far_halves(self):
+        far = self.slot(1, 3)
+        if self.inner:
+            end = self.slot(1, 0)
+            self.pass_on(self.acc[end], False, end, 0, False)
+            self.pass_on(self.acc[far] + self.got(True, far), True, far, 3, True)
+        else:
+            self.pass_on(self.acc[far], True, far, 1, True)
+
+    def relay(self, half, near):
+        slot = self.slot(half, near)
+        value = self.acc[slot] + self.got_y(slot)
         if not self.inner:
-            self.pass_z(self.slot(1, 3), self.acc[self.slot(1, 3)], True)
+            self.pass_on(value, True, slot, 1, True)
+        elif near == 0:
+            self.pass_on(value, False, slot, 0, False)
+        else:
+            self.pass_on(value + self.got(True, slot), True, slot, near, near == 3)
+
+    def relays(self):
+        if self.inner:
+            self.relay(0, 3)
+            self.relay(0, 0)
+            self.relay(0, 2)
+            self.relay(1, 2)
             return
-        self.pass_z(ODD, self.pb[self.at(3)] + self.got_z(ODD, True), True)
-        far = self.slot(1, 3)
-        self.pass_z(far, self.acc[far] + self.got_z(far, True), True)
-        self.pass_z(ODD, self.pb[self.at(0)] + self.got_z(ODD, False), False)
-        end = self.slot(1, 0)
-        self.pass_z(end, self.acc[end] + self.got_z(end, False), False)
-
-    def chain(self, half):
-        if self.inner:
-            steps = ((3, True), (0, False), (2, True)) if half == 0 else ((2, True),)
-        else:
-            steps = ((3, True), (2, True), (1, True)) if half == 0 else ((2, True), (1, True))
-        for near, upward in steps:
-            slot = self.slot(half, near)
-            value = self.acc[slot] + self.got_y(slot)
-            if self.inner:
-                value += self.got_z(slot, upward)
-            self.pass_z(slot, value, upward)
-        if half == 1 and not self.inner:
-            self.cross(self.slot(1, 0), self.pb[self.at(0)] + self.got_z(ODD, False))
+        self.relay(0, 3)
+        self.relay(0, 2)
+        self.relay(1, 2)
+        odd = self.pb[self.at(0)] + self.got(False, ODD) + self.got(True, ODD) + self.got(False, ODD + 1)
+        self.cross(self.slot(1, 0), odd)
+        self.relay(0, 1)
+        self.relay(1, 1)
+
+    def own_sum(self, half):
         slot = self.slot(half, self.own)
-        total = self.acc[slot] + self.got_z(slot, False)
-        if self.inner:
-            total += self.got_z(slot, True)
-        return total + self.got_y(slot)
+        return self.acc[slot] + self.got_y(slot) + self.got(True, slot) + self.got(False, slot)
 
 
 class Gather(Plane):
     def __init__(self, place, inner, full, sems):
         super().__init__(place, inner)
         self.full = full
-        self.ys, self.yr, self.us, self.ds, self.br, self.ar = sems
+        self.ys, self.yr, self.us, self.ds, self.zr = sems
 
     def rows(self, half, near, side):
         start = (self.at(near) * 2 + side) * ROWS + half * HALF
         return self.full.at[pl.ds(pl.multiple_of(start, HALF), HALF)]
 
-    def y_copy(self, half, near):
+    def to_row(self, part, sem, slot, target):
+        self.start(remote(part, part, sem, self.zr.at[slot], self.chip_at[target]))
+
+    def to_other_row(self, half, near):
         part = self.rows(half, near, self.y)
         slot = self.slot(half, near)
-        return remote(part, part, self.ys.at[slot], self.yr.at[slot], self.across)
-
-    def send_z(self, part, slot, upward):
-        sem = self.us if upward else self.ds
-        arrive = self.br if upward and not self.inner else self.ar
-        self.start(remote(part, part, sem.at[slot], arrive.at[slot], self.up if upward else self.down))
-
-    def got_z(self, part, slot, below):
-        sem = self.br if below else self.ar
-        arrived(part, sem.at[slot], self.across)
+        self.start(remote(part, part, self.ys.at[slot], self.yr.at[slot], self.across))
 
     def send_own(self, half):
         part = self.rows(half, self.own, self.y)
         slot = self.slot(half, self.own)
-        self.send_z(part, slot, True)
-        if self.inner:
-            self.send_z(part, slot, False)
-        self.start(self.y_copy(half, self.own))
-
-    def take(self, half, near, below):
+        self.to_row(part, self.us.at[slot], slot, 2)
+        self.to_row(part, self.ds.at[slot], slot, 0 if self.inner else 1)
+        self.to_other_row(half, self.own)
+
+    def take(self, half, near):
         part = self.rows(half, near, self.y)
         slot = self.slot(half, near)
-        self.got_z(part, slot, below)
+        arrived(part, self.zr.at[slot], self.across)
+        if self.inner and near in (2, 3):
+            self.to_row(part, self.ds.at[slot], slot, 0)
+        if half == 0 or near in (1, 2):
+            self.to_other_row(half, near)
+
+    def odd_slot(self, near):
+        return ODD + self.at(near) // 3
+
+    def take_odd(self, near):
+        arrived(self.rows(1, near, 1 - self.y), self.zr.at[self.odd_slot(near)], self.across)
+
+    def got_y(self, half, near):
+        arrived(self.rows(half, near, 1 - self.y), self.yr.at[self.slot(half, near)], self.across)
+
+    def forward(self, half):
+        others = (0, 2, 3) if self.inner else (1, 2, 3)
+        if half == 0:
+            for near in others:
+                self.take(0, near)
+            return
+        if not self.inner:
+            self.got_y(1, 0)
+            part = self.rows(1, 0, 1 - self.y)
+            slot = self.odd_slot(0)
+            self.to_row(part, self.us.at[8], slot, 3)
+            self.to_row(part, self.us.at[9], slot, 2)
+            self.to_row(part, self.ds.at[8], slot, 1)
+        for near in others:
+            self.take(1, near)
         if self.inner:
-            self.send_z(part, slot, below)
-        if half == 0 or near in (1, 2):
-            self.start(self.y_copy(half, near))
-
-    def take_odd(self, near, below):
-        part = self.rows(1, near, 1 - self.y)
-        self.got_z(part, ODD, below)
-        if self.inner:
-            self.send_z(part, ODD, below)
-
-    def got_y(self, half, near):
-        part = self.rows(half, near, 1 - self.y)
-        arrived(part, self.yr.at[self.slot(half, near)], self.across)
-
-    def forward(self, half):
-        if half == 0:
-            for near, below in ((0, True), (2, False), (3, False)) if self.inner else ((1, False), (2, False), (3, False)):
-                self.take(0, near, below)
-            return
-        if self.inner:
-            self.take(1, 0, True)
-            self.take(1, 2, False)
-            self.take(1, 3, False)
-            self.take_odd(0, True)
-            self.take_odd(3, False)
-        else:
-            self.take(1, 1, False)
-            self.got_y(1, 0)
-            self.send_z(self.rows(1, 0, 1 - self.y), ODD, True)
-            self.take(1, 2, False)
-            self.take(1, 3, False)
-            self.take_odd(3, False)
+            self.take_odd(0)
+        self.take_odd(3)
         for near in range(4):
             self.got_y(0, near)
         for near in (1, 2):
@@ -797,7 +785,8 @@
 
 def exchange(place, product, settle, full, scratch, extra=None):
     if extra is None:
-        greet_plane(place[0], place[1], place[3])
+        f, c, y, z = place
+        greet(row_peers(f, c, z) + [(f, flip(c, 2))])
     else:
         peers, sibling, twin = chip_peers(place[0], place[1])
         greet(peers + [sibling, twin])
@@ -810,15 +799,15 @@
             parts.append(more)
         reduce = Reduce(place, inner, product, scratch[:8], scratch[8:14])
         reduce.products()
-        reduce.far_halves()
         parts.append(reduce)
         if full is not None:
-            gather = Gather(place, inner, full, scratch[14:20])
+            gather = Gather(place, inner, full, scratch[14:19])
             parts.append(gather)
         if more is not None:
             more.second()
+        reduce.relays()
         for half in range(2):
-            rows = settle(half, reduce.chain(half))
+            rows = settle(half, reduce.own_sum(half))
             if full is not None:
                 start = (place[3] * 2 + place[2]) * ROWS + half * HALF
                 full[pl.ds(pl.multiple_of(start, HALF), HALF), :] = rows
@@ -842,12 +831,13 @@
     return lax.rsqrt(jnp.mean(hidden * hidden, axis=-1, keepdims=True) + NORM_EPS)
 
 
-def make_product(left_ref, right_ref, transposed):
+def make_product(left_ref, right_ref, transposed, lanes=None):
     dims = (((1,), (1,)), ((), ())) if transposed else (((1,), (0,)), ((), ()))
 
     def product(block):
         rows = left_ref[pl.ds(pl.multiple_of(block * ROWS, ROWS), ROWS), :]
-        return lax.dot_general(rows, right_ref[...], dims, preferred_element_type=F32)
+        right = right_ref[...] if lanes is None else right_ref[:, lanes[0] : lanes[1]]
+        return lax.dot_general(rows, right, dims, preferred_element_type=F32)
 
     return product
 
@@ -877,24 +867,14 @@
     return grad + inverse * (scaled - normed * mean)
 
 
-def back_kernel(left_ref, right_ref, grad_ref, hid_ref, gain_ref, new_ref, full_ref, *scratch):
-    def settle(half, total):
-        at = half_rows(half)
-        new = back_rows(total, grad_ref[at, :].astype(F32), hid_ref[at, :].astype(F32), gain_ref[...])
-        new_ref[at, :] = new
-        return new.astype(BF)
-
-    exchange(plane_place(), make_product(left_ref, right_ref, True), settle, full_ref, scratch)
-
-
-def comm_call(kernel, outs, ident, args, gathers, more=()):
+def comm_call(kernel, outs, ident, args, gathers, name, more=()):
     width = 1024
     scratch = []
-    for count, kind in ((8, BF), (8, BF), (8, F32), (4, F32), (9, BF), (9, BF), (9, BF), (9, BF)):
+    for count, kind in ((8, BF), (8, BF), (8, F32), (4, F32), (9, BF), (9, BF), (9, BF), (10, BF)):
         scratch.append(pltpu.VMEM((count, HALF, width), kind))
-    scratch += [pltpu.SemaphoreType.DMA((9,))] * 6
+    scratch += [pltpu.SemaphoreType.DMA((10,))] * 6
     if gathers:
-        scratch += [pltpu.SemaphoreType.DMA((9,))] * 6
+        scratch += [pltpu.SemaphoreType.DMA((10,))] * 5
     scratch += list(more)
     spec = pl.BlockSpec(memory_space=VMEM_SPACE)
     return pl.pallas_call(
@@ -904,9 +884,9 @@
         out_specs=[spec] * len(outs),
         scratch_shapes=scratch,
         compiler_params=pltpu.CompilerParams(
-            collective_id=ident, has_side_effects=True, vmem_limit_bytes=40 * 1024 * 1024
+            collective_id=ident, has_side_effects=True, vmem_limit_bytes=(24 if more else 14) * 1024 * 1024
         ),
-        name=kernel.__name__,
+        name=name,
     )(*args)
 
 
@@ -1032,18 +1012,51 @@
                 self.out_copy(l).wait_send()
 
 
-def begin_kernel(tok, a1, a2, dn, op, full, r1, r2, d1, d2, o1, o2, *sems):
+def pack_shards(shards, block, a):
+    pre, query, keys, values, mid, gates, upproj = shards
+    rows, units = gates.shape
+    each = units // 32
+    lane = lax.broadcasted_iota(jnp.int32, (rows, block - each), 1)
+    empty = jnp.zeros((rows, block - each), F32)
+    riders = jnp.where(lane == 0, pre[...].astype(F32), jnp.where(lane == 1, mid[...].astype(F32), empty))
+    for chip in range(8):
+        pair = 4 * (chip % 2) + chip // 2
+        for n, w in enumerate((query, keys, values)):
+            a[chip, :, 128 * n : 128 * n + 128] = w[:, 128 * pair : 128 * pair + 128]
+        for n, w in enumerate((gates, upproj)):
+            parts = []
+            for i in range(4):
+                owner = 16 * (i // 2) + 2 * chip + i % 2
+                parts.append(w[:, each * owner : each * owner + each].astype(F32))
+                parts.append(riders if n == 0 and i == 0 else empty)
+            first = 384 + 4 * block * n
+            a[chip, :, first : first + 4 * block] = jnp.concatenate(parts, axis=-1).astype(BF)
+
+
+def begin_kernel(tok, *refs):
+    ins, results, scratch = refs[:18], refs[18:25], refs[25:]
+    full, r1, r2, d1, d2, o1, o2 = results
+    a1, a2, dn, sems = scratch[0], scratch[1], scratch[2], scratch[3:]
+    block = dn.shape[1]
     place = plane_place()
     f, c, y, z = place
     peers, sibling, twin = chip_peers(f, c)
     greet(peers + [sibling, twin])
     start = (z * 2 + y) * ROWS
     full[pl.ds(pl.multiple_of(start, ROWS), ROWS), :] = tok[...]
+    outs = []
+    for l, a in enumerate((a1, a2)):
+        pre, query, keys, values, out, mid, gates, upproj, down = ins[9 * l : 9 * l + 9]
+        outs.append(out)
+        pack_shards((pre, query, keys, values, mid, gates, upproj), block, a)
+        each = down.shape[0]
+        dn[l, :each] = down[...]
+        dn[l, each:] = jnp.zeros((block - each, down.shape[1]), BF)
 
     def run(inner):
-        gather = Gather(place, inner, full, sems[:6])
+        gather = Gather(place, inner, full, sems[:5])
         spread = Spread(
-            place, ((a1, r1), (a2, r2)), ((dn.at[0], d1), (dn.at[1], d2)), ((op.at[0], o1), (op.at[1], o2)), sems[6:]
+            place, ((a1, r1), (a2, r2)), ((dn.at[0], d1), (dn.at[1], d2)), ((outs[0], o1), (outs[1], o2)), sems[5:]
         )
         gather.send_own(0)
         gather.send_own(1)
@@ -1061,23 +1074,25 @@
     both_kinds(place, run)
 
 
-def begin_call(tok, a1, a2, down, out):
-    rows, wide = a1.shape[1:]
-    block, width = down.shape[1:]
+def begin_call(tok, shards, block):
+    rows, width = shards[1].shape
+    wide = 384 + 8 * block
     spec = pl.BlockSpec(memory_space=VMEM_SPACE)
     shapes = [(8 * ROWS, width)] + [(32, rows, wide)] * 2 + [(4, block, width)] * 2 + [(4, rows, width)] * 2
-    counts = [(9,)] * 6 + [(2, 8), (2, 8), (2, 11), (2, 11), (2, 20), (2, 20), (2,), (2,)]
+    counts = [(10,)] * 5 + [(2, 8), (2, 8), (2, 11), (2, 11), (2, 20), (2, 20), (2,), (2,)]
     return pl.pallas_call(
         begin_kernel,
         out_shape=[jax.ShapeDtypeStruct(s, BF) for s in shapes],
-        in_specs=[spec] * 5,
+        in_specs=[spec] * 19,
         out_specs=[spec] * 7,
-        scratch_shapes=[pltpu.SemaphoreType.DMA(n) for n in counts],
+        scratch_shapes=[pltpu.VMEM((8, rows, wide), BF)] * 2
+        + [pltpu.VMEM((2, block, width), BF)]
+        + [pltpu.SemaphoreType.DMA(n) for n in counts],
         compiler_params=pltpu.CompilerParams(
-            collective_id=9, has_side_effects=True, vmem_limit_bytes=40 * 1024 * 1024
+            collective_id=9, has_side_effects=True, vmem_limit_bytes=60 * 1024 * 1024
         ),
         name="begin",
-    )(tok, a1, a2, down, out)
+    )(tok, *[s[:, None] if s.ndim == 1 else s for s in shards])
 
 
 class Collect:
@@ -1086,12 +1101,13 @@
         self.chip, self.core = self.c // 2, self.c % 2
         self.peers, self.sibling, self.twin = chip_peers(self.f, self.c)
         self.near = (self.f, flip(self.c, 2))
-        self.g, self.gd, self.go = ins
-        self.out, self.od, self.oo = results
-        self.sb, self.xb, self.xt, self.ut, self.sd, self.xd, self.td, self.so, self.xo, self.to, self.yo, self.yt = (
-            scratch[:12]
-        )
-        self.ss, self.sr, self.xs, self.xr, self.ps, self.pr, self.ys, self.yr = scratch[12:]
+        self.g, self.h = ins
+        self.out, self.oh = results
+        self.sb, self.xb, self.xt, self.ut, self.sh, self.xh, self.th, *near = scratch[: -6]
+        self.ss, self.sr, self.xs, self.xr, self.ps, self.pr = scratch[-6:]
+        self.crosses_near = bool(near)
+        if near:
+            self.yo, self.yt = near
         self.home = self.y == self.f
         self.sent = []
 
@@ -1105,10 +1121,10 @@
         return self.send(src, dst, self.ss.at[n], self.sr.at[n], self.sibling)
 
     def twin_copy(self):
-        return remote(self.to, self.xo, self.xs.at[9], self.xr.at[9], self.twin)
+        return remote(self.th, self.xh, self.xs.at[8], self.xr.at[8], self.twin)
 
     def near_copy(self):
-        return remote(self.yt, self.yo, self.ys, self.yr, self.near)
+        return remote(self.yt, self.yo, self.xs.at[9], self.xr.at[9], self.near)
 
     def first(self):
         other = 1 - self.core
@@ -1118,8 +1134,7 @@
             self.inner.append(
                 self.inner_send(self.g.at[pl.ds(part, 8), other], self.sb.at[pl.ds(part, 8)], half)
             )
-        self.inner.append(self.inner_send(self.gd.at[:, other], self.sd, 2))
-        self.inner.append(self.inner_send(self.go.at[:, other], self.so, 3))
+        self.inner.append(self.inner_send(self.h.at[:, other], self.sh, 2))
 
     def second(self):
         f, core = self.f, self.core
@@ -1133,11 +1148,12 @@
                 self.send(self.xt.at[t], self.xb.at[t], self.xs.at[i], self.xr.at[i], self.twin)
             )
         self.inner[2].wait_recv()
-        self.td[...] = (self.gd[1 - f, core].astype(F32) + self.sd[1 - f].astype(F32)).astype(BF)
-        self.crossed.append(self.send(self.td, self.xd, self.xs.at[8], self.xr.at[8], self.twin))
-        self.inner[3].wait_recv()
+        if not self.crosses_near:
+            self.th[...] = (self.h[1 - f, core].astype(F32) + self.sh[1 - f].astype(F32)).astype(BF)
+            self.twin_copy().start()
+            return
         for side in range(2):
-            self.to[side] = (self.go[side, core].astype(F32) + self.so[side].astype(F32)).astype(BF)
+            self.th[side] = (self.h[side, core].astype(F32) + self.sh[side].astype(F32)).astype(BF)
 
         @pl.when(jnp.logical_not(self.home))
         def _():
@@ -1159,83 +1175,77 @@
                 )
             else:
                 self.out[self.chip] = total.astype(BF)
-        self.crossed[8].wait_recv()
-        self.od[...] = self.gd[f, core].astype(F32) + self.sd[f].astype(F32) + self.xd[...].astype(F32)
+        if not self.crosses_near:
+            self.twin_copy().wait_recv()
+            self.oh[...] = self.h[f, core].astype(F32) + self.sh[f].astype(F32) + self.xh[...].astype(F32)
+            return
 
         @pl.when(self.home)
         def _():
             self.twin_copy().wait_recv()
             y = self.y
-            self.oo[...] = self.to[y].astype(F32) + self.xo[y].astype(F32)
-            self.yt[...] = (self.to[1 - y].astype(F32) + self.xo[1 - y].astype(F32)).astype(BF)
+            self.oh[...] = self.th[y].astype(F32) + self.xh[y].astype(F32)
+            self.yt[...] = (self.th[1 - y].astype(F32) + self.xh[1 - y].astype(F32)).astype(BF)
             self.near_copy().start()
 
     def finish(self):
-        @pl.when(self.home)
-        def _():
-            self.near_copy().wait_send()
-
-        @pl.when(jnp.logical_not(self.home))
-        def _():
-            self.near_copy().wait_recv()
-            self.oo[...] = self.yo[...].astype(F32)
+        if self.crosses_near:
+
+            @pl.when(self.home)
+            def _():
+                self.near_copy().wait_send()
+
+            @pl.when(jnp.logical_not(self.home))
+            def _():
+                self.near_copy().wait_recv()
+                self.oh[...] = self.yo[...].astype(F32)
+                self.twin_copy().wait_send()
+        else:
             self.twin_copy().wait_send()
-
         for copy in self.direct:
             copy.wait_recv()
         for copy in self.sent:
             copy.wait_send()
 
 
-def collect_shapes(rows, wide, block, width):
-    results = [((8, rows, wide), BF), ((block, width), F32), ((rows, width), F32)]
-    buffers = [
-        (16, rows, wide), (8, rows, wide), (8, rows, wide), (8, rows, wide),
-        (2, block, width), (block, width), (block, width),
-        (2, rows, width), (2, rows, width), (2, rows, width), (rows, width), (rows, width),
-    ]
-    counts = ((4,), (4,), (10,), (10,), (7,), (7,), (), ())
+def collect_shapes(rows, wide, block, width, crosses_near):
+    results = [((8, rows, wide), BF), ((block, width), F32)]
+    buffers = [(16, rows, wide), (8, rows, wide), (8, rows, wide), (8, rows, wide), (2, block, width)]
+    if crosses_near:
+        buffers += [(2, block, width), (2, block, width), (block, width), (block, width)]
+    else:
+        buffers += [(block, width), (block, width)]
+    counts = ((3,), (3,), (10,), (10,), (7,), (7,))
     scratch = [pltpu.VMEM(b, BF) for b in buffers] + [pltpu.SemaphoreType.DMA(n) for n in counts]
     return results, scratch
 
 
-def back_collect_kernel(
-    left_ref, right_ref, grad_ref, hid_ref, gain_ref, g, gd, go, new_ref, full_ref, c, od, oo, *scratch
-):
+def back_kernel(gathers, lanes, left_ref, right_ref, grad_ref, hid_ref, gain_ref, g, gd, new_ref, *rest):
+    full_ref = rest[0] if gathers else None
+    c, od = rest[gathers : gathers + 2]
+    scratch = rest[gathers + 2 :]
+
     def settle(half, total):
         at = half_rows(half)
         new = back_rows(total, grad_ref[at, :].astype(F32), hid_ref[at, :].astype(F32), gain_ref[...])
-        new_ref[at, :] = new
+        new_ref[at, :] = new.astype(new_ref.dtype)
         return new.astype(BF)
 
     def extra(place):
-        return Collect(place, (g, gd, go), (c, od, oo), scratch[20:])
-
-    product = make_product(left_ref, right_ref, True)
+        return Collect(place, (g, gd), (c, od), scratch[14 + 5 * gathers :])
+
+    product = make_product(left_ref, right_ref, True, lanes)
     exchange(plane_place(), product, settle, full_ref, scratch, extra)
-
-
-def last_collect_kernel(left_ref, right_ref, grad_ref, hid_ref, gain_ref, g, gd, go, out_ref, c, od, oo, *scratch):
-    def settle(half, total):
-        at = half_rows(half)
-        new = back_rows(total, grad_ref[at, :].astype(F32), hid_ref[at, :].astype(F32), gain_ref[...])
-        out_ref[at, :] = new.astype(BF)
-
-    def extra(place):
-        return Collect(place, (g, gd, go), (c, od, oo), scratch[14:])
-
-    product = make_product(left_ref, right_ref, True)
-    exchange(plane_place(), product, settle, None, scratch, extra)
 
 
 def head_lanes(head):
     lane = lax.broadcasted_iota(jnp.int32, (1, 128), 1)
-    return (lane // 32) % 2 == head
-
-
-def value_lanes(head):
+    return lane // 64 == head
+
+
+def swap_halves(values):
     lane = lax.broadcasted_iota(jnp.int32, (1, 128), 1)
-    return lane // 64 == head
+    return jnp.where(lane % 64 < 32, pltpu.roll(values, 96, 1), pltpu.roll(values, 32, 1))
 
 
 NT = (((1,), (1,)), ((), ()))
@@ -1256,7 +1266,7 @@
         lse_ref[:, head : head + 1] = top + jnp.log(total)
         mixed = jnp.dot(shares.astype(BF), v_ref[...], preferred_element_type=F32)
         parts.append(mixed / total)
-    att_ref[...] = jnp.where(value_lanes(0), parts[0], parts[1]).astype(BF)
+    att_ref[...] = jnp.where(head_lanes(0), parts[0], parts[1]).astype(BF)
 
 
 def attend_forward(q, k, v, pos_q, pos_k):
@@ -1281,24 +1291,31 @@
             pl.BlockSpec((step, 128), lambda i: (i, 0)),
             pl.BlockSpec((step, 2), lambda i: (i, 0)),
         ],
-        compiler_params=pltpu.CompilerParams(vmem_limit_bytes=40 * 1024 * 1024),
+        compiler_params=pltpu.CompilerParams(vmem_limit_bytes=14 * 1024 * 1024),
         name="attend_forward",
     )(q, k, v, pos_q, pos_k)
 
 
-def attend_back_kernel(q_ref, k_ref, v_ref, da_ref, lse_ref, pq_ref, pk_ref, dq_ref, dk_ref, dv_ref):
-    @pl.when(pl.program_id(0) == 0)
+def attend_back_kernel(
+    q_ref, k_ref, v_ref, full_ref, out_ref, att_ref, lse_ref, pq_ref, pk_ref, dq_ref, dk_ref, dv_ref, dw_ref, acc_ref
+):
+    step_no = pl.program_id(0)
+
+    @pl.when(step_no == 0)
     def _():
         dk_ref[...] = jnp.zeros_like(dk_ref)
         dv_ref[...] = jnp.zeros_like(dv_ref)
+        acc_ref[...] = jnp.zeros_like(acc_ref)
 
     allowed = pk_ref[...] <= pq_ref[...]
     queries = q_ref[...]
-    grads = da_ref[...]
+    full = full_ref[...]
+    grads = lax.dot_general(full, out_ref[...], NT, preferred_element_type=F32).astype(BF)
+    acc_ref[...] += lax.dot_general(att_ref[...], full, TN, preferred_element_type=F32)
     parts = []
     for head in range(2):
         masked = jnp.where(head_lanes(head), queries, jnp.zeros_like(queries))
-        grad_h = jnp.where(value_lanes(head), grads, jnp.zeros_like(grads))
+        grad_h = jnp.where(head_lanes(head), grads, jnp.zeros_like(grads))
         scores = lax.dot_general(k_ref[...], masked, NT, preferred_element_type=F32) * HD ** (-0.5)
         shares = jnp.where(allowed, jnp.exp(scores - lse_ref[head : head + 1, :]), 0.0)
         grad_shares = lax.dot_general(v_ref[...], grad_h, NT, preferred_element_type=F32)
@@ -1309,11 +1326,19 @@
         parts.append(lax.dot_general(grad_scores, k_ref[...], TN, preferred_element_type=F32))
     dq_ref[...] = jnp.where(head_lanes(0), parts[0], parts[1])
 
-
-def attend_backward(q, k, v, da, lse_rows, pos_q, pos_k):
+    @pl.when(step_no == pl.num_programs(0) - 1)
+    def _():
+        dw_ref[...] = acc_ref[...].astype(BF)
+
+
+def attend_backward(q, k, v, full, out_w, att, lse_rows, pos_q, pos_k):
     rows = q.shape[0]
     keys = k.shape[0]
+    width = full.shape[1]
     step = 128
+    row_block = pl.BlockSpec((step, 128), lambda i: (i, 0))
+    key_block = pl.BlockSpec((keys, 128), lambda i: (0, 0))
+    weight_block = pl.BlockSpec((128, width), lambda i: (0, 0))
     return pl.pallas_call(
         attend_back_kernel,
         grid=(rows // step,),
@@ -1321,134 +1346,200 @@
             jax.ShapeDtypeStruct((rows, 128), F32),
             jax.ShapeDtypeStruct((keys, 128), F32),
             jax.ShapeDtypeStruct((keys, 128), F32),
+            jax.ShapeDtypeStruct((128, width), BF),
         ],
         in_specs=[
-            pl.BlockSpec((step, 128), lambda i: (i, 0)),
-            pl.BlockSpec((keys, 128), lambda i: (0, 0)),
-            pl.BlockSpec((keys, 128), lambda i: (0, 0)),
-            pl.BlockSpec((step, 128), lambda i: (i, 0)),
+            row_block, key_block, key_block,
+            pl.BlockSpec((step, width), lambda i: (i, 0)),
+            weight_block, row_block,
             pl.BlockSpec((2, step), lambda i: (0, i)),
             pl.BlockSpec((1, step), lambda i: (0, i)),
             pl.BlockSpec((keys, 1), lambda i: (0, 0)),
         ],
-        out_specs=[
-            pl.BlockSpec((step, 128), lambda i: (i, 0)),
-            pl.BlockSpec((keys, 128), lambda i: (0, 0)),
-            pl.BlockSpec((keys, 128), lambda i: (0, 0)),
-        ],
-        compiler_params=pltpu.CompilerParams(vmem_limit_bytes=48 * 1024 * 1024),
+        out_specs=[row_block, key_block, key_block, weight_block],
+        scratch_shapes=[pltpu.VMEM((128, width), F32)],
+        compiler_params=pltpu.CompilerParams(vmem_limit_bytes=60 * 1024 * 1024),
         name="attend_backward",
-    )(q, k, v, da, lse_rows, pos_q, pos_k)
-
-
-def chip_first(split):
-    order = (2, 1, 0) + tuple(range(3, split.ndim))
-    return split.transpose(order).reshape(8, split.shape[0], *split.shape[3:])
-
-
-def chip_last(packed):
-    split = packed.reshape(4, 2, *packed.shape[1:])
-    return split.transpose((2, 1, 0) + tuple(range(3, split.ndim)))
-
-
-def pack_heads(weight):
-    rows = weight.shape[0]
-    split = chip_first(weight.reshape(rows, 2, 4, 2, 2, 32))
-    return split.transpose(0, 1, 3, 2, 4).reshape(8, rows, 128)
-
-
-def unpack_heads(packed):
-    rows = packed.shape[1]
-    split = packed.reshape(8, rows, 2, 2, 32).transpose(0, 1, 3, 2, 4)
-    return chip_last(split).reshape(rows, 1024)
-
-
-def pack_values(weight):
-    rows = weight.shape[0]
-    return chip_first(weight.reshape(rows, 2, 4, 128))
-
-
-def unpack_values(packed):
-    return chip_last(packed).reshape(packed.shape[1], 1024)
-
-
-def pack_units(weight, block, *extra):
-    rows, units = weight.shape
-    each = units // 32
-    split = weight.reshape(rows, 2, 8, 2, each).transpose(2, 0, 1, 3, 4).reshape(8, rows, 4, each)
-    padding = jnp.zeros((8, rows, 4, block - each), weight.dtype)
-    if extra:
-        columns = jnp.stack(extra, axis=-1)
-        columns = jnp.pad(columns, ((0, 0), (0, block - each - len(extra))))
-        first = jnp.broadcast_to(columns[None, :, None, :], (8, rows, 1, block - each))
-        padding = jnp.concatenate([first, padding[:, :, 1:]], axis=2)
-    return jnp.concatenate([split, padding], axis=-1).reshape(8, rows, 4 * block)
-
-
-def unpack_units(packed, units):
-    rows = packed.shape[1]
-    each = units // 32
-    split = packed.reshape(8, rows, 2, 2, -1)[..., :each]
-    return split.transpose(1, 2, 0, 3, 4).reshape(rows, units)
-
-
-def pair_rope(values, cosine, sine):
-    first, second = values[:, :64], values[:, 64:]
-    return jnp.concatenate(
-        [first * cosine - second * sine, second * cosine + first * sine], axis=-1
-    )
-
-
-def pair_unrope(values, cosine, sine):
-    first, second = values[:, :64], values[:, 64:]
-    return jnp.concatenate(
-        [first * cosine + second * sine, second * cosine - first * sine], axis=-1
-    )
-
-
-def swap_cores(value):
-    return lax.ppermute(value, "ctx", [(i, i + 1 - 2 * (i % 2)) for i in range(16)])
+    )(q, k, v, full, out_w, att, lse_rows, pos_q, pos_k)
+
+
+def project_kernel(layer, *refs):
+    x_ref, w_ref, cos_ref, sin_ref, more_ref = refs[:5]
+    q_ref, k_ref, v_ref, keep_ref = refs[5:9]
+    ss, sr = refs[-2:]
+    f, c, _, _ = plane_place()
+    sibling = (f, flip(c, 1))
+    greet([sibling])
+    rows_n = x_ref.shape[0]
+
+    def copies(i):
+        here = pl.ds(pl.multiple_of(i * ROWS, ROWS), ROWS)
+        there = pl.ds(pl.multiple_of(rows_n + i * ROWS, ROWS), ROWS)
+        return [
+            remote(ref.at[here], ref.at[there], ss.at[2 * i + n], sr.at[2 * i + n], sibling)
+            for n, ref in enumerate((k_ref, v_ref))
+        ]
+
+    def step(i, carry):
+        at = pl.ds(pl.multiple_of(i * ROWS, ROWS), ROWS)
+        rows = x_ref[at, :]
+        if layer == 0:
+            wide = rows.astype(F32)
+            rows = (wide * norm_rows(wide) * more_ref[...]).astype(BF)
+            keep_ref[at, :] = rows
+        raw = jnp.dot(rows, w_ref[:, :384], preferred_element_type=F32)
+        cosine, sine = cos_ref[at, :], sin_ref[at, :]
+        q, k, v = raw[:, :128], raw[:, 128:256], raw[:, 256:]
+        q_ref[at, :] = (q * cosine + swap_halves(q) * sine).astype(BF)
+        k_ref[at, :] = (k * cosine + swap_halves(k) * sine).astype(BF)
+        if layer == 0:
+            refs[9][at, :] = v
+        else:
+            v = 0.5 * v + 0.5 * more_ref[at, :]
+        v_ref[at, :] = v.astype(BF)
+        for copy in copies(i):
+            copy.start()
+        return carry
+
+    lax.fori_loop(0, rows_n // ROWS, step, 0)
+    if layer == 1:
+        keep_ref[...] = jnp.zeros_like(keep_ref)
+    for i in range(rows_n // ROWS):
+        for copy in copies(i):
+            copy.wait()
+
+
+def project(layer, x, w, cosine, sine, more):
+    rows_n = x.shape[0]
+    spec = pl.BlockSpec(memory_space=VMEM_SPACE)
+    outs = [((rows_n, 128), BF), ((2 * rows_n, 128), BF), ((2 * rows_n, 128), BF)]
+    outs += [(x.shape, BF), ((rows_n, 128), F32)] if layer == 0 else [((8, 128), F32)]
+    count = 2 * (rows_n // ROWS)
+    return pl.pallas_call(
+        functools.partial(project_kernel, layer),
+        out_shape=[jax.ShapeDtypeStruct(*o) for o in outs],
+        in_specs=[spec] * 5,
+        out_specs=[spec] * len(outs),
+        scratch_shapes=[pltpu.SemaphoreType.DMA((count,))] * 2,
+        compiler_params=pltpu.CompilerParams(
+            collective_id=10 + layer, has_side_effects=True, vmem_limit_bytes=8 * 1024 * 1024
+        ),
+        name="project",
+    )(x, w, cosine, sine, more)
+
+
+def turn_back_kernel(layer, dq_ref, dk_ref, dv_ref, cos_ref, sin_ref, more_ref, three_ref, pass_ref, sb, rb, ss, sr):
+    f, c, _, _ = plane_place()
+    sibling = (f, flip(c, 1))
+    greet([sibling])
+    rows_n = dq_ref.shape[0]
+    copies = []
+    for n, ref in enumerate((dk_ref, dv_ref)):
+        sb[n] = ref[rows_n:, :].astype(BF)
+        copies.append(remote(sb.at[n], rb.at[n], ss.at[n], sr.at[n], sibling))
+        copies[n].start()
+    cosine, sine = cos_ref[...], sin_ref[...]
+    dq = dq_ref[...]
+    three_ref[:, :128] = (dq * cosine - swap_halves(dq) * sine).astype(BF)
+    copies[0].wait()
+    dk = dk_ref[:rows_n, :] + rb[0].astype(F32)
+    three_ref[:, 128:256] = (dk * cosine - swap_halves(dk) * sine).astype(BF)
+    copies[1].wait()
+    dv = dv_ref[:rows_n, :] + rb[1].astype(F32)
+    if layer == 1:
+        dv = 0.5 * dv
+        pass_ref[...] = dv
+    else:
+        dv = dv + more_ref[...]
+        pass_ref[...] = jnp.zeros_like(pass_ref)
+    three_ref[:, 256:] = dv.astype(BF)
+
+
+def turn_back(layer, dq, dk, dv, cosine, sine, more):
+    rows_n = dq.shape[0]
+    spec = pl.BlockSpec(memory_space=VMEM_SPACE)
+    outs = [((rows_n, 384), BF), ((rows_n if layer == 1 else 8, 128), F32)]
+    return pl.pallas_call(
+        functools.partial(turn_back_kernel, layer),
+        out_shape=[jax.ShapeDtypeStruct(*o) for o in outs],
+        in_specs=[spec] * 6,
+        out_specs=[spec] * 2,
+        scratch_shapes=[pltpu.VMEM((2, rows_n, 128), BF)] * 2 + [pltpu.SemaphoreType.DMA((2,))] * 2,
+        compiler_params=pltpu.CompilerParams(
+            collective_id=12 + layer, has_side_effects=True, vmem_limit_bytes=8 * 1024 * 1024
+        ),
+        name="turn_back",
+    )(dq, dk, dv, cosine, sine, more)
+
+
+def unpack_kernel(*refs):
+    for l in range(2):
+        cu, od, cq, oo, pre, query, keys, values, mid, gates, upproj = refs[11 * l : 11 * l + 11]
+        g_pre, gq, gk, gv, g_out, g_mid, gg, gu, g_down = refs[22 + 9 * l : 31 + 9 * l]
+        rows, units = gates.shape
+        each = units // 32
+        block = cu.shape[2] // 8
+        total = jnp.zeros((rows, 1), F32)
+        for chip in range(8):
+            pair = 4 * (chip % 2) + chip // 2
+            for n, (w, g) in enumerate(((query, gq), (keys, gk), (values, gv))):
+                at = slice(128 * pair, 128 * pair + 128)
+                part = cq[chip, :, 128 * n : 128 * n + 128].astype(F32)
+                g[:, at] = part
+                total += jnp.sum(part * w[:, at].astype(F32), axis=-1, keepdims=True)
+        g_pre[...] = total / pre[...].astype(F32)
+        for n, g in enumerate((gg, gu)):
+            for chip in range(8):
+                wide = cu[chip, :, 4 * block * n : 4 * block * (n + 1)].astype(F32)
+                for i in range(4):
+                    owner = 16 * (i // 2) + 2 * chip + i % 2
+                    g[:, each * owner : each * owner + each] = wide[:, block * i : block * i + each]
+        both = gg[...] * gates[...].astype(F32) + gu[...] * upproj[...].astype(F32)
+        g_mid[...] = jnp.sum(both, axis=-1, keepdims=True) / mid[...].astype(F32)
+        g_out[...] = oo[...]
+        g_down[...] = od[: g_down.shape[0], :]
+
+
+def unpack(collected, layers):
+    args, outs = [], []
+    for l, layer in enumerate(layers):
+        pre, query, keys, values, out, mid, gates, upproj, down = layer
+        args += [*collected[l], pre[:, None], query, keys, values, mid[:, None], gates, upproj]
+        for w in layer:
+            outs.append(w.shape + (1,) if w.ndim == 1 else w.shape)
+    spec = pl.BlockSpec(memory_space=VMEM_SPACE)
+    found = pl.pallas_call(
+        unpack_kernel,
+        out_shape=[jax.ShapeDtypeStruct(o, F32) for o in outs],
+        in_specs=[spec] * len(args),
+        out_specs=[spec] * len(outs),
+        compiler_params=pltpu.CompilerParams(vmem_limit_bytes=60 * 1024 * 1024),
+        name="unpack",
+    )(*args)
+    return [g[:, 0] if g.shape[-1] == 1 else g for g in found]
 
 
 def fast_local(tokens, cotangent, pair_of, *shards):
     width = tokens.shape[2]
-    units = shards[6].shape[1]
+    rows_each, units = shards[6].shape
     each = units // 32
     block = (each + 2 + 31) // 32 * 32
     hidden_pad = 4 * block
-    c = lax.axis_index("ctx")
-    core = c % 2
-    chip = c // 2
+    wide = 384 + 2 * hidden_pad
+    core = lax.axis_index("ctx") % 2
     pos_all = storage_positions(pair_of, ROWS).reshape(8, 2, ROWS)
     own_pos = lax.dynamic_index_in_dim(pos_all, core, 1, False).reshape(-1)
     sib_pos = lax.dynamic_index_in_dim(pos_all, 1 - core, 1, False).reshape(-1)
     key_pos = jnp.concatenate([own_pos, sib_pos])
     cosine, sine = rope_tables(own_pos, HD)
-    cosine = jnp.concatenate([cosine, cosine], axis=-1)
-    sine = jnp.concatenate([sine, sine], axis=-1)
+    cosine = jnp.concatenate([cosine] * 4, axis=-1)
+    sine = jnp.concatenate([-sine, sine, -sine, sine], axis=-1)
 
     layers = [shards[:9], shards[9:]]
-    packs = []
-    for layer in layers:
-        packs.append(
-            jnp.concatenate(
-                [
-                    pack_heads(layer[1]),
-                    pack_heads(layer[2]),
-                    pack_values(layer[3]),
-                    pack_units(layer[6], block, layer[0], layer[5]),
-                    pack_units(layer[7], block),
-                ],
-                axis=-1,
-            )
-        )
-    rows_each, wide = packs[0].shape[1:]
-    down = jnp.pad(jnp.stack([layers[0][8], layers[1][8]]), ((0, 0), (0, block - each), (0, 0)))
     tok = tokens.reshape(ROWS, width)
     cot = cotangent.reshape(ROWS, width)
-    tok_full, *spread = begin_call(tok, *packs, down, jnp.stack([layers[0][4], layers[1][4]]))
+    full, *spread = begin_call(tok, shards, block)
     all_w = [w.reshape(32 * rows_each, wide) for w in spread[:2]]
-    qkv_w = [w[:, :384] for w in all_w]
     up_w = [w[:, 384:] for w in all_w]
     down_w = [w.reshape(hidden_pad, width) for w in spread[2:4]]
     out_w = [w.reshape(4 * rows_each, width) for w in spread[4:]]
@@ -1461,28 +1552,20 @@
     full_type = ((plane, width), BF)
     rows_type = ((ROWS, width), F32)
     saved = []
-    tok_wide = tok_full.astype(F32)
-    full = (tok_wide * norm_rows(tok_wide) * gains[0]).astype(BF)
     hidden = tok
     first_values = None
     pos_q = own_pos[:, None]
     pos_k = key_pos[None, :]
     for layer in range(2):
-        x_full = full
-        raw = jnp.dot(x_full, qkv_w[layer], preferred_element_type=F32)
-        values = raw[:, 256:]
-        mixed = values if layer == 0 else 0.5 * values + 0.5 * first_values
-        first_values = values
-        q = pair_rope(raw[:, :128], cosine, sine).astype(BF)
-        kv = jnp.concatenate(
-            [pair_rope(raw[:, 128:256], cosine, sine).astype(BF), mixed.astype(BF)], axis=-1
-        )
-        kv = jnp.concatenate([kv, swap_cores(kv)], axis=0)
-        k, v = kv[:, :128], kv[:, 128:]
+        if layer == 0:
+            q, k, v, x_full, first_values = project(0, full, all_w[0], cosine, sine, gains[0])
+        else:
+            x_full = full
+            q, k, v, _ = project(1, full, all_w[1], cosine, sine, first_values)
         att, lse = attend_forward(q, k, v, pos_q, pos_k)
         middle, mlp_full = comm_call(
             forward_kernel, [rows_type, full_type], 1 + layer,
-            (att, out_w[layer], hidden, gains[2 * layer + 1]), True,
+            (att, out_w[layer], hidden, gains[2 * layer + 1]), True, "middle",
         )
         both = jnp.dot(mlp_full, up_w[layer], preferred_element_type=F32)
         gate, up = both[:, :hidden_pad], both[:, hidden_pad:]
@@ -1491,16 +1574,15 @@
         if layer == 0:
             hidden, full = comm_call(
                 forward_kernel, [rows_type, full_type], 3,
-                (inner, down_w[layer], middle, gains[2]), True,
+                (inner, down_w[layer], middle, gains[2]), True, "result",
             )
         else:
             output, full = comm_call(
                 turn_kernel, [((ROWS, width), BF), full_type], 4,
-                (inner, down_w[layer], middle, cot), True,
+                (inner, down_w[layer], middle, cot), True, "turn",
             )
     grad = cot
-    passed = None
-    packed_grads = None
+    passed = cosine
     collected = [None, None]
     for layer in (1, 0):
         x_full, q, k, v, lse, att, mlp_full, gate, up, inner, hidden, middle = saved[layer]
@@ -1511,60 +1593,38 @@
         grad_up = (grad_inner * gate * sigma).astype(BF)
         both = jnp.concatenate([grad_gate, grad_up], axis=-1)
         grad_upw = left_product(mlp_full, both)
-        args = (both, up_w[layer], grad, middle, gains[2 * layer + 1])
-        results, more = collect_shapes(rows_each, wide, block, width)
+        results, more = collect_shapes(rows_each, 2 * hidden_pad, block, width, False)
+        grad_mid, full, *got_up = comm_call(
+            functools.partial(back_kernel, 1, (384, wide)), [rows_type, full_type] + results, 5 + layer,
+            (
+                both, all_w[layer], grad, middle, gains[2 * layer + 1],
+                grad_upw.astype(BF).reshape(16, 2, rows_each, 2 * hidden_pad),
+                grad_down.astype(BF).reshape(2, 2, block, width),
+            ),
+            True, "middle_back", more,
+        )
+        dq, dk, dv, grad_out = attend_backward(q, k, v, full, out_w[layer], att, lse.T, own_pos[None, :], key_pos[:, None])
+        three, passed = turn_back(layer, dq, dk, dv, cosine, sine, passed)
+        grad_qkv = left_product(x_full, three)
+        results, more = collect_shapes(rows_each, 384, rows_each, width, True)
+        args = (
+            three, all_w[layer], grad_mid, hidden, gains[2 * layer],
+            grad_qkv.astype(BF).reshape(16, 2, rows_each, 384),
+            grad_out.reshape(2, 2, rows_each, width),
+        )
         if layer == 1:
-            grad_mid, full = comm_call(back_kernel, [rows_type, full_type], 5, args, True)
+            grad, full, *got_qkv = comm_call(
+                functools.partial(back_kernel, 1, (0, 384)), [rows_type, full_type] + results, 7, args, True,
+                "layer_back", more,
+            )
         else:
-            grad_mid, full, *collected[1] = comm_call(
-                back_collect_kernel, [rows_type, full_type] + results, 6, args + packed_grads, True, more
+            tokens_grad, *got_qkv = comm_call(
+                functools.partial(back_kernel, 0, (0, 384)), [((ROWS, width), BF)] + results, 8, args, False,
+                "last_back", more,
             )
-        grad_out = left_product(att, full)
-        grad_att = right_product(full, out_w[layer]).astype(BF)
-        dq, dk, dv = attend_backward(q, k, v, grad_att, lse.T, own_pos[None, :], key_pos[:, None])
-        dkv = jnp.concatenate([dk, dv], axis=-1)
-        dkv = dkv[: 8 * ROWS] + swap_cores(dkv[8 * ROWS :].astype(BF)).astype(F32)
-        dk, dv = dkv[:, :128], dkv[:, 128:]
-        if layer == 1:
-            passed = 0.5 * dv
-            dv = passed
-        else:
-            dv = dv + passed
-        three = jnp.concatenate(
-            [pair_unrope(dq, cosine, sine), pair_unrope(dk, cosine, sine), dv], axis=-1
-        ).astype(BF)
-        grad_qkv = left_product(x_full, three)
-        grad_pack = jnp.concatenate([grad_qkv, grad_upw], axis=-1)
-        packed_grads = (
-            grad_pack.astype(BF).reshape(16, 2, rows_each, wide),
-            grad_down.astype(BF).reshape(2, 2, block, width),
-            grad_out.astype(BF).reshape(2, 2, rows_each, width),
-        )
-        args = (three, qkv_w[layer], grad_mid, hidden, gains[2 * layer])
-        if layer == 1:
-            grad, full = comm_call(back_kernel, [rows_type, full_type], 7, args, True)
-        else:
-            tokens_grad, *collected[0] = comm_call(
-                last_collect_kernel, [((ROWS, width), BF)] + results, 8, args + packed_grads, False, more
-            )
-    result = [output.reshape(1, ROWS, width), tokens_grad.reshape(1, ROWS, width)]
-    for layer in range(2):
-        pack = collected[layer][0].astype(F32)
-        both = pack * packs[layer].astype(F32)
-        pre_grad = jnp.sum(both[:, :, :384], axis=(0, 2)) / layers[layer][0].astype(F32)
-        mid_grad = jnp.sum(both[:, :, 384:], axis=(0, 2)) / layers[layer][5].astype(F32)
-        result += [
-            pre_grad,
-            unpack_heads(pack[:, :, :128]),
-            unpack_heads(pack[:, :, 128:256]),
-            unpack_values(pack[:, :, 256:384]),
-            collected[layer][2],
-            mid_grad,
-            unpack_units(pack[:, :, 384 : 384 + hidden_pad], units),
-            unpack_units(pack[:, :, 384 + hidden_pad :], units),
-            collected[layer][1][:each],
-        ]
-    return tuple(result)
+        collected[layer] = got_up + got_qkv
+    found = unpack(collected, layers)
+    return (output.reshape(1, ROWS, width), tokens_grad.reshape(1, ROWS, width), *found)
 
 
 def solution(mesh):

time: 745 us -> 652 us (0.88)
  Pallas kernels: 593 us -> 558 us
  other arithmetic: 32.7 us -> 13.6 us
  local copies, waits for them, and re-layouts: 73.5 us -> 54.8 us
  matrix products: 31.4 us -> 15.4 us
    pallas_call x8, Pallas kernels: 463 us -> 401 us  [comm_call(): pl.pallas_call(kernel, out_shape=[jax.ShapeDtypeStruct(*o) for o in outs]...]
    reshape x42 -> x0, local copies, waits for them, and re-layouts: 26.8 us -> none  [the longest x4 5.84 us: unpack_units(): return split.transpose(1, 2, 0, 3, 4).reshape(rows, units)]
    pallas_call x0 -> x5, Pallas kernels: none -> 20 us  [the longest x2 11.1 us: project(): pl.pallas_call(functools.partial(project_kernel, layer), out_shape=[jax.S...]
    unnamed x278 -> x150, local copies, waits for them, and re-layouts: 25 us -> 43.3 us
    another operation x14 -> x0, other arithmetic: 15.1 us -> none
    pallas_call x2, Pallas kernels: 36.7 us -> 46.6 us  [attend_backward(): pl.pallas_call(attend_back_kernel, grid=(rows // step,), out_shape=[jax.S...]
    dot_general x8 -> x6, matrix products: 18 us -> 8.44 us  [left_product(): lax.dot_general(left, right, (((0,), (0,)), ((), ())), preferred_element_...]
    slice x15 -> x0, local copies, waits for them, and re-layouts: 8.6 us -> none  [the longest x2 1.98 us: fast_local(): qkv_w = [w[:, :384] for w in all_w]]
  transfers between devices with their start and end apart: 4 -> 0, of which waited for: 0 -> 0; matrix products, arithmetic and copies ran while one was open for 4% -> 0% of each run, Pallas kernels for 0% -> 0%
where the time goes in v4:
time: 652 us; the launch traced here: 644 us
  Pallas kernels  558 us (86%)
  local copies, waits for them, and re-layouts  54.8 us (8%)
  matrix products  15.4 us (2%)
  other arithmetic  13.6 us (2%)
    pallas_call x8, Pallas kernels, comm_call(): pl.pallas_call(kernel, out_shape=[jax.ShapeDtypeStruct(*o) for o in outs]...  401 us
    pallas_call x1, Pallas kernels, begin_call(): pl.pallas_call(begin_kernel, out_shape=[jax.ShapeDtypeStruct(s, BF) for s...  69.8 us
    pallas_call x2, Pallas kernels, attend_backward(): pl.pallas_call(attend_back_kernel, grid=(rows // step,), out_shape=[jax.S...  46.6 us
    unnamed x150, local copies, waits for them, and re-layouts  43.3 us
    pallas_call x2, Pallas kernels, attend_forward(): pl.pallas_call(attend_kernel, grid=(rows // step,), out_shape=[jax.ShapeD...  20.2 us

profile of v4, /device:TPU:0, one launch (start us, length us, event | category | flops | bytes accessed | tf_op | source)
XLA Modules:
  0.0 643.5 jit_solution(11754496172329800415)
XLA Ops:
  0.7 1.3 copy.115.refs_0_.refs_4_
  2.0 1.3 copy.116.refs_5_.refs_8_
  3.3 1.3 copy.117.refs_9_.refs_15_
  4.7 1.3 copy.118.refs_14_.refs_19_
  6.0 69.8 %begin.1 = (bf16[1024,1024]{1,0:T(8,128)(2,1)}, bf16[32,32,1152]{2,1,0:T(8,128)(2,1)}, bf16[32,32,1152]{2,1,0:T(8,128)(2,1)}, bf16[4,96,1024]{2,1,0:T(8,128)(2,1...) custom-call(bf16[128,1024]{1,0:T(8,128)(2,1)} %bitcast.61, ...), custom_call_target="tpu_custom_call" | custom-call | tf_op jit(solution)/shard_map/begin/pallas_call | solution.py:1083
  76.1 1.9 fusion.4
  81.9 1.6 copy-done.14
  83.5 5.7 project.2
  92.3 1.4 copy-done.65
  98.8 10.1 %attend_forward.2 = (bf16[1024,128]{1,0:T(8,128)(2,1)S(1)}, f32[1024,2]{1,0:T(8,128)S(1)}) custom-call(bf16[1024,128]{1,0:T(8,128)(2,1)S(1)} %copy-done.29, bf16[2048,128]{1,0:T(8,128)(2,1)S(1)} %copy-done.21, bf16[2048,128]{1,0:T(8,128)(2,1)S(1)} %copy-done.23, s32[1024,1]{1,0:T(8,128)S(1)} %copy-done.6, s32[1,2048]{1,0:T(1,128)S(1)} %bitcast.82), custom_call_target="tpu_custom_call" | custom-call | tf_op jit(solution)/shard_map/attend_forward/pallas_call | solution.py:1276
  109.7 52.8 %middle.2 = (f32[128,1024]{1,0:T(8,128)S(1)}, bf16[1024,1024]{1,0:T(8,128)(2,1)S(1)}) custom-call(bf16[1024,128]{1,0:T(8,128)(2,1)S(1)} %get-tuple-element.96.left_ref.att_ref, bf16[128,1024]{1,0:T(8,128)(2,1)S(1)} %bitcast.69, bf16[128,1024]{1,0:T(8,128)(2,1)S(1)} %bitcast.62, f32[1,1024]{1,0:T(1,128)S(1)} %get-tuple-element.168.gain_ref), custom_call_target="tpu_custom_call" | custom-call | tf_op jit(solution)/shard_map/middle/pallas_call | solution.py:880
  163.4 1.8 fusion.2
  165.2 1.7 multiply_convert_fusion.5.left_ref
  167.1 1.9 slice_convert_fusion
  169.0 1.2 copy.147
  173.6 48.6 %result.1 = (f32[128,1024]{1,0:T(8,128)S(1)}, bf16[1024,1024]{1,0:T(8,128)(2,1)S(1)}) custom-call(bf16[1024,384]{1,0:T(8,128)(2,1)S(1)} %copy-done.4, bf16[384,1024]{1,0:T(8,128)(2,1)S(1)} %bitcast.72, f32[128,1024]{1,0:T(8,128)S(1)} %copy-done.18, f32[1,1024]{1,0:T(1,128)S(1)} %get-tuple-element.167.gain_ref), custom_call_target="tpu_custom_call" | custom-call | tf_op jit(solution)/shard_map/result/pallas_call | solution.py:880
  222.3 2.6 copy-done.1
  224.9 5.4 project.3
  230.3 10.1 %attend_forward.3 = (bf16[1024,128]{1,0:T(8,128)(2,1)S(1)}, f32[1024,2]{1,0:T(8,128)S(1)}) custom-call(bf16[1024,128]{1,0:T(8,128)(2,1)S(1)} %get-tuple-element.104.q_ref, bf16[2048,128]{1,0:T(8,128)(2,1)S(1)} %get-tuple-element.105.k_ref, bf16[2048,128]{1,0:T(8,128)(2,1)S(1)} %get-tuple-element.106.v_ref, s32[1024,1]{1,0:T(8,128)S(1)} %copy-done.7, ...), custom_call_target="tpu_custom_call" | custom-call | tf_op jit(solution)/shard_map/attend_forward/pallas_call | solution.py:1276
  241.3 49.7 %middle.3 = (f32[128,1024]{1,0:T(8,128)S(1)}, bf16[1024,1024]{1,0:T(8,128)(2,1)S(1)}) custom-call(bf16[1024,128]{1,0:T(8,128)(2,1)S(1)} %get-tuple-element.107.left_ref.att_ref, bf16[128,1024]{1,0:T(8,128)(2,1)S(1)} %bitcast.71, f32[128,1024]{1,0:T(8,128)S(1)} %get-tuple-element.109.res_ref.hid_ref, f32[1,1024]{1,0:T(1,128)S(1)} %get-tuple-element.166.gain_ref), custom_call_target="tpu_custom_call" | custom-call | tf_op jit(solution)/shard_map/middle/pallas_call | solution.py:880
  291.0 1.8 fusion
  294.1 46.7 %turn.1 = (bf16[128,1024]{1,0:T(8,128)(2,1)S(1)}, bf16[1024,1024]{1,0:T(8,128)(2,1)S(1)}) custom-call(bf16[1024,384]{1,0:T(8,128)(2,1)S(1)} %multiply_convert_fusion.4.left_ref, bf16[384,1024]{1,0:T(8,128)(2,1)S(1)} %bitcast.74, f32[128,1024]{1,0:T(8,128)S(1)} %get-tuple-element.112.res_ref.hid_ref, bf16[128,1024]{1,0:T(8,128)(2,1)S(1)} %bitcast.66), custom_call_target="tpu_custom_call" | custom-call | tf_op jit(solution)/shard_map/turn/pallas_call | solution.py:880
  341.5 1.7 multiply_convert_fusion.3
  343.3 1.9 convolution_convert_fusion.1
  346.3 58.5 %middle_back.2 = (f32[128,1024]{1,0:T(8,128)S(1)}, bf16[1024,1024]{1,0:T(8,128)(2,1)S(1)}, bf16[8,32,768]{2,1,0:T(8,128)(2,1)S(1)}, f32[96,1024]{1,0:T(8,128)S(1)}) custom-call(bf16[1024,768]{1,0:T(8,128)(2,1)S(1)} %pad_maximum_fusion.left_ref, bf16[1024,1152]{1,0:T(8,128)(2,1)S(1)} %bitcast.57, bf16[128,1024]{1,0:T(8,128)(2,1)S(1)} %bitcast.67, ...), custom_call_target="tpu_custom_call" | custom-call | tf_op jit(solution)/shard_map/middle_back/pallas_call | solution.py:880
  404.8 1.3 copy-done.16
  408.4 1.8 copy.130
  410.3 1.4 copy.131.pk_ref
  411.6 23.3 %attend_backward.2 = (f32[1024,128]{1,0:T(8,128)}, f32[2048,128]{1,0:T(8,128)}, f32[2048,128]{1,0:T(8,128)}, bf16[128,1024]{1,0:T(8,128)(2,1)}) custom-call(bf16[1024,128]{1,0:T(8,128)(2,1)} %copy-done.31, bf16[2048,128]{1,0:T(8,128)(2,1)} %copy-done.24, bf16[2048,128]{1,0:T(8,128)(2,1)} %copy-done.25, bf16[1024,1024]{1,0:T(8,128)(2,1)} %copy-done.16, ...), custom_call_target="tpu_custom_call" | custom-call | tf_op jit(solution)/shard_map/attend_backward/pallas_call | solution.py:1342
  436.1 1.2 copy-done.37
  438.4 2.1 turn_back.2
  441.3 1.3 convolution_convert_fusion.4
  443.3 55.4 %layer_back.1 = (f32[128,1024]{1,0:T(8,128)S(1)}, bf16[1024,1024]{1,0:T(8,128)(2,1)S(1)}, bf16[8,32,384]{2,1,0:T(8,128)(2,1)S(1)}, f32[32,1024]{1,0:T(8,128)S(1)}) custom-call(bf16[1024,384]{1,0:T(8,128)(2,1)S(1)} %get-tuple-element.120.left_ref, bf16[1024,1152]{1,0:T(8,128)(2,1)S(1)} %bitcast.58, f32[128,1024]{1,0:T(8,128)S(1)} %copy-done.42, ...), custom_call_target="tpu_custom_call" | custom-call | tf_op jit(solution)/shard_map/layer_back/pallas_call | solution.py:880
  498.7 1.7 multiply_convert_fusion.1
  500.5 1.4 copy-done.68
  502.0 1.9 convolution_convert_fusion
  505.0 58.2 %middle_back.3 = (f32[128,1024]{1,0:T(8,128)S(1)}, bf16[1024,1024]{1,0:T(8,128)(2,1)S(1)}, bf16[8,32,768]{2,1,0:T(8,128)(2,1)S(1)}, f32[96,1024]{1,0:T(8,128)S(1)}) custom-call(bf16[1024,768]{1,0:T(8,128)(2,1)S(1)} %pad_maximum_fusion.1.left_ref, bf16[1024,1152]{1,0:T(8,128)(2,1)S(1)} %bitcast.52, f32[128,1024]{1,0:T(8,128)S(1)} %get-tuple-element.124.grad_ref, ...), custom_call_target="tpu_custom_call" | custom-call | tf_op jit(solution)/shard_map/middle_back/pallas_call | solution.py:880
  563.2 1.3 copy-done.15
  566.9 1.8 copy.134
  568.7 23.3 %attend_backward.3 = (f32[1024,128]{1,0:T(8,128)}, f32[2048,128]{1,0:T(8,128)}, f32[2048,128]{1,0:T(8,128)}, bf16[128,1024]{1,0:T(8,128)(2,1)}) custom-call(bf16[1024,128]{1,0:T(8,128)(2,1)} %copy-done.28, bf16[2048,128]{1,0:T(8,128)(2,1)} %copy-done.20, bf16[2048,128]{1,0:T(8,128)(2,1)} %copy-done.22, bf16[1024,1024]{1,0:T(8,128)(2,1)} %copy-done.15, ...), custom_call_target="tpu_custom_call" | custom-call | tf_op jit(solution)/shard_map/attend_backward/pallas_call | solution.py:1342
  595.5 2.6 turn_back.3
  598.1 1.3 convolution_convert_fusion.2
  599.4 31.2 %last_back.1 = (bf16[128,1024]{1,0:T(8,128)(2,1)S(1)}, bf16[8,32,384]{2,1,0:T(8,128)(2,1)S(1)}, f32[32,1024]{1,0:T(8,128)S(1)}) custom-call(bf16[1024,384]{1,0:T(8,128)(2,1)S(1)} %get-tuple-element.131.left_ref, bf16[1024,1152]{1,0:T(8,128)(2,1)S(1)} %bitcast.53, f32[128,1024]{1,0:T(8,128)S(1)} %copy-done.50, bf16[128,1024]{1,0:T(8,128)(2,1)S(1)} %bitcast.63, ...), custom_call_target="tpu_custom_call" | custom-call | tf_op jit(solution)/shard_map/last_back/pallas_call | solution.py:880
  631.9 4.4 unpack.1
  636.3 1.3 reduce
  637.6 1.3 reduce.1
  639.0 1.3 reduce.2
  640.3 1.3 reduce.3
  (159 shorter events, 37.1 us)
Async XLA Ops:
  0.7 75.2 %copy-start.72 = (s32[16]{0:T(128)S(1)}, s32[16]{0:T(128)}, u32[]{:S(2)}) copy-start(s32[16]{0:T(128)} %param.23) | copy-start | bytes 196
  76.1 18.6 %copy-start.71 = (s32[8,1,128]{2,1,0:T(1,128)}, s32[8,1,128]{2,1,0:T(1,128)S(1)}, u32[]{:S(2)}) copy-start(s32[8,1,128]{2,1,0:T(1,128)S(1)} %get-tuple-element.171) | copy-start | bytes 12292
  78.0 1.7 copy-start
  81.9 1.6 copy-start.14
  92.3 1.4 copy-start.65
  98.8 10.9 %copy-start.8 = (bf16[1,128,1024]{2,1,0:T(8,128)(2,1)S(1)}, bf16[1,128,1024]{2,1,0:T(8,128)(2,1)}, u32[]{:S(2)}) copy-start(bf16[1,128,1024]{2,1,0:T(8,128)(2,1)} %param.21) | copy-start | bytes 786436
  98.8 10.9 %copy-start.27 = (bf16[4,32,1024]{2,1,0:T(8,128)(2,1)S(1)}, bf16[4,32,1024]{2,1,0:T(8,128)(2,1)}, u32[]{:S(2)}) copy-start(bf16[4,32,1024]{2,1,0:T(8,128)(2,1)} %get-tuple-element.97) | copy-start | bytes 786436
  109.7 52.9 %copy-start.30 = (bf16[1024,128]{1,0:T(8,128)(2,1)}, bf16[1024,128]{1,0:T(8,128)(2,1)S(1)}, u32[]{:S(2)}) copy-start(bf16[1024,128]{1,0:T(8,128)(2,1)S(1)} %get-tuple-element.96.left_ref.att_ref) | copy-start | bytes 786436
  163.4 1.8 copy-start.67
  165.2 1.9 copy-start.69
  170.3 1.1 copy-start.4
  172.4 1.1 copy-start.38
  173.6 48.7 %copy-start.44 = (f32[1024,128]{1,0:T(8,128)S(1)}, f32[1024,128]{1,0:T(8,128)}, u32[]{:S(2)}) copy-start(f32[1024,128]{1,0:T(8,128)} %copy-done.43) | copy-start | bytes 1572868
  222.2 8.0 %copy-start.10 = (bf16[1024,1024]{1,0:T(8,128)(2,1)}, bf16[1024,1024]{1,0:T(8,128)(2,1)S(1)}, u32[]{:S(2)}) copy-start(bf16[1024,1024]{1,0:T(8,128)(2,1)S(1)} %get-tuple-element.102.refs_0_) | copy-start | bytes 6291460
  222.2 19.0 %copy-start.12 = (f32[128,1024]{1,0:T(8,128)}, f32[128,1024]{1,0:T(8,128)S(1)}, u32[]{:S(2)}) copy-start(f32[128,1024]{1,0:T(8,128)S(1)} %get-tuple-element.109.res_ref.hid_ref) | copy-start | bytes 1572868
  222.3 2.6 copy-start.1
  224.9 5.4 copy-start.7
  224.9 16.4 %copy-start.32 = (bf16[4,32,1024]{2,1,0:T(8,128)(2,1)S(1)}, bf16[4,32,1024]{2,1,0:T(8,128)(2,1)}, u32[]{:S(2)}) copy-start(bf16[4,32,1024]{2,1,0:T(8,128)(2,1)} %get-tuple-element.108) | copy-start | bytes 786436
  230.2 11.0 %copy-start.24 = (bf16[2048,128]{1,0:T(8,128)(2,1)}, bf16[2048,128]{1,0:T(8,128)(2,1)S(1)}, u32[]{:S(2)}) copy-start(bf16[2048,128]{1,0:T(8,128)(2,1)S(1)} %get-tuple-element.105.k_ref) | copy-start | bytes 1572868
  230.2 11.0 %copy-start.31 = (bf16[1024,128]{1,0:T(8,128)(2,1)}, bf16[1024,128]{1,0:T(8,128)(2,1)S(1)}, u32[]{:S(2)}) copy-start(bf16[1024,128]{1,0:T(8,128)(2,1)S(1)} %get-tuple-element.104.q_ref) | copy-start | bytes 786436
  230.3 60.7 %copy-start.25 = (bf16[2048,128]{1,0:T(8,128)(2,1)}, bf16[2048,128]{1,0:T(8,128)(2,1)S(1)}, u32[]{:S(2)}) copy-start(bf16[2048,128]{1,0:T(8,128)(2,1)S(1)} %get-tuple-element.106.v_ref) | copy-start | bytes 1572868
  230.3 60.7 %copy-start.2 = (bf16[32,32,1152]{2,1,0:T(8,128)(2,1)S(1)}, bf16[32,32,1152]{2,1,0:T(8,128)(2,1)}, u32[]{:S(2)}) copy-start(bf16[32,32,1152]{2,1,0:T(8,128)(2,1)} %get-tuple-element.101) | copy-start | bytes 7077892
  241.2 49.8 %copy-start.33 = (bf16[1024,128]{1,0:T(8,128)(2,1)}, bf16[1024,128]{1,0:T(8,128)(2,1)S(1)}, u32[]{:S(2)}) copy-start(bf16[1024,128]{1,0:T(8,128)(2,1)S(1)} %get-tuple-element.107.left_ref.att_ref) | copy-start | bytes 786436
  292.8 1.2 copy-start.40
  404.8 1.3 copy-start.16
  434.9 1.2 copy-start.36
  436.1 1.2 copy-start.37
  438.4 2.9 copy-start.11
  441.3 1.7 copy-start.3
  441.3 1.7 copy-start.13
  441.3 1.9 copy-start.42
  441.3 2.0 copy-start.58
  443.3 55.4 %copy-start.39 = (bf16[4,96,1024]{2,1,0:T(8,128)(2,1)S(1)}, bf16[4,96,1024]{2,1,0:T(8,128)(2,1)}, u32[]{:S(2)}) copy-start(bf16[4,96,1024]{2,1,0:T(8,128)(2,1)} %get-tuple-element.99) | copy-start | bytes 2359300
  443.3 55.4 %copy-start.70 = (f32[1024,768]{1,0:T(8,128)S(1)}, f32[1024,768]{1,0:T(8,128)}, u32[]{:S(2)}) copy-start(f32[1024,768]{1,0:T(8,128)} %copy-done.69) | copy-start | bytes 9437188
  498.7 1.7 copy-start.61
  498.7 1.7 copy-start.63
  500.4 1.6 copy-start.68
  502.0 1.9 copy-start.5
  503.9 1.0 copy-start.19
  563.2 1.3 copy-start.15
  568.7 23.3 %copy-start.48 = (f32[1024,128]{1,0:T(8,128)S(1)}, f32[1024,128]{1,0:T(8,128)}, u32[]{:S(2)}) copy-start(f32[1024,128]{1,0:T(8,128)} %copy-done.47) | copy-start | bytes 1572868
  592.0 1.2 copy-start.34
  593.2 1.2 copy-start.35
  595.5 2.6 copy-start.66
  598.1 1.3 copy-start.9
  598.1 1.3 copy-start.50
  598.1 1.3 copy-start.57
  631.9 9.7 %copy-start.60 = (bf16[128,1024]{1,0:T(8,128)(2,1)S(1)}, bf16[128,1024]{1,0:T(8,128)(2,1)}, u32[]{:S(2)}) copy-start(bf16[128,1024]{1,0:T(8,128)(2,1)} %copy-done.59) | copy-start | bytes 786436
  (25 other events, 21.2 us)

commit v5 on v4

--- a/solution.py
+++ b/solution.py
@@ -794,18 +794,18 @@
     def run(inner):
         parts = []
         more = None if extra is None else extra(place)
+        reduce = Reduce(place, inner, product, scratch[:8], scratch[8:14])
+        reduce.products()
         if more is not None:
             more.first()
             parts.append(more)
-        reduce = Reduce(place, inner, product, scratch[:8], scratch[8:14])
-        reduce.products()
         parts.append(reduce)
         if full is not None:
             gather = Gather(place, inner, full, scratch[14:19])
             parts.append(gather)
+        reduce.relays()
         if more is not None:
             more.second()
-        reduce.relays()
         for half in range(2):
             rows = settle(half, reduce.own_sum(half))
             if full is not None:
@@ -842,11 +842,11 @@
     return product
 
 
-def forward_kernel(left_ref, right_ref, res_ref, gain_ref, new_ref, full_ref, *scratch):
+def forward_kernel(row, left_ref, right_ref, res_ref, gain_ref, new_ref, full_ref, *scratch):
     def settle(half, total):
         hidden = res_ref[half_rows(half), :].astype(F32) + total
         new_ref[half_rows(half), :] = hidden
-        return (hidden * norm_rows(hidden) * gain_ref[...]).astype(BF)
+        return (hidden * norm_rows(hidden) * gain_ref[row : row + 1, :]).astype(BF)
 
     exchange(plane_place(), make_product(left_ref, right_ref, False), settle, full_ref, scratch)
 
@@ -903,12 +903,12 @@
 
 
 class Spread:
-    def __init__(self, place, tables, downs, outs, sems):
+    def __init__(self, place, table, down, out, sems):
         self.f, self.c, self.y, _ = place
         self.chip, self.core = self.c // 2, self.c % 2
         self.peers, self.sibling, self.twin = chip_peers(self.f, self.c)
         self.near = (self.f, flip(self.c, 2))
-        self.tables, self.downs, self.outs = tables, downs, outs
+        self.table, self.down, self.out = table, down, out
         self.ds, self.dr, self.xs, self.xr, self.ss, self.sr, self.ws, self.wr = sems
         self.home = self.y == self.f
         self.direct, self.crossed, self.inner, self.sent = {}, {}, [], []
@@ -919,38 +919,38 @@
         self.sent.append(copy)
         return copy
 
-    def to_twin(self, src, dst, l, n):
-        self.crossed[l, n] = self.send(src, dst, self.xs.at[l, n], self.xr.at[l, n], self.twin)
-
-    def to_sibling(self, src, dst, l, n):
-        self.inner.append(self.send(src, dst, self.ss.at[l, n], self.sr.at[l, n], self.sibling))
-
-    def out_copy(self, l):
-        op, out = self.outs[l]
+    def to_twin(self, src, dst, n):
+        self.crossed[n] = self.send(src, dst, self.xs.at[n], self.xr.at[n], self.twin)
+
+    def to_sibling(self, src, dst, n):
+        self.inner.append(self.send(src, dst, self.ss.at[n], self.sr.at[n], self.sibling))
+
+    def out_copy(self):
+        op, out = self.out
         part = 2 * self.y + self.core
-        return remote(op, out.at[part], self.ws.at[l], self.wr.at[l], self.near)
-
-    def pair_copies(self, l, s, r, first, target):
-        parts = [self.outs[l][1].at[self.core], self.outs[l][1].at[2 + self.core]]
-        return [remote(p, p, s.at[l, first + n], r.at[l, first + n], target) for n, p in enumerate(parts)]
-
-    def first(self, l):
-        a, r = self.tables[l]
-        down, down_all = self.downs[l]
-        op, out = self.outs[l]
+        return remote(op, out.at[part], self.ws, self.wr, self.near)
+
+    def pair_copies(self, s, r, first, target):
+        parts = [self.out[1].at[self.core], self.out[1].at[2 + self.core]]
+        return [remote(p, p, s.at[first + n], r.at[first + n], target) for n, p in enumerate(parts)]
+
+    def first(self):
+        a, r = self.table
+        down, down_all = self.down
+        op, out = self.out
         mine = self.f * 16 + self.c
         part = 2 * self.f + self.core
-        self.to_twin(a.at[self.chip], r.at[mine], l, 0)
+        self.to_twin(a.at[self.chip], r.at[mine], 0)
         for i in range(1, 8):
             t = (self.chip + i) % 8
-            self.direct[l, i] = self.send(
-                a.at[t], r.at[mine], self.ds.at[l, i], self.dr.at[l, i], self.peers[i - 1]
+            self.direct[i] = self.send(
+                a.at[t], r.at[mine], self.ds.at[i], self.dr.at[i], self.peers[i - 1]
             )
         r[mine] = a[self.chip]
-        self.to_sibling(a.at[self.chip], r.at[mine], l, 0)
+        self.to_sibling(a.at[self.chip], r.at[mine], 0)
         down_all[part] = down[...]
-        self.to_twin(down, down_all.at[part], l, 8)
-        self.to_sibling(down, down_all.at[part], l, 16)
+        self.to_twin(down, down_all.at[part], 8)
+        self.to_sibling(down, down_all.at[part], 16)
 
         @pl.when(self.home)
         def _():
@@ -958,67 +958,79 @@
 
         @pl.when(jnp.logical_not(self.home))
         def _():
-            self.out_copy(l).start()
-
-    def second(self, l):
-        r = self.tables[l][1]
+            self.out_copy().start()
+
+    def second(self):
+        r = self.table[1]
         for i in range(1, 8):
-            self.direct[l, i].wait_recv()
+            self.direct[i].wait_recv()
             source = self.f * 16 + 2 * ((self.chip + 8 - i) % 8) + self.core
-            self.to_twin(r.at[source], r.at[source], l, i)
-            self.to_sibling(r.at[source], r.at[source], l, i)
+            self.to_twin(r.at[source], r.at[source], i)
+            self.to_sibling(r.at[source], r.at[source], i)
 
         @pl.when(self.home)
         def _():
-            self.out_copy(l).wait_recv()
-            for copy in self.pair_copies(l, self.xs, self.xr, 9, self.twin):
+            self.out_copy().wait_recv()
+            for copy in self.pair_copies(self.xs, self.xr, 9, self.twin):
                 copy.start()
 
-    def third(self, l):
-        r = self.tables[l][1]
+    def third(self):
+        r = self.table[1]
 
         @pl.when(jnp.logical_not(self.home))
         def _():
-            for copy in self.pair_copies(l, self.xs, self.xr, 9, self.twin):
+            for copy in self.pair_copies(self.xs, self.xr, 9, self.twin):
                 copy.wait_recv()
 
-        for copy in self.pair_copies(l, self.ss, self.sr, 18, self.sibling):
+        for copy in self.pair_copies(self.ss, self.sr, 18, self.sibling):
             copy.start()
         for i in range(8):
-            self.crossed[l, i].wait_recv()
+            self.crossed[i].wait_recv()
             source = (1 - self.f) * 16 + 2 * ((self.chip + 8 - i) % 8) + self.core
-            self.to_sibling(r.at[source], r.at[source], l, 8 + i)
-        self.crossed[l, 8].wait_recv()
+            self.to_sibling(r.at[source], r.at[source], 8 + i)
+        self.crossed[8].wait_recv()
         part = 2 * (1 - self.f) + self.core
-        down_all = self.downs[l][1]
-        self.to_sibling(down_all.at[part], down_all.at[part], l, 17)
+        down_all = self.down[1]
+        self.to_sibling(down_all.at[part], down_all.at[part], 17)
 
     def finish(self):
         for copy in self.inner:
             copy.wait_recv()
         for copy in self.sent:
             copy.wait_send()
-        for l in range(len(self.tables)):
-            for copy in self.pair_copies(l, self.ss, self.sr, 18, self.sibling):
-                copy.wait()
-
-            @pl.when(self.home)
-            def _():
-                for copy in self.pair_copies(l, self.xs, self.xr, 9, self.twin):
-                    copy.wait_send()
-
-            @pl.when(jnp.logical_not(self.home))
-            def _():
-                self.out_copy(l).wait_send()
-
-
-def pack_shards(shards, block, a):
-    pre, query, keys, values, mid, gates, upproj = shards
+        for copy in self.pair_copies(self.ss, self.sr, 18, self.sibling):
+            copy.wait()
+
+        @pl.when(self.home)
+        def _():
+            for copy in self.pair_copies(self.xs, self.xr, 9, self.twin):
+                copy.wait_send()
+
+        @pl.when(jnp.logical_not(self.home))
+        def _():
+            self.out_copy().wait_send()
+
+
+def turn_row(row):
+    size = row.shape[1]
+    same = lax.broadcasted_iota(jnp.int32, (size, size), 0) == lax.broadcasted_iota(jnp.int32, (size, size), 1)
+    return jnp.sum(jnp.where(same, row, 0.0), axis=1, keepdims=True)
+
+
+def turn_column(column):
+    size = column.shape[0]
+    same = lax.broadcasted_iota(jnp.int32, (size, size), 0) == lax.broadcasted_iota(jnp.int32, (size, size), 1)
+    return jnp.sum(jnp.where(same, column, 0.0), axis=0, keepdims=True)
+
+
+def pack_shards(shards, block, a, dn):
+    pre, query, keys, values, _, mid, gates, upproj, down = shards
     rows, units = gates.shape
     each = units // 32
     lane = lax.broadcasted_iota(jnp.int32, (rows, block - each), 1)
     empty = jnp.zeros((rows, block - each), F32)
-    riders = jnp.where(lane == 0, pre[...].astype(F32), jnp.where(lane == 1, mid[...].astype(F32), empty))
+    pre, mid = turn_row(pre[...].astype(F32)), turn_row(mid[...].astype(F32))
+    riders = jnp.where(lane == 0, pre, jnp.where(lane == 1, mid, empty))
     for chip in range(8):
         pair = 4 * (chip % 2) + chip // 2
         for n, w in enumerate((query, keys, values)):
@@ -1031,68 +1043,87 @@
                 parts.append(riders if n == 0 and i == 0 else empty)
             first = 384 + 4 * block * n
             a[chip, :, first : first + 4 * block] = jnp.concatenate(parts, axis=-1).astype(BF)
+    dn[:each] = down[...]
+    dn[each:] = jnp.zeros((block - each, down.shape[1]), BF)
+
+
+def read_gains(r, each, gains):
+    count = r.shape[0] * r.shape[1]
+    columns = r[:, :, 384:512].reshape(count, 128)
+    row = lax.broadcasted_iota(jnp.int32, (8, 128), 0)
+    lane = lax.broadcasted_iota(jnp.int32, (8, 128), 1)
+    pick = jnp.where(lane == row + each, 1.0, 0.0).astype(BF)
+    gains[...] = lax.dot_general(pick, columns, NT, preferred_element_type=F32)
 
 
 def begin_kernel(tok, *refs):
-    ins, results, scratch = refs[:18], refs[18:25], refs[25:]
-    full, r1, r2, d1, d2, o1, o2 = results
-    a1, a2, dn, sems = scratch[0], scratch[1], scratch[2], scratch[3:]
-    block = dn.shape[1]
+    shards, (full, r, d, o, gains), (a, dn, *sems) = refs[:9], refs[9:14], refs[14:]
     place = plane_place()
     f, c, y, z = place
     peers, sibling, twin = chip_peers(f, c)
-    greet(peers + [sibling, twin])
     start = (z * 2 + y) * ROWS
     full[pl.ds(pl.multiple_of(start, ROWS), ROWS), :] = tok[...]
-    outs = []
-    for l, a in enumerate((a1, a2)):
-        pre, query, keys, values, out, mid, gates, upproj, down = ins[9 * l : 9 * l + 9]
-        outs.append(out)
-        pack_shards((pre, query, keys, values, mid, gates, upproj), block, a)
-        each = down.shape[0]
-        dn[l, :each] = down[...]
-        dn[l, each:] = jnp.zeros((block - each, down.shape[1]), BF)
+    pack_shards(shards, dn.shape[0], a, dn)
+    greet(peers + [sibling, twin])
 
     def run(inner):
         gather = Gather(place, inner, full, sems[:5])
-        spread = Spread(
-            place, ((a1, r1), (a2, r2)), ((dn.at[0], d1), (dn.at[1], d2)), ((outs[0], o1), (outs[1], o2)), sems[5:]
-        )
+        spread = Spread(place, (a, r), (dn, d), (shards[4], o), sems[5:])
         gather.send_own(0)
+        spread.first()
         gather.send_own(1)
-        spread.first(0)
-        spread.first(1)
         gather.forward(0)
-        spread.second(0)
+        spread.second()
         gather.forward(1)
-        spread.second(1)
-        spread.third(0)
-        spread.third(1)
+        spread.third()
         gather.finish()
         spread.finish()
 
     both_kinds(place, run)
+    read_gains(r, shards[8].shape[0], gains)
+
+
+def spread_shapes(rows, width, block):
+    wide = 384 + 8 * block
+    outs = [((32, rows, wide), BF), ((4, block, width), BF), ((4, rows, width), BF), ((8, 32 * rows), F32)]
+    scratch = [pltpu.VMEM((8, rows, wide), BF), pltpu.VMEM((block, width), BF)]
+    sems = [pltpu.SemaphoreType.DMA(n) for n in ((8,), (8,), (11,), (11,), (20,), (20,), (), ())]
+    return outs, scratch, sems
 
 
 def begin_call(tok, shards, block):
     rows, width = shards[1].shape
-    wide = 384 + 8 * block
+    outs, scratch, sems = spread_shapes(rows, width, block)
+    outs = [((8 * ROWS, width), BF)] + outs
     spec = pl.BlockSpec(memory_space=VMEM_SPACE)
-    shapes = [(8 * ROWS, width)] + [(32, rows, wide)] * 2 + [(4, block, width)] * 2 + [(4, rows, width)] * 2
-    counts = [(10,)] * 5 + [(2, 8), (2, 8), (2, 11), (2, 11), (2, 20), (2, 20), (2,), (2,)]
     return pl.pallas_call(
         begin_kernel,
-        out_shape=[jax.ShapeDtypeStruct(s, BF) for s in shapes],
-        in_specs=[spec] * 19,
-        out_specs=[spec] * 7,
-        scratch_shapes=[pltpu.VMEM((8, rows, wide), BF)] * 2
-        + [pltpu.VMEM((2, block, width), BF)]
-        + [pltpu.SemaphoreType.DMA(n) for n in counts],
+        out_shape=[jax.ShapeDtypeStruct(*o) for o in outs],
+        in_specs=[spec] * 10,
+        out_specs=[spec] * len(outs),
+        scratch_shapes=scratch + [pltpu.SemaphoreType.DMA((10,))] * 5 + sems,
         compiler_params=pltpu.CompilerParams(
             collective_id=9, has_side_effects=True, vmem_limit_bytes=60 * 1024 * 1024
         ),
         name="begin",
-    )(tok, *[s[:, None] if s.ndim == 1 else s for s in shards])
+    )(tok, *shards)
+
+
+def first_middle_kernel(left_ref, right_ref, res_ref, gain_ref, *refs):
+    shards, (new_ref, full_ref, r, d, o, gains), scratch = refs[:9], refs[9:15], refs[15:]
+    a, dn, *sems = scratch[19:]
+
+    def settle(half, total):
+        hidden = res_ref[half_rows(half), :].astype(F32) + total
+        new_ref[half_rows(half), :] = hidden
+        return (hidden * norm_rows(hidden) * gain_ref[1:2, :]).astype(BF)
+
+    def extra(place):
+        return Spread(place, (a, r), (dn, d), (shards[4], o), sems)
+
+    pack_shards(shards, dn.shape[0], a, dn)
+    exchange(plane_place(), make_product(left_ref, right_ref, False), settle, full_ref, scratch, extra)
+    read_gains(r, shards[8].shape[0], gains)
 
 
 class Collect:
@@ -1220,14 +1251,14 @@
     return results, scratch
 
 
-def back_kernel(gathers, lanes, left_ref, right_ref, grad_ref, hid_ref, gain_ref, g, gd, new_ref, *rest):
+def back_kernel(gathers, row, lanes, left_ref, right_ref, grad_ref, hid_ref, gain_ref, g, gd, new_ref, *rest):
     full_ref = rest[0] if gathers else None
     c, od = rest[gathers : gathers + 2]
     scratch = rest[gathers + 2 :]
 
     def settle(half, total):
         at = half_rows(half)
-        new = back_rows(total, grad_ref[at, :].astype(F32), hid_ref[at, :].astype(F32), gain_ref[...])
+        new = back_rows(total, grad_ref[at, :].astype(F32), hid_ref[at, :].astype(F32), gain_ref[row : row + 1, :])
         new_ref[at, :] = new.astype(new_ref.dtype)
         return new.astype(BF)
 
@@ -1252,224 +1283,227 @@
 TN = (((0,), (0,)), ((), ()))
 
 
-def attend_kernel(q_ref, k_ref, v_ref, pq_ref, pk_ref, att_ref, lse_ref):
-    allowed = pk_ref[...] <= pq_ref[...]
-    queries = q_ref[...]
-    parts = []
-    for head in range(2):
-        masked = jnp.where(head_lanes(head), queries, jnp.zeros_like(queries))
-        scores = lax.dot_general(masked, k_ref[...], NT, preferred_element_type=F32) * HD ** (-0.5)
-        scores = jnp.where(allowed, scores, NEG_FILL)
-        top = jnp.max(scores, axis=-1, keepdims=True)
-        shares = jnp.exp(scores - top)
-        total = jnp.sum(shares, axis=-1, keepdims=True)
-        lse_ref[:, head : head + 1] = top + jnp.log(total)
-        mixed = jnp.dot(shares.astype(BF), v_ref[...], preferred_element_type=F32)
-        parts.append(mixed / total)
-    att_ref[...] = jnp.where(head_lanes(0), parts[0], parts[1]).astype(BF)
-
-
-def attend_forward(q, k, v, pos_q, pos_k):
-    rows = q.shape[0]
-    keys = k.shape[0]
-    step = 128
-    return pl.pallas_call(
-        attend_kernel,
-        grid=(rows // step,),
-        out_shape=[
-            jax.ShapeDtypeStruct((rows, 128), BF),
-            jax.ShapeDtypeStruct((rows, 2), F32),
-        ],
-        in_specs=[
-            pl.BlockSpec((step, 128), lambda i: (i, 0)),
-            pl.BlockSpec((keys, 128), lambda i: (0, 0)),
-            pl.BlockSpec((keys, 128), lambda i: (0, 0)),
-            pl.BlockSpec((step, 1), lambda i: (i, 0)),
-            pl.BlockSpec((1, keys), lambda i: (0, 0)),
-        ],
-        out_specs=[
-            pl.BlockSpec((step, 128), lambda i: (i, 0)),
-            pl.BlockSpec((step, 2), lambda i: (i, 0)),
-        ],
-        compiler_params=pltpu.CompilerParams(vmem_limit_bytes=14 * 1024 * 1024),
-        name="attend_forward",
-    )(q, k, v, pos_q, pos_k)
-
-
-def attend_back_kernel(
-    q_ref, k_ref, v_ref, full_ref, out_ref, att_ref, lse_ref, pq_ref, pk_ref, dq_ref, dk_ref, dv_ref, dw_ref, acc_ref
-):
-    step_no = pl.program_id(0)
-
-    @pl.when(step_no == 0)
-    def _():
-        dk_ref[...] = jnp.zeros_like(dk_ref)
-        dv_ref[...] = jnp.zeros_like(dv_ref)
-        acc_ref[...] = jnp.zeros_like(acc_ref)
-
-    allowed = pk_ref[...] <= pq_ref[...]
-    queries = q_ref[...]
-    full = full_ref[...]
-    grads = lax.dot_general(full, out_ref[...], NT, preferred_element_type=F32).astype(BF)
-    acc_ref[...] += lax.dot_general(att_ref[...], full, TN, preferred_element_type=F32)
-    parts = []
-    for head in range(2):
-        masked = jnp.where(head_lanes(head), queries, jnp.zeros_like(queries))
-        grad_h = jnp.where(head_lanes(head), grads, jnp.zeros_like(grads))
-        scores = lax.dot_general(k_ref[...], masked, NT, preferred_element_type=F32) * HD ** (-0.5)
-        shares = jnp.where(allowed, jnp.exp(scores - lse_ref[head : head + 1, :]), 0.0)
-        grad_shares = lax.dot_general(v_ref[...], grad_h, NT, preferred_element_type=F32)
-        delta = jnp.sum(shares * grad_shares, axis=0, keepdims=True)
-        grad_scores = (shares * (grad_shares - delta) * HD ** (-0.5)).astype(BF)
-        dv_ref[...] += jnp.dot(shares.astype(BF), grad_h, preferred_element_type=F32)
-        dk_ref[...] += jnp.dot(grad_scores, masked, preferred_element_type=F32)
-        parts.append(lax.dot_general(grad_scores, k_ref[...], TN, preferred_element_type=F32))
-    dq_ref[...] = jnp.where(head_lanes(0), parts[0], parts[1])
-
-    @pl.when(step_no == pl.num_programs(0) - 1)
-    def _():
-        dw_ref[...] = acc_ref[...].astype(BF)
-
-
-def attend_backward(q, k, v, full, out_w, att, lse_rows, pos_q, pos_k):
-    rows = q.shape[0]
-    keys = k.shape[0]
-    width = full.shape[1]
-    step = 128
-    row_block = pl.BlockSpec((step, 128), lambda i: (i, 0))
-    key_block = pl.BlockSpec((keys, 128), lambda i: (0, 0))
-    weight_block = pl.BlockSpec((128, width), lambda i: (0, 0))
-    return pl.pallas_call(
-        attend_back_kernel,
-        grid=(rows // step,),
-        out_shape=[
-            jax.ShapeDtypeStruct((rows, 128), F32),
-            jax.ShapeDtypeStruct((keys, 128), F32),
-            jax.ShapeDtypeStruct((keys, 128), F32),
-            jax.ShapeDtypeStruct((128, width), BF),
-        ],
-        in_specs=[
-            row_block, key_block, key_block,
-            pl.BlockSpec((step, width), lambda i: (i, 0)),
-            weight_block, row_block,
-            pl.BlockSpec((2, step), lambda i: (0, i)),
-            pl.BlockSpec((1, step), lambda i: (0, i)),
-            pl.BlockSpec((keys, 1), lambda i: (0, 0)),
-        ],
-        out_specs=[row_block, key_block, key_block, weight_block],
-        scratch_shapes=[pltpu.VMEM((128, width), F32)],
-        compiler_params=pltpu.CompilerParams(vmem_limit_bytes=60 * 1024 * 1024),
-        name="attend_backward",
-    )(q, k, v, full, out_w, att, lse_rows, pos_q, pos_k)
-
-
-def project_kernel(layer, *refs):
-    x_ref, w_ref, cos_ref, sin_ref, more_ref = refs[:5]
-    q_ref, k_ref, v_ref, keep_ref = refs[5:9]
+def two_blocks(ref, tile, half):
+    first = pl.multiple_of(2 * tile * ROWS + half * HALF, HALF)
+    second = pl.multiple_of((2 * tile + 1) * ROWS + half * HALF, HALF)
+    return jnp.concatenate([ref[pl.ds(first, HALF), :], ref[pl.ds(second, HALF), :]], axis=0)
+
+
+def put_blocks(ref, tile, half, value):
+    first = pl.multiple_of(2 * tile * ROWS + half * HALF, HALF)
+    second = pl.multiple_of((2 * tile + 1) * ROWS + half * HALF, HALF)
+    ref[pl.ds(first, HALF), :] = value[:HALF]
+    ref[pl.ds(second, HALF), :] = value[HALF:]
+
+
+def attend_kernel(layer, *refs):
+    x_ref, w_ref, cos_ref, sin_ref, more_ref, pq_ref, pk_ref = refs[:7]
+    q_ref, k_ref, v_ref, att_ref, lse_ref = refs[7:12]
     ss, sr = refs[-2:]
     f, c, _, _ = plane_place()
     sibling = (f, flip(c, 1))
     greet([sibling])
     rows_n = x_ref.shape[0]
+    half_n = rows_n // 2
 
     def copies(i):
-        here = pl.ds(pl.multiple_of(i * ROWS, ROWS), ROWS)
-        there = pl.ds(pl.multiple_of(rows_n + i * ROWS, ROWS), ROWS)
+        here = pl.ds(pl.multiple_of(i * HALF, HALF), HALF)
+        there = pl.ds(pl.multiple_of(half_n + i * HALF, HALF), HALF)
         return [
-            remote(ref.at[here], ref.at[there], ss.at[2 * i + n], sr.at[2 * i + n], sibling)
-            for n, ref in enumerate((k_ref, v_ref))
+            remote(ref.at[h, here], ref.at[h, there], ss.at[4 * i + n], sr.at[4 * i + n], sibling)
+            for n, (ref, h) in enumerate(((k_ref, 0), (k_ref, 1), (v_ref, 0), (v_ref, 1)))
         ]
 
     def step(i, carry):
         at = pl.ds(pl.multiple_of(i * ROWS, ROWS), ROWS)
+        here = pl.ds(pl.multiple_of(i * HALF, HALF), HALF)
         rows = x_ref[at, :]
         if layer == 0:
             wide = rows.astype(F32)
-            rows = (wide * norm_rows(wide) * more_ref[...]).astype(BF)
-            keep_ref[at, :] = rows
+            rows = (wide * norm_rows(wide) * more_ref[:1, :]).astype(BF)
+            refs[12][at, :] = rows
         raw = jnp.dot(rows, w_ref[:, :384], preferred_element_type=F32)
         cosine, sine = cos_ref[at, :], sin_ref[at, :]
         q, k, v = raw[:, :128], raw[:, 128:256], raw[:, 256:]
         q_ref[at, :] = (q * cosine + swap_halves(q) * sine).astype(BF)
-        k_ref[at, :] = (k * cosine + swap_halves(k) * sine).astype(BF)
+        k = (k * cosine + swap_halves(k) * sine).astype(BF)
         if layer == 0:
-            refs[9][at, :] = v
+            refs[13][at, :] = v
         else:
             v = 0.5 * v + 0.5 * more_ref[at, :]
-        v_ref[at, :] = v.astype(BF)
+        v = v.astype(BF)
+        for half in range(2):
+            k_ref[half, here, :] = k[half * HALF : (half + 1) * HALF]
+            v_ref[half, here, :] = v[half * HALF : (half + 1) * HALF]
         for copy in copies(i):
             copy.start()
         return carry
 
     lax.fori_loop(0, rows_n // ROWS, step, 0)
-    if layer == 1:
-        keep_ref[...] = jnp.zeros_like(keep_ref)
     for i in range(rows_n // ROWS):
         for copy in copies(i):
             copy.wait()
 
-
-def project(layer, x, w, cosine, sine, more):
+    def tile_step(tile, carry):
+        for late in range(2):
+            number = tile + late * (rows_n // (2 * ROWS))
+            queries = two_blocks(q_ref, tile, late) * jnp.asarray(HD ** (-0.5), BF)
+            allowed = pk_ref[late : late + 1, :] <= turn_row(pq_ref[pl.ds(number, 1), :])
+            parts = []
+            for head in range(2):
+                masked = jnp.where(head_lanes(head), queries, jnp.zeros_like(queries))
+                scores = lax.dot_general(masked, k_ref[late], NT, preferred_element_type=F32)
+                scores = jnp.where(allowed, scores, NEG_FILL)
+                top = jnp.max(scores, axis=-1, keepdims=True)
+                if late:
+                    early = lax.dot_general(masked, k_ref[0], NT, preferred_element_type=F32)
+                    top = jnp.maximum(top, jnp.max(early, axis=-1, keepdims=True))
+                shares = jnp.exp(scores - top)
+                total = jnp.sum(shares, axis=-1, keepdims=True)
+                mixed = jnp.dot(shares.astype(BF), v_ref[late], preferred_element_type=F32)
+                if late:
+                    shares = jnp.exp(early - top)
+                    total += jnp.sum(shares, axis=-1, keepdims=True)
+                    mixed += jnp.dot(shares.astype(BF), v_ref[0], preferred_element_type=F32)
+                lse_ref[number, head : head + 1, :] = turn_column(top + jnp.log(total))
+                parts.append(mixed / total)
+            put_blocks(att_ref, tile, late, jnp.where(head_lanes(0), parts[0], parts[1]).astype(BF))
+        return carry
+
+    lax.fori_loop(0, rows_n // (2 * ROWS), tile_step, 0)
+
+
+def attend(layer, x, w, cosine, sine, more, pos_q, pos_k):
     rows_n = x.shape[0]
     spec = pl.BlockSpec(memory_space=VMEM_SPACE)
-    outs = [((rows_n, 128), BF), ((2 * rows_n, 128), BF), ((2 * rows_n, 128), BF)]
-    outs += [(x.shape, BF), ((rows_n, 128), F32)] if layer == 0 else [((8, 128), F32)]
-    count = 2 * (rows_n // ROWS)
+    outs = [((rows_n, 128), BF), ((2, rows_n, 128), BF), ((2, rows_n, 128), BF), ((rows_n, 128), BF)]
+    outs += [((rows_n // ROWS, 2, ROWS), F32)]
+    if layer == 0:
+        outs += [(x.shape, BF), ((rows_n, 128), F32)]
+    count = 4 * (rows_n // ROWS)
     return pl.pallas_call(
-        functools.partial(project_kernel, layer),
+        functools.partial(attend_kernel, layer),
         out_shape=[jax.ShapeDtypeStruct(*o) for o in outs],
-        in_specs=[spec] * 5,
+        in_specs=[spec] * 7,
         out_specs=[spec] * len(outs),
         scratch_shapes=[pltpu.SemaphoreType.DMA((count,))] * 2,
         compiler_params=pltpu.CompilerParams(
-            collective_id=10 + layer, has_side_effects=True, vmem_limit_bytes=8 * 1024 * 1024
+            collective_id=10 + layer, has_side_effects=True, vmem_limit_bytes=16 * 1024 * 1024
         ),
-        name="project",
-    )(x, w, cosine, sine, more)
-
-
-def turn_back_kernel(layer, dq_ref, dk_ref, dv_ref, cos_ref, sin_ref, more_ref, three_ref, pass_ref, sb, rb, ss, sr):
+        name="attend",
+    )(x, w, cosine, sine, more, pos_q, pos_k)
+
+
+def attend_back_kernel(layer, *refs):
+    q_ref, k_ref, v_ref, full_ref, out_ref, att_ref, lse_ref, pq_ref, pk_ref, cos_ref, sin_ref, more_ref = refs[:12]
+    three_ref, dw_ref = refs[12:14]
+    pkc, dq, dk, dv, dw, sb, rb, ss, sr = refs[-9:]
     f, c, _, _ = plane_place()
     sibling = (f, flip(c, 1))
     greet([sibling])
-    rows_n = dq_ref.shape[0]
+    rows_n = q_ref.shape[0]
+    half_n = rows_n // 2
+    dk[...] = jnp.zeros_like(dk)
+    dv[...] = jnp.zeros_like(dv)
+    dw[...] = jnp.zeros_like(dw)
+    for late in range(2):
+        for i in range(rows_n // ROWS):
+            at = slice(i * ROWS, (i + 1) * ROWS)
+            pkc[late, at, :] = turn_row(pk_ref[late : late + 1, at])
+
+    def tile_step(tile, carry):
+        for late in range(2):
+            number = tile + late * (rows_n // (2 * ROWS))
+            queries = two_blocks(q_ref, tile, late) * jnp.asarray(HD ** (-0.5), BF)
+            full = two_blocks(full_ref, tile, late)
+            grads = lax.dot_general(full, out_ref[...], NT, preferred_element_type=F32).astype(BF)
+            dw[...] += lax.dot_general(two_blocks(att_ref, tile, late), full, TN, preferred_element_type=F32)
+            allowed = pkc[late] <= pq_ref[pl.ds(number, 1), :]
+            parts = []
+            for head in range(2):
+                masked = jnp.where(head_lanes(head), queries, jnp.zeros_like(queries))
+                grad_h = jnp.where(head_lanes(head), grads, jnp.zeros_like(grads))
+                lse = lse_ref[number, head : head + 1, :]
+                kinds = (1, 0) if late else (0,)
+                shares, grad_shares = [], []
+                delta = jnp.zeros((1, ROWS), F32)
+                for kind in kinds:
+                    part = jnp.exp(lax.dot_general(k_ref[kind], masked, NT, preferred_element_type=F32) - lse)
+                    if kind == late:
+                        part = jnp.where(allowed, part, 0.0)
+                    grad = lax.dot_general(v_ref[kind], grad_h, NT, preferred_element_type=F32)
+                    delta += jnp.sum(part * grad, axis=0, keepdims=True)
+                    shares.append(part)
+                    grad_shares.append(grad)
+                found = jnp.zeros((ROWS, 128), F32)
+                for kind, part, grad in zip(kinds, shares, grad_shares):
+                    grad_scores = (part * (grad - delta)).astype(BF)
+                    dv[kind] += jnp.dot(part.astype(BF), grad_h, preferred_element_type=F32)
+                    dk[kind] += jnp.dot(grad_scores, masked, preferred_element_type=F32)
+                    found += lax.dot_general(grad_scores, k_ref[kind], TN, preferred_element_type=F32)
+                parts.append(found)
+            put_blocks(dq, tile, late, jnp.where(head_lanes(0), parts[0], parts[1]) * HD ** (-0.5))
+        return carry
+
+    lax.fori_loop(0, rows_n // (2 * ROWS), tile_step, 0)
     copies = []
-    for n, ref in enumerate((dk_ref, dv_ref)):
-        sb[n] = ref[rows_n:, :].astype(BF)
+    for n, ref in enumerate((dk, dv)):
+        sb[n] = ref[:, half_n:, :].astype(BF)
         copies.append(remote(sb.at[n], rb.at[n], ss.at[n], sr.at[n], sibling))
         copies[n].start()
-    cosine, sine = cos_ref[...], sin_ref[...]
-    dq = dq_ref[...]
-    three_ref[:, :128] = (dq * cosine - swap_halves(dq) * sine).astype(BF)
-    copies[0].wait()
-    dk = dk_ref[:rows_n, :] + rb[0].astype(F32)
-    three_ref[:, 128:256] = (dk * cosine - swap_halves(dk) * sine).astype(BF)
-    copies[1].wait()
-    dv = dv_ref[:rows_n, :] + rb[1].astype(F32)
+    dw_ref[...] = dw[...].astype(BF)
+    for copy in copies:
+        copy.wait()
+
+    def rows_of(n, ref, i):
+        here = pl.ds(pl.multiple_of(i * HALF, HALF), HALF)
+        return jnp.concatenate([ref[half, here, :] + rb[n, half, here, :].astype(F32) for half in range(2)], axis=0)
+
+    def turn(i, carry):
+        at = pl.ds(pl.multiple_of(i * ROWS, ROWS), ROWS)
+        cosine, sine = cos_ref[at, :], sin_ref[at, :]
+        for n, grad in enumerate((dq[at, :], rows_of(0, dk, i))):
+            three_ref[at, 128 * n : 128 * n + 128] = (grad * cosine - swap_halves(grad) * sine).astype(BF)
+        grad = rows_of(1, dv, i)
+        if layer == 1:
+            grad = 0.5 * grad
+            refs[14][at, :] = grad
+        else:
+            grad = grad + more_ref[at, :]
+        three_ref[at, 256:] = grad.astype(BF)
+        return carry
+
+    lax.fori_loop(0, rows_n // ROWS, turn, 0)
+
+
+def attend_backward(layer, q, k, v, full, out_w, att, lse, pos_q, pos_k, cosine, sine, more):
+    rows_n = q.shape[0]
+    width = full.shape[1]
+    spec = pl.BlockSpec(memory_space=VMEM_SPACE)
+    outs = [((rows_n, 384), BF), ((128, width), BF)]
     if layer == 1:
-        dv = 0.5 * dv
-        pass_ref[...] = dv
-    else:
-        dv = dv + more_ref[...]
-        pass_ref[...] = jnp.zeros_like(pass_ref)
-    three_ref[:, 256:] = dv.astype(BF)
-
-
-def turn_back(layer, dq, dk, dv, cosine, sine, more):
-    rows_n = dq.shape[0]
-    spec = pl.BlockSpec(memory_space=VMEM_SPACE)
-    outs = [((rows_n, 384), BF), ((rows_n if layer == 1 else 8, 128), F32)]
+        outs += [((rows_n, 128), F32)]
     return pl.pallas_call(
-        functools.partial(turn_back_kernel, layer),
+        functools.partial(attend_back_kernel, layer),
         out_shape=[jax.ShapeDtypeStruct(*o) for o in outs],
-        in_specs=[spec] * 6,
-        out_specs=[spec] * 2,
-        scratch_shapes=[pltpu.VMEM((2, rows_n, 128), BF)] * 2 + [pltpu.SemaphoreType.DMA((2,))] * 2,
+        in_specs=[spec] * 12,
+        out_specs=[spec] * len(outs),
+        scratch_shapes=[
+            pltpu.VMEM((2, rows_n, 1), F32),
+            pltpu.VMEM((rows_n, 128), F32),
+            pltpu.VMEM((2, rows_n, 128), F32),
+            pltpu.VMEM((2, rows_n, 128), F32),
+            pltpu.VMEM((128, width), F32),
+            pltpu.VMEM((2, 2, rows_n // 2, 128), BF),
+            pltpu.VMEM((2, 2, rows_n // 2, 128), BF),
+            pltpu.SemaphoreType.DMA((2,)),
+            pltpu.SemaphoreType.DMA((2,)),
+        ],
         compiler_params=pltpu.CompilerParams(
-            collective_id=12 + layer, has_side_effects=True, vmem_limit_bytes=8 * 1024 * 1024
+            collective_id=12 + layer, has_side_effects=True, vmem_limit_bytes=24 * 1024 * 1024
         ),
-        name="turn_back",
-    )(dq, dk, dv, cosine, sine, more)
+        name="attend_back",
+    )(q, k, v, full, out_w, att, lse, pos_q, pos_k, cosine, sine, more)
 
 
 def unpack_kernel(*refs):
@@ -1487,7 +1521,7 @@
                 part = cq[chip, :, 128 * n : 128 * n + 128].astype(F32)
                 g[:, at] = part
                 total += jnp.sum(part * w[:, at].astype(F32), axis=-1, keepdims=True)
-        g_pre[...] = total / pre[...].astype(F32)
+        g_pre[...] = turn_column(total) / pre[...].astype(F32)
         for n, g in enumerate((gg, gu)):
             for chip in range(8):
                 wide = cu[chip, :, 4 * block * n : 4 * block * (n + 1)].astype(F32)
@@ -1495,7 +1529,7 @@
                     owner = 16 * (i // 2) + 2 * chip + i % 2
                     g[:, each * owner : each * owner + each] = wide[:, block * i : block * i + each]
         both = gg[...] * gates[...].astype(F32) + gu[...] * upproj[...].astype(F32)
-        g_mid[...] = jnp.sum(both, axis=-1, keepdims=True) / mid[...].astype(F32)
+        g_mid[...] = turn_column(jnp.sum(both, axis=-1, keepdims=True)) / mid[...].astype(F32)
         g_out[...] = oo[...]
         g_down[...] = od[: g_down.shape[0], :]
 
@@ -1504,9 +1538,9 @@
     args, outs = [], []
     for l, layer in enumerate(layers):
         pre, query, keys, values, out, mid, gates, upproj, down = layer
-        args += [*collected[l], pre[:, None], query, keys, values, mid[:, None], gates, upproj]
+        args += [*collected[l], pre, query, keys, values, mid, gates, upproj]
         for w in layer:
-            outs.append(w.shape + (1,) if w.ndim == 1 else w.shape)
+            outs.append(w.shape)
     spec = pl.BlockSpec(memory_space=VMEM_SPACE)
     found = pl.pallas_call(
         unpack_kernel,
@@ -1516,7 +1550,7 @@
         compiler_params=pltpu.CompilerParams(vmem_limit_bytes=60 * 1024 * 1024),
         name="unpack",
     )(*args)
-    return [g[:, 0] if g.shape[-1] == 1 else g for g in found]
+    return [g[0] if g.shape[0] == 1 else g for g in found]
 
 
 def fast_local(tokens, cotangent, pair_of, *shards):
@@ -1530,23 +1564,25 @@
     pos_all = storage_positions(pair_of, ROWS).reshape(8, 2, ROWS)
     own_pos = lax.dynamic_index_in_dim(pos_all, core, 1, False).reshape(-1)
     sib_pos = lax.dynamic_index_in_dim(pos_all, 1 - core, 1, False).reshape(-1)
-    key_pos = jnp.concatenate([own_pos, sib_pos])
+    own_split = own_pos.reshape(8, 2, HALF).transpose(1, 0, 2)
+    sib_split = sib_pos.reshape(8, 2, HALF).transpose(1, 0, 2)
+    pos_q = own_split.reshape(8, ROWS).astype(F32)
+    pos_k = jnp.concatenate([own_split, sib_split], axis=1).reshape(2, -1).astype(F32)
     cosine, sine = rope_tables(own_pos, HD)
     cosine = jnp.concatenate([cosine] * 4, axis=-1)
     sine = jnp.concatenate([-sine, sine, -sine, sine], axis=-1)
 
+    shards = [s[None, :] if s.ndim == 1 else s for s in shards]
     layers = [shards[:9], shards[9:]]
     tok = tokens.reshape(ROWS, width)
     cot = cotangent.reshape(ROWS, width)
-    full, *spread = begin_call(tok, shards, block)
-    all_w = [w.reshape(32 * rows_each, wide) for w in spread[:2]]
-    up_w = [w[:, 384:] for w in all_w]
-    down_w = [w.reshape(hidden_pad, width) for w in spread[2:4]]
-    out_w = [w.reshape(4 * rows_each, width) for w in spread[4:]]
-    gains = []
-    for w in all_w:
-        columns = w[:, 384 + each : 384 + each + 2].astype(F32).T
-        gains += [columns[:1], columns[1:]]
+
+    def weights(spread):
+        columns = spread[0].reshape(32 * rows_each, wide)
+        return columns, spread[1].reshape(hidden_pad, width), spread[2].reshape(4 * rows_each, width), spread[3]
+
+    full, *spread = begin_call(tok, layers[0], block)
+    ready = [weights(spread), None]
 
     plane = 8 * ROWS
     full_type = ((plane, width), BF)
@@ -1554,40 +1590,46 @@
     saved = []
     hidden = tok
     first_values = None
-    pos_q = own_pos[:, None]
-    pos_k = key_pos[None, :]
     for layer in range(2):
+        all_w, down_w, out_w, gains = ready[layer]
+        more = gains if layer == 0 else first_values
+        q, k, v, att, lse, *kept = attend(layer, full, all_w, cosine, sine, more, pos_q, pos_k)
+        x_full = full
         if layer == 0:
-            q, k, v, x_full, first_values = project(0, full, all_w[0], cosine, sine, gains[0])
+            x_full, first_values = kept
+        args = (att, out_w, hidden, gains)
+        if layer == 0:
+            outs, packs, sems = spread_shapes(rows_each, width, block)
+            middle, mlp_full, *spread = comm_call(
+                first_middle_kernel, [rows_type, full_type] + outs, 1, args + tuple(layers[1]), True, "middle", packs + sems
+            )
+            ready[1] = weights(spread)
         else:
-            x_full = full
-            q, k, v, _ = project(1, full, all_w[1], cosine, sine, first_values)
-        att, lse = attend_forward(q, k, v, pos_q, pos_k)
-        middle, mlp_full = comm_call(
-            forward_kernel, [rows_type, full_type], 1 + layer,
-            (att, out_w[layer], hidden, gains[2 * layer + 1]), True, "middle",
-        )
-        both = jnp.dot(mlp_full, up_w[layer], preferred_element_type=F32)
+            middle, mlp_full = comm_call(
+                functools.partial(forward_kernel, 1), [rows_type, full_type], 2, args, True, "middle"
+            )
+        both = jnp.dot(mlp_full, all_w[:, 384:], preferred_element_type=F32)
         gate, up = both[:, :hidden_pad], both[:, hidden_pad:]
         inner = (jax.nn.silu(gate) * up).astype(BF)
         saved.append((x_full, q, k, v, lse, att, mlp_full, gate, up, inner, hidden, middle))
         if layer == 0:
             hidden, full = comm_call(
-                forward_kernel, [rows_type, full_type], 3,
-                (inner, down_w[layer], middle, gains[2]), True, "result",
+                functools.partial(forward_kernel, 0), [rows_type, full_type], 3,
+                (inner, down_w, middle, ready[1][3]), True, "result",
             )
         else:
             output, full = comm_call(
                 turn_kernel, [((ROWS, width), BF), full_type], 4,
-                (inner, down_w[layer], middle, cot), True, "turn",
+                (inner, down_w, middle, cot), True, "turn",
             )
     grad = cot
     passed = cosine
     collected = [None, None]
     for layer in (1, 0):
         x_full, q, k, v, lse, att, mlp_full, gate, up, inner, hidden, middle = saved[layer]
+        all_w, down_w, out_w, gains = ready[layer]
         grad_down = left_product(inner, full)
-        grad_inner = right_product(full, down_w[layer])
+        grad_inner = right_product(full, down_w)
         sigma = jax.nn.sigmoid(gate)
         grad_gate = (grad_inner * up * sigma * (1.0 + gate * (1.0 - sigma))).astype(BF)
         grad_up = (grad_inner * gate * sigma).astype(BF)
@@ -1595,31 +1637,34 @@
         grad_upw = left_product(mlp_full, both)
         results, more = collect_shapes(rows_each, 2 * hidden_pad, block, width, False)
         grad_mid, full, *got_up = comm_call(
-            functools.partial(back_kernel, 1, (384, wide)), [rows_type, full_type] + results, 5 + layer,
+            functools.partial(back_kernel, 1, 1, (384, wide)), [rows_type, full_type] + results, 5 + layer,
             (
-                both, all_w[layer], grad, middle, gains[2 * layer + 1],
+                both, all_w, grad, middle, gains,
                 grad_upw.astype(BF).reshape(16, 2, rows_each, 2 * hidden_pad),
                 grad_down.astype(BF).reshape(2, 2, block, width),
             ),
             True, "middle_back", more,
         )
-        dq, dk, dv, grad_out = attend_backward(q, k, v, full, out_w[layer], att, lse.T, own_pos[None, :], key_pos[:, None])
-        three, passed = turn_back(layer, dq, dk, dv, cosine, sine, passed)
+        three, grad_out, *kept = attend_backward(
+            layer, q, k, v, full, out_w, att, lse, pos_q, pos_k, cosine, sine, passed
+        )
+        if layer == 1:
+            (passed,) = kept
         grad_qkv = left_product(x_full, three)
         results, more = collect_shapes(rows_each, 384, rows_each, width, True)
         args = (
-            three, all_w[layer], grad_mid, hidden, gains[2 * layer],
+            three, all_w, grad_mid, hidden, gains,
             grad_qkv.astype(BF).reshape(16, 2, rows_each, 384),
             grad_out.reshape(2, 2, rows_each, width),
         )
         if layer == 1:
             grad, full, *got_qkv = comm_call(
-                functools.partial(back_kernel, 1, (0, 384)), [rows_type, full_type] + results, 7, args, True,
+                functools.partial(back_kernel, 1, 0, (0, 384)), [rows_type, full_type] + results, 7, args, True,
                 "layer_back", more,
             )
         else:
             tokens_grad, *got_qkv = comm_call(
-                functools.partial(back_kernel, 0, (0, 384)), [((ROWS, width), BF)] + results, 8, args, False,
+                functools.partial(back_kernel, 0, 0, (0, 384)), [((ROWS, width), BF)] + results, 8, args, False,
                 "last_back", more,
             )
         collected[layer] = got_up + got_qkv

time: 652 us -> 570 us (0.87)
  local copies, waits for them, and re-layouts: 54.8 us -> 8.33 us
  Pallas kernels: 558 us -> 532 us
  other arithmetic: 13.6 us -> 4.75 us
    pallas_call x9 -> x5, Pallas kernels: 152 us -> 114 us  [the longest x1 50.9 us: begin_call(): pl.pallas_call(begin_kernel, out_shape=[jax.ShapeDtypeStruct(*o) for o in...]
    unnamed x150 -> x54, local copies, waits for them, and re-layouts: 43.3 us -> 8.03 us
    pallas_call x8, Pallas kernels: 401 us -> 414 us  [comm_call(): pl.pallas_call(kernel, out_shape=[jax.ShapeDtypeStruct(*o) for o in outs]...]
    broadcast_in_dim x5 -> x0, local copies, waits for them, and re-layouts: 6.72 us -> none  [the longest x4 5.36 us: begin_call(): s[:, None]]
where the time goes in v5:
time: 570 us; the launch traced here: 562 us
  Pallas kernels  532 us (93%)
  matrix products  15.3 us (3%)
  local copies, waits for them, and re-layouts  8.33 us (1%)
    pallas_call x8, Pallas kernels, comm_call(): pl.pallas_call(kernel, out_shape=[jax.ShapeDtypeStruct(*o) for o in outs]...  414 us
    pallas_call x1, Pallas kernels, begin_call(): pl.pallas_call(begin_kernel, out_shape=[jax.ShapeDtypeStruct(*o) for o in...  50.9 us
    pallas_call x2, Pallas kernels, attend_backward(): pl.pallas_call(functools.partial(attend_back_kernel, layer), out_shape=[j...  35.7 us
    pallas_call x2, Pallas kernels, attend(): pl.pallas_call(functools.partial(attend_kernel, layer), out_shape=[jax.Sh...  26.9 us

profile of v5, /device:TPU:0, one launch (start us, length us, event | category | flops | bytes accessed | tf_op | source)
XLA Modules:
  0.0 562.2 jit_solution(8478544496728716637)
XLA Ops:
  0.7 0.8 select_reduce_fusion
  1.5 0.1 reshape_reshape.7
  1.6 0.1 reshape_reshape.6
  1.7 0.1 convert_element_type.61.refs_6_.refs_8_
  1.8 0.1 convert_element_type.59.refs_5_.refs_7_
  1.9 1.9 fusion.4
  3.8 0.9 pad_maximum_fusion.2
  4.7 50.9 %begin.1 = (bf16[1024,1024]{1,0:T(8,128)(2,1)}, bf16[32,32,1152]{2,1,0:T(8,128)(2,1)}, bf16[4,96,1024]{2,1,0:T(8,128)(2,1)}, bf16[4,32,1024]{2,1,0:T(8,128)(2,1)}, f32[8,1024]{1,0:T(8,128)}) custom-call(bf16[128,1024]{1,0:T(8,128)(2,1)} %bitcast.60, bf16[1,32]{1,0:T(2,128)(2,1)} %bitcast.87, bf16[32,1024]{1,0:T(8,128)(2,1)} %refs_5_.1, ...), custom_call_target="tpu_custom_call" | custom-call | tf_op jit(solution)/shard_map/begin/pallas_call | solution.py:1099
  55.6 1.7 copy-done
  57.3 1.6 copy-done.3
  58.9 0.8 copy-done.9
  59.7 0.0 copy-start.16
  59.7 0.0 copy-start.17
  59.7 0.0 copy-start.24
  59.7 0.0 copy-start.25
  59.7 13.9 %attend.2 = (bf16[1024,128]{1,0:T(8,128)(2,1)S(1)}, bf16[2,1024,128]{2,1,0:T(8,128)(2,1)S(1)}, bf16[2,1024,128]{2,1,0:T(8,128)(2,1)S(1)}, bf16[1024,128]{1,0:T(8...) custom-call(bf16[1024,1024]{1,0:T(8,128)(2,1)S(1)} %copy-done.3, ...), custom_call_target="tpu_custom_call" | custom-call | tf_op jit(solution)/shard_map/attend/pallas_call | solution.py:1384
  73.8 67.4 %middle.2 = (f32[128,1024]{1,0:T(8,128)S(1)}, bf16[1024,1024]{1,0:T(8,128)(2,1)S(1)}, bf16[32,32,1152]{2,1,0:T(8,128)(2,1)S(1)}, bf16[4,96,1024]{2,1,0:T(8,128)(...) custom-call(bf16[1024,128]{1,0:T(8,128)(2,1)S(1)} %get-tuple-element.90.left_ref.refs_5_, ...), custom_call_target="tpu_custom_call" | custom-call | tf_op jit(solution)/shard_map/middle/pallas_call | solution.py:880
  141.2 1.8 fusion.2
  143.0 0.4 multiply_convert_fusion.5.left_ref
  143.4 0.7 copy-done.6
  144.1 47.5 %result.1 = (f32[128,1024]{1,0:T(8,128)S(1)}, bf16[1024,1024]{1,0:T(8,128)(2,1)S(1)}) custom-call(bf16[1024,384]{1,0:T(8,128)(2,1)S(1)} %multiply_convert_fusion.5.left_ref, bf16[384,1024]{1,0:T(8,128)(2,1)S(1)} %bitcast.73, f32[128,1024]{1,0:T(8,128)S(1)} %get-tuple-element.94.res_ref.hid_ref, f32[8,1024]{1,0:T(8,128)S(1)} %get-tuple-element.95.gain_ref), custom_call_target="tpu_custom_call" | custom-call | tf_op jit(solution)/shard_map/result/pallas_call | solution.py:880
  191.6 13.0 %attend.3 = (bf16[1024,128]{1,0:T(8,128)(2,1)S(1)}, bf16[2,1024,128]{2,1,0:T(8,128)(2,1)S(1)}, bf16[2,1024,128]{2,1,0:T(8,128)(2,1)S(1)}, bf16[1024,128]{1,0:T(8,128)(2,1)S(1)}, f32[8,2,128]{2,1,0:T(2,128)S(1)}) custom-call(bf16[1024,1024]{1,0:T(8,128)(2,1)S(1)} %get-tuple-element.96.refs_0_, bf16[1024,1152]{1,0:T(8,128)(2,1)S(1)} %bitcast.50, ...), custom_call_target="tpu_custom_call" | custom-call | tf_op jit(solution)/shard_map/attend/pallas_call | solution.py:1384
  204.6 51.3 %middle.3 = (f32[128,1024]{1,0:T(8,128)S(1)}, bf16[1024,1024]{1,0:T(8,128)(2,1)S(1)}) custom-call(bf16[1024,128]{1,0:T(8,128)(2,1)S(1)} %get-tuple-element.99.left_ref.refs_5_, bf16[128,1024]{1,0:T(8,128)(2,1)S(1)} %bitcast.69, f32[128,1024]{1,0:T(8,128)S(1)} %get-tuple-element.101.res_ref.hid_ref, f32[8,1024]{1,0:T(8,128)S(1)} %get-tuple-element.95.gain_ref), custom_call_target="tpu_custom_call" | custom-call | tf_op jit(solution)/shard_map/middle/pallas_call | solution.py:880
  256.0 1.8 fusion
  257.8 0.4 multiply_convert_fusion.4.left_ref
  258.2 0.5 copy-done.4
  258.7 46.2 %turn.1 = (bf16[128,1024]{1,0:T(8,128)(2,1)S(1)}, bf16[1024,1024]{1,0:T(8,128)(2,1)S(1)}) custom-call(bf16[1024,384]{1,0:T(8,128)(2,1)S(1)} %multiply_convert_fusion.4.left_ref, bf16[384,1024]{1,0:T(8,128)(2,1)S(1)} %bitcast.75, f32[128,1024]{1,0:T(8,128)S(1)} %get-tuple-element.104.res_ref.hid_ref, bf16[128,1024]{1,0:T(8,128)(2,1)S(1)} %bitcast.65), custom_call_target="tpu_custom_call" | custom-call | tf_op jit(solution)/shard_map/turn/pallas_call | solution.py:880
  305.0 1.7 multiply_convert_fusion.3
  306.6 1.9 convolution_convert_fusion.1
  308.6 0.1 pad_maximum_fusion.left_ref
  308.7 1.0 convolution_convert_fusion.5
  309.7 56.5 %middle_back.2 = (f32[128,1024]{1,0:T(8,128)S(1)}, bf16[1024,1024]{1,0:T(8,128)(2,1)S(1)}, bf16[8,32,768]{2,1,0:T(8,128)(2,1)S(1)}, f32[96,1024]{1,0:T(8,128)S(1)}) custom-call(bf16[1024,768]{1,0:T(8,128)(2,1)S(1)} %pad_maximum_fusion.left_ref, bf16[1024,1152]{1,0:T(8,128)(2,1)S(1)} %bitcast.52, bf16[128,1024]{1,0:T(8,128)(2,1)S(1)} %bitcast.66, ...), custom_call_target="tpu_custom_call" | custom-call | tf_op jit(solution)/shard_map/middle_back/pallas_call | solution.py:880
  366.2 17.9 %attend_back.2 = (bf16[1024,384]{1,0:T(8,128)(2,1)S(1)}, bf16[128,1024]{1,0:T(8,128)(2,1)S(1)}, f32[1024,128]{1,0:T(8,128)S(1)}) custom-call(bf16[1024,128]{1,0:T(8,128)(2,1)S(1)} %get-tuple-element.109.refs_0_, bf16[2,1024,128]{2,1,0:T(8,128)(2,1)S(1)} %get-tuple-element.110.refs_1_, bf16[2,1024,128]{2,1,0:T(8,128)(2,1)S(1)} %get-tuple-element.111.refs_2_, ...), custom_call_target="tpu_custom_call" | custom-call | tf_op jit(solution)/shard_map/attend_back/pallas_call | solution.py:1486
  384.2 1.3 convolution_convert_fusion.4
  385.5 56.5 %layer_back.1 = (f32[128,1024]{1,0:T(8,128)S(1)}, bf16[1024,1024]{1,0:T(8,128)(2,1)S(1)}, bf16[8,32,384]{2,1,0:T(8,128)(2,1)S(1)}, f32[32,1024]{1,0:T(8,128)S(1)}) custom-call(bf16[1024,384]{1,0:T(8,128)(2,1)S(1)} %get-tuple-element.115.left_ref, bf16[1024,1152]{1,0:T(8,128)(2,1)S(1)} %bitcast.53, f32[128,1024]{1,0:T(8,128)S(1)} %get-tuple-element.116.grad_ref, ...), custom_call_target="tpu_custom_call" | custom-call | tf_op jit(solution)/shard_map/layer_back/pallas_call | solution.py:880
  442.0 1.7 multiply_convert_fusion.1
  443.7 1.9 convolution_convert_fusion
  445.6 0.1 pad_maximum_fusion.1.left_ref
  445.7 1.0 convolution_convert_fusion.3
  446.7 56.8 %middle_back.3 = (f32[128,1024]{1,0:T(8,128)S(1)}, bf16[1024,1024]{1,0:T(8,128)(2,1)S(1)}, bf16[8,32,768]{2,1,0:T(8,128)(2,1)S(1)}, f32[96,1024]{1,0:T(8,128)S(1)}) custom-call(bf16[1024,768]{1,0:T(8,128)(2,1)S(1)} %pad_maximum_fusion.1.left_ref, bf16[1024,1152]{1,0:T(8,128)(2,1)S(1)} %bitcast.56, f32[128,1024]{1,0:T(8,128)S(1)} %get-tuple-element.119.grad_ref, ...), custom_call_target="tpu_custom_call" | custom-call | tf_op jit(solution)/shard_map/middle_back/pallas_call | solution.py:880
  503.6 17.9 %attend_back.3 = (bf16[1024,384]{1,0:T(8,128)(2,1)S(1)}, bf16[128,1024]{1,0:T(8,128)(2,1)S(1)}) custom-call(bf16[1024,128]{1,0:T(8,128)(2,1)S(1)} %get-tuple-element.106.refs_0_, bf16[2,1024,128]{2,1,0:T(8,128)(2,1)S(1)} %get-tuple-element.107.refs_1_, bf16[2,1024,128]{2,1,0:T(8,128)(2,1)S(1)} %get-tuple-element.108.refs_2_, ...), custom_call_target="tpu_custom_call" | custom-call | tf_op jit(solution)/shard_map/attend_back/pallas_call | solution.py:1486
  521.4 1.3 convolution_convert_fusion.2
  522.7 32.0 %last_back.1 = (bf16[128,1024]{1,0:T(8,128)(2,1)S(1)}, bf16[8,32,384]{2,1,0:T(8,128)(2,1)S(1)}, f32[32,1024]{1,0:T(8,128)S(1)}) custom-call(bf16[1024,384]{1,0:T(8,128)(2,1)S(1)} %get-tuple-element.123.left_ref, bf16[1024,1152]{1,0:T(8,128)(2,1)S(1)} %bitcast.57, f32[128,1024]{1,0:T(8,128)S(1)} %get-tuple-element.124.grad_ref, ...), custom_call_target="tpu_custom_call" | custom-call | tf_op jit(solution)/shard_map/last_back/pallas_call | solution.py:880
  554.7 0.7 copy-done.19
  555.4 0.6 copy-done.22
  556.0 4.3 unpack.1
  560.4 0.7 copy.100
  561.1 0.7 copy.101
  (47 shorter events, 0.2 us)
Async XLA Ops:
  55.6 1.7 copy-start
  57.3 1.6 copy-start.3
  58.9 0.8 copy-start.9
  59.6 14.0 %copy-start.2 = (bf16[1,128,1024]{2,1,0:T(8,128)(2,1)S(1)}, bf16[1,128,1024]{2,1,0:T(8,128)(2,1)}, u32[]{:S(2)}) copy-start(bf16[1,128,1024]{2,1,0:T(8,128)(2,1)} %param.21) | copy-start | bytes 786436
  59.6 14.0 %copy-start.5 = (bf16[4,32,1024]{2,1,0:T(8,128)(2,1)S(1)}, bf16[4,32,1024]{2,1,0:T(8,128)(2,1)}, u32[]{:S(2)}) copy-start(bf16[4,32,1024]{2,1,0:T(8,128)(2,1)} %get-tuple-element.91) | copy-start | bytes 786436
  59.6 14.0 %copy-start.7 = (bf16[32,2816]{1,0:T(8,128)(2,1)S(1)}, bf16[32,2816]{1,0:T(8,128)(2,1)}, u32[]{:S(2)}) copy-start(bf16[32,2816]{1,0:T(8,128)(2,1)} %refs_20_.1) | copy-start | bytes 540676
  59.6 14.0 %copy-start.8 = (bf16[32,2816]{1,0:T(8,128)(2,1)S(1)}, bf16[32,2816]{1,0:T(8,128)(2,1)}, u32[]{:S(2)}) copy-start(bf16[32,2816]{1,0:T(8,128)(2,1)} %refs_21_.1) | copy-start | bytes 540676
  59.6 14.0 %copy-start.10 = (f32[8,1024]{1,0:T(8,128)S(1)}, f32[8,1024]{1,0:T(8,128)}, u32[]{:S(2)}) copy-start(f32[8,1024]{1,0:T(8,128)} %get-tuple-element.89.refs_4_.gain_ref) | copy-start | bytes 98308
  59.6 14.0 %copy-start.15 = (bf16[32,1024]{1,0:T(8,128)(2,1)S(1)}, bf16[32,1024]{1,0:T(8,128)(2,1)}, u32[]{:S(2)}) copy-start(bf16[32,1024]{1,0:T(8,128)(2,1)} %refs_16_.1) | copy-start | bytes 196612
  59.7 14.0 %copy-start.16 = (bf16[32,1024]{1,0:T(8,128)(2,1)S(1)}, bf16[32,1024]{1,0:T(8,128)(2,1)}, u32[]{:S(2)}) copy-start(bf16[32,1024]{1,0:T(8,128)(2,1)} %refs_17_.1) | copy-start | bytes 196612
  59.7 14.0 %copy-start.17 = (bf16[32,1024]{1,0:T(8,128)(2,1)S(1)}, bf16[32,1024]{1,0:T(8,128)(2,1)}, u32[]{:S(2)}) copy-start(bf16[32,1024]{1,0:T(8,128)(2,1)} %refs_18_.1) | copy-start | bytes 196612
  59.7 14.0 %copy-start.20 = (bf16[88,1024]{1,0:T(8,128)(2,1)S(1)}, bf16[88,1024]{1,0:T(8,128)(2,1)}, u32[]{:S(2)}) copy-start(bf16[88,1024]{1,0:T(8,128)(2,1)} %refs_8_.3) | copy-start | bytes 540676
  59.7 14.0 %copy-start.23 = (bf16[32,1024]{1,0:T(8,128)(2,1)S(1)}, bf16[32,1024]{1,0:T(8,128)(2,1)}, u32[]{:S(2)}) copy-start(bf16[32,1024]{1,0:T(8,128)(2,1)} %refs_4_.3) | copy-start | bytes 196612
  59.7 14.0 %copy-start.24 = (bf16[32]{0:T(256)(128)(2,1)S(1)}, bf16[32]{0:T(256)(128)(2,1)}, u32[]{:S(2)}) copy-start(bf16[32]{0:T(256)(128)(2,1)} %param.33) | copy-start | bytes 196
  59.7 14.0 %copy-start.25 = (bf16[32]{0:T(256)(128)(2,1)S(1)}, bf16[32]{0:T(256)(128)(2,1)}, u32[]{:S(2)}) copy-start(bf16[32]{0:T(256)(128)(2,1)} %param.38) | copy-start | bytes 196
  59.7 81.4 %copy-start.1 = (bf16[32,32,1152]{2,1,0:T(8,128)(2,1)S(1)}, bf16[32,32,1152]{2,1,0:T(8,128)(2,1)}, u32[]{:S(2)}) copy-start(bf16[32,32,1152]{2,1,0:T(8,128)(2,1)} %get-tuple-element.88) | copy-start | bytes 7077892
  143.0 1.1 copy-start.6
  257.7 1.0 copy-start.4
  366.2 17.9 %copy-start.11 = (bf16[8,32,768]{2,1,0:T(8,128)(2,1)}, bf16[8,32,768]{2,1,0:T(8,128)(2,1)S(1)}, u32[]{:S(2)}) copy-start(bf16[8,32,768]{2,1,0:T(8,128)(2,1)S(1)} %get-tuple-element.132.refs_11_) | copy-start | bytes 1179652
  366.2 17.9 %copy-start.12 = (f32[96,1024]{1,0:T(8,128)}, f32[96,1024]{1,0:T(8,128)S(1)}, u32[]{:S(2)}) copy-start(f32[96,1024]{1,0:T(8,128)S(1)} %get-tuple-element.133.refs_12_) | copy-start | bytes 1179652
  442.0 1.7 copy-start.18
  442.0 1.7 copy-start.21
  503.5 17.9 %copy-start.13 = (bf16[8,32,768]{2,1,0:T(8,128)(2,1)}, bf16[8,32,768]{2,1,0:T(8,128)(2,1)S(1)}, u32[]{:S(2)}) copy-start(bf16[8,32,768]{2,1,0:T(8,128)(2,1)S(1)} %get-tuple-element.128.refs_0_) | copy-start | bytes 1179652
  503.5 17.9 %copy-start.14 = (f32[96,1024]{1,0:T(8,128)}, f32[96,1024]{1,0:T(8,128)S(1)}, u32[]{:S(2)}) copy-start(f32[96,1024]{1,0:T(8,128)S(1)} %get-tuple-element.129.refs_1_) | copy-start | bytes 1179652
  554.7 0.7 copy-start.19
  555.4 0.7 copy-start.22

commit v6 on v5

--- a/solution.py
+++ b/solution.py
@@ -531,6 +531,7 @@
 F32 = jnp.float32
 MESH = pl.DeviceIdType.MESH
 VMEM_SPACE = pltpu.VMEM
+HBM_SPACE = pltpu.HBM
 
 
 def flip(value, weight):
@@ -783,13 +784,16 @@
         run(False)
 
 
-def exchange(place, product, settle, full, scratch, extra=None):
+def exchange(place, product, settle, full, scratch, extra=None, rows=None):
+    f, c, y, z = place
     if extra is None:
-        f, c, y, z = place
         greet(row_peers(f, c, z) + [(f, flip(c, 2))])
     else:
-        peers, sibling, twin = chip_peers(place[0], place[1])
+        peers, sibling, twin = chip_peers(f, c)
         greet(peers + [sibling, twin])
+    own = (z * 2 + y) * ROWS
+    if rows is not None:
+        full[pl.ds(pl.multiple_of(own, ROWS), ROWS), :] = rows
 
     def run(inner):
         parts = []
@@ -798,24 +802,30 @@
         reduce.products()
         if more is not None:
             more.first()
+            more.early()
             parts.append(more)
         parts.append(reduce)
         if full is not None:
             gather = Gather(place, inner, full, scratch[14:19])
             parts.append(gather)
         reduce.relays()
+        if rows is not None:
+            gather.send_own(0)
+            gather.send_own(1)
         if more is not None:
             more.second()
         for half in range(2):
-            rows = settle(half, reduce.own_sum(half))
-            if full is not None:
-                start = (place[3] * 2 + place[2]) * ROWS + half * HALF
-                full[pl.ds(pl.multiple_of(start, HALF), HALF), :] = rows
+            new = settle(half, reduce.own_sum(half))
+            if full is not None and rows is None:
+                full[pl.ds(pl.multiple_of(own + half * HALF, HALF), HALF), :] = new
                 gather.send_own(half)
             if more is not None and half == 0:
                 more.third()
         if full is not None:
             gather.forward(0)
+        if more is not None:
+            more.fourth()
+        if full is not None:
             gather.forward(1)
         for part in parts:
             part.finish()
@@ -854,9 +864,9 @@
 def turn_kernel(left_ref, right_ref, res_ref, cot_ref, out_ref, full_ref, *scratch):
     def settle(half, total):
         out_ref[half_rows(half), :] = (res_ref[half_rows(half), :] + total).astype(BF)
-        return cot_ref[half_rows(half), :]
-
-    exchange(plane_place(), make_product(left_ref, right_ref, False), settle, full_ref, scratch)
+
+    product = make_product(left_ref, right_ref, False)
+    exchange(plane_place(), product, settle, full_ref, scratch, None, cot_ref[...])
 
 
 def back_rows(total, grad, hidden, gain):
@@ -902,16 +912,71 @@
     pl.semaphore_wait(barrier, len(targets))
 
 
-class Spread:
-    def __init__(self, place, table, down, out, sems):
+class OutRows:
+    def __init__(self, place, shard, out, sems):
+        self.f, self.c, self.y, _ = place
+        self.core = self.c % 2
+        _, self.sibling, self.twin = chip_peers(self.f, self.c)
+        self.near = (self.f, flip(self.c, 2))
+        self.shard, self.out = shard, out
+        self.ws, self.wr = sems
+        self.home = self.y == self.f
+
+    def near_copy(self):
+        part = 2 * self.y + self.core
+        return remote(self.shard, self.out.at[part], self.ws.at[0], self.wr.at[0], self.near)
+
+    def pair_copies(self, first, target):
+        parts = [self.out.at[self.core], self.out.at[2 + self.core]]
+        return [
+            remote(p, p, self.ws.at[first + n], self.wr.at[first + n], target) for n, p in enumerate(parts)
+        ]
+
+    def first(self):
+        @pl.when(self.home)
+        def _():
+            self.out[2 * self.y + self.core] = self.shard[...]
+
+        @pl.when(jnp.logical_not(self.home))
+        def _():
+            self.near_copy().start()
+
+    def second(self):
+        @pl.when(self.home)
+        def _():
+            self.near_copy().wait_recv()
+            for copy in self.pair_copies(1, self.twin):
+                copy.start()
+
+    def third(self):
+        @pl.when(jnp.logical_not(self.home))
+        def _():
+            for copy in self.pair_copies(1, self.twin):
+                copy.wait_recv()
+
+        for copy in self.pair_copies(3, self.sibling):
+            copy.start()
+
+    def finish(self):
+        for copy in self.pair_copies(3, self.sibling):
+            copy.wait()
+
+        @pl.when(self.home)
+        def _():
+            for copy in self.pair_copies(1, self.twin):
+                copy.wait_send()
+
+        @pl.when(jnp.logical_not(self.home))
+        def _():
+            self.near_copy().wait_send()
+
+
+class Sender:
+    def __init__(self, place):
         self.f, self.c, self.y, _ = place
         self.chip, self.core = self.c // 2, self.c % 2
         self.peers, self.sibling, self.twin = chip_peers(self.f, self.c)
-        self.near = (self.f, flip(self.c, 2))
-        self.table, self.down, self.out = table, down, out
-        self.ds, self.dr, self.xs, self.xr, self.ss, self.sr, self.ws, self.wr = sems
-        self.home = self.y == self.f
-        self.direct, self.crossed, self.inner, self.sent = {}, {}, [], []
+        self.sent = []
 
     def send(self, src, dst, send_sem, recv_sem, target):
         copy = remote(src, dst, send_sem, recv_sem, target)
@@ -919,96 +984,114 @@
         self.sent.append(copy)
         return copy
 
-    def to_twin(self, src, dst, n):
-        self.crossed[n] = self.send(src, dst, self.xs.at[n], self.xr.at[n], self.twin)
-
-    def to_sibling(self, src, dst, n):
-        self.inner.append(self.send(src, dst, self.ss.at[n], self.sr.at[n], self.sibling))
-
-    def out_copy(self):
-        op, out = self.out
-        part = 2 * self.y + self.core
-        return remote(op, out.at[part], self.ws, self.wr, self.near)
-
-    def pair_copies(self, s, r, first, target):
-        parts = [self.out[1].at[self.core], self.out[1].at[2 + self.core]]
-        return [remote(p, p, s.at[first + n], r.at[first + n], target) for n, p in enumerate(parts)]
+
+class Spread(Sender):
+    def __init__(self, place, a, r, sems):
+        super().__init__(place)
+        self.a, self.r = a, r
+        self.ds, self.dr, self.xs, self.xr, self.ss, self.sr = sems
+        self.direct, self.crossed, self.inner = {}, {}, []
+
+    def forward(self, part, n):
+        self.crossed[n] = self.send(part[0], part[1], self.xs.at[n], self.xr.at[n], self.twin)
+
+    def to_sibling(self, part, n):
+        self.inner.append(self.send(part[0], part[1], self.ss.at[n], self.sr.at[n], self.sibling))
 
     def first(self):
-        a, r = self.table
-        down, down_all = self.down
-        op, out = self.out
-        mine = self.f * 16 + self.c
-        part = 2 * self.f + self.core
-        self.to_twin(a.at[self.chip], r.at[mine], 0)
+        mine = self.r.at[self.f, self.chip, self.core]
+        own = self.a.at[self.chip]
+        self.forward((own, mine), 0)
         for i in range(1, 8):
             t = (self.chip + i) % 8
-            self.direct[i] = self.send(
-                a.at[t], r.at[mine], self.ds.at[i], self.dr.at[i], self.peers[i - 1]
-            )
-        r[mine] = a[self.chip]
-        self.to_sibling(a.at[self.chip], r.at[mine], 0)
-        down_all[part] = down[...]
-        self.to_twin(down, down_all.at[part], 8)
-        self.to_sibling(down, down_all.at[part], 16)
-
-        @pl.when(self.home)
-        def _():
-            out[2 * self.y + self.core] = op[...]
-
-        @pl.when(jnp.logical_not(self.home))
-        def _():
-            self.out_copy().start()
+            self.direct[i] = self.send(self.a.at[t], mine, self.ds.at[i], self.dr.at[i], self.peers[i - 1])
+        self.r[self.f, self.chip, self.core] = self.a[self.chip]
+        self.to_sibling((own, mine), 0)
 
     def second(self):
-        r = self.table[1]
         for i in range(1, 8):
             self.direct[i].wait_recv()
-            source = self.f * 16 + 2 * ((self.chip + 8 - i) % 8) + self.core
-            self.to_twin(r.at[source], r.at[source], i)
-            self.to_sibling(r.at[source], r.at[source], i)
-
-        @pl.when(self.home)
-        def _():
-            self.out_copy().wait_recv()
-            for copy in self.pair_copies(self.xs, self.xr, 9, self.twin):
-                copy.start()
+            part = self.r.at[self.f, (self.chip + 8 - i) % 8, self.core]
+            self.forward((part, part), i)
+            self.to_sibling((part, part), i)
 
     def third(self):
-        r = self.table[1]
-
-        @pl.when(jnp.logical_not(self.home))
-        def _():
-            for copy in self.pair_copies(self.xs, self.xr, 9, self.twin):
-                copy.wait_recv()
-
-        for copy in self.pair_copies(self.ss, self.sr, 18, self.sibling):
-            copy.start()
         for i in range(8):
             self.crossed[i].wait_recv()
-            source = (1 - self.f) * 16 + 2 * ((self.chip + 8 - i) % 8) + self.core
-            self.to_sibling(r.at[source], r.at[source], 8 + i)
-        self.crossed[8].wait_recv()
-        part = 2 * (1 - self.f) + self.core
-        down_all = self.down[1]
-        self.to_sibling(down_all.at[part], down_all.at[part], 17)
+            part = self.r.at[1 - self.f, (self.chip + 8 - i) % 8, self.core]
+            self.to_sibling((part, part), 8 + i)
 
     def finish(self):
         for copy in self.inner:
             copy.wait_recv()
         for copy in self.sent:
             copy.wait_send()
-        for copy in self.pair_copies(self.ss, self.sr, 18, self.sibling):
-            copy.wait()
-
-        @pl.when(self.home)
-        def _():
-            for copy in self.pair_copies(self.xs, self.xr, 9, self.twin):
-                copy.wait_send()
-
-        @pl.when(jnp.logical_not(self.home))
-        def _():
-            self.out_copy().wait_send()
+
+
+class Share(Sender):
+    def __init__(self, place, tables, downs, out, sems):
+        super().__init__(place)
+        self.tables, self.downs = tables, downs
+        self.xs, self.xr, self.ss, self.sr, *more = sems
+        self.out = OutRows(place, *out, more) if out else None
+
+    def places(self, f):
+        found = [r.at[f, :, self.core] for _, r in self.tables]
+        return found + [d.at[2 * f + self.core] for _, d in self.downs]
+
+    def first(self):
+        self.crossed, self.inner = [], []
+        sources = [s for s, _ in self.tables] + [n for n, _ in self.downs]
+        for n, (src, dst) in enumerate(zip(sources, self.places(self.f))):
+            self.crossed.append(self.send(src, dst, self.xs.at[n], self.xr.at[n], self.twin))
+            self.inner.append(self.send(src, dst, self.ss.at[n], self.sr.at[n], self.sibling))
+        for src, r in self.tables:
+            for j in range(8):
+                r[self.f, j, self.core] = src[j]
+        for src, d in self.downs:
+            d[2 * self.f + self.core] = src[...]
+        if self.out:
+            self.out.first()
+
+    def early(self):
+        pass
+
+    def second(self):
+        if self.out:
+            self.out.second()
+
+    def third(self):
+        pass
+
+    def fourth(self):
+        count = len(self.crossed)
+        for n, part in enumerate(self.places(1 - self.f)):
+            self.crossed[n].wait_recv()
+            self.inner.append(
+                self.send(part, part, self.ss.at[count + n], self.sr.at[count + n], self.sibling)
+            )
+        if self.out:
+            self.out.third()
+
+    def finish(self):
+        for copy in self.inner:
+            copy.wait_recv()
+        for copy in self.sent:
+            copy.wait_send()
+        if self.out:
+            self.out.finish()
+
+
+def start_leg(parts, peers, chip, sends, receives):
+    copies = []
+    for n, (src, dst) in enumerate(parts):
+        for i in range(1, 8):
+            sem = 8 * n + i
+            part = src.at[(chip + i) % 8]
+            copies.append(remote(part, dst.at[chip], sends.at[sem], receives.at[sem], peers[i - 1]))
+            copies[-1].start()
+        dst[chip] = src[chip]
+    return copies
 
 
 def turn_row(row):
@@ -1023,133 +1106,180 @@
     return jnp.sum(jnp.where(same, column, 0.0), axis=0, keepdims=True)
 
 
-def pack_shards(shards, block, a, dn):
-    pre, query, keys, values, _, mid, gates, upproj, down = shards
-    rows, units = gates.shape
-    each = units // 32
-    lane = lax.broadcasted_iota(jnp.int32, (rows, block - each), 1)
-    empty = jnp.zeros((rows, block - each), F32)
-    pre, mid = turn_row(pre[...].astype(F32)), turn_row(mid[...].astype(F32))
-    riders = jnp.where(lane == 0, pre, jnp.where(lane == 1, mid, empty))
+def pack_heads(query, keys, values, a):
     for chip in range(8):
         pair = 4 * (chip % 2) + chip // 2
         for n, w in enumerate((query, keys, values)):
             a[chip, :, 128 * n : 128 * n + 128] = w[:, 128 * pair : 128 * pair + 128]
+
+
+def pack_units(gates, upproj, block, a):
+    rows, units = gates.shape
+    each = units // 32
+    empty = jnp.zeros((rows, block - each), F32)
+    for chip in range(8):
         for n, w in enumerate((gates, upproj)):
             parts = []
             for i in range(4):
                 owner = 16 * (i // 2) + 2 * chip + i % 2
-                parts.append(w[:, each * owner : each * owner + each].astype(F32))
-                parts.append(riders if n == 0 and i == 0 else empty)
-            first = 384 + 4 * block * n
-            a[chip, :, first : first + 4 * block] = jnp.concatenate(parts, axis=-1).astype(BF)
+                parts += [w[:, each * owner : each * owner + each].astype(F32), empty]
+            at = 4 * block * n
+            a[chip, :, at : at + 4 * block] = jnp.concatenate(parts, axis=-1).astype(BF)
+
+
+def pack_down(down, dn):
+    each = down.shape[0]
     dn[:each] = down[...]
-    dn[each:] = jnp.zeros((block - each, down.shape[1]), BF)
-
-
-def read_gains(r, each, gains):
-    count = r.shape[0] * r.shape[1]
-    columns = r[:, :, 384:512].reshape(count, 128)
-    row = lax.broadcasted_iota(jnp.int32, (8, 128), 0)
-    lane = lax.broadcasted_iota(jnp.int32, (8, 128), 1)
-    pick = jnp.where(lane == row + each, 1.0, 0.0).astype(BF)
-    gains[...] = lax.dot_general(pick, columns, NT, preferred_element_type=F32)
+    dn[each:] = jnp.zeros((dn.shape[0] - each, down.shape[1]), BF)
 
 
 def begin_kernel(tok, *refs):
-    shards, (full, r, d, o, gains), (a, dn, *sems) = refs[:9], refs[9:14], refs[14:]
+    given, (full, r, o, gains, u1, h2, u2, n1, n2), shards = refs[:18], refs[18:27], refs[27:45]
+    ones, twos = shards[:9], shards[9:]
+    loads, a, *sems = refs[45:]
+    copies = [pltpu.make_async_copy(src, dst, loads.at[n]) for n, (src, dst) in enumerate(zip(given, shards))]
+    soon = (0, 1, 2, 3, 4, 5, 9, 14)
+    for n in soon:
+        copies[n].start()
+    for n in range(18):
+        if n not in soon:
+            copies[n].start()
     place = plane_place()
     f, c, y, z = place
     peers, sibling, twin = chip_peers(f, c)
     start = (z * 2 + y) * ROWS
     full[pl.ds(pl.multiple_of(start, ROWS), ROWS), :] = tok[...]
-    pack_shards(shards, dn.shape[0], a, dn)
+    for n in soon:
+        copies[n].wait()
+    pack_heads(ones[1], ones[2], ones[3], a)
+    lane = lax.broadcasted_iota(jnp.int32, (tok.shape[1] // 32, 128), 1)
+    riders = jnp.zeros(lane.shape, F32)
+    for n, gain in enumerate((ones[0], ones[5], twos[0], twos[5])):
+        riders = jnp.where(lane == n, turn_row(gain[...].astype(F32)), riders)
+    for chip in range(8):
+        a[chip, :, 384:] = riders.astype(BF)
     greet(peers + [sibling, twin])
 
     def run(inner):
         gather = Gather(place, inner, full, sems[:5])
-        spread = Spread(place, (a, r), (dn, d), (shards[4], o), sems[5:])
+        spread = Spread(place, a, r, sems[5:11])
+        out = OutRows(place, ones[4], o, sems[11:])
         gather.send_own(0)
         spread.first()
+        out.first()
         gather.send_own(1)
+        for n in range(18):
+            if n not in soon:
+                copies[n].wait()
+        pack_units(ones[6], ones[7], n1.shape[0], u1)
+        pack_heads(twos[1], twos[2], twos[3], h2)
+        pack_units(twos[6], twos[7], n1.shape[0], u2)
+        pack_down(ones[8], n1)
+        pack_down(twos[8], n2)
         gather.forward(0)
         spread.second()
+        out.second()
         gather.forward(1)
         spread.third()
+        out.third()
         gather.finish()
         spread.finish()
+        out.finish()
 
     both_kinds(place, run)
-    read_gains(r, shards[8].shape[0], gains)
-
-
-def spread_shapes(rows, width, block):
-    wide = 384 + 8 * block
-    outs = [((32, rows, wide), BF), ((4, block, width), BF), ((4, rows, width), BF), ((8, 32 * rows), F32)]
-    scratch = [pltpu.VMEM((8, rows, wide), BF), pltpu.VMEM((block, width), BF)]
-    sems = [pltpu.SemaphoreType.DMA(n) for n in ((8,), (8,), (11,), (11,), (20,), (20,), (), ())]
-    return outs, scratch, sems
+    count = tok.shape[1]
+    columns = r[:, :, :, :, 384:].reshape(count, 128)
+    pick = lax.broadcasted_iota(jnp.int32, (8, 128), 0) == lax.broadcasted_iota(jnp.int32, (8, 128), 1)
+    gains[...] = lax.dot_general(jnp.where(pick, 1.0, 0.0).astype(BF), columns, NT, preferred_element_type=F32)
 
 
 def begin_call(tok, shards, block):
     rows, width = shards[1].shape
-    outs, scratch, sems = spread_shapes(rows, width, block)
-    outs = [((8 * ROWS, width), BF)] + outs
     spec = pl.BlockSpec(memory_space=VMEM_SPACE)
+    wide = 8 * block
+    outs = [
+        ((8 * ROWS, width), BF), ((2, 8, 2, rows, 512), BF), ((4, rows, width), BF), ((8, width), F32),
+        ((8, rows, wide), BF), ((8, rows, 384), BF), ((8, rows, wide), BF), ((block, width), BF), ((block, width), BF),
+    ]
+    counts = [(10,)] * 5 + [(8,), (8,), (8,), (8,), (16,), (16,), (5,), (5,)]
     return pl.pallas_call(
         begin_kernel,
         out_shape=[jax.ShapeDtypeStruct(*o) for o in outs],
-        in_specs=[spec] * 10,
+        in_specs=[spec] + [pl.BlockSpec(memory_space=HBM_SPACE)] * 18,
         out_specs=[spec] * len(outs),
-        scratch_shapes=scratch + [pltpu.SemaphoreType.DMA((10,))] * 5 + sems,
+        scratch_shapes=[pltpu.VMEM(s.shape, s.dtype) for s in shards]
+        + [pltpu.SemaphoreType.DMA((18,)), pltpu.VMEM((8, rows, 512), BF)]
+        + [pltpu.SemaphoreType.DMA(n) for n in counts],
         compiler_params=pltpu.CompilerParams(
-            collective_id=9, has_side_effects=True, vmem_limit_bytes=60 * 1024 * 1024
+            collective_id=9, has_side_effects=True, vmem_limit_bytes=10 * 1024 * 1024
         ),
         name="begin",
     )(tok, *shards)
 
 
-def first_middle_kernel(left_ref, right_ref, res_ref, gain_ref, *refs):
-    shards, (new_ref, full_ref, r, d, o, gains), scratch = refs[:9], refs[9:15], refs[15:]
-    a, dn, *sems = scratch[19:]
+def middle_kernel(row, count, left_ref, right_ref, res_ref, gain_ref, *refs):
+    given = 2 * count
+    ins, refs = refs[:given], refs[given:]
+    outs = 2 + count + 1 + (count == 2)
+    new_ref, full_ref, *results = refs[:outs]
+    scratch = refs[outs:]
 
     def settle(half, total):
         hidden = res_ref[half_rows(half), :].astype(F32) + total
         new_ref[half_rows(half), :] = hidden
-        return (hidden * norm_rows(hidden) * gain_ref[1:2, :]).astype(BF)
+        return (hidden * norm_rows(hidden) * gain_ref[row : row + 1, :]).astype(BF)
 
     def extra(place):
-        return Spread(place, (a, r), (dn, d), (shards[4], o), sems)
-
-    pack_shards(shards, dn.shape[0], a, dn)
+        tables = list(zip(ins[:count], results[:count]))
+        downs = [(ins[count], results[count])]
+        out = (ins[3], results[3]) if count == 2 else None
+        return Share(place, tables, downs, out, scratch[19:])
+
     exchange(plane_place(), make_product(left_ref, right_ref, False), settle, full_ref, scratch, extra)
-    read_gains(r, shards[8].shape[0], gains)
+
+
+def share_shapes(rows, width, block, widths):
+    outs = [((2, 8, 2, rows, w), BF) for w in widths] + [((4, block, width), BF)]
+    if len(widths) == 2:
+        outs += [((4, rows, width), BF)]
+    return outs, [pltpu.SemaphoreType.DMA(n) for n in ((3,), (3,), (6,), (6,), (5,), (5,))]
 
 
 class Collect:
-    def __init__(self, place, ins, results, scratch):
+    def __init__(self, place, ins, results, scratch, final):
         self.f, self.c, self.y, _ = place
         self.chip, self.core = self.c // 2, self.c % 2
         self.peers, self.sibling, self.twin = chip_peers(self.f, self.c)
         self.near = (self.f, flip(self.c, 2))
+        self.final = final
         self.g, self.h = ins
         self.out, self.oh = results
-        self.sb, self.xb, self.xt, self.ut, self.sh, self.xh, self.th, *near = scratch[: -6]
+        self.sb, self.xb, self.xt, self.ut, self.sh, self.xh, self.th, *near = scratch[:-6]
         self.ss, self.sr, self.xs, self.xr, self.ps, self.pr = scratch[-6:]
         self.crosses_near = bool(near)
         if near:
             self.yo, self.yt = near
         self.home = self.y == self.f
-        self.sent = []
-
-    def send(self, src, dst, send_sem, recv_sem, target):
-        copy = remote(src, dst, send_sem, recv_sem, target)
-        copy.start()
-        self.sent.append(copy)
-        return copy
-
-    def inner_send(self, src, dst, n):
-        return self.send(src, dst, self.ss.at[n], self.sr.at[n], self.sibling)
+
+    def inner_copy(self, n):
+        other = 1 - self.core
+        if n == 2:
+            src, dst = self.h.at[:, other], self.sh
+        else:
+            part = 8 * ((1 - self.f) if n == 0 else self.f)
+            src, dst = self.g.at[pl.ds(part, 8), other], self.sb.at[pl.ds(part, 8)]
+        return remote(src, dst, self.ss.at[n], self.sr.at[n], self.sibling)
+
+    def target(self, i):
+        return (self.chip + i + 1) % 8
+
+    def cross_copy(self, i):
+        t = self.target(i)
+        return remote(self.xt.at[t], self.xb.at[t], self.xs.at[i], self.xr.at[i], self.twin)
+
+    def direct_copy(self, i):
+        src = self.ut.at[self.target(i)]
+        return remote(src, self.out.at[self.chip], self.ps.at[i], self.pr.at[i], self.peers[i])
 
     def twin_copy(self):
         return remote(self.th, self.xh, self.xs.at[8], self.xr.at[8], self.twin)
@@ -1158,27 +1288,18 @@
         return remote(self.yt, self.yo, self.xs.at[9], self.xr.at[9], self.near)
 
     def first(self):
-        other = 1 - self.core
-        self.inner = []
-        for half in range(2):
-            part = 8 * ((1 - self.f) if half == 0 else self.f)
-            self.inner.append(
-                self.inner_send(self.g.at[pl.ds(part, 8), other], self.sb.at[pl.ds(part, 8)], half)
-            )
-        self.inner.append(self.inner_send(self.h.at[:, other], self.sh, 2))
-
-    def second(self):
+        for n in range(3):
+            self.inner_copy(n).start()
+
+    def early(self):
         f, core = self.f, self.core
-        self.crossed = []
-        self.inner[0].wait_recv()
+        self.inner_copy(0).wait_recv()
         for i in range(8):
-            t = (self.chip + i + 1) % 8
+            t = self.target(i)
             at = (1 - f) * 8 + t
             self.xt[t] = (self.g[at, core].astype(F32) + self.sb[at].astype(F32)).astype(BF)
-            self.crossed.append(
-                self.send(self.xt.at[t], self.xb.at[t], self.xs.at[i], self.xr.at[i], self.twin)
-            )
-        self.inner[2].wait_recv()
+            self.cross_copy(i).start()
+        self.inner_copy(2).wait_recv()
         if not self.crosses_near:
             self.th[...] = (self.h[1 - f, core].astype(F32) + self.sh[1 - f].astype(F32)).astype(BF)
             self.twin_copy().start()
@@ -1190,20 +1311,19 @@
         def _():
             self.twin_copy().start()
 
-    def third(self):
+    def second(self):
         f, core = self.f, self.core
-        self.direct = []
-        self.inner[1].wait_recv()
+        self.inner_copy(1).wait_recv()
         for i in range(8):
-            t = (self.chip + i + 1) % 8
+            t = self.target(i)
             at = f * 8 + t
-            self.crossed[i].wait_recv()
+            self.cross_copy(i).wait_recv()
             total = self.g[at, core].astype(F32) + self.sb[at].astype(F32) + self.xb[t].astype(F32)
-            if i < 7:
+            if not self.final:
+                self.out[t] = total.astype(BF)
+            elif i < 7:
                 self.ut[t] = total.astype(BF)
-                self.direct.append(
-                    self.send(self.ut.at[t], self.out.at[self.chip], self.ps.at[i], self.pr.at[i], self.peers[i])
-                )
+                self.direct_copy(i).start()
             else:
                 self.out[self.chip] = total.astype(BF)
         if not self.crosses_near:
@@ -1219,6 +1339,12 @@
             self.yt[...] = (self.th[1 - y].astype(F32) + self.xh[1 - y].astype(F32)).astype(BF)
             self.near_copy().start()
 
+    def third(self):
+        pass
+
+    def fourth(self):
+        pass
+
     def finish(self):
         if self.crosses_near:
 
@@ -1233,10 +1359,12 @@
                 self.twin_copy().wait_send()
         else:
             self.twin_copy().wait_send()
-        for copy in self.direct:
-            copy.wait_recv()
-        for copy in self.sent:
-            copy.wait_send()
+        for i in range(7 if self.final else 0):
+            self.direct_copy(i).wait()
+        for i in range(8):
+            self.cross_copy(i).wait_send()
+        for n in range(3):
+            self.inner_copy(n).wait_send()
 
 
 def collect_shapes(rows, wide, block, width, crosses_near):
@@ -1251,20 +1379,22 @@
     return results, scratch
 
 
-def back_kernel(gathers, row, lanes, left_ref, right_ref, grad_ref, hid_ref, gain_ref, g, gd, new_ref, *rest):
-    full_ref = rest[0] if gathers else None
-    c, od = rest[gathers : gathers + 2]
-    scratch = rest[gathers + 2 :]
+def back_kernel(gathers, row, crosses, left_ref, right_ref, grad_ref, hid_ref, gain_ref, g, h, new_ref, *refs):
+    full_ref = refs[0] if gathers else None
+    results, scratch = refs[gathers : gathers + 2], refs[gathers + 2 :]
 
     def settle(half, total):
         at = half_rows(half)
-        new = back_rows(total, grad_ref[at, :].astype(F32), hid_ref[at, :].astype(F32), gain_ref[row : row + 1, :])
+        new = back_rows(
+            total, grad_ref[at, :].astype(F32), hid_ref[at, :].astype(F32), gain_ref[row : row + 1, :]
+        )
         new_ref[at, :] = new.astype(new_ref.dtype)
         return new.astype(BF)
 
     def extra(place):
-        return Collect(place, (g, gd), (c, od), scratch[14 + 5 * gathers :])
-
+        return Collect(place, (g, h), results, scratch[14 + 5 * gathers :], not gathers)
+
+    lanes = (0, 384) if crosses else None
     product = make_product(left_ref, right_ref, True, lanes)
     exchange(plane_place(), product, settle, full_ref, scratch, extra)
 
@@ -1298,13 +1428,18 @@
 
 def attend_kernel(layer, *refs):
     x_ref, w_ref, cos_ref, sin_ref, more_ref, pq_ref, pk_ref = refs[:7]
-    q_ref, k_ref, v_ref, att_ref, lse_ref = refs[7:12]
-    ss, sr = refs[-2:]
+    count = 2 - layer
+    tables, refs = refs[7 : 7 + count], refs[7 + count :]
+    q_ref, k_ref, v_ref, att_ref, lse_ref = refs[:5]
+    kept = refs[5:7]
+    placed = refs[-4 - count : -4]
+    sends, receives, ss, sr = refs[-4:]
     f, c, _, _ = plane_place()
-    sibling = (f, flip(c, 1))
-    greet([sibling])
+    peers, sibling, _ = chip_peers(f, c)
     rows_n = x_ref.shape[0]
     half_n = rows_n // 2
+    greet(peers + [sibling])
+    leg = start_leg(list(zip(tables, placed)), peers, c // 2, sends, receives)
 
     def copies(i):
         here = pl.ds(pl.multiple_of(i * HALF, HALF), HALF)
@@ -1321,14 +1456,14 @@
         if layer == 0:
             wide = rows.astype(F32)
             rows = (wide * norm_rows(wide) * more_ref[:1, :]).astype(BF)
-            refs[12][at, :] = rows
+            kept[0][at, :] = rows
         raw = jnp.dot(rows, w_ref[:, :384], preferred_element_type=F32)
         cosine, sine = cos_ref[at, :], sin_ref[at, :]
         q, k, v = raw[:, :128], raw[:, 128:256], raw[:, 256:]
         q_ref[at, :] = (q * cosine + swap_halves(q) * sine).astype(BF)
         k = (k * cosine + swap_halves(k) * sine).astype(BF)
         if layer == 0:
-            refs[13][at, :] = v
+            kept[1][at, :] = v
         else:
             v = 0.5 * v + 0.5 * more_ref[at, :]
         v = v.astype(BF)
@@ -1371,36 +1506,45 @@
         return carry
 
     lax.fori_loop(0, rows_n // (2 * ROWS), tile_step, 0)
-
-
-def attend(layer, x, w, cosine, sine, more, pos_q, pos_k):
-    rows_n = x.shape[0]
+    for copy in leg:
+        copy.wait()
+
+
+def attend(layer, *args):
+    rows_n = args[0].shape[0]
     spec = pl.BlockSpec(memory_space=VMEM_SPACE)
     outs = [((rows_n, 128), BF), ((2, rows_n, 128), BF), ((2, rows_n, 128), BF), ((rows_n, 128), BF)]
     outs += [((rows_n // ROWS, 2, ROWS), F32)]
+    count = 4 * (rows_n // ROWS)
+    sems = [pltpu.SemaphoreType.DMA((count,))] * 2
     if layer == 0:
-        outs += [(x.shape, BF), ((rows_n, 128), F32)]
-    count = 4 * (rows_n // ROWS)
+        outs += [(args[0].shape, BF), ((rows_n, 128), F32)]
+    outs += [(p.shape, BF) for p in args[7:]]
+    sems = [pltpu.SemaphoreType.DMA((16,))] * 2 + sems
     return pl.pallas_call(
         functools.partial(attend_kernel, layer),
         out_shape=[jax.ShapeDtypeStruct(*o) for o in outs],
-        in_specs=[spec] * 7,
+        in_specs=[spec] * len(args),
         out_specs=[spec] * len(outs),
-        scratch_shapes=[pltpu.SemaphoreType.DMA((count,))] * 2,
+        scratch_shapes=sems,
         compiler_params=pltpu.CompilerParams(
             collective_id=10 + layer, has_side_effects=True, vmem_limit_bytes=16 * 1024 * 1024
         ),
         name="attend",
-    )(x, w, cosine, sine, more, pos_q, pos_k)
+    )(*args)
 
 
 def attend_back_kernel(layer, *refs):
     q_ref, k_ref, v_ref, full_ref, out_ref, att_ref, lse_ref, pq_ref, pk_ref, cos_ref, sin_ref, more_ref = refs[:12]
-    three_ref, dw_ref = refs[12:14]
-    pkc, dq, dk, dv, dw, sb, rb, ss, sr = refs[-9:]
-    f, c, _, _ = plane_place()
-    sibling = (f, flip(c, 1))
-    greet([sibling])
+    count = 2 - layer
+    tables, refs = refs[12 : 12 + count], refs[12 + count :]
+    three_ref, dw_ref, *placed = refs[: 2 + count]
+    pkc, dq, dk, dv, dw, sb, rb, ss, sr, sends, receives = refs[-11:]
+    place = plane_place()
+    f, c, _, _ = place
+    peers, sibling, _ = chip_peers(f, c)
+    greet(peers + [sibling])
+    leg = start_leg(list(zip(tables, placed)), peers, c // 2, sends, receives)
     rows_n = q_ref.shape[0]
     half_n = rows_n // 2
     dk[...] = jnp.zeros_like(dk)
@@ -1467,26 +1611,27 @@
         grad = rows_of(1, dv, i)
         if layer == 1:
             grad = 0.5 * grad
-            refs[14][at, :] = grad
+            refs[2 + count][at, :] = grad
         else:
             grad = grad + more_ref[at, :]
         three_ref[at, 256:] = grad.astype(BF)
         return carry
 
     lax.fori_loop(0, rows_n // ROWS, turn, 0)
-
-
-def attend_backward(layer, q, k, v, full, out_w, att, lse, pos_q, pos_k, cosine, sine, more):
-    rows_n = q.shape[0]
-    width = full.shape[1]
+    for copy in leg:
+        copy.wait()
+
+
+def attend_backward(layer, *args):
+    rows_n, width = args[3].shape
     spec = pl.BlockSpec(memory_space=VMEM_SPACE)
-    outs = [((rows_n, 384), BF), ((128, width), BF)]
+    outs = [((rows_n, 384), BF), ((128, width), BF)] + [(u.shape, BF) for u in args[12:]]
     if layer == 1:
         outs += [((rows_n, 128), F32)]
     return pl.pallas_call(
         functools.partial(attend_back_kernel, layer),
         out_shape=[jax.ShapeDtypeStruct(*o) for o in outs],
-        in_specs=[spec] * 12,
+        in_specs=[spec] * len(args),
         out_specs=[spec] * len(outs),
         scratch_shapes=[
             pltpu.VMEM((2, rows_n, 1), F32),
@@ -1498,15 +1643,20 @@
             pltpu.VMEM((2, 2, rows_n // 2, 128), BF),
             pltpu.SemaphoreType.DMA((2,)),
             pltpu.SemaphoreType.DMA((2,)),
+            pltpu.SemaphoreType.DMA((16,)),
+            pltpu.SemaphoreType.DMA((16,)),
         ],
         compiler_params=pltpu.CompilerParams(
-            collective_id=12 + layer, has_side_effects=True, vmem_limit_bytes=24 * 1024 * 1024
+            collective_id=12 + layer, has_side_effects=True, vmem_limit_bytes=32 * 1024 * 1024
         ),
         name="attend_back",
-    )(q, k, v, full, out_w, att, lse, pos_q, pos_k, cosine, sine, more)
-
-
-def unpack_kernel(*refs):
+    )(*args)
+
+
+def unpack_kernel(*every):
+    every[24][...] = every[0][...]
+    every[25][...] = every[1][...]
+    refs = every[2:24] + every[26:]
     for l in range(2):
         cu, od, cq, oo, pre, query, keys, values, mid, gates, upproj = refs[11 * l : 11 * l + 11]
         g_pre, gq, gk, gv, g_out, g_mid, gg, gu, g_down = refs[22 + 9 * l : 31 + 9 * l]
@@ -1534,17 +1684,17 @@
         g_down[...] = od[: g_down.shape[0], :]
 
 
-def unpack(collected, layers):
-    args, outs = [], []
+def unpack(output, tokens_grad, collected, layers):
+    args, outs = [output, tokens_grad], [(output.shape, BF), (tokens_grad.shape, BF)]
     for l, layer in enumerate(layers):
         pre, query, keys, values, out, mid, gates, upproj, down = layer
         args += [*collected[l], pre, query, keys, values, mid, gates, upproj]
         for w in layer:
-            outs.append(w.shape)
+            outs.append((w.shape, F32))
     spec = pl.BlockSpec(memory_space=VMEM_SPACE)
     found = pl.pallas_call(
         unpack_kernel,
-        out_shape=[jax.ShapeDtypeStruct(o, F32) for o in outs],
+        out_shape=[jax.ShapeDtypeStruct(*o) for o in outs],
         in_specs=[spec] * len(args),
         out_specs=[spec] * len(outs),
         compiler_params=pltpu.CompilerParams(vmem_limit_bytes=60 * 1024 * 1024),
@@ -1577,12 +1727,9 @@
     tok = tokens.reshape(ROWS, width)
     cot = cotangent.reshape(ROWS, width)
 
-    def weights(spread):
-        columns = spread[0].reshape(32 * rows_each, wide)
-        return columns, spread[1].reshape(hidden_pad, width), spread[2].reshape(4 * rows_each, width), spread[3]
-
-    full, *spread = begin_call(tok, layers[0], block)
-    ready = [weights(spread), None]
+    full, heads, out_rows, gains, units_one, heads_two, units_two, *downs = begin_call(tok, shards, block)
+    heads_w = [heads.reshape(32 * rows_each, 512), None]
+    units_w, down_w, out_w = [None, None], [None, None], [out_rows.reshape(4 * rows_each, width), None]
 
     plane = 8 * ROWS
     full_type = ((plane, width), BF)
@@ -1591,84 +1738,90 @@
     hidden = tok
     first_values = None
     for layer in range(2):
-        all_w, down_w, out_w, gains = ready[layer]
-        more = gains if layer == 0 else first_values
-        q, k, v, att, lse, *kept = attend(layer, full, all_w, cosine, sine, more, pos_q, pos_k)
+        args = (full, heads_w[layer], cosine, sine, gains if layer == 0 else first_values, pos_q, pos_k)
         x_full = full
         if layer == 0:
-            x_full, first_values = kept
-        args = (att, out_w, hidden, gains)
+            q, k, v, att, lse, x_full, first_values, *legs = attend(0, *args, units_one, heads_two)
+            widths, more = (2 * hidden_pad, 384), (downs[0], layers[1][4])
+        else:
+            q, k, v, att, lse, *legs = attend(1, *args, units_two)
+            widths, more = (2 * hidden_pad,), (downs[1],)
+        outs, sems = share_shapes(rows_each, width, block, widths)
+        middle, mlp_full, table, *found = comm_call(
+            functools.partial(middle_kernel, 2 * layer + 1, len(widths)), [rows_type, full_type] + outs, 1 + layer,
+            (att, out_w[layer], hidden, gains, *legs, *more), True, "middle", sems,
+        )
+        units_w[layer] = table.reshape(32 * rows_each, 2 * hidden_pad)
         if layer == 0:
-            outs, packs, sems = spread_shapes(rows_each, width, block)
-            middle, mlp_full, *spread = comm_call(
-                first_middle_kernel, [rows_type, full_type] + outs, 1, args + tuple(layers[1]), True, "middle", packs + sems
-            )
-            ready[1] = weights(spread)
+            heads_w[1] = found[0].reshape(32 * rows_each, 384)
+            down_w[0] = found[1].reshape(hidden_pad, width)
+            out_w[1] = found[2].reshape(4 * rows_each, width)
         else:
-            middle, mlp_full = comm_call(
-                functools.partial(forward_kernel, 1), [rows_type, full_type], 2, args, True, "middle"
-            )
-        both = jnp.dot(mlp_full, all_w[:, 384:], preferred_element_type=F32)
+            down_w[1] = found[0].reshape(hidden_pad, width)
+        both = jnp.dot(mlp_full, units_w[layer], preferred_element_type=F32)
         gate, up = both[:, :hidden_pad], both[:, hidden_pad:]
         inner = (jax.nn.silu(gate) * up).astype(BF)
         saved.append((x_full, q, k, v, lse, att, mlp_full, gate, up, inner, hidden, middle))
         if layer == 0:
             hidden, full = comm_call(
-                functools.partial(forward_kernel, 0), [rows_type, full_type], 3,
-                (inner, down_w, middle, ready[1][3]), True, "result",
+                functools.partial(forward_kernel, 2), [rows_type, full_type], 3,
+                (inner, down_w[layer], middle, gains), True, "result",
             )
         else:
             output, full = comm_call(
                 turn_kernel, [((ROWS, width), BF), full_type], 4,
-                (inner, down_w, middle, cot), True, "turn",
+                (inner, down_w[layer], middle, cot), True, "turn",
             )
     grad = cot
     passed = cosine
     collected = [None, None]
     for layer in (1, 0):
         x_full, q, k, v, lse, att, mlp_full, gate, up, inner, hidden, middle = saved[layer]
-        all_w, down_w, out_w, gains = ready[layer]
         grad_down = left_product(inner, full)
-        grad_inner = right_product(full, down_w)
+        grad_inner = right_product(full, down_w[layer])
         sigma = jax.nn.sigmoid(gate)
         grad_gate = (grad_inner * up * sigma * (1.0 + gate * (1.0 - sigma))).astype(BF)
         grad_up = (grad_inner * gate * sigma).astype(BF)
         both = jnp.concatenate([grad_gate, grad_up], axis=-1)
         grad_upw = left_product(mlp_full, both)
         results, more = collect_shapes(rows_each, 2 * hidden_pad, block, width, False)
-        grad_mid, full, *got_up = comm_call(
-            functools.partial(back_kernel, 1, 1, (384, wide)), [rows_type, full_type] + results, 5 + layer,
+        grad_mid, full, units_sum, got_down = comm_call(
+            functools.partial(back_kernel, 1, 2 * layer + 1, False), [rows_type, full_type] + results, 5 + layer,
             (
-                both, all_w, grad, middle, gains,
+                both, units_w[layer], grad, middle, gains,
                 grad_upw.astype(BF).reshape(16, 2, rows_each, 2 * hidden_pad),
                 grad_down.astype(BF).reshape(2, 2, block, width),
             ),
             True, "middle_back", more,
         )
-        three, grad_out, *kept = attend_backward(
-            layer, q, k, v, full, out_w, att, lse, pos_q, pos_k, cosine, sine, passed
+        legs = (units_sum,) if layer == 1 else (units_sum, heads_sum)
+        three, grad_out, got_units, *kept = attend_backward(
+            layer, q, k, v, full, out_w[layer], att, lse, pos_q, pos_k, cosine, sine, passed, *legs
         )
+        collected[layer] = [got_units, got_down]
         if layer == 1:
             (passed,) = kept
+        else:
+            collected[1] += [kept[0], two_out]
         grad_qkv = left_product(x_full, three)
         results, more = collect_shapes(rows_each, 384, rows_each, width, True)
         args = (
-            three, all_w, grad_mid, hidden, gains,
+            three, heads_w[layer], grad_mid, hidden, gains,
             grad_qkv.astype(BF).reshape(16, 2, rows_each, 384),
             grad_out.reshape(2, 2, rows_each, width),
         )
         if layer == 1:
-            grad, full, *got_qkv = comm_call(
-                functools.partial(back_kernel, 1, 0, (0, 384)), [rows_type, full_type] + results, 7, args, True,
+            grad, full, heads_sum, two_out = comm_call(
+                functools.partial(back_kernel, 1, 2, True), [rows_type, full_type] + results, 7, args, True,
                 "layer_back", more,
             )
         else:
-            tokens_grad, *got_qkv = comm_call(
-                functools.partial(back_kernel, 0, 0, (0, 384)), [((ROWS, width), BF)] + results, 8, args, False,
+            tokens_grad, *got_heads = comm_call(
+                functools.partial(back_kernel, 0, 0, True), [((ROWS, width), BF)] + results, 8, args, False,
                 "last_back", more,
             )
-        collected[layer] = got_up + got_qkv
-    found = unpack(collected, layers)
+            collected[0] += got_heads
+    output, tokens_grad, *found = unpack(output, tokens_grad, collected, layers)
     return (output.reshape(1, ROWS, width), tokens_grad.reshape(1, ROWS, width), *found)
 
 

time: 570 us -> 542 us (0.951)
  Pallas kernels: 532 us -> 507 us
    pallas_call x8, Pallas kernels: 414 us -> 384 us  [comm_call(): pl.pallas_call(kernel, out_shape=[jax.ShapeDtypeStruct(*o) for o in outs]...]
    pallas_call x1, Pallas kernels: 50.9 us -> 40.3 us  [begin_call(): pl.pallas_call(begin_kernel, out_shape=[jax.ShapeDtypeStruct(*o) for o in...]
    pallas_call x2, Pallas kernels: 26.9 us -> 36.1 us  [attend(): pl.pallas_call(functools.partial(attend_kernel, layer), out_shape=[jax.Sh...]
    pallas_call x2, Pallas kernels: 35.7 us -> 41.6 us  [attend_backward(): pl.pallas_call(functools.partial(attend_back_kernel, layer), out_shape=[j...]
where the time goes in v6:
time: 542 us; the launch traced here: 533 us
  Pallas kernels  507 us (94%)
  matrix products  15.4 us (3%)
    pallas_call x8, Pallas kernels, comm_call(): pl.pallas_call(kernel, out_shape=[jax.ShapeDtypeStruct(*o) for o in outs]...  384 us
    pallas_call x2, Pallas kernels, attend_backward(): pl.pallas_call(functools.partial(attend_back_kernel, layer), out_shape=[j...  41.6 us
    pallas_call x1, Pallas kernels, begin_call(): pl.pallas_call(begin_kernel, out_shape=[jax.ShapeDtypeStruct(*o) for o in...  40.3 us
    pallas_call x2, Pallas kernels, attend(): pl.pallas_call(functools.partial(attend_kernel, layer), out_shape=[jax.Sh...  36.1 us

profile of v6, /device:TPU:0, one launch (start us, length us, event | category | flops | bytes accessed | tf_op | source)
XLA Modules:
  0.0 532.7 jit_solution(15512082253446607140)
XLA Ops:
  0.7 0.8 select_reduce_fusion
  1.5 0.1 reshape_reshape.7
  1.6 0.1 reshape_reshape.6
  1.7 0.1 convert_element_type.61.refs_6_.refs_8_
  1.8 0.1 convert_element_type.59.refs_5_.refs_7_
  1.9 1.9 fusion
  4.0 0.9 pad_maximum_fusion.2
  4.9 0.0 copy-done.4
  5.0 0.1 copy-done.5
  5.0 0.0 copy-done.13
  5.0 0.0 copy-done.14
  5.1 0.0 copy-done.15
  5.1 0.0 copy-done.18
  5.1 0.1 copy-done.21
  5.2 0.1 copy-done.22
  5.3 40.3 %begin.1 = (bf16[1024,1024]{1,0:T(8,128)(2,1)S(1)}, bf16[2,8,2,32,512]{4,3,2,1,0:T(8,128)(2,1)S(1)}, bf16[4,32,1024]{2,1,0:T(8,128)(2,1)S(1)}, f32[8,1024]{1,0:T...) custom-call(bf16[128,1024]{1,0:T(8,128)(2,1)S(1)} %bitcast.60, ...), custom_call_target="tpu_custom_call" | custom-call | tf_op jit(solution)/shard_map/begin/pallas_call | solution.py:1205
  45.6 18.8 %attend.2 = (bf16[1024,128]{1,0:T(8,128)(2,1)S(1)}, bf16[2,1024,128]{2,1,0:T(8,128)(2,1)S(1)}, bf16[2,1024,128]{2,1,0:T(8,128)(2,1)S(1)}, bf16[1024,128]{1,0:T(8...) custom-call(bf16[1024,1024]{1,0:T(8,128)(2,1)S(1)} %get-tuple-elemen, ...), custom_call_target="tpu_custom_call" | custom-call | tf_op jit(solution)/shard_map/attend/pallas_call | solution.py:1524
  64.4 51.0 %middle.2 = (f32[128,1024]{1,0:T(8,128)S(1)}, bf16[1024,1024]{1,0:T(8,128)(2,1)S(1)}, bf16[2,8,2,32,768]{4,3,2,1,0:T(8,128)(2,1)S(1)}, bf16[2,8,2,32,384]{4,3,2,...) custom-call(bf16[1024,128]{1,0:T(8,128)(2,1)S(1)} %get-tuple-element.106.left_ref.refs_5_, ...), custom_call_target="tpu_custom_call" | custom-call | tf_op jit(solution)/shard_map/middle/pallas_call | solution.py:890
  115.5 1.8 fusion.9
  117.3 0.5 multiply_convert_fusion.5.left_ref
  117.8 46.1 %result.1 = (f32[128,1024]{1,0:T(8,128)S(1)}, bf16[1024,1024]{1,0:T(8,128)(2,1)S(1)}) custom-call(bf16[1024,384]{1,0:T(8,128)(2,1)S(1)} %multiply_convert_fusion.5.left_ref, bf16[384,1024]{1,0:T(8,128)(2,1)S(1)} %bitcast.77, f32[128,1024]{1,0:T(8,128)S(1)} %get-tuple-element.114.res_ref.hid_ref, f32[8,1024]{1,0:T(8,128)S(1)} %get-tuple-element.103.refs_4_.gain_ref), custom_call_target="tpu_custom_call" | custom-call | tf_op jit(solution)/shard_map/result/pallas_call | solution.py:890
  163.9 17.3 %attend.3 = (bf16[1024,128]{1,0:T(8,128)(2,1)S(1)}, bf16[2,1024,128]{2,1,0:T(8,128)(2,1)S(1)}, bf16[2,1024,128]{2,1,0:T(8,128)(2,1)S(1)}, bf16[1024,128]{1,0:T(8...) custom-call(bf16[1024,1024]{1,0:T(8,128)(2,1)S(1)} %get-tuple-element.115.refs_0_, ...), custom_call_target="tpu_custom_call" | custom-call | tf_op jit(solution)/shard_map/attend/pallas_call | solution.py:1524
  181.1 49.2 %middle.3 = (f32[128,1024]{1,0:T(8,128)S(1)}, bf16[1024,1024]{1,0:T(8,128)(2,1)S(1)}, bf16[2,8,2,32,768]{4,3,2,1,0:T(8,128)(2,1)S(1)}, bf16[4,96,1024]{2,1,0:T(8,128)(2,1)S(1)}) custom-call(bf16[1024,128]{1,0:T(8,128)(2,1)S(1)} %get-tuple-element.119.left_ref.refs_5_, bf16[128,1024]{1,0:T(8,128)(2,1)S(1)} %bitcast.71, ...), custom_call_target="tpu_custom_call" | custom-call | tf_op jit(solution)/shard_map/middle/pallas_call | solution.py:890
  230.4 1.8 fusion.10
  232.2 0.4 multiply_convert_fusion.4.left_ref
  232.6 0.5 copy-done.1
  233.1 48.8 %turn.1 = (bf16[128,1024]{1,0:T(8,128)(2,1)S(1)}, bf16[1024,1024]{1,0:T(8,128)(2,1)S(1)}) custom-call(bf16[1024,384]{1,0:T(8,128)(2,1)S(1)} %multiply_convert_fusion.4.left_ref, bf16[384,1024]{1,0:T(8,128)(2,1)S(1)} %bitcast.79, f32[128,1024]{1,0:T(8,128)S(1)} %get-tuple-element.127.res_ref.hid_ref, bf16[128,1024]{1,0:T(8,128)(2,1)S(1)} %bitcast.69), custom_call_target="tpu_custom_call" | custom-call | tf_op jit(solution)/shard_map/turn/pallas_call | solution.py:890
  281.9 1.7 multiply_convert_fusion.3
  283.6 1.9 convolution_convert_fusion.1
  285.5 0.1 pad_maximum_fusion.left_ref
  285.6 1.0 convolution_convert_fusion.5
  286.7 54.6 %middle_back.2 = (f32[128,1024]{1,0:T(8,128)S(1)}, bf16[1024,1024]{1,0:T(8,128)(2,1)S(1)}, bf16[8,32,768]{2,1,0:T(8,128)(2,1)S(1)}, f32[96,1024]{1,0:T(8,128)S(1)}) custom-call(bf16[1024,768]{1,0:T(8,128)(2,1)S(1)} %pad_maximum_fusion.left_ref, bf16[1024,768]{1,0:T(8,128)(2,1)S(1)} %bitcast.66, bf16[128,1024]{1,0:T(8,128)(2,1)S(1)} %bitcast.70, ...), custom_call_target="tpu_custom_call" | custom-call | tf_op jit(solution)/shard_map/middle_back/pallas_call | solution.py:890
  341.3 0.7 copy-done.6
  342.0 19.5 %attend_back.2 = (bf16[1024,384]{1,0:T(8,128)(2,1)S(1)}, bf16[128,1024]{1,0:T(8,128)(2,1)S(1)}, bf16[8,32,768]{2,1,0:T(8,128)(2,1)S(1)}, f32[1024,128]{1,0:T(8,128)S(1)}) custom-call(bf16[1024,128]{1,0:T(8,128)(2,1)S(1)} %get-tuple-element.132.refs_0_, bf16[2,1024,128]{2,1,0:T(8,128)(2,1)S(1)} %get-tuple-element.133.refs_1_, ...), custom_call_target="tpu_custom_call" | custom-call | tf_op jit(solution)/shard_map/attend_back/pallas_call | solution.py:1631
  361.5 1.3 convolution_convert_fusion.4
  362.8 53.0 %layer_back.1 = (f32[128,1024]{1,0:T(8,128)S(1)}, bf16[1024,1024]{1,0:T(8,128)(2,1)S(1)}, bf16[8,32,384]{2,1,0:T(8,128)(2,1)S(1)}, f32[32,1024]{1,0:T(8,128)S(1)}) custom-call(bf16[1024,384]{1,0:T(8,128)(2,1)S(1)} %get-tuple-element.139.left_ref, bf16[1024,384]{1,0:T(8,128)(2,1)S(1)} %bitcast.59, f32[128,1024]{1,0:T(8,128)S(1)} %get-tuple-element.140.grad_ref, ...), custom_call_target="tpu_custom_call" | custom-call | tf_op jit(solution)/shard_map/layer_back/pallas_call | solution.py:890
  415.7 1.7 multiply_convert_fusion.1
  417.5 1.9 convolution_convert_fusion
  419.4 0.1 pad_maximum_fusion.1.left_ref
  419.5 1.0 convolution_convert_fusion.3
  420.5 51.2 %middle_back.3 = (f32[128,1024]{1,0:T(8,128)S(1)}, bf16[1024,1024]{1,0:T(8,128)(2,1)S(1)}, bf16[8,32,768]{2,1,0:T(8,128)(2,1)S(1)}, f32[96,1024]{1,0:T(8,128)S(1)}) custom-call(bf16[1024,768]{1,0:T(8,128)(2,1)S(1)} %pad_maximum_fusion.1.left_ref, bf16[1024,768]{1,0:T(8,128)(2,1)S(1)} %bitcast.64, f32[128,1024]{1,0:T(8,128)S(1)} %get-tuple-element.143.grad_ref, ...), custom_call_target="tpu_custom_call" | custom-call | tf_op jit(solution)/shard_map/middle_back/pallas_call | solution.py:890
  471.7 22.2 %attend_back.3 = (bf16[1024,384]{1,0:T(8,128)(2,1)S(1)}, bf16[128,1024]{1,0:T(8,128)(2,1)S(1)}, bf16[8,32,768]{2,1,0:T(8,128)(2,1)S(1)}, bf16[8,32,384]{2,1,0:T(8,128)(2,1)S(1)}) custom-call(bf16[1024,128]{1,0:T(8,128)(2,1)S(1)} %get-tuple-element.129.refs_0_, bf16[2,1024,128]{2,1,0:T(8,128)(2,1)S(1)} %get-tuple-element.130.refs_1_, ...), custom_call_target="tpu_custom_call" | custom-call | tf_op jit(solution)/shard_map/attend_back/pallas_call | solution.py:1631
  494.0 1.3 convolution_convert_fusion.2
  495.3 30.3 %last_back.1 = (bf16[128,1024]{1,0:T(8,128)(2,1)S(1)}, bf16[8,32,384]{2,1,0:T(8,128)(2,1)S(1)}, f32[32,1024]{1,0:T(8,128)S(1)}) custom-call(bf16[1024,384]{1,0:T(8,128)(2,1)S(1)} %get-tuple-element.149.left_ref, bf16[1024,512]{1,0:T(8,128)(2,1)S(1)} %bitcast.55, f32[128,1024]{1,0:T(8,128)S(1)} %get-tuple-element.150.grad_ref, ...), custom_call_target="tpu_custom_call" | custom-call | tf_op jit(solution)/shard_map/last_back/pallas_call | solution.py:890
  525.6 0.7 copy-done.17
  526.3 0.7 copy-done.20
  527.0 0.6 copy-done.24
  527.6 4.6 unpack.1
  (53 shorter events, 0.2 us)
Async XLA Ops:
  3.8 1.1 copy-start
  3.8 1.1 copy-start.2
  3.8 1.1 copy-start.3
  3.8 1.1 copy-start.4
  3.8 1.2 copy-start.5
  3.8 1.2 copy-start.10
  3.8 1.2 copy-start.11
  3.9 1.2 copy-start.12
  3.9 1.2 copy-start.13
  3.9 1.2 copy-start.14
  3.9 1.2 copy-start.15
  3.9 1.2 copy-start.18
  3.9 1.3 copy-start.21
  3.9 1.4 copy-start.22
  3.9 1.4 copy-start.25
  4.0 1.3 copy-start.26
  4.0 1.3 copy-start.27
  4.0 1.3 copy-start.28
  4.0 1.3 copy-start.29
  232.2 1.0 copy-start.1
  281.9 1.7 copy-start.16
  341.2 0.7 copy-start.6
  361.5 1.3 copy-start.7
  415.7 1.7 copy-start.23
  471.7 22.2 %copy-start.8 = (f32[96,1024]{1,0:T(8,128)}, f32[96,1024]{1,0:T(8,128)S(1)}, u32[]{:S(2)}) copy-start(f32[96,1024]{1,0:T(8,128)S(1)} %get-tuple-element.155.every_3_) | copy-start | bytes 1179652
  493.9 1.3 copy-start.9
  493.9 1.3 copy-start.19
  525.6 0.7 copy-start.17
  526.3 0.7 copy-start.20
  526.9 0.6 copy-start.24

commit v7 on v6

--- a/solution.py
+++ b/solution.py
@@ -572,15 +572,15 @@
 
 
 class Plane:
-    def __init__(self, place, inner):
-        f, c, y, z = place
-        self.y, self.inner = y, inner
-        self.mirrored = z // 2
-        sign = 1 - 2 * self.mirrored
-        self.own = 1 if inner else 0
-        self.across = (f, flip(c, 2))
-        self.chip_at = [(f, c + 4 * sign * (near - self.own)) for near in range(4)]
-        self.sent = []
+    def __init__(self, place):
+        self.f, self.c, self.y, self.z = place
+        self.mirrored = self.z // 2
+        self.sign = 1 - 2 * self.mirrored
+        self.own = self.z * (3 - self.z) // 2
+        self.across = (self.f, flip(self.c, 2))
+
+    def chip(self, near):
+        return self.f, self.c + 4 * self.sign * (near - self.own)
 
     def at(self, near):
         return near + self.mirrored * (3 - 2 * near)
@@ -588,18 +588,26 @@
     def slot(self, half, near):
         return 4 * half + self.at(near)
 
-    def start(self, copy):
+    def both_kinds(self, run):
+        @pl.when(self.own == 1)
+        def _():
+            run(True)
+
+        @pl.when(self.own == 0)
+        def _():
+            run(False)
+
+
+def emit(copy, live):
+    if live:
         copy.start()
-        self.sent.append(copy)
-
-    def finish(self):
-        for copy in self.sent:
-            copy.wait_send()
+    else:
+        copy.wait_send()
 
 
 class Reduce(Plane):
-    def __init__(self, place, inner, product, bufs, sems):
-        super().__init__(place, inner)
+    def __init__(self, place, product, bufs, sems):
+        super().__init__(place)
         self.product = product
         self.sy, self.ry, self.acc, self.pb, self.su, self.sd, self.rb, self.ra = bufs
         self.ys, self.yr, self.us, self.ds, self.br, self.ar = sems
@@ -620,17 +628,14 @@
         there = slot if there is None else there
         src, send = (self.su, self.us) if upward else (self.sd, self.ds)
         dst, sem = (self.rb, self.br) if first else (self.ra, self.ar)
-        src[slot] = value.astype(BF)
-        self.start(remote(src.at[slot], dst.at[there], send.at[slot], sem.at[there], self.chip_at[target]))
-
-    def cross(self, slot, value):
-        self.sy[slot] = value.astype(BF)
-        self.start(self.y_copy(slot))
+        if value is not None:
+            src[slot] = value.astype(BF)
+        copy = remote(src.at[slot], dst.at[there], send.at[slot], sem.at[there], self.chip(target))
+        emit(copy, value is not None)
 
     def order(self, step):
-        near = 3 - step
-        if self.inner:
-            near = jnp.where(step == 0, 3, jnp.where(step == 1, 0, 4 - step))
+        inner = jnp.where(step == 0, 3, jnp.where(step == 1, 0, 4 - step))
+        near = jnp.where(self.own == 1, inner, 3 - step)
         return near, near + self.mirrored * (3 - 2 * near)
 
     def products(self):
@@ -648,17 +653,6 @@
 
             return carry
 
-        lax.fori_loop(0, 4, other_row, 0)
-        for near in range(4):
-            self.sent.append(self.y_copy(self.slot(0, near)))
-        for near in (1, 2):
-            self.sent.append(self.y_copy(self.slot(1, near)))
-        if self.inner:
-            self.pass_on(self.pb[self.at(3)], True, ODD, 3, True)
-            self.pass_on(self.pb[self.at(0)], False, ODD, 0, False)
-        else:
-            self.pass_on(self.pb[self.at(3)], True, ODD, 3, False, ODD + 1)
-
         def own_row(step, carry):
             near, block = self.order(step)
             value = self.product(2 * block + self.y)
@@ -666,48 +660,69 @@
             self.acc[4 + block] = value[HALF:]
             return carry
 
+        lax.fori_loop(0, 4, other_row, 0)
+        self.both_kinds(lambda inner: self.odd(inner, True))
         lax.fori_loop(0, 4, own_row, 0)
-        far = self.slot(1, 3)
-        if self.inner:
-            end = self.slot(1, 0)
-            self.pass_on(self.acc[end], False, end, 0, False)
-            self.pass_on(self.acc[far] + self.got(True, far), True, far, 3, True)
+
+    def odd(self, inner, live):
+        far = self.pb[self.at(3)] if live else None
+        if inner:
+            self.pass_on(far, True, ODD, 3, True)
+            self.pass_on(self.pb[self.at(0)] if live else None, False, ODD, 0, False)
         else:
-            self.pass_on(self.acc[far], True, far, 1, True)
-
-    def relay(self, half, near):
+            self.pass_on(far, True, ODD, 3, False, ODD + 1)
+
+    def relay(self, half, near, inner, live, plain=False):
         slot = self.slot(half, near)
-        value = self.acc[slot] + self.got_y(slot)
-        if not self.inner:
+        upward = not inner or near != 0
+        value = None
+        if live:
+            value = self.acc[slot]
+            if not plain:
+                value = value + self.got_y(slot)
+            if inner and upward:
+                value = value + self.got(True, slot)
+        if not inner:
             self.pass_on(value, True, slot, 1, True)
         elif near == 0:
             self.pass_on(value, False, slot, 0, False)
         else:
-            self.pass_on(value + self.got(True, slot), True, slot, near, near == 3)
-
-    def relays(self):
-        if self.inner:
-            self.relay(0, 3)
-            self.relay(0, 0)
-            self.relay(0, 2)
-            self.relay(1, 2)
+            self.pass_on(value, True, slot, near, near == 3)
+
+    def relays(self, inner, live):
+        if inner:
+            self.relay(1, 0, inner, live, True)
+            self.relay(1, 3, inner, live, True)
+            for half, near in ((0, 3), (0, 0), (0, 2), (1, 2)):
+                self.relay(half, near, inner, live)
             return
-        self.relay(0, 3)
-        self.relay(0, 2)
-        self.relay(1, 2)
-        odd = self.pb[self.at(0)] + self.got(False, ODD) + self.got(True, ODD) + self.got(False, ODD + 1)
-        self.cross(self.slot(1, 0), odd)
-        self.relay(0, 1)
-        self.relay(1, 1)
+        self.relay(1, 3, inner, live, True)
+        for half, near in ((0, 3), (0, 2), (1, 2), (0, 1), (1, 1)):
+            self.relay(half, near, inner, live)
+        slot = self.slot(1, 0)
+        if live:
+            odd = self.pb[self.at(0)] + self.got(False, ODD) + self.got(True, ODD) + self.got(False, ODD + 1)
+            self.sy[slot] = odd.astype(BF)
+        emit(self.y_copy(slot), live)
 
     def own_sum(self, half):
         slot = self.slot(half, self.own)
         return self.acc[slot] + self.got_y(slot) + self.got(True, slot) + self.got(False, slot)
 
+    def finish(self):
+        for half, near in ((0, 0), (0, 1), (0, 2), (0, 3), (1, 1), (1, 2)):
+            self.y_copy(self.slot(half, near)).wait_send()
+
+        def left(inner):
+            self.odd(inner, False)
+            self.relays(inner, False)
+
+        self.both_kinds(left)
+
 
 class Gather(Plane):
-    def __init__(self, place, inner, full, sems):
-        super().__init__(place, inner)
+    def __init__(self, place, full, sems):
+        super().__init__(place)
         self.full = full
         self.ys, self.yr, self.us, self.ds, self.zr = sems
 
@@ -715,29 +730,30 @@
         start = (self.at(near) * 2 + side) * ROWS + half * HALF
         return self.full.at[pl.ds(pl.multiple_of(start, HALF), HALF)]
 
-    def to_row(self, part, sem, slot, target):
-        self.start(remote(part, part, sem, self.zr.at[slot], self.chip_at[target]))
-
-    def to_other_row(self, half, near):
+    def to_row(self, part, sem, slot, target, live):
+        emit(remote(part, part, sem, self.zr.at[slot], self.chip(target)), live)
+
+    def to_other_row(self, half, near, live):
         part = self.rows(half, near, self.y)
         slot = self.slot(half, near)
-        self.start(remote(part, part, self.ys.at[slot], self.yr.at[slot], self.across))
-
-    def send_own(self, half):
+        emit(remote(part, part, self.ys.at[slot], self.yr.at[slot], self.across), live)
+
+    def send_own(self, half, live=True):
         part = self.rows(half, self.own, self.y)
         slot = self.slot(half, self.own)
-        self.to_row(part, self.us.at[slot], slot, 2)
-        self.to_row(part, self.ds.at[slot], slot, 0 if self.inner else 1)
-        self.to_other_row(half, self.own)
-
-    def take(self, half, near):
+        self.to_other_row(half, self.own, live)
+        self.to_row(part, self.ds.at[slot], slot, 1 - self.own, live)
+        self.to_row(part, self.us.at[slot], slot, 2, live)
+
+    def take(self, half, near, inner, live):
         part = self.rows(half, near, self.y)
         slot = self.slot(half, near)
-        arrived(part, self.zr.at[slot], self.across)
-        if self.inner and near in (2, 3):
-            self.to_row(part, self.ds.at[slot], slot, 0)
+        if live:
+            arrived(part, self.zr.at[slot], self.across)
         if half == 0 or near in (1, 2):
-            self.to_other_row(half, near)
+            self.to_other_row(half, near, live)
+        if inner and near in (2, 3):
+            self.to_row(part, self.ds.at[slot], slot, 0, live)
 
     def odd_slot(self, near):
         return ODD + self.at(near) // 3
@@ -748,89 +764,80 @@
     def got_y(self, half, near):
         arrived(self.rows(half, near, 1 - self.y), self.yr.at[self.slot(half, near)], self.across)
 
-    def forward(self, half):
-        others = (0, 2, 3) if self.inner else (1, 2, 3)
-        if half == 0:
-            for near in others:
-                self.take(0, near)
-            return
-        if not self.inner:
-            self.got_y(1, 0)
+    def forward(self, half, inner, live):
+        others = (2, 3, 0) if inner else (1, 2, 3)
+        if half == 1 and not inner:
             part = self.rows(1, 0, 1 - self.y)
             slot = self.odd_slot(0)
-            self.to_row(part, self.us.at[8], slot, 3)
-            self.to_row(part, self.us.at[9], slot, 2)
-            self.to_row(part, self.ds.at[8], slot, 1)
+            if live:
+                self.got_y(1, 0)
+            self.to_row(part, self.us.at[8], slot, 3, live)
+            self.to_row(part, self.us.at[9], slot, 2, live)
+            self.to_row(part, self.ds.at[8], slot, 1, live)
         for near in others:
-            self.take(1, near)
-        if self.inner:
+            self.take(half, near, inner, live)
+        if half == 1 and inner and live:
             self.take_odd(0)
-        self.take_odd(3)
-        for near in range(4):
-            self.got_y(0, near)
-        for near in (1, 2):
-            self.got_y(1, near)
-
-
-def both_kinds(place, run):
-    z = place[3]
-
-    @pl.when((z > 0) & (z < 3))
-    def _():
-        run(True)
-
-    @pl.when((z == 0) | (z == 3))
-    def _():
-        run(False)
-
-
-def exchange(place, product, settle, full, scratch, extra=None, rows=None):
+
+    def pass_half(self, half):
+        self.both_kinds(lambda inner: self.forward(half, inner, True))
+        if half == 1:
+            self.take_odd(3)
+            for near in range(4):
+                self.got_y(0, near)
+            for near in (1, 2):
+                self.got_y(1, near)
+
+    def finish(self):
+        self.send_own(0, False)
+        self.send_own(1, False)
+
+        def left(inner):
+            self.forward(0, inner, False)
+            self.forward(1, inner, False)
+
+        self.both_kinds(left)
+
+
+def exchange(place, product, settle, full, scratch, more=None, rows=None):
     f, c, y, z = place
-    if extra is None:
+    if more is None:
         greet(row_peers(f, c, z) + [(f, flip(c, 2))])
     else:
         peers, sibling, twin = chip_peers(f, c)
         greet(peers + [sibling, twin])
     own = (z * 2 + y) * ROWS
+    reduce = Reduce(place, product, scratch[:8], scratch[8:14])
+    gather = None if full is None else Gather(place, full, scratch[14:19])
     if rows is not None:
         full[pl.ds(pl.multiple_of(own, ROWS), ROWS), :] = rows
-
-    def run(inner):
-        parts = []
-        more = None if extra is None else extra(place)
-        reduce = Reduce(place, inner, product, scratch[:8], scratch[8:14])
-        reduce.products()
-        if more is not None:
-            more.first()
-            more.early()
-            parts.append(more)
-        parts.append(reduce)
-        if full is not None:
-            gather = Gather(place, inner, full, scratch[14:19])
-            parts.append(gather)
-        reduce.relays()
-        if rows is not None:
-            gather.send_own(0)
-            gather.send_own(1)
-        if more is not None:
-            more.second()
-        for half in range(2):
-            new = settle(half, reduce.own_sum(half))
-            if full is not None and rows is None:
-                full[pl.ds(pl.multiple_of(own + half * HALF, HALF), HALF), :] = new
-                gather.send_own(half)
-            if more is not None and half == 0:
-                more.third()
-        if full is not None:
-            gather.forward(0)
-        if more is not None:
-            more.fourth()
-        if full is not None:
-            gather.forward(1)
-        for part in parts:
-            part.finish()
-
-    both_kinds(place, run)
+    reduce.products()
+    if more is not None:
+        more.first()
+        more.early()
+    reduce.both_kinds(lambda inner: reduce.relays(inner, True))
+    if rows is not None:
+        gather.send_own(0)
+        gather.send_own(1)
+    if more is not None:
+        more.second()
+    for half in range(2):
+        new = settle(half, reduce.own_sum(half))
+        if gather is not None and rows is None:
+            full[pl.ds(pl.multiple_of(own + half * HALF, HALF), HALF), :] = new
+            gather.send_own(half)
+        if more is not None and half == 0:
+            more.third()
+    if gather is not None:
+        gather.pass_half(0)
+    if more is not None:
+        more.fourth()
+    if gather is not None:
+        gather.pass_half(1)
+        gather.finish()
+    reduce.finish()
+    if more is not None:
+        more.finish()
 
 
 def half_rows(half):
@@ -1045,25 +1052,25 @@
         for n, (src, dst) in enumerate(zip(sources, self.places(self.f))):
             self.crossed.append(self.send(src, dst, self.xs.at[n], self.xr.at[n], self.twin))
             self.inner.append(self.send(src, dst, self.ss.at[n], self.sr.at[n], self.sibling))
+        if self.out:
+            self.out.first()
+
+    def early(self):
+        pass
+
+    def second(self):
+        if self.out:
+            self.out.second()
+
+    def third(self):
+        pass
+
+    def fourth(self):
         for src, r in self.tables:
             for j in range(8):
                 r[self.f, j, self.core] = src[j]
         for src, d in self.downs:
             d[2 * self.f + self.core] = src[...]
-        if self.out:
-            self.out.first()
-
-    def early(self):
-        pass
-
-    def second(self):
-        if self.out:
-            self.out.second()
-
-    def third(self):
-        pass
-
-    def fourth(self):
         count = len(self.crossed)
         for n, part in enumerate(self.places(1 - self.f)):
             self.crossed[n].wait_recv()
@@ -1160,33 +1167,30 @@
         a[chip, :, 384:] = riders.astype(BF)
     greet(peers + [sibling, twin])
 
-    def run(inner):
-        gather = Gather(place, inner, full, sems[:5])
-        spread = Spread(place, a, r, sems[5:11])
-        out = OutRows(place, ones[4], o, sems[11:])
-        gather.send_own(0)
-        spread.first()
-        out.first()
-        gather.send_own(1)
-        for n in range(18):
-            if n not in soon:
-                copies[n].wait()
-        pack_units(ones[6], ones[7], n1.shape[0], u1)
-        pack_heads(twos[1], twos[2], twos[3], h2)
-        pack_units(twos[6], twos[7], n1.shape[0], u2)
-        pack_down(ones[8], n1)
-        pack_down(twos[8], n2)
-        gather.forward(0)
-        spread.second()
-        out.second()
-        gather.forward(1)
-        spread.third()
-        out.third()
-        gather.finish()
-        spread.finish()
-        out.finish()
-
-    both_kinds(place, run)
+    gather = Gather(place, full, sems[:5])
+    spread = Spread(place, a, r, sems[5:11])
+    out = OutRows(place, ones[4], o, sems[11:])
+    gather.send_own(0)
+    spread.first()
+    out.first()
+    gather.send_own(1)
+    for n in range(18):
+        if n not in soon:
+            copies[n].wait()
+    pack_units(ones[6], ones[7], n1.shape[0], u1)
+    gather.pass_half(0)
+    spread.second()
+    out.second()
+    pack_heads(twos[1], twos[2], twos[3], h2)
+    pack_units(twos[6], twos[7], n1.shape[0], u2)
+    pack_down(ones[8], n1)
+    pack_down(twos[8], n2)
+    gather.pass_half(1)
+    spread.third()
+    out.third()
+    gather.finish()
+    spread.finish()
+    out.finish()
     count = tok.shape[1]
     columns = r[:, :, :, :, 384:].reshape(count, 128)
     pick = lax.broadcasted_iota(jnp.int32, (8, 128), 0) == lax.broadcasted_iota(jnp.int32, (8, 128), 1)
@@ -1229,13 +1233,12 @@
         new_ref[half_rows(half), :] = hidden
         return (hidden * norm_rows(hidden) * gain_ref[row : row + 1, :]).astype(BF)
 
-    def extra(place):
-        tables = list(zip(ins[:count], results[:count]))
-        downs = [(ins[count], results[count])]
-        out = (ins[3], results[3]) if count == 2 else None
-        return Share(place, tables, downs, out, scratch[19:])
-
-    exchange(plane_place(), make_product(left_ref, right_ref, False), settle, full_ref, scratch, extra)
+    tables = list(zip(ins[:count], results[:count]))
+    downs = [(ins[count], results[count])]
+    out = (ins[3], results[3]) if count == 2 else None
+    place = plane_place()
+    share = Share(place, tables, downs, out, scratch[19:])
+    exchange(place, make_product(left_ref, right_ref, False), settle, full_ref, scratch, share)
 
 
 def share_shapes(rows, width, block, widths):
@@ -1291,7 +1294,7 @@
         for n in range(3):
             self.inner_copy(n).start()
 
-    def early(self):
+    def cross(self):
         f, core = self.f, self.core
         self.inner_copy(0).wait_recv()
         for i in range(8):
@@ -1311,7 +1314,7 @@
         def _():
             self.twin_copy().start()
 
-    def second(self):
+    def add_up(self):
         f, core = self.f, self.core
         self.inner_copy(1).wait_recv()
         for i in range(8):
@@ -1339,11 +1342,22 @@
             self.yt[...] = (self.th[1 - y].astype(F32) + self.xh[1 - y].astype(F32)).astype(BF)
             self.near_copy().start()
 
+    def early(self):
+        if self.final:
+            self.cross()
+
+    def second(self):
+        if self.final:
+            self.add_up()
+        else:
+            self.cross()
+
     def third(self):
         pass
 
     def fourth(self):
-        pass
+        if not self.final:
+            self.add_up()
 
     def finish(self):
         if self.crosses_near:
@@ -1391,12 +1405,11 @@
         new_ref[at, :] = new.astype(new_ref.dtype)
         return new.astype(BF)
 
-    def extra(place):
-        return Collect(place, (g, h), results, scratch[14 + 5 * gathers :], not gathers)
-
+    place = plane_place()
+    collect = Collect(place, (g, h), results, scratch[14 + 5 * gathers :], not gathers)
     lanes = (0, 384) if crosses else None
     product = make_product(left_ref, right_ref, True, lanes)
-    exchange(plane_place(), product, settle, full_ref, scratch, extra)
+    exchange(place, product, settle, full_ref, scratch, collect)
 
 
 def head_lanes(head):

time: 542 us -> 513 us (0.946)
  Pallas kernels: 507 us -> 479 us
    pallas_call x8, Pallas kernels: 384 us -> 360 us  [comm_call(): pl.pallas_call(kernel, out_shape=[jax.ShapeDtypeStruct(*o) for o in outs]...]
where the time goes in v7:
time: 513 us; the launch traced here: 505 us
  Pallas kernels  479 us (93%)
  matrix products  15.4 us (3%)
    pallas_call x8, Pallas kernels, comm_call(): pl.pallas_call(kernel, out_shape=[jax.ShapeDtypeStruct(*o) for o in outs]...  360 us
    pallas_call x2, Pallas kernels, attend_backward(): pl.pallas_call(functools.partial(attend_back_kernel, layer), out_shape=[j...  41.7 us
    pallas_call x1, Pallas kernels, begin_call(): pl.pallas_call(begin_kernel, out_shape=[jax.ShapeDtypeStruct(*o) for o in...  38.3 us
    pallas_call x2, Pallas kernels, attend(): pl.pallas_call(functools.partial(attend_kernel, layer), out_shape=[jax.Sh...  34.2 us

profile of v7, /device:TPU:0, one launch (start us, length us, event | category | flops | bytes accessed | tf_op | source)
XLA Modules:
  0.0 504.6 jit_solution(8690231574715223966)
XLA Ops:
  0.7 0.8 select_reduce_fusion
  1.5 0.1 reshape_reshape.7
  1.6 0.1 reshape_reshape.6
  1.7 0.1 convert_element_type.61.refs_6_.refs_8_
  1.8 0.1 convert_element_type.59.refs_5_.refs_7_
  1.9 1.9 fusion
  4.0 0.9 pad_maximum_fusion.2
  4.9 0.0 copy-done.4
  5.0 0.1 copy-done.5
  5.0 0.0 copy-done.13
  5.0 0.0 copy-done.14
  5.1 0.0 copy-done.15
  5.1 0.0 copy-done.18
  5.1 0.1 copy-done.21
  5.2 0.1 copy-done.22
  5.3 38.3 %begin.1 = (bf16[1024,1024]{1,0:T(8,128)(2,1)S(1)}, bf16[2,8,2,32,512]{4,3,2,1,0:T(8,128)(2,1)S(1)}, bf16[4,32,1024]{2,1,0:T(8,128)(2,1)S(1)}, f32[8,1024]{1,0:T...) custom-call(bf16[128,1024]{1,0:T(8,128)(2,1)S(1)} %bitcast.60, ...), custom_call_target="tpu_custom_call" | custom-call | tf_op jit(solution)/shard_map/begin/pallas_call | solution.py:1209
  43.6 18.6 %attend.2 = (bf16[1024,128]{1,0:T(8,128)(2,1)S(1)}, bf16[2,1024,128]{2,1,0:T(8,128)(2,1)S(1)}, bf16[2,1024,128]{2,1,0:T(8,128)(2,1)S(1)}, bf16[1024,128]{1,0:T(8...) custom-call(bf16[1024,1024]{1,0:T(8,128)(2,1)S(1)} %get-tuple-elemen, ...), custom_call_target="tpu_custom_call" | custom-call | tf_op jit(solution)/shard_map/attend/pallas_call | solution.py:1537
  62.2 48.7 %middle.2 = (f32[128,1024]{1,0:T(8,128)S(1)}, bf16[1024,1024]{1,0:T(8,128)(2,1)S(1)}, bf16[2,8,2,32,768]{4,3,2,1,0:T(8,128)(2,1)S(1)}, bf16[2,8,2,32,384]{4,3,2,...) custom-call(bf16[1024,128]{1,0:T(8,128)(2,1)S(1)} %get-tuple-element.106.left_ref.refs_5_, ...), custom_call_target="tpu_custom_call" | custom-call | tf_op jit(solution)/shard_map/middle/pallas_call | solution.py:897
  111.0 1.8 fusion.9
  112.8 0.5 multiply_convert_fusion.5.left_ref
  113.2 44.0 %result.1 = (f32[128,1024]{1,0:T(8,128)S(1)}, bf16[1024,1024]{1,0:T(8,128)(2,1)S(1)}) custom-call(bf16[1024,384]{1,0:T(8,128)(2,1)S(1)} %multiply_convert_fusion.5.left_ref, bf16[384,1024]{1,0:T(8,128)(2,1)S(1)} %bitcast.77, f32[128,1024]{1,0:T(8,128)S(1)} %get-tuple-element.114.res_ref.hid_ref, f32[8,1024]{1,0:T(8,128)S(1)} %get-tuple-element.103.refs_4_.gain_ref), custom_call_target="tpu_custom_call" | custom-call | tf_op jit(solution)/shard_map/result/pallas_call | solution.py:897
  157.2 15.6 %attend.3 = (bf16[1024,128]{1,0:T(8,128)(2,1)S(1)}, bf16[2,1024,128]{2,1,0:T(8,128)(2,1)S(1)}, bf16[2,1024,128]{2,1,0:T(8,128)(2,1)S(1)}, bf16[1024,128]{1,0:T(8...) custom-call(bf16[1024,1024]{1,0:T(8,128)(2,1)S(1)} %get-tuple-element.115.refs_0_, ...), custom_call_target="tpu_custom_call" | custom-call | tf_op jit(solution)/shard_map/attend/pallas_call | solution.py:1537
  172.8 46.8 %middle.3 = (f32[128,1024]{1,0:T(8,128)S(1)}, bf16[1024,1024]{1,0:T(8,128)(2,1)S(1)}, bf16[2,8,2,32,768]{4,3,2,1,0:T(8,128)(2,1)S(1)}, bf16[4,96,1024]{2,1,0:T(8,128)(2,1)S(1)}) custom-call(bf16[1024,128]{1,0:T(8,128)(2,1)S(1)} %get-tuple-element.119.left_ref.refs_5_, bf16[128,1024]{1,0:T(8,128)(2,1)S(1)} %bitcast.71, ...), custom_call_target="tpu_custom_call" | custom-call | tf_op jit(solution)/shard_map/middle/pallas_call | solution.py:897
  219.7 1.8 fusion.10
  221.5 0.4 multiply_convert_fusion.4.left_ref
  221.9 0.5 copy-done.1
  222.4 44.2 %turn.1 = (bf16[128,1024]{1,0:T(8,128)(2,1)S(1)}, bf16[1024,1024]{1,0:T(8,128)(2,1)S(1)}) custom-call(bf16[1024,384]{1,0:T(8,128)(2,1)S(1)} %multiply_convert_fusion.4.left_ref, bf16[384,1024]{1,0:T(8,128)(2,1)S(1)} %bitcast.79, f32[128,1024]{1,0:T(8,128)S(1)} %get-tuple-element.127.res_ref.hid_ref, bf16[128,1024]{1,0:T(8,128)(2,1)S(1)} %bitcast.69), custom_call_target="tpu_custom_call" | custom-call | tf_op jit(solution)/shard_map/turn/pallas_call | solution.py:897
  266.6 1.7 multiply_convert_fusion.3
  268.3 1.9 convolution_convert_fusion.1
  270.2 0.1 pad_maximum_fusion.left_ref
  270.4 1.0 convolution_convert_fusion.5
  271.4 48.1 %middle_back.2 = (f32[128,1024]{1,0:T(8,128)S(1)}, bf16[1024,1024]{1,0:T(8,128)(2,1)S(1)}, bf16[8,32,768]{2,1,0:T(8,128)(2,1)S(1)}, f32[96,1024]{1,0:T(8,128)S(1)}) custom-call(bf16[1024,768]{1,0:T(8,128)(2,1)S(1)} %pad_maximum_fusion.left_ref, bf16[1024,768]{1,0:T(8,128)(2,1)S(1)} %bitcast.66, bf16[128,1024]{1,0:T(8,128)(2,1)S(1)} %bitcast.70, ...), custom_call_target="tpu_custom_call" | custom-call | tf_op jit(solution)/shard_map/middle_back/pallas_call | solution.py:897
  319.5 0.7 copy-done.6
  320.2 20.6 %attend_back.2 = (bf16[1024,384]{1,0:T(8,128)(2,1)S(1)}, bf16[128,1024]{1,0:T(8,128)(2,1)S(1)}, bf16[8,32,768]{2,1,0:T(8,128)(2,1)S(1)}, f32[1024,128]{1,0:T(8,128)S(1)}) custom-call(bf16[1024,128]{1,0:T(8,128)(2,1)S(1)} %get-tuple-element.132.refs_0_, bf16[2,1024,128]{2,1,0:T(8,128)(2,1)S(1)} %get-tuple-element.133.refs_1_, ...), custom_call_target="tpu_custom_call" | custom-call | tf_op jit(solution)/shard_map/attend_back/pallas_call | solution.py:1644
  340.9 1.3 convolution_convert_fusion.4
  342.2 48.7 %layer_back.1 = (f32[128,1024]{1,0:T(8,128)S(1)}, bf16[1024,1024]{1,0:T(8,128)(2,1)S(1)}, bf16[8,32,384]{2,1,0:T(8,128)(2,1)S(1)}, f32[32,1024]{1,0:T(8,128)S(1)}) custom-call(bf16[1024,384]{1,0:T(8,128)(2,1)S(1)} %get-tuple-element.139.left_ref, bf16[1024,384]{1,0:T(8,128)(2,1)S(1)} %bitcast.59, f32[128,1024]{1,0:T(8,128)S(1)} %get-tuple-element.140.grad_ref, ...), custom_call_target="tpu_custom_call" | custom-call | tf_op jit(solution)/shard_map/layer_back/pallas_call | solution.py:897
  391.0 1.7 multiply_convert_fusion.1
  392.7 1.9 convolution_convert_fusion
  394.6 0.1 pad_maximum_fusion.1.left_ref
  394.7 1.0 convolution_convert_fusion.3
  395.8 49.7 %middle_back.3 = (f32[128,1024]{1,0:T(8,128)S(1)}, bf16[1024,1024]{1,0:T(8,128)(2,1)S(1)}, bf16[8,32,768]{2,1,0:T(8,128)(2,1)S(1)}, f32[96,1024]{1,0:T(8,128)S(1)}) custom-call(bf16[1024,768]{1,0:T(8,128)(2,1)S(1)} %pad_maximum_fusion.1.left_ref, bf16[1024,768]{1,0:T(8,128)(2,1)S(1)} %bitcast.64, f32[128,1024]{1,0:T(8,128)S(1)} %get-tuple-element.143.grad_ref, ...), custom_call_target="tpu_custom_call" | custom-call | tf_op jit(solution)/shard_map/middle_back/pallas_call | solution.py:897
  445.4 21.1 %attend_back.3 = (bf16[1024,384]{1,0:T(8,128)(2,1)S(1)}, bf16[128,1024]{1,0:T(8,128)(2,1)S(1)}, bf16[8,32,768]{2,1,0:T(8,128)(2,1)S(1)}, bf16[8,32,384]{2,1,0:T(8,128)(2,1)S(1)}) custom-call(bf16[1024,128]{1,0:T(8,128)(2,1)S(1)} %get-tuple-element.129.refs_0_, bf16[2,1024,128]{2,1,0:T(8,128)(2,1)S(1)} %get-tuple-element.130.refs_1_, ...), custom_call_target="tpu_custom_call" | custom-call | tf_op jit(solution)/shard_map/attend_back/pallas_call | solution.py:1644
  466.5 1.3 convolution_convert_fusion.2
  467.8 29.6 %last_back.1 = (bf16[128,1024]{1,0:T(8,128)(2,1)S(1)}, bf16[8,32,384]{2,1,0:T(8,128)(2,1)S(1)}, f32[32,1024]{1,0:T(8,128)S(1)}) custom-call(bf16[1024,384]{1,0:T(8,128)(2,1)S(1)} %get-tuple-element.149.left_ref, bf16[1024,512]{1,0:T(8,128)(2,1)S(1)} %bitcast.55, f32[128,1024]{1,0:T(8,128)S(1)} %get-tuple-element.150.grad_ref, ...), custom_call_target="tpu_custom_call" | custom-call | tf_op jit(solution)/shard_map/last_back/pallas_call | solution.py:897
  497.4 0.7 copy-done.17
  498.1 0.7 copy-done.20
  498.8 0.6 copy-done.24
  499.5 4.6 unpack.1
  (53 shorter events, 0.2 us)
Async XLA Ops:
  3.8 1.1 copy-start
  3.8 1.1 copy-start.2
  3.8 1.1 copy-start.3
  3.8 1.1 copy-start.4
  3.8 1.2 copy-start.5
  3.8 1.2 copy-start.10
  3.8 1.2 copy-start.11
  3.9 1.2 copy-start.12
  3.9 1.2 copy-start.13
  3.9 1.2 copy-start.14
  3.9 1.2 copy-start.15
  3.9 1.2 copy-start.18
  3.9 1.3 copy-start.21
  3.9 1.4 copy-start.22
  3.9 1.4 copy-start.25
  4.0 1.3 copy-start.26
  4.0 1.3 copy-start.27
  4.0 1.3 copy-start.28
  4.0 1.3 copy-start.29
  221.5 1.0 copy-start.1
  266.6 1.7 copy-start.16
  319.5 0.7 copy-start.6
  340.9 1.3 copy-start.7
  390.9 1.7 copy-start.23
  445.4 21.1 %copy-start.8 = (f32[96,1024]{1,0:T(8,128)}, f32[96,1024]{1,0:T(8,128)S(1)}, u32[]{:S(2)}) copy-start(f32[96,1024]{1,0:T(8,128)S(1)} %get-tuple-element.155.every_3_) | copy-start | bytes 1179652
  466.5 1.3 copy-start.9
  466.5 1.3 copy-start.19
  497.4 0.7 copy-start.17
  498.1 0.7 copy-start.20
  498.8 0.6 copy-start.24

commit v8 on v7

--- a/solution.py
+++ b/solution.py
@@ -658,6 +658,15 @@
             value = self.product(2 * block + self.y)
             self.acc[block] = value[:HALF]
             self.acc[4 + block] = value[HALF:]
+
+            @pl.when((self.own == 0) & (near == 3))
+            def _():
+                self.pass_on(value[HALF:], True, 4 + block, 1, True)
+
+            @pl.when((self.own == 1) & (near == 0))
+            def _():
+                self.pass_on(value[HALF:], False, 4 + block, 0, False)
+
             return carry
 
         lax.fori_loop(0, 4, other_row, 0)
@@ -691,12 +700,14 @@
 
     def relays(self, inner, live):
         if inner:
-            self.relay(1, 0, inner, live, True)
+            if not live:
+                self.relay(1, 0, inner, live, True)
             self.relay(1, 3, inner, live, True)
             for half, near in ((0, 3), (0, 0), (0, 2), (1, 2)):
                 self.relay(half, near, inner, live)
             return
-        self.relay(1, 3, inner, live, True)
+        if not live:
+            self.relay(1, 3, inner, live, True)
         for half, near in ((0, 3), (0, 2), (1, 2), (0, 1), (1, 1)):
             self.relay(half, near, inner, live)
         slot = self.slot(1, 0)
@@ -871,9 +882,10 @@
 def turn_kernel(left_ref, right_ref, res_ref, cot_ref, out_ref, full_ref, *scratch):
     def settle(half, total):
         out_ref[half_rows(half), :] = (res_ref[half_rows(half), :] + total).astype(BF)
+        return cot_ref[half_rows(half), :]
 
     product = make_product(left_ref, right_ref, False)
-    exchange(plane_place(), product, settle, full_ref, scratch, None, cot_ref[...])
+    exchange(plane_place(), product, settle, full_ref, scratch)
 
 
 def back_rows(total, grad, hidden, gain):

time: 513 us -> 514 us (level)
  no operation moved by 1% of the time
where the time goes in v8:
time: 514 us; the launch traced here: 506 us
  Pallas kernels  480 us (93%)
  matrix products  15.4 us (3%)
    pallas_call x8, Pallas kernels, comm_call(): pl.pallas_call(kernel, out_shape=[jax.ShapeDtypeStruct(*o) for o in outs]...  359 us
    pallas_call x2, Pallas kernels, attend_backward(): pl.pallas_call(functools.partial(attend_back_kernel, layer), out_shape=[j...  43.1 us
    pallas_call x1, Pallas kernels, begin_call(): pl.pallas_call(begin_kernel, out_shape=[jax.ShapeDtypeStruct(*o) for o in...  38.3 us
    pallas_call x2, Pallas kernels, attend(): pl.pallas_call(functools.partial(attend_kernel, layer), out_shape=[jax.Sh...  34.3 us

profile of v8, /device:TPU:0, one launch (start us, length us, event | category | flops | bytes accessed | tf_op | source)
XLA Modules:
  0.0 505.5 jit_solution(5746518816726452851)
XLA Ops:
  0.7 0.8 select_reduce_fusion
  1.5 0.1 reshape_reshape.7
  1.6 0.1 reshape_reshape.6
  1.7 0.1 convert_element_type.61.refs_6_.refs_8_
  1.8 0.1 convert_element_type.59.refs_5_.refs_7_
  1.9 1.9 fusion
  4.0 0.9 pad_maximum_fusion.2
  4.9 0.0 copy-done.4
  5.0 0.1 copy-done.5
  5.0 0.0 copy-done.13
  5.0 0.0 copy-done.14
  5.1 0.0 copy-done.15
  5.1 0.0 copy-done.18
  5.1 0.1 copy-done.21
  5.2 0.1 copy-done.22
  5.3 38.3 %begin.1 = (bf16[1024,1024]{1,0:T(8,128)(2,1)S(1)}, bf16[2,8,2,32,512]{4,3,2,1,0:T(8,128)(2,1)S(1)}, bf16[4,32,1024]{2,1,0:T(8,128)(2,1)S(1)}, f32[8,1024]{1,0:T...) custom-call(bf16[128,1024]{1,0:T(8,128)(2,1)S(1)} %bitcast.60, ...), custom_call_target="tpu_custom_call" | custom-call | tf_op jit(solution)/shard_map/begin/pallas_call | solution.py:1221
  43.6 18.6 %attend.2 = (bf16[1024,128]{1,0:T(8,128)(2,1)S(1)}, bf16[2,1024,128]{2,1,0:T(8,128)(2,1)S(1)}, bf16[2,1024,128]{2,1,0:T(8,128)(2,1)S(1)}, bf16[1024,128]{1,0:T(8...) custom-call(bf16[1024,1024]{1,0:T(8,128)(2,1)S(1)} %get-tuple-elemen, ...), custom_call_target="tpu_custom_call" | custom-call | tf_op jit(solution)/shard_map/attend/pallas_call | solution.py:1549
  62.2 48.7 %middle.2 = (f32[128,1024]{1,0:T(8,128)S(1)}, bf16[1024,1024]{1,0:T(8,128)(2,1)S(1)}, bf16[2,8,2,32,768]{4,3,2,1,0:T(8,128)(2,1)S(1)}, bf16[2,8,2,32,384]{4,3,2,...) custom-call(bf16[1024,128]{1,0:T(8,128)(2,1)S(1)} %get-tuple-element.106.left_ref.refs_5_, ...), custom_call_target="tpu_custom_call" | custom-call | tf_op jit(solution)/shard_map/middle/pallas_call | solution.py:909
  111.0 1.8 fusion.9
  112.8 0.5 multiply_convert_fusion.5.left_ref
  113.2 43.9 %result.1 = (f32[128,1024]{1,0:T(8,128)S(1)}, bf16[1024,1024]{1,0:T(8,128)(2,1)S(1)}) custom-call(bf16[1024,384]{1,0:T(8,128)(2,1)S(1)} %multiply_convert_fusion.5.left_ref, bf16[384,1024]{1,0:T(8,128)(2,1)S(1)} %bitcast.77, f32[128,1024]{1,0:T(8,128)S(1)} %get-tuple-element.114.res_ref.hid_ref, f32[8,1024]{1,0:T(8,128)S(1)} %get-tuple-element.103.refs_4_.gain_ref), custom_call_target="tpu_custom_call" | custom-call | tf_op jit(solution)/shard_map/result/pallas_call | solution.py:909
  157.1 15.7 %attend.3 = (bf16[1024,128]{1,0:T(8,128)(2,1)S(1)}, bf16[2,1024,128]{2,1,0:T(8,128)(2,1)S(1)}, bf16[2,1024,128]{2,1,0:T(8,128)(2,1)S(1)}, bf16[1024,128]{1,0:T(8...) custom-call(bf16[1024,1024]{1,0:T(8,128)(2,1)S(1)} %get-tuple-element.115.refs_0_, ...), custom_call_target="tpu_custom_call" | custom-call | tf_op jit(solution)/shard_map/attend/pallas_call | solution.py:1549
  172.8 46.8 %middle.3 = (f32[128,1024]{1,0:T(8,128)S(1)}, bf16[1024,1024]{1,0:T(8,128)(2,1)S(1)}, bf16[2,8,2,32,768]{4,3,2,1,0:T(8,128)(2,1)S(1)}, bf16[4,96,1024]{2,1,0:T(8,128)(2,1)S(1)}) custom-call(bf16[1024,128]{1,0:T(8,128)(2,1)S(1)} %get-tuple-element.119.left_ref.refs_5_, bf16[128,1024]{1,0:T(8,128)(2,1)S(1)} %bitcast.71, ...), custom_call_target="tpu_custom_call" | custom-call | tf_op jit(solution)/shard_map/middle/pallas_call | solution.py:909
  219.7 1.8 fusion.10
  221.5 0.4 multiply_convert_fusion.4.left_ref
  221.9 0.5 copy-done.1
  222.4 45.3 %turn.1 = (bf16[128,1024]{1,0:T(8,128)(2,1)S(1)}, bf16[1024,1024]{1,0:T(8,128)(2,1)S(1)}) custom-call(bf16[1024,384]{1,0:T(8,128)(2,1)S(1)} %multiply_convert_fusion.4.left_ref, bf16[384,1024]{1,0:T(8,128)(2,1)S(1)} %bitcast.79, f32[128,1024]{1,0:T(8,128)S(1)} %get-tuple-element.127.res_ref.hid_ref, bf16[128,1024]{1,0:T(8,128)(2,1)S(1)} %bitcast.69), custom_call_target="tpu_custom_call" | custom-call | tf_op jit(solution)/shard_map/turn/pallas_call | solution.py:909
  267.7 1.7 multiply_convert_fusion.3
  269.4 1.9 convolution_convert_fusion.1
  271.4 0.1 pad_maximum_fusion.left_ref
  271.5 1.0 convolution_convert_fusion.5
  272.5 47.9 %middle_back.2 = (f32[128,1024]{1,0:T(8,128)S(1)}, bf16[1024,1024]{1,0:T(8,128)(2,1)S(1)}, bf16[8,32,768]{2,1,0:T(8,128)(2,1)S(1)}, f32[96,1024]{1,0:T(8,128)S(1)}) custom-call(bf16[1024,768]{1,0:T(8,128)(2,1)S(1)} %pad_maximum_fusion.left_ref, bf16[1024,768]{1,0:T(8,128)(2,1)S(1)} %bitcast.66, bf16[128,1024]{1,0:T(8,128)(2,1)S(1)} %bitcast.70, ...), custom_call_target="tpu_custom_call" | custom-call | tf_op jit(solution)/shard_map/middle_back/pallas_call | solution.py:909
  320.4 0.7 copy-done.6
  321.2 22.0 %attend_back.2 = (bf16[1024,384]{1,0:T(8,128)(2,1)S(1)}, bf16[128,1024]{1,0:T(8,128)(2,1)S(1)}, bf16[8,32,768]{2,1,0:T(8,128)(2,1)S(1)}, f32[1024,128]{1,0:T(8,128)S(1)}) custom-call(bf16[1024,128]{1,0:T(8,128)(2,1)S(1)} %get-tuple-element.132.refs_0_, bf16[2,1024,128]{2,1,0:T(8,128)(2,1)S(1)} %get-tuple-element.133.refs_1_, ...), custom_call_target="tpu_custom_call" | custom-call | tf_op jit(solution)/shard_map/attend_back/pallas_call | solution.py:1656
  343.2 1.3 convolution_convert_fusion.4
  344.5 48.6 %layer_back.1 = (f32[128,1024]{1,0:T(8,128)S(1)}, bf16[1024,1024]{1,0:T(8,128)(2,1)S(1)}, bf16[8,32,384]{2,1,0:T(8,128)(2,1)S(1)}, f32[32,1024]{1,0:T(8,128)S(1)}) custom-call(bf16[1024,384]{1,0:T(8,128)(2,1)S(1)} %get-tuple-element.139.left_ref, bf16[1024,384]{1,0:T(8,128)(2,1)S(1)} %bitcast.59, f32[128,1024]{1,0:T(8,128)S(1)} %get-tuple-element.140.grad_ref, ...), custom_call_target="tpu_custom_call" | custom-call | tf_op jit(solution)/shard_map/layer_back/pallas_call | solution.py:909
  393.0 1.7 multiply_convert_fusion.1
  394.8 1.9 convolution_convert_fusion
  396.7 0.1 pad_maximum_fusion.1.left_ref
  396.8 1.0 convolution_convert_fusion.3
  397.9 48.8 %middle_back.3 = (f32[128,1024]{1,0:T(8,128)S(1)}, bf16[1024,1024]{1,0:T(8,128)(2,1)S(1)}, bf16[8,32,768]{2,1,0:T(8,128)(2,1)S(1)}, f32[96,1024]{1,0:T(8,128)S(1)}) custom-call(bf16[1024,768]{1,0:T(8,128)(2,1)S(1)} %pad_maximum_fusion.1.left_ref, bf16[1024,768]{1,0:T(8,128)(2,1)S(1)} %bitcast.64, f32[128,1024]{1,0:T(8,128)S(1)} %get-tuple-element.143.grad_ref, ...), custom_call_target="tpu_custom_call" | custom-call | tf_op jit(solution)/shard_map/middle_back/pallas_call | solution.py:909
  446.7 21.1 %attend_back.3 = (bf16[1024,384]{1,0:T(8,128)(2,1)S(1)}, bf16[128,1024]{1,0:T(8,128)(2,1)S(1)}, bf16[8,32,768]{2,1,0:T(8,128)(2,1)S(1)}, bf16[8,32,384]{2,1,0:T(8,128)(2,1)S(1)}) custom-call(bf16[1024,128]{1,0:T(8,128)(2,1)S(1)} %get-tuple-element.129.refs_0_, bf16[2,1024,128]{2,1,0:T(8,128)(2,1)S(1)} %get-tuple-element.130.refs_1_, ...), custom_call_target="tpu_custom_call" | custom-call | tf_op jit(solution)/shard_map/attend_back/pallas_call | solution.py:1656
  467.8 1.3 convolution_convert_fusion.2
  469.1 29.2 %last_back.1 = (bf16[128,1024]{1,0:T(8,128)(2,1)S(1)}, bf16[8,32,384]{2,1,0:T(8,128)(2,1)S(1)}, f32[32,1024]{1,0:T(8,128)S(1)}) custom-call(bf16[1024,384]{1,0:T(8,128)(2,1)S(1)} %get-tuple-element.149.left_ref, bf16[1024,512]{1,0:T(8,128)(2,1)S(1)} %bitcast.55, f32[128,1024]{1,0:T(8,128)S(1)} %get-tuple-element.150.grad_ref, ...), custom_call_target="tpu_custom_call" | custom-call | tf_op jit(solution)/shard_map/last_back/pallas_call | solution.py:909
  498.4 0.7 copy-done.17
  499.1 0.7 copy-done.20
  499.7 0.6 copy-done.24
  500.4 4.6 unpack.1
  (53 shorter events, 0.2 us)
Async XLA Ops:
  3.8 1.1 copy-start
  3.8 1.1 copy-start.2
  3.8 1.1 copy-start.3
  3.8 1.1 copy-start.4
  3.8 1.2 copy-start.5
  3.8 1.2 copy-start.10
  3.8 1.2 copy-start.11
  3.9 1.2 copy-start.12
  3.9 1.2 copy-start.13
  3.9 1.2 copy-start.14
  3.9 1.2 copy-start.15
  3.9 1.2 copy-start.18
  3.9 1.3 copy-start.21
  3.9 1.4 copy-start.22
  3.9 1.4 copy-start.25
  4.0 1.3 copy-start.26
  4.0 1.3 copy-start.27
  4.0 1.3 copy-start.28
  4.0 1.3 copy-start.29
  221.5 1.0 copy-start.1
  267.7 1.7 copy-start.16
  320.4 0.7 copy-start.6
  343.2 1.3 copy-start.7
  393.0 1.7 copy-start.23
  446.7 21.1 %copy-start.8 = (f32[96,1024]{1,0:T(8,128)}, f32[96,1024]{1,0:T(8,128)S(1)}, u32[]{:S(2)}) copy-start(f32[96,1024]{1,0:T(8,128)S(1)} %get-tuple-element.155.every_3_) | copy-start | bytes 1179652
  467.8 1.3 copy-start.9
  467.8 1.3 copy-start.19
  498.4 0.7 copy-start.17
  499.1 0.7 copy-start.20
  499.7 0.6 copy-start.24
